TPU v7x, 32 devices: a whole 2x2x4 slice. The times are simulated.
32 devices in a mesh: dp: 8 (over z, x), tensor: 4 (over y, core).
Axes of the slice: x: 2, y: 2, z: 4, core: 2. Of those that a mesh axis runs over, the one named last changes fastest.
Arguments:
- features: bfloat16 [32768, 768], P(('dp', 'tensor')), may hold values from -6 to 6
- first_gain: bfloat16 [768], replicated, may hold values from 0.5 to 1.5
- first_shift: bfloat16 [768], replicated, may hold values from -2 to 2
- qkv_weight: bfloat16 [768, 3, 768], P('dp', None, 'tensor'), may hold values from -0.21875 to 0.21875
- qv_bias: bfloat16 [2, 768], P(None, 'tensor'), may hold values from -1.1953125 to 1.1953125
- rel_height: bfloat16 [27, 64], replicated, may hold values from -0.59765625 to 0.59765625
- rel_width: bfloat16 [27, 64], replicated, may hold values from -0.59765625 to 0.59765625
- output_weight: bfloat16 [768, 768], P('dp', 'tensor'), may hold values from -1.25 to 1.25
- output_bias: bfloat16 [768], replicated, may hold values from -2 to 2
- second_gain: bfloat16 [768], replicated, may hold values from 0.5 to 1.5
- second_shift: bfloat16 [768], replicated, may hold values from -2 to 2
- up_weight: bfloat16 [768, 3072], P('dp', 'tensor'), may hold values from -0.21875 to 0.21875
- up_bias: bfloat16 [3072], P('tensor'), may hold values from -2 to 2
- down_weight: bfloat16 [768, 3072], P('dp', 'tensor'), may hold values from -0.109375 to 0.109375
- down_bias: bfloat16 [768], replicated, may hold values from -2 to 2
- cotangent: bfloat16 [32768, 768], P(('dp', 'tensor')), may hold values from -6 to 6
Outputs:
- output: bfloat16 [32768, 768], P(('dp', 'tensor'))
- grad_features: bfloat16 [32768, 768], P(('dp', 'tensor'))
- grad_first_gain: float32 [768], replicated
- grad_first_shift: float32 [768], replicated
- grad_qkv_weight: float32 [768, 3, 768], P('dp', None, 'tensor')
- grad_qv_bias: float32 [2, 768], P(None, 'tensor')
- grad_rel_height: float32 [27, 64], replicated
- grad_rel_width: float32 [27, 64], replicated
- grad_output_weight: float32 [768, 768], P('dp', 'tensor')
- grad_output_bias: float32 [768], replicated
- grad_second_gain: float32 [768], replicated
- grad_second_shift: float32 [768], replicated
- grad_up_weight: float32 [768, 3072], P('dp', 'tensor')
- grad_up_bias: float32 [3072], P('tensor')
- grad_down_weight: float32 [768, 3072], P('dp', 'tensor')
- grad_down_bias: float32 [768], replicated
All inputs are finite; a program needn't handle non-finite values.
Results may differ from a plain program's by a relative error of at most 0.015.
Values may be sent and summed in bfloat16 or wider, within the bound.
No kernel may reach another device: no remote copies, remote signals or barrier semaphores. Data moves between devices by JAX's collectives and lax.ppermute only.
A program may use at most 192 MiB of HBM per device.

v0:
```python
from functools import partial
import math

import jax
import jax.numpy as jnp
from jax import lax
from jax.sharding import PartitionSpec as P

D = 768
HD = 64
GRID = 64
WIN = 14
SIDE = 5


EPSILON = 1e-06
HIGH = lax.Precision.HIGHEST


def norm_parts(value):
    mean_value = jnp.mean(value, -1, keepdims=True)
    centered = value - mean_value
    inverse_deviation = lax.rsqrt(jnp.mean(centered * centered, -1, keepdims=True) + EPSILON)
    return (centered * inverse_deviation, inverse_deviation)


def norm_backward(upstream_gradient, normalized_input, inverse_deviation, gain_factor):
    scaled_input = upstream_gradient * gain_factor
    inner_product = (
        scaled_input
        - jnp.mean(scaled_input, -1, keepdims=True)
        - normalized_input * jnp.mean(scaled_input * normalized_input, -1, keepdims=True)
    )
    return (
        inverse_deviation * inner_product,
        jnp.sum(upstream_gradient * normalized_input, 0),
        jnp.sum(upstream_gradient, 0),
    )


def to_windows(flat, images):
    width = flat.shape[-1]
    extra = SIDE * WIN - GRID
    grid = jnp.pad(
        flat.reshape(images, GRID, GRID, width), ((0, 0), (0, extra), (0, extra), (0, 0))
    )
    grid = grid.reshape(images, SIDE, WIN, SIDE, WIN, width).transpose(0, 1, 3, 2, 4, 5)
    return grid.reshape(images * SIDE * SIDE, WIN * WIN, width)


def from_windows(windows, images):
    width = windows.shape[-1]
    grid = windows.reshape(images, SIDE, SIDE, WIN, WIN, width).transpose(0, 1, 3, 2, 4, 5)
    grid = grid.reshape(images, SIDE * WIN, SIDE * WIN, width)
    return grid[:, :GRID, :GRID].reshape(images * GRID * GRID, width)


def offset_table():
    offsets = jnp.arange(WIN)[:, None] - jnp.arange(WIN)[None, :] + WIN - 1
    return (offsets[:, :, None] == jnp.arange(2 * WIN - 1)[None, None, :]).astype(jnp.float32)


def spread_table():
    places = jnp.arange(WIN * WIN)
    marks = jnp.arange(WIN)[:, None]
    row_part = places[None, :] // WIN == marks
    col_part = places[None, :] % WIN == marks
    return jnp.concatenate([row_part, col_part], 0).astype(jnp.float32)


def contract_first(left, right):
    return lax.dot_general(
        left, right, (((0,), (0,)), ((), ())), preferred_element_type=jnp.float32
    )


def contract_last(left, right):
    return lax.dot_general(
        left, right, (((1,), (1,)), ((), ())), preferred_element_type=jnp.float32
    )


def scores_of(query, keys, table_rows, table_cols, spread):
    blocks, heads = (query.shape[0], query.shape[2])
    scores = jnp.einsum(
        "nqhc,nkhc->nhqk", query, keys, preferred_element_type=jnp.float32
    ) * HD ** (-0.5)
    query_grid = query.reshape(blocks, WIN, WIN, heads, HD)
    along_rows = jnp.einsum(
        "nabhc,akc->nhabk", query_grid, table_rows, preferred_element_type=jnp.float32
    )
    along_cols = jnp.einsum(
        "nabhc,bkc->nhabk", query_grid, table_cols, preferred_element_type=jnp.float32
    )
    along = jnp.concatenate([along_rows, along_cols], -1).reshape(blocks, heads, WIN * WIN, 2 * WIN)
    return scores + jnp.einsum("nhqj,jk->nhqk", along, spread, precision=HIGH)


def attend(tables, block):
    scores = scores_of(block[:, :, 0], block[:, :, 1], tables[0], tables[1], tables[2])
    largest = jnp.max(scores, -1, keepdims=True)
    log_total = largest + jnp.log(jnp.sum(jnp.exp(scores - largest), -1, keepdims=True))
    probs = jnp.exp(scores - log_total).astype(jnp.bfloat16)
    attended = jnp.einsum(
        "nhqk,nkhc->nqhc", probs, block[:, :, 2], preferred_element_type=jnp.float32
    )
    return (attended.astype(jnp.bfloat16), log_total)


def attend_back(tables, carry, items):
    block, upstream_gradient, log_total = items
    query, keys, values = (block[:, :, 0], block[:, :, 1], block[:, :, 2])
    blocks, heads = (query.shape[0], query.shape[2])
    probs = jnp.exp(scores_of(query, keys, tables[0], tables[1], tables[2]) - log_total)
    grad_values = jnp.einsum(
        "nhqk,nqhc->nkhc",
        probs.astype(jnp.bfloat16),
        upstream_gradient,
        preferred_element_type=jnp.float32,
    )
    grad_probs = jnp.einsum(
        "nqhc,nkhc->nhqk", upstream_gradient, values, preferred_element_type=jnp.float32
    )
    grad_scores = (probs * (grad_probs - jnp.sum(probs * grad_probs, -1, keepdims=True))).astype(
        jnp.bfloat16
    )
    grad_query = jnp.einsum(
        "nhqk,nkhc->nqhc", grad_scores, keys, preferred_element_type=jnp.float32
    ) * HD ** (-0.5)
    grad_keys = jnp.einsum(
        "nhqk,nqhc->nkhc", grad_scores, query, preferred_element_type=jnp.float32
    ) * HD ** (-0.5)
    key_sums = jnp.einsum(
        "nhqk,jk->nhqj", grad_scores, tables[3], preferred_element_type=jnp.float32
    )
    key_sums = key_sums.reshape(blocks, heads, WIN, WIN, 2 * WIN)
    sum_rows = key_sums[..., :WIN]
    sum_cols = key_sums[..., WIN:]
    rows_float = tables[0].astype(jnp.float32)
    cols_float = tables[1].astype(jnp.float32)
    extra = jnp.einsum("nhabk,akc->nabhc", sum_rows, rows_float, precision=HIGH)
    extra = extra + jnp.einsum("nhabk,bkc->nabhc", sum_cols, cols_float, precision=HIGH)
    grad_query = grad_query + extra.reshape(blocks, WIN * WIN, heads, HD)
    query_float = query.astype(jnp.float32).reshape(blocks, WIN, WIN, heads, HD)
    table_grad_rows = carry[0] + jnp.einsum(
        "nhabk,nabhc->akc", sum_rows, query_float, precision=HIGH
    )
    table_grad_cols = carry[1] + jnp.einsum(
        "nhabk,nabhc->bkc", sum_cols, query_float, precision=HIGH
    )
    grads = jnp.stack([grad_query, grad_keys, grad_values], axis=2).astype(jnp.bfloat16)
    return ((table_grad_rows, table_grad_cols), grads)


def gelu_slope(upper):
    return 0.5 * (1.0 + lax.erf(upper / math.sqrt(2.0))) + upper * jnp.exp(
        -0.5 * upper * upper
    ) / math.sqrt(2.0 * math.pi)


def feed_rows(normed, up_full, up_shift, down_full):
    upper = jnp.dot(normed, up_full, preferred_element_type=jnp.float32) + up_shift
    active = jax.nn.gelu(upper, approximate=False).astype(jnp.bfloat16)
    return contract_last(active, down_full)


def feed_back_rows(normed, grads, up_full, up_shift, down_full, block):
    steps = normed.shape[0] // block
    hidden = up_full.shape[1]

    def step(carry, items):
        part_in, part_grad = items
        upper = jnp.dot(part_in, up_full, preferred_element_type=jnp.float32) + up_shift
        active = jax.nn.gelu(upper, approximate=False).astype(jnp.bfloat16)
        slope = jnp.dot(part_grad, down_full, preferred_element_type=jnp.float32)
        delta = (slope * gelu_slope(upper)).astype(jnp.bfloat16)
        grad_up = carry[0] + contract_first(part_in, delta)
        grad_down = carry[1] + contract_first(part_grad, active)
        grad_shift = carry[2] + jnp.sum(delta.astype(jnp.float32), 0)
        return ((grad_up, grad_down, grad_shift), delta)

    start_carry = (
        jnp.zeros((D, hidden), jnp.float32),
        jnp.zeros((D, hidden), jnp.float32),
        jnp.zeros((hidden,), jnp.float32),
    )
    carry, deltas = lax.scan(
        step, start_carry, (normed.reshape(steps, block, D), grads.reshape(steps, block, D))
    )
    return (deltas.reshape(steps * block, hidden), carry[0], carry[1], carry[2])


def body(
    features,
    first_gain,
    first_shift,
    qkv_weight,
    qv_bias,
    rel_height,
    rel_width,
    output_weight,
    output_bias,
    second_gain,
    second_shift,
    up_weight,
    up_bias,
    down_weight,
    down_bias,
    cotangent,
):
    qkv_full, output_full, up_full, down_full = (
        lax.all_gather(qkv_weight, "dp", axis=0, tiled=True),
        lax.all_gather(output_weight, "dp", axis=0, tiled=True),
        lax.all_gather(up_weight, "dp", axis=0, tiled=True),
        lax.all_gather(down_weight, "dp", axis=0, tiled=True),
    )
    local_width = qkv_weight.shape[2]
    heads_here = local_width // HD
    own_rows = features.shape[0]
    gain_one = first_gain.astype(jnp.float32)
    gain_two = second_gain.astype(jnp.float32)
    feature_float = features.astype(jnp.float32)
    hat_one, inverse_one = norm_parts(feature_float)
    normed_one = (hat_one * gain_one + first_shift.astype(jnp.float32)).astype(jnp.bfloat16)
    normed_all = lax.all_gather(normed_one, "tensor", axis=0, tiled=True)
    images = normed_all.shape[0] // (GRID * GRID)
    normed_windows = to_windows(normed_all, images)
    bias_float = qv_bias.astype(jnp.float32)
    bias_all = jnp.stack([bias_float[0], jnp.zeros_like(bias_float[0]), bias_float[1]]).reshape(
        3 * local_width
    )
    qkv_matrix = qkv_full.reshape(D, 3 * local_width)
    qkv = (
        jnp.dot(normed_windows.reshape(-1, D), qkv_matrix, preferred_element_type=jnp.float32)
        + bias_all
    )
    qkv = qkv.astype(jnp.bfloat16).reshape(images * SIDE, SIDE, WIN * WIN, 3, heads_here, HD)
    onehot = offset_table()
    onehot_low = onehot.astype(jnp.bfloat16)
    spread = spread_table()
    table_rows = jnp.einsum(
        "akr,rc->akc", onehot_low, rel_height, preferred_element_type=jnp.float32
    ).astype(jnp.bfloat16)
    table_cols = jnp.einsum(
        "akr,rc->akc", onehot_low, rel_width, preferred_element_type=jnp.float32
    ).astype(jnp.bfloat16)
    tables = (table_rows, table_cols, spread, spread.astype(jnp.bfloat16))
    attended, log_total = lax.map(partial(attend, tables), qkv)
    on_grid = from_windows(attended.reshape(images * SIDE * SIDE, WIN * WIN, local_width), images)
    branch = lax.psum_scatter(
        contract_last(on_grid, output_full), "tensor", scatter_dimension=0, tiled=True
    )
    branch = branch + output_bias.astype(jnp.float32)
    hidden_one = feature_float + branch
    hat_two, inverse_two = norm_parts(hidden_one)
    normed_two = (hat_two * gain_two + second_shift.astype(jnp.float32)).astype(jnp.bfloat16)
    up_shift = up_bias.astype(jnp.float32)
    normed_two_all = lax.all_gather(normed_two, "tensor", axis=0, tiled=True)
    feed = lax.psum_scatter(
        feed_rows(normed_two_all, up_full, up_shift, down_full).astype(jnp.bfloat16),
        "tensor",
        scatter_dimension=0,
        tiled=True,
    ).astype(jnp.float32)
    grads_all = lax.all_gather(cotangent, "tensor", axis=0, tiled=True)
    deltas, grad_up, grad_down, grad_up_shift = feed_back_rows(
        normed_two_all, grads_all, up_full, up_shift, down_full, own_rows
    )
    grad_normed_two = lax.psum_scatter(
        contract_last(deltas, up_full), "tensor", scatter_dimension=0, tiled=True
    )
    output = (hidden_one + feed + down_bias.astype(jnp.float32)).astype(jnp.bfloat16)
    grad_float = cotangent.astype(jnp.float32)
    grad_down_shift = jnp.sum(grad_float, 0)
    back_two, grad_gain_two, grad_shift_two = norm_backward(
        grad_normed_two, hat_two, inverse_two, gain_two
    )
    grad_hidden_one = grad_float + back_two
    grad_branch = grad_hidden_one.astype(jnp.bfloat16)
    grad_output_shift = jnp.sum(grad_branch.astype(jnp.float32), 0)
    grad_branch_all = lax.all_gather(grad_branch, "tensor", axis=0, tiled=True)
    grad_output = contract_first(grad_branch_all, on_grid)
    grad_on_grid = jnp.dot(grad_branch_all, output_full, preferred_element_type=jnp.float32).astype(
        jnp.bfloat16
    )
    grad_windows = to_windows(grad_on_grid, images).reshape(
        images * SIDE, SIDE, WIN * WIN, heads_here, HD
    )
    zero_table = jnp.zeros((WIN, WIN, HD), jnp.float32)
    table_grads, grad_qkv = lax.scan(
        partial(attend_back, tables), (zero_table, zero_table), (qkv, grad_windows, log_total)
    )
    grad_qkv = grad_qkv.reshape(images * SIDE * SIDE, WIN * WIN, 3 * local_width)
    shift_sums = jnp.sum(grad_qkv.astype(jnp.float32), (0, 1)).reshape(3, local_width)
    grad_qv_shift = jnp.stack([shift_sums[0], shift_sums[2]])
    grad_qkv_grid = from_windows(grad_qkv, images)
    grad_qkv_weight = contract_first(normed_all, grad_qkv_grid).reshape(D, 3, local_width)
    grad_normed_one = lax.psum_scatter(
        contract_last(grad_qkv_grid, qkv_matrix).astype(jnp.bfloat16),
        "tensor",
        scatter_dimension=0,
        tiled=True,
    ).astype(jnp.float32)
    grad_rel_rows = jnp.einsum("akr,akc->rc", onehot, table_grads[0], precision=HIGH)
    grad_rel_cols = jnp.einsum("akr,akc->rc", onehot, table_grads[1], precision=HIGH)
    back_one, grad_gain_one, grad_shift_one = norm_backward(
        grad_normed_one, hat_one, inverse_one, gain_one
    )
    grad_features = (grad_hidden_one + back_one).astype(jnp.bfloat16)
    grad_qkv_weight, grad_output, grad_up, grad_down = (
        lax.psum_scatter(grad_qkv_weight, "dp", scatter_dimension=0, tiled=True),
        lax.psum_scatter(grad_output, "dp", scatter_dimension=0, tiled=True),
        lax.psum_scatter(grad_up, "dp", scatter_dimension=0, tiled=True),
        lax.psum_scatter(grad_down, "dp", scatter_dimension=0, tiled=True),
    )
    (
        grad_gain_one,
        grad_shift_one,
        grad_gain_two,
        grad_shift_two,
        grad_output_shift,
        grad_down_shift,
        grad_rel_rows,
        grad_rel_cols,
    ) = lax.psum(
        (
            grad_gain_one,
            grad_shift_one,
            grad_gain_two,
            grad_shift_two,
            grad_output_shift,
            grad_down_shift,
            grad_rel_rows,
            grad_rel_cols,
        ),
        ("dp", "tensor"),
    )
    grad_qv_shift, grad_up_shift = lax.psum((grad_qv_shift, grad_up_shift), "dp")
    return (
        output,
        grad_features,
        grad_gain_one,
        grad_shift_one,
        grad_qkv_weight,
        grad_qv_shift,
        grad_rel_rows,
        grad_rel_cols,
        grad_output,
        grad_output_shift,
        grad_gain_two,
        grad_shift_two,
        grad_up,
        grad_up_shift,
        grad_down,
        grad_down_shift,
    )


def solution(mesh):
    placed = (
        P(("dp", "tensor"), None),
        P(),
        P(),
        P("dp", None, "tensor"),
        P(None, "tensor"),
        P(),
        P(),
        P("dp", "tensor"),
        P(),
        P(),
        P(),
        P("dp", "tensor"),
        P("tensor"),
        P("dp", "tensor"),
        P(),
        P(("dp", "tensor"), None),
    )
    return jax.shard_map(
        body,
        mesh=mesh,
        in_specs=placed,
        out_specs=(
            P(("dp", "tensor"), None),
            P(("dp", "tensor"), None),
            P(),
            P(),
            P("dp", None, "tensor"),
            P(None, "tensor"),
            P(),
            P(),
            P("dp", "tensor"),
            P(),
            P(),
            P(),
            P("dp", "tensor"),
            P("tensor"),
            P("dp", "tensor"),
            P(),
        ),
        check_vma=False,
    )
```

profile of v0, /device:TPU:0, one launch (start us, length us, event | category | flops | bytes accessed | tf_op | source)
XLA Modules:
  0.0 1442.5 jit_solution(18093629953301397693)
XLA Ops:
  14.9 38.8 %all_gather.25 = bf16[768,3,192]{2,1,0:T(4,128)(2,1)S(1)} all-gather(bf16[96,3,192]{2,1,0:T(4,128)(2,1)S(1)} %copy.162), channel_id=1, replica_groups=mesh['dp'=8,'tensor'=4] {'dp'}, dimensions={0}, use_global_device_ids=true | all-gather | bytes 995328 | tf_op jit(solution)/shard_map/all_gather | solution.py:212
  55.4 33.1 %all_gather.26 = bf16[768,192]{1,0:T(8,128)(2,1)} all-gather(bf16[96,192]{1,0:T(8,128)(2,1)S(1)} %copy-done.48), channel_id=1, replica_groups=mesh['dp'=8,'tensor'=4] {'dp'}, dimensions={0}, use_global_device_ids=true | all-gather | bytes 331776 | tf_op jit(solution)/shard_map/all_gather | solution.py:213
  89.0 6.5 pad.8
  95.5 11.5 reshape.269
  107.0 7.8 copy.161
  114.8 12.2 reshape_reshape.12
  127.0 9.8 add_convert_fusion
  136.8 17.7 %reshape.271 = bf16[5,5,196,3,3,64]{2,1,0,5,4,3:T(8,128)(2,1)} reshape(bf16[4900,576]{0,1:T(8,128)(2,1)} %add_convert_fusion) | data formatting | bytes 11289600 | tf_op jit(solution)/shard_map/reshape | solution.py:237
  154.5 9.7 copy.164
  164.1 62.1 %while.44 = (s32[]{:T(128)}, bf16[5,5,196,3,64]{2,4,3,1,0:T(8,128)(2,1)}, f32[5,5,3,196,1]{3,2,1,4,0:T(4,128)}, bf16[5,5,196,3,3,64]{2,5,4,1,3,0:T(8,128)(2,1)},...) while((s32[]{:T(128)}, ...), condition=%wide.region_5.6_spmd, body=%wide.region_2.5_spmd.sunk | while | flops 355972256 | bytes 23991828 | solution.py:248
  226.2 8.9 copy.165
  235.1 9.3 reshape_reshape.13
  251.9 6.3 fusion.247
  260.1 96.7 %reduce-scatter.9.cloned.1.call-done = f32[1024,768]{1,0:T(8,128)} async-done(((f32[4096,768]{1,0:T(8,128)}), f32[1024,768]{1,0:T(8,128)}) %reduce-scatter.9.cloned.1.call-update) | async-done | bytes 3145744 | tf_op jit(solution)/shard_map/reduce_scatter | solution.py:250
  363.5 26.8 %all-gather.15.cloned.1.call-done = bf16[4096,768]{1,0:T(8,128)(2,1)} async-done(((bf16[1024,768]{1,0:T(8,128)(2,1)}), bf16[4096,768]{1,0:T(8,128)(2,1)}) %all-gather.15.cloned.1.call-update) | async-done | bytes 6291472 | tf_op jit(solution)/shard_map/all_gather | solution.py:265
  390.3 48.4 %all-gather.9.cloned.1.call-done = bf16[4096,768]{1,0:T(8,128)(2,1)} async-done(((bf16[1024,768]{1,0:T(8,128)(2,1)}), bf16[4096,768]{1,0:T(8,128)(2,1)}) %all-gather.9.cloned.1.call-update) | async-done | bytes 6291472 | tf_op jit(solution)/shard_map/all_gather | solution.py:258
  438.7 102.0 %while.45 = (s32[]{:T(128)}, f32[768,768]{1,0:T(8,128)}, f32[768,768]{1,0:T(8,128)}, f32[768]{0:T(1024)S(1)}, bf16[4,1024,768]{2,1,0:T(8,128)(2,1)}, /*index=5*/...) while((s32[]{:T(128)}, f32[768,768]{1,0:T(8,128)}, ...), condition=%wide.region_12.13_spmd.clone, body=%wide.region_10.12_spmd.clone.sunk | while | flops 4896326144 | bytes 63722192 | solution.py:187
  442.3 5.3 convert_reduce_fusion.7
  453.5 10.3 select_add_fusion.7
  467.0 5.3 convert_reduce_fusion.7
  478.9 10.5 select_add_fusion.7
  492.7 5.3 convert_reduce_fusion.7
  504.5 10.5 select_add_fusion.7
  518.3 5.3 convert_reduce_fusion.7
  530.1 10.5 select_add_fusion.7
  540.7 10.1 fusion.248
  552.4 38.0 %convolution_convert_fusion.1 = bf16[4096,768]{1,0:T(8,128)(2,1)} fusion(bf16[768,768]{1,0:T(8,128)(2,1)S(1)} %copy-done.63, f32[768]{0:T(1024)S(1)} %get-tuple-element.757, bf16[4096,768]{1,0:T(8,128)(2,1)} %bitcast.323, bf16[768,768]{1,0:T(8,128)(2,1)S(1)} %copy-done.61), kind=kOutput, calls=%fused_computation.213 | convolution fusion | flops 9874440192 | bytes 14945280 | tf_op jit(solution)/shard_map/dot_general | solution.py:78
  591.1 58.7 %reduce-scatter.13.cloned.1.call-done = f32[1024,768]{1,0:T(8,128)} async-done(((f32[4096,768]{1,0:T(8,128)}), f32[1024,768]{1,0:T(8,128)}) %reduce-scatter.13.cloned.1.call-update) | async-done | bytes 3145744 | tf_op jit(solution)/shard_map/reduce_scatter | solution.py:269
  653.5 57.1 %reduce-scatter.11.cloned.1.call-done = bf16[1024,768]{1,0:T(8,128)(2,1)} async-done(((bf16[4096,768]{1,0:T(8,128)(2,1)}), bf16[1024,768]{1,0:T(8,128)(2,1)}) %reduce-scatter.11.cloned.1.call-update) | async-done | bytes 1572880 | tf_op jit(solution)/shard_map/reduce_scatter | solution.py:259
  710.7 6.1 convert_reduce_fusion.5
  716.8 46.5 %all-gather.17.cloned.1.call-done = bf16[4096,768]{1,0:T(8,128)(2,1)} async-done(((bf16[1024,768]{1,0:T(8,128)(2,1)}), bf16[4096,768]{1,0:T(8,128)(2,1)}) %all-gather.17.cloned.1.call-update) | async-done | bytes 6291472 | tf_op jit(solution)/shard_map/all_gather | solution.py:281
  778.1 5.3 reshape_reshape.14
  783.4 8.5 copy.170
  791.9 224.1 %while.46 = (s32[]{:T(128)}, f32[14,14,64]{2,1,0:T(8,128)S(1)}, f32[14,14,64]{2,1,0:T(8,128)S(1)}, bf16[5,5,196,3,3,64]{2,5,4,1,3,0:T(8,128)(2,1)}, bf16[5,5,196...) while((s32[]{:T(128)}, f32[14,14,64]{2,1,0:T(8,128)S(1)}, ...), condition=%wide.region_18.19_spmd.clone, body=%wide.region_16.18_spmd.clone.sunk | while | flops 741679872 | bytes 70086392 | solution.py:290
  1016.0 20.7 %copy.171 = bf16[5,5,196,3,3,64]{5,4,3,2,1,0:T(4,128)(2,1)} copy(bf16[5,5,196,3,3,64]{2,5,4,1,3,0:T(8,128)(2,1)} %get-tuple-element.171) | data formatting | bytes 11289600 | tf_op jit(solution)/shard_map/while | solution.py:290
  1036.7 26.7 %reshape_reshape.15 = bf16[1,5,5,14,14,576]{5,4,3,2,1,0:T(8,128)(2,1)} reshape(bf16[5,5,196,3,3,64]{5,4,3,2,1,0:T(4,128)(2,1)} %copy.171) | data formatting | bytes 11289600 | tf_op jit(solution)/shard_map/reshape;reshape | solution.py:53
  1063.4 6.5 copy.172
  1069.8 10.7 reshape.279
  1085.8 6.9 convolution_convert_fusion
  1094.0 8.0 copy.173
  1102.0 6.4 fusion.249
  1108.5 9.7 fusion.182
  1123.0 22.4 %all-reduce.3 = (f32[2,192]{1,0:T(2,128)}, f32[768]{0:T(1024)}) all-reduce(f32[2,192]{1,0:T(2,128)S(1)} %pad_maximum_fusion.3, f32[768]{0:T(1024)S(1)} %copy-done.32), channel_id=1, replica_groups=mesh['dp'=8,'tensor'=4] {'dp'}, use_global_device_ids=true, to_apply=%region_28.29 | all-reduce | flops 1152 | bytes 9216 | tf_op jit(solution)/shard_map/psum | solution.py:338
  1154.4 41.8 %all-reduce.2 = (f32[768]{0:T(1024)}, f32[768]{0:T(1024)}, f32[27,64]{1,0:T(8,128)}, f32[27,64]{1,0:T(8,128)}, f32[768]{0:T(1024)}, /*index=5*/f32[768]{0:T(1024)}, f32[768]{0:T(1024)}, f32[768]{0:T(1024)}) all-reduce(f32[768]{0:T(1024)S(1)} %get-tuple-element.320, ...), channel_id=1, replica_groups=mesh['dp'=8,'tensor'=4] {'dp','tensor'}, use_global_device_ids=true, to_apply=%region_23.24 | all-reduce | flops 8064 | bytes 64512 | tf_op jit(solution)/shard_map/psum | solution.py:325
  1199.9 25.1 %reduce-scatter.21.cloned.1.call-done = f32[96,768]{1,0:T(8,128)} async-done(((f32[768,768]{1,0:T(8,128)}), f32[96,768]{1,0:T(8,128)}) %reduce-scatter.21.cloned.1.call-update) | async-done | bytes 294928 | tf_op jit(solution)/shard_map/reduce_scatter | solution.py:313
  1225.0 72.0 %reduce-scatter.23.cloned.1.call-done = f32[96,768]{1,0:T(8,128)} async-done(((f32[768,768]{1,0:T(8,128)}), f32[96,768]{1,0:T(8,128)}) %reduce-scatter.23.cloned.1.call-update) | async-done | bytes 294928 | tf_op jit(solution)/shard_map/reduce_scatter | solution.py:314
  1297.0 65.4 %reduce-scatter.19.cloned.1.call-done = f32[96,192]{1,0:T(8,128)} async-done(((f32[768,192]{1,0:T(8,128)}), f32[96,192]{1,0:T(8,128)}) %reduce-scatter.19.cloned.1.call-update) | async-done | bytes 73744 | tf_op jit(solution)/shard_map/reduce_scatter | solution.py:312
  1362.4 72.4 %reduce-scatter.17.cloned.1.call-done = f32[96,3,192]{2,0,1:T(8,128)} async-done(((f32[768,3,192]{2,0,1:T(8,128)}), f32[96,3,192]{2,0,1:T(8,128)}) %reduce-scatter.17.cloned.1.call-update) | async-done | bytes 221200 | tf_op jit(solution)/shard_map/reduce_scatter | solution.py:311
  (562 shorter events, 391.6 us)
Async XLA Ops:
  8.0 80.5 %copy-start = (bf16[27,64]{1,0:T(8,128)(2,1)S(1)}, bf16[27,64]{1,0:T(8,128)(2,1)}, u32[]{:S(2)}) copy-start(bf16[27,64]{1,0:T(8,128)(2,1)} %param.28) | copy-start | bytes 10372
  8.1 80.9 %all-gather.7.cloned.1.call-start = ((), (), s32[]{:S(2)}) async-start(), calls=%async_computation.8 | async-start | bytes 7864320 | tf_op jit(solution)/shard_map/all_gather | solution.py:225
  14.4 41.0 %copy-start.48 = (bf16[96,192]{1,0:T(8,128)(2,1)S(1)}, bf16[96,192]{1,0:T(8,128)(2,1)}, u32[]{:S(2)}) copy-start(bf16[96,192]{1,0:T(8,128)(2,1)} %param.29) | copy-start | bytes 110596
  14.4 74.3 %copy-start.64 = (bf16[27,64]{1,0:T(8,128)(2,1)S(1)}, bf16[27,64]{1,0:T(8,128)(2,1)}, u32[]{:S(2)}) copy-start(bf16[27,64]{1,0:T(8,128)(2,1)} %param.27) | copy-start | bytes 10372
  14.5 342.4 %reduce-scatter.9.cloned.1.call-start = ((), (), s32[]{:S(2)}) async-start(), calls=%async_computation.9 | async-start | bytes 15728640 | tf_op jit(solution)/shard_map/reduce_scatter | solution.py:250
  54.6 72.4 %copy-start.28 = (bf16[768,3,192]{0,2,1:T(8,128)(2,1)}, bf16[768,3,192]{0,2,1:T(8,128)(2,1)S(1)}, u32[]{:S(2)}) copy-start(bf16[768,3,192]{0,2,1:T(8,128)(2,1)S(1)} %copy.163) | copy-start | bytes 2654212
  54.7 40.8 %copy-start.38 = (s32[14,14]{1,0:T(8,128)}, s32[14,14]{1,0:T(8,128)S(1)}, u32[]{:S(2)}) copy-start(s32[14,14]{1,0:T(8,128)S(1)} %subtract_add_fusion) | copy-start | bytes 2356
  226.2 8.9 copy-start.20
  226.2 8.9 copy-start.22
  226.2 8.9 copy-start.25
  258.2 98.6 %copy-start.15 = (bf16[1024,768]{1,0:T(8,128)(2,1)S(1)}, bf16[1024,768]{1,0:T(8,128)(2,1)}, u32[]{:S(2)}) copy-start(bf16[1024,768]{1,0:T(8,128)(2,1)} %param.22) | copy-start | bytes 4718596
  258.2 105.2 %all-gather.11.cloned.1.call-start = ((), (), s32[]{:S(2)}) async-start(), calls=%async_computation.11 | async-start | bytes 1327104 | tf_op jit(solution)/shard_map/all_gather | solution.py:214
  258.8 104.6 %all-gather.13.cloned.1.call-start = ((), (), s32[]{:S(2)}) async-start(), calls=%async_computation.12 | async-start | bytes 1327104 | tf_op jit(solution)/shard_map/all_gather | solution.py:215
  259.4 130.9 %all-gather.15.cloned.1.call-start = ((), (), s32[]{:S(2)}) async-start(), calls=%async_computation.14 | async-start | bytes 7864320 | tf_op jit(solution)/shard_map/all_gather | solution.py:265
  260.0 178.7 %all-gather.9.cloned.1.call-start = ((), (), s32[]{:S(2)}) async-start(), calls=%async_computation.10 | async-start | bytes 7864320 | tf_op jit(solution)/shard_map/all_gather | solution.py:258
  260.1 99.8 %copy-start.44 = (f32[768]{0:T(1024)}, f32[768]{0:T(1024)S(1)}, u32[]{:S(2)}) copy-start(f32[768]{0:T(1024)S(1)} %convert_element_type.146) | copy-start | bytes 9220
  363.3 286.6 %reduce-scatter.13.cloned.1.call-start = ((), (), s32[]{:S(2)}) async-start(), calls=%async_computation.15 | async-start | bytes 15728640 | tf_op jit(solution)/shard_map/reduce_scatter | solution.py:269
  540.7 10.1 copy-start.31
  550.8 159.9 %reduce-scatter.11.cloned.1.call-start = ((), (), s32[]{:S(2)}) async-start(), calls=%async_computation.13 | async-start | bytes 7864320 | tf_op jit(solution)/shard_map/reduce_scatter | solution.py:259
  590.4 59.4 %copy-start.13 = (f32[1024,768]{1,0:T(8,128)S(1)}, f32[1024,768]{1,0:T(8,128)}, u32[]{:S(2)}) copy-start(f32[1024,768]{1,0:T(8,128)} %copy-done.12) | copy-start | bytes 9437188
  590.4 59.4 %copy-start.37 = (f32[1024]{0:T(1024)S(1)}, f32[1024]{0:T(1024)}, u32[]{:S(2)}) copy-start(f32[1024]{0:T(1024)} %copy-done.36) | copy-start | bytes 12292
  590.4 59.4 %copy-start.45 = (f32[768]{0:T(1024)S(1)}, f32[768]{0:T(1024)}, u32[]{:S(2)}) copy-start(f32[768]{0:T(1024)} %copy-done.44) | copy-start | bytes 9220
  590.5 59.4 %copy-start.47 = (f32[1024]{0:T(1024)S(1)}, f32[1024]{0:T(1024)}, u32[]{:S(2)}) copy-start(f32[1024]{0:T(1024)} %copy-done.46) | copy-start | bytes 12292
  590.5 172.8 %all-gather.17.cloned.1.call-start = ((), (), s32[]{:S(2)}) async-start(), calls=%async_computation.16 | async-start | bytes 7864320 | tf_op jit(solution)/shard_map/all_gather | solution.py:281
  716.8 434.6 %reduce-scatter.15.cloned.1.call-start = ((), (), s32[]{:S(2)}) async-start(), calls=%async_computation.17 | async-start | bytes 7864320 | tf_op jit(solution)/shard_map/reduce_scatter | solution.py:298
  783.4 8.5 copy-start.21
  783.4 8.5 copy-start.23
  783.4 8.5 copy-start.26
  783.4 8.5 copy-start.30
  838.5 8.1 copy-start.9
  883.2 8.1 copy-start.9
  928.0 8.1 copy-start.9
  972.6 8.1 copy-start.9
  1092.8 132.2 %reduce-scatter.21.cloned.1.call-start = ((), (), s32[]{:S(2)}) async-start(), calls=%async_computation.20 | async-start | bytes 2654208 | tf_op jit(solution)/shard_map/reduce_scatter | solution.py:313
  1093.4 203.6 %reduce-scatter.23.cloned.1.call-start = ((), (), s32[]{:S(2)}) async-start(), calls=%async_computation.21 | async-start | bytes 2654208 | tf_op jit(solution)/shard_map/reduce_scatter | solution.py:314
  1094.0 268.4 %reduce-scatter.19.cloned.1.call-start = ((), (), s32[]{:S(2)}) async-start(), calls=%async_computation.19 | async-start | bytes 884736 | tf_op jit(solution)/shard_map/reduce_scatter | solution.py:312
  1108.4 326.3 %reduce-scatter.17.cloned.1.call-start = ((), (), s32[]{:S(2)}) async-start(), calls=%async_computation.18 | async-start | bytes 2654208 | tf_op jit(solution)/shard_map/reduce_scatter | solution.py:311
  1118.2 27.2 %copy-start.39 = (s32[14,14]{1,0:T(8,128)S(1)}, s32[14,14]{1,0:T(8,128)}, u32[]{:S(2)}) copy-start(s32[14,14]{1,0:T(8,128)} %copy-done.38) | copy-start | bytes 2356
  1118.2 33.1 %copy-start.16 = (bf16[1024,768]{1,0:T(8,128)(2,1)S(1)}, bf16[1024,768]{1,0:T(8,128)(2,1)}, u32[]{:S(2)}) copy-start(bf16[1024,768]{1,0:T(8,128)(2,1)} %param.22) | copy-start | bytes 4718596
  1118.2 33.1 %copy-start.35 = (f32[1024]{0:T(1024)S(1)}, f32[1024]{0:T(1024)}, u32[]{:S(2)}) copy-start(f32[1024]{0:T(1024)} %copy-done.34) | copy-start | bytes 12292
  1118.2 33.1 %copy-start.41 = (f32[1024]{0:T(1024)S(1)}, f32[1024]{0:T(1024)}, u32[]{:S(2)}) copy-start(f32[1024]{0:T(1024)} %copy-done.40) | copy-start | bytes 12292
  1118.3 33.1 %copy-start.43 = (f32[768]{0:T(1024)S(1)}, f32[768]{0:T(1024)}, u32[]{:S(2)}) copy-start(f32[768]{0:T(1024)} %copy-done.42) | copy-start | bytes 9220
  1122.8 31.7 %copy-start.49 = (f32[768]{0:T(1024)S(1)}, f32[768]{0:T(1024)}, u32[]{:S(2)}) copy-start(f32[768]{0:T(1024)} %get-tuple-element.318) | copy-start | bytes 9220
  1122.8 31.7 %copy-start.50 = (f32[768]{0:T(1024)S(1)}, f32[768]{0:T(1024)}, u32[]{:S(2)}) copy-start(f32[768]{0:T(1024)} %get-tuple-element.323) | copy-start | bytes 9220
  1122.8 31.7 %copy-start.51 = (f32[768]{0:T(1024)S(1)}, f32[768]{0:T(1024)}, u32[]{:S(2)}) copy-start(f32[768]{0:T(1024)} %get-tuple-element.394) | copy-start | bytes 9220
  1122.8 31.7 %copy-start.52 = (f32[768]{0:T(1024)S(1)}, f32[768]{0:T(1024)}, u32[]{:S(2)}) copy-start(f32[768]{0:T(1024)} %get-tuple-element.408) | copy-start | bytes 9220
  1151.3 44.9 %copy-start.24 = (bf16[1024,768]{1,0:T(8,128)(2,1)S(1)}, bf16[1024,768]{1,0:T(8,128)(2,1)}, u32[]{:S(2)}) copy-start(bf16[1024,768]{1,0:T(8,128)(2,1)} %reduce-scatter.15.cloned.1.call-done) | copy-start | bytes 4718596
  1196.2 238.6 %copy-start.1 = (bf16[27,64]{1,0:T(8,128)(2,1)S(1)}, bf16[27,64]{1,0:T(8,128)(2,1)}, u32[]{:S(2)}) copy-start(bf16[27,64]{1,0:T(8,128)(2,1)} %param.28) | copy-start | bytes 10372
  (82 other events, 235.9 us)
Sparse Core Ops, SparseCore 0:
  14.6 49.0 all-gather.6
  258.4 98.4 reduce-scatter.8
  716.9 46.3 all-gather.16
  1092.9 58.3 reduce-scatter.14
  1155.3 69.6 reduce-scatter.20
  1228.9 68.0 reduce-scatter.22
  1300.8 61.5 reduce-scatter.18
  1366.8 67.8 reduce-scatter.16
Sparse Core Ops, SparseCore 1:
  260.9 40.6 all-gather.10
  303.6 39.8 all-gather.12
  344.9 45.3 all-gather.14
  392.4 46.2 all-gather.8
  550.9 98.9 reduce-scatter.12
  652.4 58.2 reduce-scatter.10
where the time goes:
time: 1460 us; the launch traced here: 1440 us
  waiting for transfers between devices  577 us (40%)
  local copies, waits for them, and re-layouts  329 us (23%)
  matrix products  327 us (22%)
  blocking collectives  136 us (9%)
  other arithmetic  53.1 us (4%)
  between operations  16.6 us (1%)
    reduce_scatter x1, waiting for transfers between devices, body(): lax.psum_scatter(contract_last(on_grid, output_full), 'tensor', scatter_d...  96.7 us
    dot_general x10, matrix products, contract_first(): lax.dot_general(left, right, (((0,), (0,)), ((), ())), preferred_element_...  78 us
    reduce_scatter x1, waiting for transfers between devices, body(): lax.psum_scatter(grad_qkv_weight, 'dp', scatter_dimension=0, tiled=True)  72.4 us
    reduce_scatter x1, waiting for transfers between devices, body(): lax.psum_scatter(grad_down, 'dp', scatter_dimension=0, tiled=True)  72 us
    reduce_scatter x1, waiting for transfers between devices, body(): lax.psum_scatter(grad_output, 'dp', scatter_dimension=0, tiled=True)  65.4 us
    dot_general x4, matrix products, contract_last(): lax.dot_general(left, right, (((1,), (1,)), ((), ())), preferred_element_...  61.4 us
    reduce_scatter x1, waiting for transfers between devices, body(): lax.psum_scatter(contract_last(deltas, up_full), 'tensor', scatter_dimens...  58.7 us
    reduce_scatter x1, waiting for transfers between devices, body(): lax.psum_scatter(feed_rows(normed_two_all, up_full, up_shift, down_full)....  57.1 us
  transfers between devices with their start and end apart: 14, of which 11 were waited for; matrix products, arithmetic and copies ran while one was open for 6% of the time, Pallas kernels for 0%

commit v1 on v0

v1 whole, which is shorter than its diff:
```python
from functools import partial
import math

import jax
import jax.numpy as jnp
from jax import lax
from jax.experimental import pallas as pl
from jax.experimental.pallas import tpu as pltpu
from jax.sharding import PartitionSpec as P
import numpy as np

D = 768
HD = 64
GRID = 64
WIN = 14
SIDE = 5
PITCH = 16
KEYS = WIN * PITCH
EXT = 2 * WIN
PAIRS = D // (2 * HD)
OFFS = 2 * WIN - 1
EPSILON = 1e-06
FAR = -1e30
BF = jnp.bfloat16
F32 = jnp.float32
HIGH = lax.Precision.HIGHEST


def mm(left, right):
    return jnp.dot(left, right, preferred_element_type=F32)


def mm_t(left, right):
    return lax.dot_general(left, right, (((1,), (1,)), ((), ())), preferred_element_type=F32)


def t_mm(left, right):
    return lax.dot_general(left, right, (((0,), (0,)), ((), ())), preferred_element_type=F32)


def norm_parts(value):
    centered = value - jnp.mean(value, -1, keepdims=True)
    inverse = lax.rsqrt(jnp.mean(centered * centered, -1, keepdims=True) + EPSILON)
    return centered * inverse, inverse


def norm_back(upstream, hat, inverse, gain):
    scaled = upstream * gain
    return inverse * (
        scaled
        - jnp.mean(scaled, -1, keepdims=True)
        - hat * jnp.mean(scaled * hat, -1, keepdims=True)
    )


def score_tables():
    ahead = np.zeros((2, KEYS, 128), np.float32)
    back = np.zeros((2, KEYS, 128), np.float32)
    for head in range(2):
        base = 64 - 64 * head
        for c in range(WIN):
            for e in range(PITCH):
                k = c * PITCH + e
                if e >= WIN:
                    ahead[head, k, base] = FAR
                    continue
                ahead[head, k, base + 15 + c] = 1
                ahead[head, k, base + 1 + c] = 1
                ahead[head, k, base + 46 + e] = 1
                ahead[head, k, base + 32 + e] = 1
                back[head, k, base + WIN - 1 - c] = 1
                back[head, k, base + 32 + WIN - 1 - e] = 1
    return ahead, back


def offset_tables(rel_height, rel_width):
    def place(first, second, at_rows, at_cols):
        slab = jnp.zeros((64, HD), BF)
        slab = slab.at[at_rows : at_rows + OFFS].set(first)
        slab = slab.at[at_cols : at_cols + OFFS].set(second)
        low = jnp.concatenate([slab, jnp.zeros_like(slab)], 1)
        high = jnp.concatenate([jnp.zeros_like(slab), slab], 1)
        return jnp.concatenate([jnp.zeros_like(low), low, high, jnp.zeros_like(high)], 0)

    return (
        place(rel_height[::-1], rel_width[::-1], 2, 33),
        place(rel_height, rel_width, 0, 32),
    )


def project_body(place_ref, x_ref, vec_ref, w_ref, nw_ref, q_ref, k_ref, v_ref, nat_ref, *, rows):
    band = pl.program_id(0)
    slot = place_ref[0]

    @pl.when(band == 0)
    def _():
        def one(i, carry):
            hat, _ = norm_parts(x_ref[i].astype(F32))
            normed = hat * vec_ref[0:1] + vec_ref[1:2]
            inside = WIN * slot + i < GRID
            nat_ref[i, 0:GRID, :] = jnp.where(inside, normed, 0.0)
            nat_ref[i, GRID : GRID + PITCH, :] = jnp.zeros((PITCH, D), F32)
            return carry

        lax.fori_loop(0, EXT, one, 0)

    for b in range(SIDE):
        @pl.when(band == b)
        def _(b=b):
            def one(i, carry):
                piece = nat_ref[i, WIN * b : WIN * b + PITCH, :]
                keep = lax.broadcasted_iota(jnp.int32, (PITCH, D), 0) < WIN
                start = pl.multiple_of(i * PITCH, PITCH)
                nw_ref[pl.ds(start, PITCH), :] = jnp.where(keep, piece, 0.0).astype(BF)
                return carry

            lax.fori_loop(0, EXT, one, 0)

    normed = nw_ref[...]
    k_ref[...] = mm(normed, w_ref[:, D : 2 * D]).astype(BF)
    v_ref[...] = (mm(normed, w_ref[:, 2 * D : 3 * D]) + vec_ref[3:4]).astype(BF)
    own = nw_ref[pl.ds(pl.multiple_of(slot * 2 * PITCH, 2 * PITCH), rows * PITCH), :]
    q_ref[...] = (mm(own, w_ref[:, 0:D]) + vec_ref[2:3]).astype(BF)


def project(slot, x_ext, vectors, weight, rows):
    keys, queries = SIDE * EXT * PITCH, SIDE * rows * PITCH
    whole = lambda shape: pl.BlockSpec(shape, lambda b, s: (0,) * len(shape), pipeline_mode=pl.Buffered(1))
    return pl.pallas_call(
        partial(project_body, rows=rows),
        grid_spec=pltpu.PrefetchScalarGridSpec(
            num_scalar_prefetch=1,
            grid=(SIDE,),
            in_specs=[whole((EXT, GRID, D)), whole((8, D)), whole((D, 3 * D))],
            out_specs=[
                pl.BlockSpec((EXT * PITCH, D), lambda b, s: (b, 0)),
                pl.BlockSpec((rows * PITCH, D), lambda b, s: (b, 0)),
                pl.BlockSpec((EXT * PITCH, D), lambda b, s: (b, 0)),
                pl.BlockSpec((EXT * PITCH, D), lambda b, s: (b, 0)),
            ],
            scratch_shapes=[pltpu.VMEM((EXT, GRID + PITCH, D), F32)],
        ),
        out_shape=[
            jax.ShapeDtypeStruct((keys, D), BF),
            jax.ShapeDtypeStruct((queries, D), BF),
            jax.ShapeDtypeStruct((keys, D), BF),
            jax.ShapeDtypeStruct((keys, D), BF),
        ],
        compiler_params=pltpu.CompilerParams(vmem_limit_bytes=60 << 20),
        name="project",
    )(slot, x_ext, vectors, weight)


def head_lanes(shape, head):
    lane = lax.broadcasted_iota(jnp.int32, shape, 1)
    return lane < HD if head == 0 else lane >= HD


def window_split(slot, rows):
    first = WIN - 2 * slot
    return ((0, first * PITCH, 0), (first * PITCH, rows * PITCH, KEYS))


def attend_body(place_ref, q_ref, k_ref, v_ref, rel_ref, tab_ref, o_ref, p_ref, *, rows, slots):
    def variant(slot):
        queries = q_ref[...]
        count = rows * PITCH
        lane = lax.broadcasted_iota(jnp.int32, (PITCH, 128), 1)
        raw = mm(queries, rel_ref[...])
        outs = [None, None]
        for head in range(2):
            base = 64 - 64 * head
            parts = []
            for r in range(rows):
                here = raw[r * PITCH : (r + 1) * PITCH, 128 * head : 128 * head + 128]
                along_row = pltpu.roll(here, (2 * slot + r) % WIN, 1)
                along_col = pltpu.roll(here, 0, 1, stride=1, stride_axis=0)
                both = jnp.where(lane < base + 32, along_row, along_col)
                wanted = ((lane >= base + 15) & (lane < base + 29)) | ((lane >= base + 46) & (lane < base + 60))
                parts.append(jnp.where(wanted, both, 0.0))
            along = jnp.concatenate(parts, 0)
            high = along.astype(BF).astype(F32)
            extra = high + pltpu.roll(along - high, 114, 1)
            wide = lax.broadcasted_iota(jnp.int32, (count, 128), 1)
            extra = jnp.where(wide == base, 1.0, extra)
            mine = head_lanes((count, 128), head)
            left = jnp.where(mine, queries.astype(F32) * HD ** (-0.5), extra).astype(BF)
            out_parts = []
            for start, stop, key in window_split(slot, rows):
                keys = k_ref[key : key + KEYS]
                right = jnp.where(head_lanes((KEYS, 128), head), keys, tab_ref[head])
                scores = mm_t(left[start:stop], right)
                grown = jnp.exp(scores - jnp.max(scores, -1, keepdims=True))
                probs = (grown * (1.0 / jnp.sum(grown, -1, keepdims=True))).astype(BF)
                p_ref[0, head, start:stop, :] = probs
                out_parts.append(mm(probs, v_ref[key : key + KEYS]))
            outs[head] = jnp.concatenate(out_parts, 0)
        o_ref[...] = jnp.where(head_lanes((count, 128), 0), outs[0], outs[1]).astype(BF)

    for slot in range(slots):
        pl.when(place_ref[0] == slot)(partial(variant, slot))


def attend(slot, q, k, v, rel, table, rows, slots):
    queries = rows * PITCH
    steps = SIDE * PAIRS
    return pl.pallas_call(
        partial(attend_body, rows=rows, slots=slots),
        grid_spec=pltpu.PrefetchScalarGridSpec(
            num_scalar_prefetch=1,
            grid=(SIDE, PAIRS),
            in_specs=[
                pl.BlockSpec((queries, 128), lambda b, p, s: (b, p)),
                pl.BlockSpec((EXT * PITCH, 128), lambda b, p, s: (b, p)),
                pl.BlockSpec((EXT * PITCH, 128), lambda b, p, s: (b, p)),
                pl.BlockSpec((128, 256), lambda b, p, s: (0, 0)),
                pl.BlockSpec((2, KEYS, 128), lambda b, p, s: (0, 0, 0)),
            ],
            out_specs=[
                pl.BlockSpec((queries, 128), lambda b, p, s: (b, p)),
                pl.BlockSpec((1, 2, queries, KEYS), lambda b, p, s: (b * PAIRS + p, 0, 0, 0)),
            ],
        ),
        out_shape=[
            jax.ShapeDtypeStruct((SIDE * queries, D), BF),
            jax.ShapeDtypeStruct((steps, 2, queries, KEYS), BF),
        ],
        compiler_params=pltpu.CompilerParams(vmem_limit_bytes=60 << 20),
        name="attend",
    )(slot, q, k, v, rel, table)


def attend_back_body(
    place_ref, q_ref, k_ref, v_ref, p_ref, do_ref, rel_ref, tab_ref,
    dq_ref, dk_ref, dv_ref, drel_ref, *, rows, slots,
):
    count = rows * PITCH

    @pl.when((pl.program_id(0) == 0) & (pl.program_id(1) == 0))
    def _():
        drel_ref[...] = jnp.zeros_like(drel_ref)

    def variant(slot):
        queries = q_ref[...]
        scaled = (queries.astype(F32) * HD ** (-0.5)).astype(BF)
        lane = lax.broadcasted_iota(jnp.int32, (PITCH, 128), 1)
        upstream = do_ref[...]
        split = window_split(slot, rows)
        grad_keys = [[None, None], [None, None]]
        grad_values = [[None, None], [None, None]]
        grad_left, grad_raw = [], []
        for head in range(2):
            base = 64 - 64 * head
            grad_out = jnp.where(head_lanes((count, 128), head), upstream, jnp.zeros_like(upstream))
            lefts = []
            for w, (start, stop, key) in enumerate(split):
                keys, values = k_ref[key : key + KEYS], v_ref[key : key + KEYS]
                probs = p_ref[0, head, start:stop, :]
                grad_probs = mm_t(grad_out[start:stop], values)
                exact = probs.astype(F32)
                inner = jnp.sum(exact * grad_probs, -1, keepdims=True)
                grad_scores = (exact * (grad_probs - inner)).astype(BF)
                grad_values[head][w] = t_mm(probs, grad_out[start:stop])
                right = jnp.where(head_lanes((KEYS, 128), head), keys, tab_ref[head])
                lefts.append(mm(grad_scores, right))
                grad_keys[head][w] = t_mm(grad_scores, scaled[start:stop])
            left = jnp.concatenate(lefts, 0)
            grad_left.append(left)
            parts = []
            for r in range(rows):
                here = left[r * PITCH : (r + 1) * PITCH]
                on_row = jnp.where((lane >= base) & (lane < base + WIN), here, 0.0)
                on_col = jnp.where((lane >= base + 32) & (lane < base + 32 + WIN), here, 0.0)
                on_row = pltpu.roll(on_row, (2 * slot + r) % WIN, 1)
                on_col = pltpu.roll(on_col, 0, 1, stride=1, stride_axis=0)
                parts.append(on_row + on_col)
            grad_raw.append(jnp.concatenate(parts, 0))
        raw = jnp.concatenate(grad_raw, 1).astype(BF)
        first = head_lanes((count, 128), 0)
        direct = jnp.where(first, grad_left[0], grad_left[1]) * HD ** (-0.5)
        dq_ref[...] = (direct + mm(raw, rel_ref[...])).astype(BF)
        drel_ref[...] += t_mm(raw, queries)
        first = head_lanes((KEYS, 128), 0)
        for w, (_, _, key) in enumerate(split):
            dk_ref[key : key + KEYS] = jnp.where(first, grad_keys[0][w], grad_keys[1][w]).astype(BF)
            dv_ref[key : key + KEYS] = (grad_values[0][w] + grad_values[1][w]).astype(BF)

    for slot in range(slots):
        pl.when(place_ref[0] == slot)(partial(variant, slot))


def attend_back(slot, q, k, v, probs, grad_out, rel, table, rows, slots):
    queries = rows * PITCH
    of_q = pl.BlockSpec((queries, 128), lambda b, p, s: (b, p))
    of_k = pl.BlockSpec((EXT * PITCH, 128), lambda b, p, s: (b, p))
    return pl.pallas_call(
        partial(attend_back_body, rows=rows, slots=slots),
        grid_spec=pltpu.PrefetchScalarGridSpec(
            num_scalar_prefetch=1,
            grid=(SIDE, PAIRS),
            in_specs=[
                of_q, of_k, of_k,
                pl.BlockSpec((1, 2, queries, KEYS), lambda b, p, s: (b * PAIRS + p, 0, 0, 0)),
                of_q,
                pl.BlockSpec((256, 128), lambda b, p, s: (0, 0)),
                pl.BlockSpec((2, KEYS, 128), lambda b, p, s: (0, 0, 0)),
            ],
            out_specs=[of_q, of_k, of_k, pl.BlockSpec((256, 128), lambda b, p, s: (0, 0))],
        ),
        out_shape=[
            jax.ShapeDtypeStruct(q.shape, BF),
            jax.ShapeDtypeStruct(k.shape, BF),
            jax.ShapeDtypeStruct(k.shape, BF),
            jax.ShapeDtypeStruct((256, 128), F32),
        ],
        compiler_params=pltpu.CompilerParams(vmem_limit_bytes=60 << 20),
        name="attend_back",
    )(slot, q, k, v, probs, grad_out, rel, table)


def feed_body(
    o_ref, x_ref, g_ref, wo_ref, up_ref, down_ref, vec_ref, bias_ref,
    out_ref, dh_ref, do_ref, gwo_ref, gup_ref, gdown_ref, gvec_ref, gbias_ref,
    nat_ref, onat_ref, n2_ref, h_ref, y_ref, dn_ref, a_ref, du_ref, *, rows, chunks,
):
    step = pl.program_id(0)
    steps = rows * GRID // 256
    lines = 256 // GRID
    blocks = up_ref.shape[0]

    @pl.when(step == 0)
    def _():
        def one(i, carry):
            at = pl.ds(pl.multiple_of(i * 256, 256), 256)
            for b in range(SIDE):
                piece = o_ref[b, pl.ds(i * lines, lines)]
                nat_ref[:, WIN * b : WIN * b + PITCH, :] = piece.astype(F32)
            natural = nat_ref[:, 0:GRID, :].reshape(256, D).astype(BF)
            onat_ref[at, :] = natural
            hidden = x_ref[at, :].astype(F32) + mm_t(natural, wo_ref[...]) + vec_ref[0:1]
            h_ref[at, :] = hidden
            hat, _ = norm_parts(hidden)
            n2_ref[at, :] = (hat * vec_ref[1:2] + vec_ref[2:3]).astype(BF)
            y_ref[at, :] = jnp.zeros((256, D), F32)
            dn_ref[at, :] = jnp.zeros((256, D), F32)
            return carry

        lax.fori_loop(0, steps, one, 0)

    up = up_ref[...].reshape(D, D)
    down = down_ref[...].reshape(D, D)

    def two(i, total):
        at = pl.ds(pl.multiple_of(i * 256, 256), 256)
        upper = mm(n2_ref[at, :], up) + bias_ref[...].reshape(1, D)
        cdf = 0.5 * (1.0 + lax.erf(upper * (1.0 / math.sqrt(2.0))))
        active = (upper * cdf).astype(BF)
        a_ref[at, :] = active
        y_ref[at, :] += mm_t(active, down)
        slope = cdf + upper * jnp.exp(-0.5 * upper * upper) * (1.0 / math.sqrt(2.0 * math.pi))
        delta = (mm(g_ref[at, :], down) * slope).astype(BF)
        du_ref[at, :] = delta
        dn_ref[at, :] += mm_t(delta, up)
        return total + jnp.sum(delta.astype(F32), 0, keepdims=True)

    total = lax.fori_loop(0, steps, two, jnp.zeros((1, D), F32))
    gbias_ref[...] = total.reshape(gbias_ref.shape)
    gup_ref[...] = t_mm(n2_ref[...], du_ref[...]).astype(BF).reshape(gup_ref.shape)
    gdown_ref[...] = t_mm(g_ref[...], a_ref[...]).astype(BF).reshape(gdown_ref.shape)

    @pl.when(step == chunks - 1)
    def _():
        nat_ref[...] = jnp.zeros_like(nat_ref)
        gvec_ref[...] = jnp.zeros_like(gvec_ref)

        def three(i, carry):
            at = pl.ds(pl.multiple_of(i * 256, 256), 256)
            hidden = h_ref[at, :]
            grad = g_ref[at, :].astype(F32)
            hat, inverse = norm_parts(hidden)
            grad_normed = dn_ref[at, :]
            out_ref[at, :] = (hidden + y_ref[at, :] + vec_ref[3:4]).astype(BF)
            grad_hidden = grad + norm_back(grad_normed, hat, inverse, vec_ref[1:2])
            dh_ref[at, :] = grad_hidden
            branch = grad_hidden.astype(BF)
            n2_ref[at, :] = branch
            gvec_ref[0:1] += jnp.sum(grad_normed * hat, 0, keepdims=True)
            gvec_ref[1:2] += jnp.sum(grad_normed, 0, keepdims=True)
            gvec_ref[2:3] += jnp.sum(branch.astype(F32), 0, keepdims=True)
            gvec_ref[3:4] += jnp.sum(grad, 0, keepdims=True)
            grad_out = mm(branch, wo_ref[...])
            nat_ref[:, 0:GRID, :] = grad_out.reshape(lines, GRID, D)
            keep = lax.broadcasted_iota(jnp.int32, (lines, PITCH, D), 1) < WIN
            for b in range(SIDE):
                piece = nat_ref[:, WIN * b : WIN * b + PITCH, :]
                do_ref[b, pl.ds(i * lines, lines)] = jnp.where(keep, piece, 0.0).astype(BF)
            return carry

        lax.fori_loop(0, steps, three, 0)
        gwo_ref[...] = t_mm(n2_ref[...], onat_ref[...]).astype(BF)


def feed(o, x, g, wo, up, down, vectors, up_bias, rows):
    tokens = rows * GRID
    blocks, chunks, depth = up.shape[:3]
    whole = lambda shape: pl.BlockSpec(shape, lambda c: (0,) * len(shape), pipeline_mode=pl.Buffered(1))
    slab = pl.BlockSpec((blocks, None, depth, D), lambda c: (0, c, 0, 0))
    line = pl.BlockSpec((None, 1, D), lambda c: (c, 0, 0))
    grid = (SIDE, rows, PITCH, D)
    return pl.pallas_call(
        partial(feed_body, rows=rows, chunks=chunks),
        grid=(chunks,),
        in_specs=[
            whole(grid), whole((tokens, D)), whole((tokens, D)), whole((D, D)), slab, slab, whole((8, D)), line,
        ],
        out_specs=[
            whole((tokens, D)), whole((tokens, D)), whole(grid), whole((D, D)), slab, slab, whole((8, D)), line,
        ],
        out_shape=[
            jax.ShapeDtypeStruct((tokens, D), BF),
            jax.ShapeDtypeStruct((tokens, D), F32),
            jax.ShapeDtypeStruct(grid, BF),
            jax.ShapeDtypeStruct((D, D), BF),
            jax.ShapeDtypeStruct(up.shape, BF),
            jax.ShapeDtypeStruct(down.shape, BF),
            jax.ShapeDtypeStruct((8, D), F32),
            jax.ShapeDtypeStruct((chunks, 1, D), F32),
        ],
        scratch_shapes=[
            pltpu.VMEM((256 // GRID, GRID + PITCH, D), F32),
            pltpu.VMEM((tokens, D), BF),
            pltpu.VMEM((tokens, D), BF),
            pltpu.VMEM((tokens, D), F32),
            pltpu.VMEM((tokens, D), F32),
            pltpu.VMEM((tokens, D), F32),
            pltpu.VMEM((tokens, D), BF),
            pltpu.VMEM((tokens, D), BF),
        ],
        compiler_params=pltpu.CompilerParams(vmem_limit_bytes=63 << 20),
        name="feed",
    )(o, x, g, wo, up, down, vectors, up_bias)


def body(
    features, first_gain, first_shift, qkv_weight, qv_bias, rel_height, rel_width, output_weight,
    output_bias, second_gain, second_shift, up_weight, up_bias, down_weight, down_bias, cotangent,
    *, groups, slots,
):
    both = ("dp", "tensor")
    depth, _, width = qkv_weight.shape
    hidden = up_weight.shape[1]
    tokens = features.shape[0]
    rows = tokens // GRID
    above, below = 2 * (slots - 1), WIN - 2
    slot = lax.axis_index("tensor")
    place = slot.astype(jnp.int32).reshape(1)

    qkv_all = lax.all_gather(qkv_weight.reshape(depth, 3 * width), both, axis=0)
    rest = jnp.concatenate([output_weight, up_weight, down_weight], 1)
    rest_all = lax.all_gather(rest, both, axis=0).reshape(groups, slots, depth, width + 2 * hidden)
    qkv_full = qkv_all.reshape(groups, slots, depth, 3, width).transpose(0, 2, 3, 1, 4).reshape(D, 3 * D)
    out_full = rest_all[..., :width].transpose(0, 2, 1, 3).reshape(D, D)
    up_all = rest_all[..., width : width + hidden]
    down_all = rest_all[..., width + hidden :]
    biases = lax.all_gather(jnp.concatenate([qv_bias.reshape(-1), up_bias]), "tensor", axis=0)
    qv_all = biases[:, : 2 * width].reshape(slots, 2, width).transpose(1, 0, 2).reshape(2, D)
    up_bias_all = biases[:, 2 * width :].astype(F32).reshape(slots, 1, hidden)

    grid_x = features.reshape(rows, GRID, D)
    up_pairs = [(s, s + 1) for s in range(slots - 1)]
    down_pairs = [(s + 1, s) for s in range(slots - 1)]
    from_above = lax.ppermute(grid_x[rows - above :], "tensor", up_pairs)
    from_below = lax.ppermute(grid_x[:below], "tensor", down_pairs)
    x_ext = lax.dynamic_slice_in_dim(
        jnp.concatenate([from_above, grid_x, from_below], 0), above - 2 * slot, EXT, 0
    )

    vec_one = jnp.concatenate(
        [first_gain[None], first_shift[None], qv_all, jnp.zeros((4, D), BF)], 0
    ).astype(F32)
    normed, q, k, v = project(place, x_ext, vec_one, qkv_full, rows)
    ahead, back = score_tables()
    rel_ahead, rel_back = offset_tables(rel_height, rel_width)
    attended, probs = attend(
        place, q, k, v, rel_ahead.T, jnp.asarray(ahead, BF), rows, slots
    )

    vec_two = jnp.concatenate(
        [output_bias[None], second_gain[None], second_shift[None], down_bias[None], jnp.zeros((4, D), BF)], 0
    ).astype(F32)
    output, grad_hidden, grad_out, grad_wo, grad_up, grad_down, grad_vec, grad_up_bias = feed(
        attended.reshape(SIDE, rows, PITCH, D), features, cotangent, out_full, up_all, down_all,
        vec_two, up_bias_all, rows,
    )
    dq, dk, dv, drel = attend_back(
        place, q, k, v, probs, grad_out.reshape(-1, D), rel_back, jnp.asarray(back, BF), rows, slots
    )

    banded = normed.reshape(SIDE, EXT, PITCH, D)
    own = lax.dynamic_slice_in_dim(banded, 2 * slot, rows, 1).reshape(-1, D)
    grad_wq, grad_wk, grad_wv = t_mm(own, dq), t_mm(normed, dk), t_mm(normed, dv)
    grad_normed = mm_t(dk, qkv_full[:, D : 2 * D]) + mm_t(dv, qkv_full[:, 2 * D :])
    grad_own = mm_t(dq, qkv_full[:, :D])

    def natural(windows, lines):
        grid = windows.reshape(SIDE, lines, PITCH, D)[:, :, :WIN]
        return grid.transpose(1, 0, 2, 3).reshape(lines, SIDE * WIN, D)[:, :GRID]

    wide = jnp.zeros((above + rows + below, GRID, D), F32)
    wide = lax.dynamic_update_slice_in_dim(wide, natural(grad_normed, EXT), above - 2 * slot, 0)
    to_above = wide[:above].astype(BF)
    to_below = wide[above + rows :].astype(BF)
    from_below = lax.ppermute(to_above, "tensor", down_pairs).astype(F32)
    from_above = lax.ppermute(to_below, "tensor", up_pairs).astype(F32)
    total = wide[above : above + rows] + natural(grad_own, rows)
    total = total + jnp.pad(from_above, ((0, rows - below), (0, 0), (0, 0)))
    total = total + jnp.pad(from_below, ((rows - above, 0), (0, 0), (0, 0)))
    total = total.reshape(tokens, D)
    hat, inverse = norm_parts(features.astype(F32))
    grad_features = (grad_hidden + norm_back(total, hat, inverse, vec_one[0:1])).astype(BF)
    grad_gain_one = jnp.sum(total * hat, 0)
    grad_shift_one = jnp.sum(total, 0)
    grad_qv = jnp.stack([jnp.sum(dq.astype(F32), 0), jnp.sum(dv.astype(F32), 0)])

    grad_rest = jnp.concatenate(
        [grad_wo.reshape(groups, depth, slots, width).transpose(0, 2, 1, 3), grad_up, grad_down], -1
    )
    grad_rest = lax.psum_scatter(
        grad_rest.reshape(groups * slots, depth, width + 2 * hidden), both, scatter_dimension=0
    ).astype(F32)
    grad_qkv = jnp.stack([grad_wq, grad_wk, grad_wv], 1).astype(BF)
    grad_qkv = grad_qkv.reshape(groups, depth, 3, slots, width).transpose(0, 3, 1, 2, 4)
    grad_qkv = lax.psum_scatter(
        grad_qkv.reshape(groups * slots, depth, 3 * width), both, scatter_dimension=0
    ).astype(F32)
    small = lax.psum(
        jnp.concatenate(
            [
                grad_vec[:4].reshape(-1), grad_gain_one, grad_shift_one, grad_qv.reshape(-1),
                grad_up_bias.reshape(-1), drel.reshape(-1),
            ]
        ),
        both,
    )
    vec = small[: 6 * D].reshape(6, D)
    qv = small[6 * D : 8 * D].reshape(2, slots, width)
    qv = lax.dynamic_index_in_dim(qv, slot, 1, keepdims=False)
    bias = small[8 * D : 8 * D + slots * hidden].reshape(slots, hidden)
    bias = lax.dynamic_index_in_dim(bias, slot, 0, keepdims=False)
    drel = small[8 * D + slots * hidden :].reshape(4, 64, 128)
    drel = drel[1, :, :HD] + drel[2, :, HD:]
    return (
        output,
        grad_features,
        vec[4],
        vec[5],
        grad_qkv.reshape(depth, 3, width),
        qv,
        drel[0:OFFS],
        drel[32 : 32 + OFFS],
        grad_rest[:, :width],
        vec[2],
        vec[0],
        vec[1],
        grad_rest[:, width : width + hidden],
        bias,
        grad_rest[:, width + hidden :],
        vec[3],
    )


def solution(mesh):
    token = P(("dp", "tensor"), None)
    square = P("dp", "tensor")
    cube = P("dp", None, "tensor")
    return jax.shard_map(
        partial(body, groups=mesh.shape["dp"], slots=mesh.shape["tensor"]),
        mesh=mesh,
        in_specs=(
            token, P(), P(), cube, P(None, "tensor"), P(), P(), square, P(), P(), P(), square,
            P("tensor"), square, P(), token,
        ),
        out_specs=(
            token, token, P(), P(), cube, P(None, "tensor"), P(), P(), square, P(), P(), P(), square,
            P("tensor"), square, P(),
        ),
        check_vma=False,
    )
```

time: 1460 us -> 811 us (0.56)
  matrix products: 327 us -> 24.8 us
  waiting for transfers between devices: 577 us -> 378 us
  Pallas kernels: 0 us -> 162 us
  local copies, waits for them, and re-layouts: 329 us -> 170 us
  blocking collectives: 136 us -> 14.1 us
  other arithmetic: 53.1 us -> 25.2 us
    dot_general x118 -> x6, matrix products: 327 us -> 24.8 us  [the longest x3 13.6 us: t_mm(): lax.dot_general(left, right, (((0,), (0,)), ((), ())), preferred_element_...]
    reduce_scatter x8 -> x2, waiting for transfers between devices: 453 us -> 256 us  [the longest x1 148 us: body(): lax.psum_scatter(grad_rest.reshape(groups * slots, depth, width + 2 * hid...]
    pallas_call x0 -> x4, Pallas kernels: none -> 162 us  [the longest x1 53.7 us: feed(): pl.pallas_call(partial(feed_body, rows=rows, chunks=chunks), grid=(chunks...]
    all_gather x6 -> x2, waiting for transfers between devices: 122 us -> 35.2 us  [the longest x1 34.9 us: body(): qkv_all = lax.all_gather(qkv_weight.reshape(depth, 3 * width), both, axis=0)]
    psum x0 -> x1, waiting for transfers between devices: none -> 86.4 us  [body(): lax.psum(jnp.concatenate([grad_vec[:4].reshape(-1), grad_gain_one, grad_s...]
    reshape x30 -> x14, local copies, waits for them, and re-layouts: 105 us -> 19.5 us  [the longest x1 8.8 us: body(): qkv_all.reshape(groups, slots, depth, 3, width).transpose(0, 2, 3, 1, 4)]
    psum x2 -> x0, blocking collectives: 64.2 us -> none  [the longest x1 41.8 us: body(): lax.psum((grad_gain_one, grad_shift_one, grad_gain_two, grad_shift_two, g...]
    all_gather x2 -> x1, blocking collectives: 71.9 us -> 14.1 us  [body(): lax.all_gather(jnp.concatenate([qv_bias.reshape(-1), up_bias]), 'tensor',...]
  transfers between devices with their start and end apart: 14 -> 9, of which waited for: 11 -> 5; matrix products, arithmetic and copies ran while one was open for 6% -> 15% of each run, Pallas kernels for 0% -> 8%
where the time goes in v1:
time: 811 us; the launch traced here: 800 us
  waiting for transfers between devices  378 us (47%)
  local copies, waits for them, and re-layouts  170 us (21%)
  Pallas kernels  162 us (20%)
  other arithmetic  25.2 us (3%)
  matrix products  24.8 us (3%)
  between operations  14.6 us (2%)
  blocking collectives  14.1 us (2%)
  starting transfers between devices  10.6 us (1%)
    reduce_scatter x1, waiting for transfers between devices, body(): lax.psum_scatter(grad_rest.reshape(groups * slots, depth, width + 2 * hid...  148 us
    reduce_scatter x1, waiting for transfers between devices, body(): lax.psum_scatter(grad_qkv.reshape(groups * slots, depth, 3 * width), both...  109 us
    psum x1, waiting for transfers between devices, body(): lax.psum(jnp.concatenate([grad_vec[:4].reshape(-1), grad_gain_one, grad_s...  86.4 us
    pallas_call x1, Pallas kernels, feed(): pl.pallas_call(partial(feed_body, rows=rows, chunks=chunks), grid=(chunks...  53.7 us
    pallas_call x1, Pallas kernels, attend_back(): pl.pallas_call(partial(attend_back_body, rows=rows, slots=slots), grid_sp...  47 us
    pallas_call x1, Pallas kernels, attend(): pl.pallas_call(partial(attend_body, rows=rows, slots=slots), grid_spec=pl...  42.6 us
    all_gather x1, waiting for transfers between devices, body(): qkv_all = lax.all_gather(qkv_weight.reshape(depth, 3 * width), both, axis=0)  34.9 us
    dynamic_update_slice x1, local copies, waits for them, and re-layouts, body(): lax.dynamic_update_slice_in_dim(wide, natural(grad_normed, EXT), above -...  28.5 us
  transfers between devices with their start and end apart: 9, of which 5 were waited for; matrix products, arithmetic and copies ran while one was open for 15% of the time, Pallas kernels for 8%

profile of v1, /device:TPU:0, one launch (start us, length us, event | category | flops | bytes accessed | tf_op | source)
XLA Modules:
  0.0 800.2 jit_solution(9698927349926876087)
XLA Ops:
  9.3 2.0 concatenate.55
  14.9 3.1 collective-permute-start
  19.6 14.1 %all-gather.2 = bf16[4,1,1152]{2,1,0:T(2,128)(2,1)S(1)} all-gather(bf16[1,1,1152]{2,1,0:T(2,128)(2,1)S(1)} %reshape.326), channel_id=2, replica_groups=mesh['dp'=8,'tensor'=4] {'tensor'}, dimensions={0}, use_global_device_ids=true | all-gather | bytes 11520 | tf_op jit(solution)/shard_map/all_gather | solution.py:465
  36.7 3.8 fusion.15.x_ref
  40.6 34.9 %all-gather.6.cloned.1.call-done = bf16[32,96,576]{2,1,0:T(8,128)(2,1)} async-done(((bf16[1,96,576]{2,1,0:T(8,128)(2,1)}), bf16[32,96,576]{2,1,0:T(8,128)(2,1)}) %all-gather.6.cloned.1.call-update) | async-done | bytes 3538960 | tf_op jit(solution)/shard_map/all_gather | solution.py:458
  75.5 7.0 copy.112
  82.5 9.8 %copy.113 = bf16[8,96,3,4,192]{4,3,2,1,0:T(4,128)(2,1)} copy(bf16[8,96,3,4,192]{1,4,2,3,0:T(8,128)(2,1)} %bitcast.88) | data formatting | bytes 7077888 | tf_op jit(solution)/shard_map/transpose | solution.py:461
  92.4 8.8 %reshape.294.w_ref = bf16[768,2304]{1,0:T(8,128)(2,1)} reshape(bf16[8,96,3,4,192]{4,3,2,1,0:T(4,128)(2,1)} %copy.113) | data formatting | bytes 7077888 | tf_op jit(solution)/shard_map/reshape | solution.py:461
  101.2 19.1 %project.1 = (bf16[2240,768]{1,0:T(8,128)(2,1)}, bf16[1280,768]{1,0:T(8,128)(2,1)}, bf16[2240,768]{1,0:T(8,128)(2,1)}, bf16[2240,768]{1,0:T(8,128)(2,1)}) custom-call(s32[1]{0:T(128)} %bitcast.place_ref, bf16[28,64,768]{2,1,0:T(8,128)(2,1)} %fusion.15.x_ref, f32[8,768]{1,0:T(8,128)} %copy-done.15, bf16[768,2304]{1,0:T(8,128)(2,1)} %reshape.294.w_ref), custom_call_target="tpu_custom_call" | custom-call | tf_op jit(solution)/shard_map/project/pallas_call | solution.py:129
  120.2 1.7 constant_dynamic-slice_fusion.1
  121.9 2.3 copy.125
  124.2 42.6 %attend.1 = (bf16[1280,768]{1,0:T(8,128)(2,1)}, bf16[30,2,256,224]{3,2,1,0:T(8,128)(2,1)}) custom-call(s32[1]{0:T(128)} %bitcast.place_ref, bf16[1280,768]{1,0:T(8,128)(2,1)} %get-tuple-element.82.q_ref, bf16[2240,768]{1,0:T(8,128)(2,1)} %get-tuple-element.83.k_ref, bf16[2240,768]{1,0:T(8,128)(2,1)} %get-tuple-element.84.v_ref, ...), custom_call_target="tpu_custom_call" | custom-call | tf_op jit(solution)/shard_map/attend/pallas_call | solution.py:207
  167.0 13.6 %fusion.33 = (bf16[8,4,96,768]{3,2,1,0:T(8,128)(2,1)}, bf16[8,4,96,768]{3,2,1,0:T(8,128)(2,1)}) fusion(bf16[8,4,96,1728]{3,2,1,0:T(8,128)(2,1)} %bitcast.90), kind=kLoop, calls=%fused_computation.83 | loop fusion | bytes 18874368 | tf_op jit(solution)/shard_map/slice | solution.py:464
  180.7 1.5 slice_bitcast_fusion.1
  183.4 2.2 reshape.331.wo_ref
  185.7 53.7 %feed.1 = (bf16[1024,768]{1,0:T(8,128)(2,1)}, f32[1024,768]{1,0:T(8,128)}, bf16[5,16,16,768]{3,2,1,0:T(8,128)(2,1)}, bf16[768,768]{1,0:T(8,128)(2,1)}, bf16[8,4,...) custom-call(bf16[5,16,16,768]{3,2,1,0:T(8,128)(2,1)} %bitcast.98, ...), custom_call_target="tpu_custom_call" | custom-call | tf_op jit(solution)/shard_map/feed/pallas_call | solution.py:410
  239.4 47.0 %attend_back.1 = (bf16[1280,768]{1,0:T(8,128)(2,1)}, bf16[2240,768]{1,0:T(8,128)(2,1)}, bf16[2240,768]{1,0:T(8,128)(2,1)}, f32[256,128]{1,0:T(8,128)}) custom-call(s32[1]{0:T(128)} %bitcast.place_ref, bf16[1280,768]{1,0:T(8,128)(2,1)} %get-tuple-element.82.q_ref, bf16[2240,768]{1,0:T(8,128)(2,1)} %get-tuple-element.83.k_ref, ...), custom_call_target="tpu_custom_call" | custom-call | tf_op jit(solution)/shard_map/attend_back/pallas_call | solution.py:296
  286.4 6.1 convolution_convert_fusion.1
  294.5 4.1 convolution_convert_fusion.2
  298.6 2.9 fusion.20
  301.4 3.1 convolution_add_fusion
  305.4 3.7 copy.117
  309.1 3.1 slice.245
  312.2 3.7 broadcast_in_dim.31
  315.8 28.5 %dynamic_update_slice.3 = f32[34,64,768]{2,0,1:T(8,128)} dynamic-update-slice(f32[34,64,768]{2,0,1:T(8,128)} %broadcast_in_dim.31, f32[28,64,768]{2,0,1:T(8,128)} %slice.245, s32[]{:T(128)S(6)} %select_n.13, s32[]{:T(128)} %constant.144.clone.1, s32[]{:T(128)} %constant.144.clone.1) | dynamic-update-slice | bytes 11010052 | tf_op jit(solution)/shard_map/dynamic_update_slice | solution.py:510
  344.3 3.6 convert.23
  348.6 2.3 copy-done.5
  353.7 4.8 collective-permute-start.2
  364.0 5.3 fusion.17
  369.3 4.4 copy.126
  375.4 3.5 reshape.333
  378.9 1.4 copy.130
  380.4 4.2 copy.146
  384.6 3.4 fusion.16
  389.4 1.9 copy.120
  391.3 3.8 fusion.31
  395.1 1.8 copy.123
  397.0 1.6 copy-done.2
  400.6 4.2 maximum_bitcast_fusion
  404.9 6.9 copy.131
  411.8 3.5 reshape.334
  415.3 1.4 copy.151
  416.7 19.2 %concatenate.61 = bf16[8,4,96,1728]{3,2,1,0:T(8,128)(2,1)} concatenate(bf16[8,4,96,192]{3,2,1,0:T(8,128)(2,1)} %bitcast.95, bf16[8,4,96,768]{3,2,1,0:T(8,128)(2,1)} %get-tuple-element.98, bf16[8,4,96,768]{3,2,1,0:T(8,128)(2,1)} %get-tuple-element.99), dimensions={3} | concatenate | bytes 21233664 | tf_op jit(solution)/shard_map/concatenate | solution.py:525
  436.0 4.3 fusion.9
  440.4 86.4 %all-reduce.10.cloned.1.call-done = f32[41984]{0:T(1024)} async-done(((f32[41984]{0:T(1024)}), f32[41984]{0:T(1024)}) %all-reduce.10.cloned.1.call-update) | async-done | bytes 167952 | tf_op jit(solution)/shard_map/psum | solution.py:536
  532.5 108.7 %reduce-scatter.3.cloned.1.call-done = bf16[1,96,576]{1,2,0:T(8,128)(2,1)} async-done(((bf16[32,96,576]{1,2,0:T(8,128)(2,1)}), bf16[1,96,576]{1,2,0:T(8,128)(2,1)}) %reduce-scatter.3.cloned.1.call-update) | async-done | bytes 110608 | tf_op jit(solution)/shard_map/reduce_scatter | solution.py:533
  641.2 1.8 copy.134
  642.9 147.8 %reduce-scatter.5.cloned.1.call-done = bf16[1,96,1728]{2,1,0:T(8,128)(2,1)} async-done(((bf16[32,96,1728]{2,1,0:T(8,128)(2,1)}), bf16[1,96,1728]{2,1,0:T(8,128)(2,1)}) %reduce-scatter.5.cloned.1.call-update) | async-done | bytes 331792 | tf_op jit(solution)/shard_map/reduce_scatter | solution.py:528
  (158 shorter events, 37.1 us)
Async XLA Ops:
  7.2 6.9 copy-start
  7.2 10.8 %copy-start.29 = (bf16[2,192]{1,0:T(2,128)(2,1)S(1)}, bf16[2,192]{1,0:T(2,128)(2,1)}, u32[]{:S(2)}) copy-start(bf16[2,192]{1,0:T(2,128)(2,1)} %param.30) | copy-start | bytes 2308
  7.2 10.9 %copy-start.16 = (bf16[27,64]{1,0:T(8,128)(2,1)S(1)}, bf16[27,64]{1,0:T(8,128)(2,1)}, u32[]{:S(2)}) copy-start(bf16[27,64]{1,0:T(8,128)(2,1)} %param.31) | copy-start | bytes 10372
  7.2 11.0 %copy-start.17 = (bf16[27,64]{1,0:T(8,128)(2,1)S(1)}, bf16[27,64]{1,0:T(8,128)(2,1)}, u32[]{:S(2)}) copy-start(bf16[27,64]{1,0:T(8,128)(2,1)} %param.32) | copy-start | bytes 10372
  7.2 68.3 %all-gather.6.cloned.1.call-start = ((), (), s32[]{:S(2)}) async-start(), calls=%async_computation.2 | async-start | bytes 4055040 | tf_op jit(solution)/shard_map/all_gather | solution.py:458
  9.3 10.3 %copy-start.22 = (bf16[768]{0:T(1024)(128)(2,1)S(1)}, bf16[768]{0:T(1024)(128)(2,1)}, u32[]{:S(2)}) copy-start(bf16[768]{0:T(1024)(128)(2,1)} %param.38) | copy-start | bytes 4612
  9.3 24.6 %copy-start.23 = (bf16[768]{0:T(1024)(128)(2,1)S(1)}, bf16[768]{0:T(1024)(128)(2,1)}, u32[]{:S(2)}) copy-start(bf16[768]{0:T(1024)(128)(2,1)} %param.27) | copy-start | bytes 4612
  9.3 24.6 %copy-start.24 = (bf16[768]{0:T(1024)(128)(2,1)S(1)}, bf16[768]{0:T(1024)(128)(2,1)}, u32[]{:S(2)}) copy-start(bf16[768]{0:T(1024)(128)(2,1)} %param.28) | copy-start | bytes 4612
  9.3 157.8 %all-gather.8.cloned.1.call-start = ((), (), s32[]{:S(2)}) async-start(), calls=%async_computation.6 | async-start | bytes 11354112 | tf_op jit(solution)/shard_map/all_gather | solution.py:460
  11.3 24.0 %copy-start.25 = (bf16[768]{0:T(1024)(128)(2,1)S(1)}, bf16[768]{0:T(1024)(128)(2,1)}, u32[]{:S(2)}) copy-start(bf16[768]{0:T(1024)(128)(2,1)} %param.34) | copy-start | bytes 4612
  11.3 24.0 %copy-start.26 = (bf16[768]{0:T(1024)(128)(2,1)S(1)}, bf16[768]{0:T(1024)(128)(2,1)}, u32[]{:S(2)}) copy-start(bf16[768]{0:T(1024)(128)(2,1)} %param.35) | copy-start | bytes 4612
  11.3 24.1 %copy-start.27 = (bf16[768]{0:T(1024)(128)(2,1)S(1)}, bf16[768]{0:T(1024)(128)(2,1)}, u32[]{:S(2)}) copy-start(bf16[768]{0:T(1024)(128)(2,1)} %param.36) | copy-start | bytes 4612
  11.3 24.1 %copy-start.28 = (bf16[768]{0:T(1024)(128)(2,1)S(1)}, bf16[768]{0:T(1024)(128)(2,1)}, u32[]{:S(2)}) copy-start(bf16[768]{0:T(1024)(128)(2,1)} %param.40) | copy-start | bytes 4612
  11.4 515.4 %all-reduce.10.cloned.1.call-start = ((), (), s32[]{:S(2)}) async-start(), calls=%async_computation.3 | async-start | bytes 335872 | tf_op jit(solution)/shard_map/psum | solution.py:536
  12.8 24.0 %collective-permute-start.1 = (bf16[12,64,768]{2,1,0:T(8,128)(2,1)S(1)}, bf16[12,64,768]{2,1,0:T(8,128)(2,1)}, u32[]{:S(2)}, u32[]{:S(2)}) collective-permute-start(bf16[12,64,768]{2,1,0:T(8,128)(2,1)S(1)} %bitcast.101), channel_id=1, source_target_pairs={{1,0},{2,1},{3,2},{5,4},{6,5},{7,6},{9,8},{10,9},{11,10},{13,12},{... | collective-permute-start | bytes 3538952 | tf_op jit(solution)/shard_map/ppermute | solution.py:473
  14.9 21.8 %collective-permute-start = (bf16[6,64,768]{2,1,0:T(8,128)(2,1)}, bf16[6,64,768]{2,1,0:T(8,128)(2,1)S(1)}, u32[]{:S(2)}, u32[]{:S(2)}) collective-permute-start(bf16[6,64,768]{2,1,0:T(8,128)(2,1)} %bitcast.1), channel_id=1, source_target_pairs={{0,1},{1,2},{2,3},{4,5},{5,6},{6,7},{8,9},{9,10},{10,11},{12,13},{... | collective-permute-start | bytes 1769480 | tf_op jit(solution)/shard_map/ppermute | solution.py:472
  34.0 6.6 copy-start.15
  239.4 47.0 %copy-start.10 = (bf16[2240,768]{1,0:T(8,128)(2,1)S(1)}, bf16[2240,768]{1,0:T(8,128)(2,1)}, u32[]{:S(2)}) copy-start(bf16[2240,768]{1,0:T(8,128)(2,1)} %get-tuple-element.96) | copy-start | bytes 10321924
  286.4 6.1 copy-start.6
  286.4 6.7 copy-start.30
  292.5 2.0 copy-start.11
  294.5 4.1 copy-start.3
  347.9 3.3 copy-start.4
  347.9 3.0 copy-start.5
  348.6 12.2 %copy-start.21 = (f32[8,768]{1,0:T(8,128)S(1)}, f32[8,768]{1,0:T(8,128)}, u32[]{:S(2)}) copy-start(f32[8,768]{1,0:T(8,128)} %get-tuple-element.93) | copy-start | bytes 73732
  351.8 6.8 slice-start
  353.7 35.7 %collective-permute-start.2 = (bf16[12,64,768]{2,1,0:T(8,128)(2,1)}, bf16[12,64,768]{2,1,0:T(8,128)(2,1)}, u32[]{:S(2)}, u32[]{:S(2)}) collective-permute-start(bf16[12,64,768]{2,1,0:T(8,128)(2,1)} %copy.119), channel_id=1, source_target_pairs={{0,1},{1,2},{2,3},{4,5},{5,6},{6,7},{8,9},{9,10},{10,11},{12,13},{... | collective-permute-start | bytes 3538952 | tf_op jit(solution)/shard_map/ppermute | solution.py:514
  359.5 28.5 %collective-permute-start.3 = (bf16[6,64,768]{2,1,0:T(8,128)(2,1)}, bf16[6,64,768]{2,1,0:T(8,128)(2,1)}, u32[]{:S(2)}, u32[]{:S(2)}) collective-permute-start(bf16[6,64,768]{2,1,0:T(8,128)(2,1)} %copy.121), channel_id=1, source_target_pairs={{1,0},{2,1},{3,2},{5,4},{6,5},{7,6},{9,8},{10,9},{11,10},{13,12},{... | collective-permute-start | bytes 1769480 | tf_op jit(solution)/shard_map/ppermute | solution.py:513
  364.0 5.3 copy-start.19
  364.0 5.3 copy-start.20
  369.3 4.4 copy-start.9
  380.4 4.2 copy-start.7
  380.4 4.2 copy-start.8
  395.1 3.5 copy-start.1
  397.0 1.6 copy-start.2
  398.6 1.2 copy-start.12
  398.6 1.2 copy-start.18
  398.6 1.2 copy-start.14
  399.9 0.7 copy-start.13
  400.6 240.6 %reduce-scatter.3.cloned.1.call-start = ((), (), s32[]{:S(2)}) async-start(), calls=%async_computation.4 | async-start | bytes 4866048 | tf_op jit(solution)/shard_map/reduce_scatter | solution.py:533
  411.7 379.0 %reduce-scatter.5.cloned.1.call-start = ((), (), s32[]{:S(2)}) async-start(), calls=%async_computation.5 | async-start | bytes 11354112 | tf_op jit(solution)/shard_map/reduce_scatter | solution.py:528
Sparse Core Ops, SparseCore 0:
  11.5 63.9 all-gather.5
  79.0 88.0 all-gather.7
  400.7 126.0 all-reduce.9
  532.1 109.0 reduce-scatter.2
  648.0 142.6 reduce-scatter.4

commit v2 on v1

v2 whole, which is shorter than its diff:
```python
from functools import partial
import math

import jax
import jax.numpy as jnp
from jax import lax
from jax.experimental import pallas as pl
from jax.experimental.pallas import tpu as pltpu
from jax.sharding import PartitionSpec as P
import numpy as np

D = 768
HD = 64
GRID = 64
WIN = 14
SIDE = 5
PITCH = 16
KEYS = WIN * PITCH
EXT = 2 * WIN
PAIRS = D // (2 * HD)
OFFS = 2 * WIN - 1
EPSILON = 1e-06
FAR = -1e30
BF = jnp.bfloat16
F32 = jnp.float32
HIGH = lax.Precision.HIGHEST


def mm(left, right):
    return jnp.dot(left, right, preferred_element_type=F32)


def mm_t(left, right):
    return lax.dot_general(left, right, (((1,), (1,)), ((), ())), preferred_element_type=F32)


def t_mm(left, right):
    return lax.dot_general(left, right, (((0,), (0,)), ((), ())), preferred_element_type=F32)


def norm_parts(value):
    centered = value - jnp.mean(value, -1, keepdims=True)
    inverse = lax.rsqrt(jnp.mean(centered * centered, -1, keepdims=True) + EPSILON)
    return centered * inverse, inverse


def norm_back(upstream, hat, inverse, gain):
    scaled = upstream * gain
    return inverse * (
        scaled
        - jnp.mean(scaled, -1, keepdims=True)
        - hat * jnp.mean(scaled * hat, -1, keepdims=True)
    )


def score_tables():
    ahead = np.zeros((2, KEYS, 128), np.float32)
    back = np.zeros((2, KEYS, 128), np.float32)
    for head in range(2):
        base = 64 - 64 * head
        for c in range(WIN):
            for e in range(PITCH):
                k = c * PITCH + e
                if e >= WIN:
                    ahead[head, k, base] = FAR
                    continue
                ahead[head, k, base + 15 + c] = 1
                ahead[head, k, base + 1 + c] = 1
                ahead[head, k, base + 46 + e] = 1
                ahead[head, k, base + 32 + e] = 1
                back[head, k, base + WIN - 1 - c] = 1
                back[head, k, base + 32 + WIN - 1 - e] = 1
    return ahead, back


def offset_tables(rel_height, rel_width):
    def place(first, second, at_rows, at_cols):
        slab = jnp.zeros((64, HD), BF)
        slab = slab.at[at_rows : at_rows + OFFS].set(first)
        slab = slab.at[at_cols : at_cols + OFFS].set(second)
        low = jnp.concatenate([slab, jnp.zeros_like(slab)], 1)
        high = jnp.concatenate([jnp.zeros_like(slab), slab], 1)
        return jnp.concatenate([jnp.zeros_like(low), low, high, jnp.zeros_like(high)], 0)

    return (
        place(rel_height[::-1], rel_width[::-1], 2, 33),
        place(rel_height, rel_width, 0, 32),
    )


def whole(shape):
    return pl.BlockSpec(shape, lambda *_: (0,) * len(shape), pipeline_mode=pl.Buffered(1))


def windows_body(place_ref, above_ref, x_ref, below_ref, vec_ref, nw_ref, nat_ref, *, rows):
    band = pl.program_id(0)
    slot = place_ref[0]
    above, below = above_ref.shape[0], below_ref.shape[0]

    @pl.when(band == 0)
    def _():
        def normed(piece):
            hat, _ = norm_parts(piece.astype(F32))
            return hat * vec_ref[0:1] + vec_ref[1:2]

        def clear(i, carry):
            nat_ref[i, GRID : GRID + PITCH, :] = jnp.zeros((PITCH, D), F32)
            return carry

        def own(i, carry):
            nat_ref[2 * slot + i, 0:GRID, :] = normed(x_ref[i])
            return carry

        def before(i, carry):
            nat_ref[i, 0:GRID, :] = normed(above_ref[above - 2 * slot + i])
            return carry

        def after(i, carry):
            at = 2 * slot + rows + i
            inside = WIN * slot + at < GRID
            nat_ref[at, 0:GRID, :] = jnp.where(inside, normed(below_ref[i]), 0.0)
            return carry

        lax.fori_loop(0, EXT, clear, 0)
        lax.fori_loop(0, rows, own, 0)
        lax.fori_loop(0, 2 * slot, before, 0)
        lax.fori_loop(0, EXT - rows - 2 * slot, after, 0)

    keep = lax.broadcasted_iota(jnp.int32, (PITCH, D), 0) < WIN
    for b in range(SIDE):
        @pl.when(band == b)
        def _(b=b):
            def one(i, carry):
                piece = nat_ref[i, WIN * b : WIN * b + PITCH, :]
                start = pl.multiple_of(i * PITCH, PITCH)
                nw_ref[pl.ds(start, PITCH), :] = jnp.where(keep, piece, 0.0).astype(BF)
                return carry

            lax.fori_loop(0, EXT, one, 0)


def windows(place, above, x, below, vectors):
    rows = x.shape[0]
    return pl.pallas_call(
        partial(windows_body, rows=rows),
        grid_spec=pltpu.PrefetchScalarGridSpec(
            num_scalar_prefetch=1,
            grid=(SIDE,),
            in_specs=[whole(above.shape), whole(x.shape), whole(below.shape), whole((8, D))],
            out_specs=pl.BlockSpec((EXT * PITCH, D), lambda b, s: (b, 0)),
            scratch_shapes=[pltpu.VMEM((EXT, GRID + PITCH, D), F32)],
        ),
        out_shape=jax.ShapeDtypeStruct((SIDE * EXT * PITCH, D), BF),
        compiler_params=pltpu.CompilerParams(vmem_limit_bytes=63 << 20),
        cost_estimate=guess(8),
        name="windows",
    )(place, above, x, below, vectors)


def project_body(place_ref, nw_ref, *refs, rows, depth):
    *pieces, bias_ref, q_ref, k_ref, v_ref, w_ref, stage_ref = refs
    slot, z, x, y, c = (place_ref[i] for i in range(5))
    width = D // 4

    @pl.when(pl.program_id(0) == 0)
    def _():
        if len(pieces) == 1:
            w_ref[...] = pieces[0][...]
            return
        half = depth // 2
        for sibling in range(2):
            for part in range(2):
                ref = pieces[2 * sibling + part]
                count = ref.shape[2]
                for first in range(2):
                    for second in range(2):
                        dy, dx = (first, second) if part == 0 else (second, first)
                        from_slot = (y ^ dy) * 2 + (c ^ sibling)
                        for dz in range(count):
                            group = lax.rem(z - dz + count, count) * 2 + (x ^ dx)
                            at = pl.multiple_of(group * depth + part * half, half)
                            stage_ref[from_slot, pl.ds(at, half), :] = ref[first, second, dz]

        def join(i, carry):
            at = pl.ds(pl.multiple_of(i * 64, 64), 64)
            for kind in range(3):
                w_ref[at, kind * D : (kind + 1) * D] = jnp.concatenate(
                    [stage_ref[t, at, kind * width : (kind + 1) * width] for t in range(4)], 1
                )
            return carry

        lax.fori_loop(0, D // 64, join, 0)

    normed = nw_ref[...]
    own = nw_ref[pl.ds(pl.multiple_of(slot * 2 * PITCH, 2 * PITCH), rows * PITCH), :]
    q_ref[...] = (mm(own, w_ref[:, 0:D]) + bias_ref[0:1]).astype(BF)
    k_ref[...] = mm(normed, w_ref[:, D : 2 * D]).astype(BF)
    v_ref[...] = (mm(normed, w_ref[:, 2 * D :]) + bias_ref[1:2]).astype(BF)


def guess(us):
    return pl.CostEstimate(flops=int(us * 1.1e9), bytes_accessed=int(us * 3e6), transcendentals=0)


def project(place, normed, pieces, bias, rows, depth):
    of_k = pl.BlockSpec((EXT * PITCH, D), lambda b, s: (b, 0))
    of_q = pl.BlockSpec((rows * PITCH, D), lambda b, s: (b, 0))
    keys = jax.ShapeDtypeStruct((SIDE * EXT * PITCH, D), BF)
    return pl.pallas_call(
        partial(project_body, rows=rows, depth=depth),
        grid_spec=pltpu.PrefetchScalarGridSpec(
            num_scalar_prefetch=1,
            grid=(SIDE,),
            in_specs=[of_k] + [whole(p.shape) for p in pieces] + [whole((2, D))],
            out_specs=[of_q, of_k, of_k, whole((D, 3 * D))],
            scratch_shapes=[pltpu.VMEM((4, D, 3 * D // 4), BF)],
        ),
        out_shape=[
            jax.ShapeDtypeStruct((SIDE * rows * PITCH, D), BF), keys, keys,
            jax.ShapeDtypeStruct((D, 3 * D), BF),
        ],
        compiler_params=pltpu.CompilerParams(vmem_limit_bytes=63 << 20),
        cost_estimate=guess(18),
        name="project",
    )(place, normed, *pieces, bias)


def store_shards(place_ref, refs, value, first=0, lane=0):
    z, x = place_ref[1], place_ref[2]
    count, _, depth = refs.shape[:3]
    lanes = slice(lane, lane + value.shape[1])
    if depth % 32:
        refs[:, :, :, lanes] = value.reshape(count, 2, depth, value.shape[1])
        return
    for zd in range(value.shape[0] // (2 * depth)):
        for xd in range(2):
            start = (zd * 2 + xd) * depth
            refs[lax.rem(first + zd - z + count, count), x ^ xd, :, lanes] = value[start : start + depth]


def project_grad_body(place_ref, nw_ref, dq_ref, dk_ref, dv_ref, send_ref, keep_ref, bias_ref, *, rows, parts):
    step = pl.program_id(0)
    slot, c = place_ref[0], place_ref[4]
    width = D // 4
    lines = rows * PITCH

    @pl.when(step == 0)
    def _():
        bias_ref[0:1] = jnp.sum(dq_ref[...].astype(F32), 0, keepdims=True)
        bias_ref[1:2] = jnp.sum(dv_ref[...].astype(F32), 0, keepdims=True)

    grad_q = None
    for b in range(SIDE):
        start = pl.multiple_of(b * EXT * PITCH + slot * 2 * PITCH, 2 * PITCH)
        term = t_mm(nw_ref[pl.ds(start, lines), :], dq_ref[b * lines : (b + 1) * lines])
        grad_q = term if grad_q is None else grad_q + term
    grads = [grad_q.astype(BF)] + [t_mm(nw_ref[...], ref[...]).astype(BF) for ref in (dk_ref, dv_ref)]
    first = step * (keep_ref.shape[0] // parts)
    for core in range(2):
        value = jnp.concatenate([g[:, core * width : (core + 1) * width] for g in grads], 1)
        for sibling, ref in ((1, send_ref), (0, keep_ref)):
            @pl.when(c ^ core == sibling)
            def _(ref=ref, value=value):
                store_shards(place_ref, ref, value, first)


def project_grad(place, normed, dq, dk, dv, rows, shards):
    count, depth = shards[1], shards[3]
    parts = 2 if depth % 32 == 0 else 1
    out = jax.ShapeDtypeStruct((count, 2, depth, 3 * D // 4), BF)
    return pl.pallas_call(
        partial(project_grad_body, rows=rows, parts=parts),
        grid_spec=pltpu.PrefetchScalarGridSpec(
            num_scalar_prefetch=1,
            grid=(parts,),
            in_specs=[
                pl.BlockSpec((normed.shape[0], D // parts), lambda i, s: (0, i)),
                whole(dq.shape), whole(dk.shape), whole(dv.shape),
            ],
            out_specs=[whole(out.shape), whole(out.shape), whole((2, D // 2))],
        ),
        out_shape=[out, out, jax.ShapeDtypeStruct((2, D // 2), F32)],
        compiler_params=pltpu.CompilerParams(vmem_limit_bytes=63 << 20),
        cost_estimate=guess(6),
        name="project_grad",
    )(place, normed, dq, dk, dv)


def project_back_body(place_ref, *refs, rows):
    dqs, dks, dvs = refs[0:2], refs[2:4], refs[4:6]
    w_ref, above_ref, own_ref, below_ref, nat_ref, dq_ref, dk_ref, dv_ref = refs[6:]
    band = pl.program_id(0)
    slot, y = place_ref[0], place_ref[5]
    above, below = above_ref.shape[0], below_ref.shape[0]

    @pl.when(band == 0)
    def _():
        nat_ref[...] = jnp.zeros_like(nat_ref)

    for halves, ref in ((dqs, dq_ref), (dks, dk_ref), (dvs, dv_ref)):
        for i in range(2):
            at = pl.multiple_of((y ^ (1 - i)) * (D // 2), D // 2)
            ref[:, pl.ds(at, D // 2)] = halves[i][...]
    grad = mm_t(dk_ref[...], w_ref[:, D : 2 * D]) + mm_t(dv_ref[...], w_ref[:, 2 * D :])
    grad = grad.reshape(EXT, PITCH, D)
    direct = mm_t(dq_ref[...], w_ref[:, 0:D]).reshape(rows, PITCH, D)
    base = above - 2 * slot
    for b in range(SIDE):
        @pl.when(band == b)
        def _(b=b):
            at = slice(WIN * b, WIN * b + PITCH)
            nat_ref[pl.ds(base, EXT), at, :] = grad
            nat_ref[above : above + rows, at, :] += direct

    @pl.when(band == SIDE - 1)
    def _():
        above_ref[...] = nat_ref[0:above, 0:GRID, :].astype(BF)
        own_ref[...] = nat_ref[above : above + rows, 0:GRID, :]
        below_ref[...] = nat_ref[above + rows :, 0:GRID, :].astype(BF)


def project_back(place, dqs, dks, dvs, weight, rows, slots):
    above, below = 2 * (slots - 1), WIN - 2
    of_k = pl.BlockSpec((EXT * PITCH, D // 2), lambda b, s: (b, 0))
    of_q = pl.BlockSpec((rows * PITCH, D // 2), lambda b, s: (b, 0))
    shapes = [
        jax.ShapeDtypeStruct((above, GRID, D), BF),
        jax.ShapeDtypeStruct((rows, GRID, D), F32),
        jax.ShapeDtypeStruct((below, GRID, D), BF),
    ]
    return pl.pallas_call(
        partial(project_back_body, rows=rows),
        grid_spec=pltpu.PrefetchScalarGridSpec(
            num_scalar_prefetch=1,
            grid=(SIDE,),
            in_specs=[of_q, of_q, of_k, of_k, of_k, of_k, whole((D, 3 * D))],
            out_specs=[whole(s.shape) for s in shapes],
            scratch_shapes=[
                pltpu.VMEM((above + rows + below, GRID + PITCH, D), F32),
                pltpu.VMEM((rows * PITCH, D), BF),
                pltpu.VMEM((EXT * PITCH, D), BF),
                pltpu.VMEM((EXT * PITCH, D), BF),
            ],
        ),
        out_shape=shapes,
        compiler_params=pltpu.CompilerParams(vmem_limit_bytes=63 << 20),
        cost_estimate=guess(14),
        name="project_back",
    )(place, *dqs, *dks, *dvs, weight)


def head_lanes(shape, head):
    lane = lax.broadcasted_iota(jnp.int32, shape, 1)
    return lane < HD if head == 0 else lane >= HD


def window_split(slot, rows):
    first = WIN - 2 * slot
    return ((0, first * PITCH, 0), (first * PITCH, rows * PITCH, KEYS))


def attend_body(place_ref, q_ref, k_ref, v_ref, rel_ref, tab_ref, o_ref, p_ref, *, rows, slots):
    def variant(slot):
        queries = q_ref[...]
        count = rows * PITCH
        lane = lax.broadcasted_iota(jnp.int32, (PITCH, 128), 1)
        raw = mm(queries, rel_ref[...])
        outs = [None, None]
        for head in range(2):
            base = 64 - 64 * head
            parts = []
            for r in range(rows):
                here = raw[r * PITCH : (r + 1) * PITCH, 128 * head : 128 * head + 128]
                along_row = pltpu.roll(here, (2 * slot + r) % WIN, 1)
                along_col = pltpu.roll(here, 0, 1, stride=1, stride_axis=0)
                both = jnp.where(lane < base + 32, along_row, along_col)
                wanted = ((lane >= base + 15) & (lane < base + 29)) | ((lane >= base + 46) & (lane < base + 60))
                parts.append(jnp.where(wanted, both, 0.0))
            along = jnp.concatenate(parts, 0)
            high = along.astype(BF).astype(F32)
            extra = high + pltpu.roll(along - high, 114, 1)
            wide = lax.broadcasted_iota(jnp.int32, (count, 128), 1)
            extra = jnp.where(wide == base, 1.0, extra)
            mine = head_lanes((count, 128), head)
            left = jnp.where(mine, queries.astype(F32) * HD ** (-0.5), extra).astype(BF)
            out_parts = []
            for start, stop, key in window_split(slot, rows):
                keys = k_ref[key : key + KEYS]
                right = jnp.where(head_lanes((KEYS, 128), head), keys, tab_ref[head])
                scores = mm_t(left[start:stop], right)
                grown = jnp.exp(scores - jnp.max(scores, -1, keepdims=True))
                probs = (grown * (1.0 / jnp.sum(grown, -1, keepdims=True))).astype(BF)
                p_ref[0, head, start:stop, :] = probs
                out_parts.append(mm(probs, v_ref[key : key + KEYS]))
            outs[head] = jnp.concatenate(out_parts, 0)
        o_ref[...] = jnp.where(head_lanes((count, 128), 0), outs[0], outs[1]).astype(BF)

    for slot in range(slots):
        pl.when(place_ref[0] == slot)(partial(variant, slot))


def attend(slot, q, k, v, rel, table, rows, slots):
    queries = rows * PITCH
    steps = SIDE * PAIRS
    return pl.pallas_call(
        partial(attend_body, rows=rows, slots=slots),
        grid_spec=pltpu.PrefetchScalarGridSpec(
            num_scalar_prefetch=1,
            grid=(SIDE, PAIRS),
            in_specs=[
                pl.BlockSpec((queries, 128), lambda b, p, s: (b, p)),
                pl.BlockSpec((EXT * PITCH, 128), lambda b, p, s: (b, p)),
                pl.BlockSpec((EXT * PITCH, 128), lambda b, p, s: (b, p)),
                pl.BlockSpec((128, 256), lambda b, p, s: (0, 0)),
                pl.BlockSpec((2, KEYS, 128), lambda b, p, s: (0, 0, 0)),
            ],
            out_specs=[
                pl.BlockSpec((queries, 128), lambda b, p, s: (b, p)),
                pl.BlockSpec((1, 2, queries, KEYS), lambda b, p, s: (b * PAIRS + p, 0, 0, 0)),
            ],
        ),
        out_shape=[
            jax.ShapeDtypeStruct((SIDE * queries, D), BF),
            jax.ShapeDtypeStruct((steps, 2, queries, KEYS), BF),
        ],
        compiler_params=pltpu.CompilerParams(vmem_limit_bytes=63 << 20),
        cost_estimate=guess(43),
        name="attend",
    )(slot, q, k, v, rel, table)


def attend_back_body(
    place_ref, q_ref, k_ref, v_ref, p_ref, do_ref, rel_ref, tab_ref,
    dq_ref, dk_ref, dv_ref, drel_ref, *, rows, slots,
):
    count = rows * PITCH

    @pl.when((pl.program_id(0) == 0) & (pl.program_id(1) == 0))
    def _():
        drel_ref[...] = jnp.zeros_like(drel_ref)

    def variant(slot):
        queries = q_ref[...]
        scaled = (queries.astype(F32) * HD ** (-0.5)).astype(BF)
        lane = lax.broadcasted_iota(jnp.int32, (PITCH, 128), 1)
        upstream = do_ref[...]
        split = window_split(slot, rows)
        grad_keys = [[None, None], [None, None]]
        grad_values = [[None, None], [None, None]]
        grad_left, grad_raw = [], []
        for head in range(2):
            base = 64 - 64 * head
            grad_out = jnp.where(head_lanes((count, 128), head), upstream, jnp.zeros_like(upstream))
            lefts = []
            for w, (start, stop, key) in enumerate(split):
                keys, values = k_ref[key : key + KEYS], v_ref[key : key + KEYS]
                probs = p_ref[0, head, start:stop, :]
                grad_probs = mm_t(grad_out[start:stop], values)
                exact = probs.astype(F32)
                inner = jnp.sum(exact * grad_probs, -1, keepdims=True)
                grad_scores = (exact * (grad_probs - inner)).astype(BF)
                grad_values[head][w] = t_mm(probs, grad_out[start:stop])
                right = jnp.where(head_lanes((KEYS, 128), head), keys, tab_ref[head])
                lefts.append(mm(grad_scores, right))
                grad_keys[head][w] = t_mm(grad_scores, scaled[start:stop])
            left = jnp.concatenate(lefts, 0)
            grad_left.append(left)
            parts = []
            for r in range(rows):
                here = left[r * PITCH : (r + 1) * PITCH]
                on_row = jnp.where((lane >= base) & (lane < base + WIN), here, 0.0)
                on_col = jnp.where((lane >= base + 32) & (lane < base + 32 + WIN), here, 0.0)
                on_row = pltpu.roll(on_row, (2 * slot + r) % WIN, 1)
                on_col = pltpu.roll(on_col, 0, 1, stride=1, stride_axis=0)
                parts.append(on_row + on_col)
            grad_raw.append(jnp.concatenate(parts, 0))
        raw = jnp.concatenate(grad_raw, 1).astype(BF)
        first = head_lanes((count, 128), 0)
        direct = jnp.where(first, grad_left[0], grad_left[1]) * HD ** (-0.5)
        dq_ref[...] = (direct + mm(raw, rel_ref[...])).astype(BF)
        drel_ref[...] += t_mm(raw, queries)
        first = head_lanes((KEYS, 128), 0)
        for w, (_, _, key) in enumerate(split):
            dk_ref[key : key + KEYS] = jnp.where(first, grad_keys[0][w], grad_keys[1][w]).astype(BF)
            dv_ref[key : key + KEYS] = (grad_values[0][w] + grad_values[1][w]).astype(BF)

    for slot in range(slots):
        pl.when(place_ref[0] == slot)(partial(variant, slot))


def attend_back(slot, q, k, v, probs, grad_out, rel, table, rows, slots, group):
    queries = rows * PITCH
    half = PAIRS // 2
    pair = lambda p, s: p + half * (s[5] ^ (1 - group))
    of_q = pl.BlockSpec((queries, 128), lambda b, p, s: (b, pair(p, s)))
    of_k = pl.BlockSpec((EXT * PITCH, 128), lambda b, p, s: (b, pair(p, s)))
    to_q = pl.BlockSpec((queries, 128), lambda b, p, s: (b, p))
    to_k = pl.BlockSpec((EXT * PITCH, 128), lambda b, p, s: (b, p))
    return pl.pallas_call(
        partial(attend_back_body, rows=rows, slots=slots),
        grid_spec=pltpu.PrefetchScalarGridSpec(
            num_scalar_prefetch=1,
            grid=(SIDE, half),
            in_specs=[
                of_q, of_k, of_k,
                pl.BlockSpec((1, 2, queries, KEYS), lambda b, p, s: (b * PAIRS + pair(p, s), 0, 0, 0)),
                of_q,
                pl.BlockSpec((256, 128), lambda b, p, s: (0, 0)),
                pl.BlockSpec((2, KEYS, 128), lambda b, p, s: (0, 0, 0)),
            ],
            out_specs=[to_q, to_k, to_k, pl.BlockSpec((256, 128), lambda b, p, s: (0, 0))],
        ),
        out_shape=[
            jax.ShapeDtypeStruct((q.shape[0], D // 2), BF),
            jax.ShapeDtypeStruct((k.shape[0], D // 2), BF),
            jax.ShapeDtypeStruct((k.shape[0], D // 2), BF),
            jax.ShapeDtypeStruct((256, 128), F32),
        ],
        compiler_params=pltpu.CompilerParams(vmem_limit_bytes=63 << 20),
        cost_estimate=guess(24),
        name="attend_back",
    )(slot, q, k, v, probs, grad_out, rel, table)


def chunk_of(step, place):
    return (place[3] ^ (1 - step % 2)) * 2 + (place[4] ^ (1 - step // 2))


def feed_body(
    place_ref, o_ref, x_ref, g_ref, wo_ref, up_ref, down_ref, vec_ref, bias_ref,
    out_ref, dh_ref, do_ref, gas_ref, gak_ref, gbs_ref, gbk_ref, gvec_ref, gbias_ref,
    nat_ref, onat_ref, n2_ref, h_ref, y_ref, dn_ref, a_ref, du_ref, w_ref, *, rows,
):
    step = pl.program_id(0)
    steps = rows * GRID // 256
    lines = 256 // GRID
    width = D // 4

    @pl.when(step == 0)
    def _():
        for t in range(4):
            w_ref[:, t * width : (t + 1) * width] = wo_ref[:, t, :, 0:width].reshape(D, width)

        def one(i, carry):
            at = pl.ds(pl.multiple_of(i * 256, 256), 256)
            for b in range(SIDE):
                piece = o_ref[b, pl.ds(i * lines, lines)]
                nat_ref[:, WIN * b : WIN * b + PITCH, :] = piece.astype(F32)
            natural = nat_ref[:, 0:GRID, :].reshape(256, D).astype(BF)
            onat_ref[at, :] = natural
            hidden = x_ref[at, :].astype(F32) + mm_t(natural, w_ref[...]) + vec_ref[0:1]
            h_ref[at, :] = hidden
            hat, _ = norm_parts(hidden)
            n2_ref[at, :] = (hat * vec_ref[1:2] + vec_ref[2:3]).astype(BF)
            y_ref[at, :] = jnp.zeros((256, D), F32)
            dn_ref[at, :] = jnp.zeros((256, D), F32)
            return carry

        lax.fori_loop(0, steps, one, 0)

    up = up_ref[...].reshape(D, D)
    down = down_ref[...].reshape(D, D)

    def two(i, total):
        at = pl.ds(pl.multiple_of(i * 256, 256), 256)
        upper = mm(n2_ref[at, :], up) + bias_ref[...].reshape(1, D)
        cdf = 0.5 * (1.0 + lax.erf(upper * (1.0 / math.sqrt(2.0))))
        active = (upper * cdf).astype(BF)
        a_ref[at, :] = active
        y_ref[at, :] += mm_t(active, down)
        slope = cdf + upper * jnp.exp(-0.5 * upper * upper) * (1.0 / math.sqrt(2.0 * math.pi))
        delta = (mm(g_ref[at, :], down) * slope).astype(BF)
        du_ref[at, :] = delta
        dn_ref[at, :] += mm_t(delta, up)
        return total + jnp.sum(delta.astype(F32), 0, keepdims=True)

    total = lax.fori_loop(0, steps, two, jnp.zeros((1, D), F32))
    gbias_ref[...] = total.reshape(gbias_ref.shape)
    grad_up = t_mm(n2_ref[...], du_ref[...]).astype(BF)
    grad_down = t_mm(g_ref[...], a_ref[...]).astype(BF)

    other_chip = 1 - step % 2

    @pl.when(step < 2)
    def _():
        store_shards(place_ref, gas_ref.at[other_chip], grad_up)
        store_shards(place_ref, gbs_ref.at[other_chip], grad_down)

    @pl.when(step >= 2)
    def _():
        store_shards(place_ref, gak_ref.at[other_chip], grad_up)
        store_shards(place_ref, gbk_ref.at[other_chip], grad_down)

    @pl.when(step == pl.num_programs(0) - 1)
    def _():
        nat_ref[...] = jnp.zeros_like(nat_ref)
        gvec_ref[...] = jnp.zeros_like(gvec_ref)

        def three(i, carry):
            at = pl.ds(pl.multiple_of(i * 256, 256), 256)
            hidden = h_ref[at, :]
            grad = g_ref[at, :].astype(F32)
            hat, inverse = norm_parts(hidden)
            grad_normed = dn_ref[at, :]
            out_ref[at, :] = (hidden + y_ref[at, :] + vec_ref[3:4]).astype(BF)
            grad_hidden = grad + norm_back(grad_normed, hat, inverse, vec_ref[1:2])
            dh_ref[at, :] = grad_hidden
            branch = grad_hidden.astype(BF)
            n2_ref[at, :] = branch
            gvec_ref[0:1] += jnp.sum(grad_normed * hat, 0, keepdims=True)
            gvec_ref[1:2] += jnp.sum(grad_normed, 0, keepdims=True)
            gvec_ref[2:3] += jnp.sum(branch.astype(F32), 0, keepdims=True)
            gvec_ref[3:4] += jnp.sum(grad, 0, keepdims=True)
            grad_out = mm(branch, w_ref[...])
            nat_ref[:, 0:GRID, :] = grad_out.reshape(lines, GRID, D)
            keep = lax.broadcasted_iota(jnp.int32, (lines, PITCH, D), 1) < WIN
            for b in range(SIDE):
                piece = nat_ref[:, WIN * b : WIN * b + PITCH, :]
                do_ref[b, pl.ds(i * lines, lines)] = jnp.where(keep, piece, 0.0).astype(BF)
            return carry

        lax.fori_loop(0, steps, three, 0)
        grad_wo = t_mm(n2_ref[...], onat_ref[...]).astype(BF)
        for sibling, ref in ((1, gas_ref), (0, gak_ref)):
            for t in range(4):
                @pl.when(place_ref[4] ^ (t % 2) == sibling)
                def _(t=t, ref=ref):
                    store_shards(
                        place_ref, ref.at[place_ref[3] ^ (t // 2)], grad_wo[:, t * width : (t + 1) * width], lane=D
                    )


def feed(place, o, x, g, rest, vectors, up_bias, rows, shards):
    tokens = rows * GRID
    blocks, chunks, depth = rest.shape[:3]
    width = D // chunks
    slab = lambda column: pl.BlockSpec(
        (blocks, None, depth, D), lambda s, p: (0, chunk_of(s, p), 0, column)
    )
    line = pl.BlockSpec((None, 1, D), lambda s, p: (chunk_of(s, p), 0, 0))
    grid = (SIDE, rows, PITCH, D)
    first = jax.ShapeDtypeStruct((*shards, D + width), BF)
    second = jax.ShapeDtypeStruct((*shards, D), BF)
    shapes = [
        jax.ShapeDtypeStruct((tokens, D), BF),
        jax.ShapeDtypeStruct((tokens, D), F32),
        jax.ShapeDtypeStruct(grid, BF),
        first, first, second, second,
        jax.ShapeDtypeStruct((8, D), F32),
        jax.ShapeDtypeStruct((chunks, 1, D), F32),
    ]
    specs = [whole(s.shape) for s in shapes]
    specs[8] = line
    return pl.pallas_call(
        partial(feed_body, rows=rows),
        grid_spec=pltpu.PrefetchScalarGridSpec(
            num_scalar_prefetch=1,
            grid=(chunks,),
            in_specs=[
                whole(grid), whole((tokens, D)), whole((tokens, D)),
                pl.BlockSpec((blocks, chunks, depth, 256), lambda s, p: (0, 0, 0, 2 * D // 256), pipeline_mode=pl.Buffered(1)),
                slab(0), slab(1), whole((8, D)), line,
            ],
            out_specs=specs,
            scratch_shapes=[
                pltpu.VMEM((256 // GRID, GRID + PITCH, D), F32),
                pltpu.VMEM((tokens, D), BF),
                pltpu.VMEM((tokens, D), BF),
                pltpu.VMEM((tokens, D), F32),
                pltpu.VMEM((tokens, D), F32),
                pltpu.VMEM((tokens, D), F32),
                pltpu.VMEM((tokens, D), BF),
                pltpu.VMEM((tokens, D), BF),
                pltpu.VMEM((D, D), BF),
            ],
        ),
        out_shape=shapes,
        compiler_params=pltpu.CompilerParams(vmem_limit_bytes=63 << 20),
        cost_estimate=guess(55),
        name="feed",
    )(place, o, x, g, rest, rest, rest, vectors, up_bias)


def finish_body(own_ref, head_ref, tail_ref, x_ref, dh_ref, vec_ref, out_ref, sum_ref):
    rows, below, above = own_ref.shape[0], head_ref.shape[0], tail_ref.shape[0]
    sum_ref[...] = jnp.zeros_like(sum_ref)

    def line(i, low, high):
        grad = own_ref[i]
        if low:
            grad = grad + head_ref[i].astype(F32)
        if high:
            grad = grad + tail_ref[i - (rows - above)].astype(F32)
        hat, inverse = norm_parts(x_ref[i].astype(F32))
        out_ref[i] = (dh_ref[i] + norm_back(grad, hat, inverse, vec_ref[0:1])).astype(BF)
        sum_ref[0:1] += jnp.sum(grad * hat, 0, keepdims=True)
        sum_ref[1:2] += jnp.sum(grad, 0, keepdims=True)

    def over(start, stop, low, high):
        lax.fori_loop(start, stop, lambda i, carry: (line(i, low, high), carry)[1], 0)

    over(0, rows - above, True, False)
    over(rows - above, below, True, True)
    over(below, rows, False, True)


def finish(own, head, tail, x, dh, vectors):
    shapes = [jax.ShapeDtypeStruct(own.shape, BF), jax.ShapeDtypeStruct((8, D), F32)]
    return pl.pallas_call(
        finish_body,
        grid=(1,),
        in_specs=[whole(v.shape) for v in (own, head, tail, x, dh, vectors)],
        out_specs=[whole(v.shape) for v in shapes],
        out_shape=shapes,
        compiler_params=pltpu.CompilerParams(vmem_limit_bytes=63 << 20),
        cost_estimate=guess(5),
        name="finish",
    )(own, head, tail, x, dh, vectors)


def fold_body(*refs, plan):
    terms = sum(count for count, *_ in plan)
    ins, outs = refs[:terms], refs[terms:]
    for (count, axis, index), out in zip(plan, outs):
        here, ins = ins[:count], ins[count:]
        lead = out.shape[:-2]
        for at in np.ndindex(*lead):
            spot = at if axis is None else at[:axis] + (index,) + at[axis:]
            total = here[0][spot].astype(F32)
            for ref in here[1:]:
                total = total + ref[spot].astype(F32)
            out[at] = total.astype(out.dtype)


def fold(*results):
    count = None
    args, in_specs, out_specs, shapes, plan = [], [], [], [], []
    for terms, z_axis, axis, index in results:
        shape = terms[0].shape
        count = shape[z_axis]
        block = tuple(None if i == z_axis else n for i, n in enumerate(shape))
        spec = pl.BlockSpec(block, lambda i, z_axis=z_axis, n=len(shape): tuple(i if k == z_axis else 0 for k in range(n)))
        args += terms
        in_specs += [spec] * len(terms)
        left = [n for i, n in enumerate(shape) if i != axis]
        z_left = z_axis if axis is None or axis > z_axis else z_axis - 1
        block = tuple(None if i == z_left else n for i, n in enumerate(left))
        out_specs.append(
            pl.BlockSpec(block, lambda i, z_left=z_left, n=len(left): tuple(i if k == z_left else 0 for k in range(n)))
        )
        shapes.append(jax.ShapeDtypeStruct(tuple(left), BF))
        inner = None if axis is None else (axis if axis < z_axis else axis - 1)
        plan.append((len(terms), inner, index))
    size = sum(2 * int(np.prod(a.shape)) for a in args)
    return pl.pallas_call(
        partial(fold_body, plan=plan),
        grid=(count,),
        in_specs=in_specs,
        out_specs=out_specs,
        out_shape=shapes,
        compiler_params=pltpu.CompilerParams(vmem_limit_bytes=63 << 20),
        cost_estimate=guess(1 + size / 2e6),
        name="fold",
    )(*args)


AXES = ("z", "x", "y", "c")
SWAP = [(0, 1), (1, 0)]


def swap(value, axis):
    return lax.ppermute(value, axis, SWAP)


def shift(value, count, by):
    return lax.ppermute(value, "z", [(i, (i + by) % count) for i in range(count)])


def gather_lines(shard, count):
    half = shard.shape[0] // 2
    lines = [shard] + [shift(shard, count, k) for k in range(1, count)]
    first = jnp.stack([line[:half] for line in lines])
    second = jnp.stack([line[half:] for line in lines])
    return jnp.stack([first, swap(first, "x")]), jnp.stack([second, swap(second, "y")])


def gather_planes(first, second):
    first = jnp.stack([first, swap(first, "y")])
    second = jnp.stack([second, swap(second, "x")])
    return first, second, swap(first, "c"), swap(second, "c")


def along_z(pieces):
    count = pieces.shape[0]
    total = pieces[0].astype(F32)
    for k in range(1, count):
        total = total + shift(pieces[k], count, k).astype(F32)
    return total


def sum_all(value, count, fast):
    for axis in ("c", "y", "x"):
        value = value + swap(value, axis)
    if not fast:
        return lax.psum(value, "z")
    step = 1
    while step < count:
        value = value + lax.ppermute(value, "z", [(i, i ^ step) for i in range(count)])
        step *= 2
    return value


def body(
    features, first_gain, first_shift, qkv_weight, qv_bias, rel_height, rel_width, output_weight,
    output_bias, second_gain, second_shift, up_weight, up_bias, down_weight, down_bias, cotangent,
    *, count,
):
    depth, _, width = qkv_weight.shape
    hidden = up_weight.shape[1]
    tokens = features.shape[0]
    rows = tokens // GRID
    slots = 4
    fast = count <= 4 and depth % 32 == 0
    z, x, y, c = (lax.axis_index(a).astype(jnp.int32) for a in AXES)
    slot = 2 * y + c
    nought = jnp.zeros((), jnp.int32)
    place = jnp.stack([slot, z, x, y, c, y] if fast else [slot] + [nought] * 4 + [y])
    shards = (2, count, 2, depth)
    above, below = 2 * (slots - 1), WIN - 2

    grid_x = features.reshape(rows, GRID, D)
    pair = ("y", "c")
    up_pairs = [(s, s + 1) for s in range(slots - 1)]
    down_pairs = [(s + 1, s) for s in range(slots - 1)]
    from_above = lax.ppermute(grid_x[rows - above :], pair, up_pairs)
    from_below = lax.ppermute(grid_x[:below], pair, down_pairs)

    rest = jnp.concatenate([up_weight, down_weight, output_weight, jnp.zeros((depth, 256 - width), BF)], 1)
    rest_all = lax.all_gather(rest, AXES, axis=0).reshape(2 * count, slots, depth, 2 * hidden + 256)
    biases = jnp.concatenate([qv_bias.reshape(-1), up_bias])
    biases = jnp.where(jnp.arange(slots)[:, None] == slot, biases[None], jnp.zeros((), BF))
    biases = biases + swap(biases, "c")
    biases = (biases + swap(biases, "y")).astype(F32)
    qv_all = biases[:, : 2 * width].reshape(slots, 2, width).transpose(1, 0, 2).reshape(2, D)
    up_bias_all = biases[:, 2 * width :].reshape(slots, 1, hidden)

    vec_one = jnp.concatenate([first_gain[None], first_shift[None], jnp.zeros((6, D), BF)], 0).astype(F32)
    normed = windows(place, from_above, grid_x, from_below, vec_one)
    if fast:
        lines = gather_lines(qkv_weight.reshape(depth, 3 * width), count)
        normed, *lines = lax.optimization_barrier((normed, *lines))
        pieces = gather_planes(*lines)
    else:
        full = lax.all_gather(qkv_weight, AXES, axis=0).reshape(2 * count, slots, depth, 3, width)
        pieces = [full.transpose(0, 2, 3, 1, 4).reshape(D, 3 * D)]
    q, k, v, weight = project(place, normed, pieces, qv_all, rows, depth)
    ahead, back = score_tables()
    rel_ahead, rel_back = offset_tables(rel_height, rel_width)
    attended, probs = attend(place, q, k, v, rel_ahead.T, jnp.asarray(ahead, BF), rows, slots)

    vec_two = jnp.concatenate(
        [output_bias[None], second_gain[None], second_shift[None], down_bias[None], jnp.zeros((4, D), BF)], 0
    ).astype(F32)
    (
        output, grad_hidden, grad_out, a_send, a_keep, b_send, b_keep, grad_vec, grad_up_bias,
    ) = feed(
        place, attended.reshape(SIDE, rows, PITCH, D), features, cotangent, rest_all, vec_two, up_bias_all,
        rows, shards,
    )
    grad_windows = grad_out.reshape(-1, D)
    table = jnp.asarray(back, BF)
    if fast:
        a_got, b_got = swap(a_send, "c"), swap(b_send, "c")
    *half0, drel0 = attend_back(place, q, k, v, probs, grad_windows, rel_back, table, rows, slots, 0)
    if fast:
        a, b = [a_keep, a_got], [b_keep, b_got]
        a_away, a_here, b_away, b_here = fold((a, 1, 0, 1), (a, 1, 0, 0), (b, 1, 2, 1), (b, 1, 2, 0))
        place, a_away, b_away = lax.optimization_barrier((place, a_away, b_away))
        a_got, b_got = swap(a_away, "y"), swap(b_away, "x")
    first_send, first_keep, first_bias = project_grad(place, normed, *half0, rows, shards)
    if fast:
        first_got = swap(first_send, "c")
    *half1, drel1 = attend_back(place, q, k, v, probs, grad_windows, rel_back, table, rows, slots, 1)
    if fast:
        a, b = [a_here, a_got], [b_here, b_got]
        a_away, a_here, b_away, b_here, crossing = fold(
            (a, 0, 1, 1), (a, 0, 1, 0), (b, 1, 0, 1), (b, 1, 0, 0), ([first_keep, first_got], 0, None, None)
        )
        place, a_away, b_away, crossing = lax.optimization_barrier((place, a_away, b_away, crossing))
        a_got, b_got, crossing = swap(a_away, "x"), swap(b_away, "y"), swap(crossing, "y")
    dqs, dks, dvs = zip(half0, half1)
    to_above, total, to_below = project_back(place, dqs, dks, dvs, weight, rows, slots)
    from_below = lax.ppermute(to_above, pair, down_pairs)
    from_above = lax.ppermute(to_below, pair, up_pairs)
    place, to_above = lax.optimization_barrier((place, to_above))
    last_send, last_keep, last_bias = project_grad(place, normed, *half1, rows, shards)
    if fast:
        last_got = swap(last_send, "c")
        a, b = fold(([a_here, a_got], 0, None, None), ([b_here, b_got], 0, None, None))
        a, b = along_z(a), along_z(b)
        grad_up, grad_wo, grad_down = a[:, :hidden], a[:, hidden:], b
    grad_features, sums_one = finish(
        total, from_above, from_below, grid_x, grad_hidden.reshape(rows, GRID, D), vec_one
    )
    if fast:
        last = [last_keep, last_got, crossing]
        away, here = fold((last, 0, 1, 1), (last, 0, 1, 0))
        (last,) = fold(([here, swap(away, "x")], 0, None, None))
        grad_qkv = along_z(last)
    else:
        pairs = [
            (a_send, a_keep), (b_send, b_keep),
            [
                jnp.where(y == 0, jnp.stack([last, first]), jnp.stack([first, last]))
                for first, last in ((first_send, last_send), (first_keep, last_keep))
            ],
        ]
        a, grad_down, grad_qkv = [
            lax.psum_scatter(
                jnp.stack([keep, send], 3).transpose(1, 2, 0, 3, 4, 5).reshape(8 * count, depth, -1),
                AXES, scatter_dimension=0,
            ).astype(F32)
            for send, keep in pairs
        ]
        grad_up, grad_wo = a[:, :hidden], a[:, hidden:]
    drel = (drel0 + drel1).reshape(4, 64, 128)
    drel = drel[1, :, :HD] + drel[2, :, HD:]
    grad_qv = jnp.where(y == 0, jnp.concatenate([last_bias, first_bias], 1), jnp.concatenate([first_bias, last_bias], 1))
    small = jnp.concatenate(
        [grad_vec[:4], grad_up_bias.reshape(slots, hidden), sums_one[:2], grad_qv], 0
    )
    small = sum_all(jnp.concatenate([small.reshape(-1), drel.reshape(-1)]).reshape(-1, 512), count, fast).reshape(-1)
    vec = small[: 12 * D].reshape(12, D)
    drel = small[12 * D :].reshape(64, HD)
    qv = lax.dynamic_index_in_dim(vec[10:12].reshape(2, slots, width), slot, 1, keepdims=False)
    bias = lax.dynamic_index_in_dim(vec[4:8], slot, 0, keepdims=False)
    return (
        output,
        grad_features.reshape(tokens, D),
        vec[8],
        vec[9],
        grad_qkv.reshape(depth, 3, width),
        qv,
        drel[0:OFFS],
        drel[32 : 32 + OFFS],
        grad_wo,
        vec[2],
        vec[0],
        vec[1],
        grad_up,
        bias,
        grad_down,
        vec[3],
    )


def solution(mesh):
    token = P(AXES, None)
    square = P(("z", "x"), ("y", "c"))
    cube = P(("z", "x"), None, ("y", "c"))
    lane = P(("y", "c"))
    count = mesh.shape["dp"] // 2
    assert mesh.shape["tensor"] == 4
    return jax.shard_map(
        partial(body, count=count),
        mesh=jax.sharding.Mesh(mesh.devices.reshape(count, 2, 2, 2), AXES),
        in_specs=(
            token, P(), P(), cube, P(None, ("y", "c")), P(), P(), square, P(), P(), P(), square,
            lane, square, P(), token,
        ),
        out_specs=(
            token, token, P(), P(), cube, P(None, ("y", "c")), P(), P(), square, P(), P(), P(), square,
            lane, square, P(),
        ),
        check_vma=False,
    )
```

time: 811 us -> 421 us (0.52)
  waiting for transfers between devices: 378 us -> 47.1 us
  local copies, waits for them, and re-layouts: 170 us -> 22.4 us
  Pallas kernels: 162 us -> 256 us
  starting transfers between devices: 10.6 us -> 63.5 us
  matrix products: 24.8 us -> 0 us
  other arithmetic: 25.2 us -> 9.6 us
  blocking collectives: 14.1 us -> 0 us
    reduce_scatter x2 -> x0, waiting for transfers between devices: 256 us -> none  [the longest x1 148 us: body(): lax.psum_scatter(grad_rest.reshape(groups * slots, depth, width + 2 * hid...]
    pallas_call x2 -> x12, Pallas kernels: 72.8 us -> 161 us  [the longest x1 58.2 us: feed(): pl.pallas_call(partial(feed_body, rows=rows), grid_spec=pltpu.PrefetchSca...]
    psum x1 -> x0, waiting for transfers between devices: 86.4 us -> none  [body(): lax.psum(jnp.concatenate([grad_vec[:4].reshape(-1), grad_gain_one, grad_s...]
    ppermute x4 -> x39, starting transfers between devices: 10.4 us -> 63.4 us  [the longest x21 33.8 us: swap(): return lax.ppermute(value, axis, SWAP)]
    ppermute x4 -> x39, waiting for transfers between devices: 0.01 us -> 47.1 us  [the longest x21 34.1 us: swap(): return lax.ppermute(value, axis, SWAP)]
    all_gather x2 -> x1, waiting for transfers between devices: 35.2 us -> 0.01 us  [body(): lax.all_gather(rest, AXES, axis=0)]
    dynamic_update_slice x1 -> x0, local copies, waits for them, and re-layouts: 28.5 us -> none  [body(): lax.dynamic_update_slice_in_dim(wide, natural(grad_normed, EXT), above -...]
    dot_general x6 -> x0, matrix products: 24.8 us -> none  [the longest x3 13.6 us: t_mm(): lax.dot_general(left, right, (((0,), (0,)), ((), ())), preferred_element_...]
  transfers between devices with their start and end apart: 9 -> 40, of which waited for: 5 -> 9; matrix products, arithmetic and copies ran while one was open for 15% -> 6% of each run, Pallas kernels for 8% -> 39%
where the time goes in v2:
time: 421 us; the launch traced here: 413 us
  Pallas kernels  256 us (61%)
  starting transfers between devices  63.5 us (15%)
  waiting for transfers between devices  47.1 us (11%)
  local copies, waits for them, and re-layouts  22.4 us (5%)
  between operations  15.2 us (4%)
  other arithmetic  9.6 us (2%)
    pallas_call x1, Pallas kernels, feed(): pl.pallas_call(partial(feed_body, rows=rows), grid_spec=pltpu.PrefetchSca...  58.2 us
    pallas_call x2, Pallas kernels, attend_back(): pl.pallas_call(partial(attend_back_body, rows=rows, slots=slots), grid_sp...  51.3 us
    pallas_call x1, Pallas kernels, attend(): pl.pallas_call(partial(attend_body, rows=rows, slots=slots), grid_spec=pl...  43 us
    ppermute x21, waiting for transfers between devices, swap(): return lax.ppermute(value, axis, SWAP)  34.1 us
    ppermute x21, starting transfers between devices, swap(): return lax.ppermute(value, axis, SWAP)  33.8 us
    pallas_call x5, Pallas kernels, fold(): pl.pallas_call(partial(fold_body, plan=plan), grid=(count,), in_specs=in_...  29.9 us
    pallas_call x2, Pallas kernels, project_grad(): pl.pallas_call(partial(project_grad_body, rows=rows, parts=parts), grid_s...  21.7 us
    ppermute x12, starting transfers between devices, shift(): lax.ppermute(value, 'z', [(i, (i + by) % count) for i in range(count)])  21.3 us
  transfers between devices with their start and end apart: 40, of which 9 were waited for; matrix products, arithmetic and copies ran while one was open for 6% of the time, Pallas kernels for 39%

profile of v2, /device:TPU:0, one launch (start us, length us, event | category | flops | bytes accessed | tf_op | source)
XLA Modules:
  0.0 413.4 jit_solution(10085959270883671987)
XLA Ops:
  7.2 1.9 concatenate.55
  10.5 5.1 %collective-permute-start.4 = (bf16[96,576]{1,0:T(8,128)(2,1)S(1)}, bf16[96,576]{1,0:T(8,128)(2,1)S(1)}, u32[]{:S(2)}, u32[]{:S(2)}) collective-permute-start(bf16[96,576]{1,0:T(8,128)(2,1)S(1)} %copy.43), channel_id=1, source_target_pairs={{0,24},{8,0},{16,8},{24,16},{1,25},{9,1},{17,9},{25,17},{2,26},{10... | collective-permute-start | bytes 331784 | tf_op jit(solution)/shard_map/ppermute | solution.py:776
  16.6 2.1 collective-permute-start
  19.9 1.3 collective-permute-start.1
  23.7 2.6 collective-permute-done.3
  26.4 1.6 collective-permute-start.6
  28.0 1.6 collective-permute-start.5
  30.1 18.5 %collective-permute-done.6 = bf16[4,48,576]{2,1,0:T(8,128)(2,1)S(1)} collective-permute-done((bf16[4,48,576]{2,1,0:T(8,128)(2,1)S(1)}, bf16[4,48,576]{2,1,0:T(8,128)(2,1)S(1)}, u32[]{:S(2)}, u32[]{:S(2)}) %collective-permute-start.6) | collective-permute-done | bytes 221216 | tf_op jit(solution)/shard_map/ppermute | solution.py:772
  48.8 11.8 %windows.1.nw_ref = bf16[2240,768]{1,0:T(8,128)(2,1)} custom-call(s32[6]{0:T(128)} %stack.90.place_ref, bf16[6,64,768]{2,1,0:T(8,128)(2,1)} %collective-permute-done.above_ref, bf16[16,64,768]{2,1,0:T(8,128)(2,1)} %bitcast.76, bf16[12,64,768]{2,1,0:T(8,128)(2,1)} %collective-permute-done.1.below_ref, f32[8,768]{1,0:T(8,128)} %maximum_convert_fusion.vec_ref), custom_call_target="tpu_custom_call" | custom-call | flops 8800000000 | bytes 24000000 | tf_op jit(solution)/shard_map/windows/pallas_call | solution.py:144
  60.5 1.4 collective-permute-start.8
  66.0 6.2 %collective-permute-done.8 = bf16[2,4,48,576]{3,2,1,0:T(8,128)(2,1)S(1)} collective-permute-done((bf16[2,4,48,576]{3,2,1,0:T(8,128)(2,1)S(1)}, bf16[2,4,48,576]{3,2,1,0:T(8,128)(2,1)S(1)}, u32[]{:S(2)}, u32[]{:S(2)}) %collective-permute-start.8) | collective-permute-done | bytes 442400 | tf_op jit(solution)/shard_map/ppermute | solution.py:772
  73.4 2.7 collective-permute-start.12
  80.8 13.7 %project.1 = (bf16[1280,768]{1,0:T(8,128)(2,1)}, bf16[2240,768]{1,0:T(8,128)(2,1)}, bf16[2240,768]{1,0:T(8,128)(2,1)}, bf16[768,2304]{1,0:T(8,128)(2,1)}) custom-call(s32[6]{0:T(128)} %stack.90.place_ref, bf16[2240,768]{1,0:T(8,128)(2,1)} %windows.1.nw_ref, bf16[2,2,4,48,576]{4,3,2,1,0:T(8,128)(2,1)} %copy-done.2, bf16[2,2,4,48,576]{4,3,2,1,0:T(8,128)(2,1)} %copy-done.1, ...), custom_call_target="tpu_custom_call" | custom-call | flops 19800000512 | bytes 54000000 | tf_op jit(solution)/shard_map/project/pallas_call | solution.py:209
  94.4 43.0 %attend.1 = (bf16[1280,768]{1,0:T(8,128)(2,1)}, bf16[30,2,256,224]{3,2,1,0:T(8,128)(2,1)}) custom-call(s32[6]{0:T(128)} %stack.90.place_ref, bf16[1280,768]{1,0:T(8,128)(2,1)} %get-tuple-element.125.q_ref, bf16[2240,768]{1,0:T(8,128)(2,1)} %get-tuple-element.126.k_ref, bf16[2240,768]{1,0:T(8,128)(2,1)} %get-tuple-element.127.v_ref, ...), custom_call_target="tpu_custom_call" | custom-call | flops 47300001792 | bytes 129000000 | tf_op jit(solution)/shard_map/attend/pallas_call | solution.py:405
  137.4 58.2 %feed.1 = (bf16[1024,768]{1,0:T(8,128)(2,1)}, f32[1024,768]{1,0:T(8,128)}, bf16[5,16,16,768]{3,2,1,0:T(8,128)(2,1)}, bf16[2,4,2,96,960]{4,3,2,1,0:T(8,128)(2,1)}...) custom-call(s32[6]{0:T(128)} %stack.90.place_ref, ...), custom_call_target="tpu_custom_call" | custom-call | flops 60500000768 | bytes 165000000 | tf_op jit(solution)/shard_map/feed/pallas_call | solution.py:654
  195.7 2.6 collective-permute-start.13
  198.3 25.7 %attend_back.2 = (bf16[1280,384]{1,0:T(8,128)(2,1)}, bf16[2240,384]{1,0:T(8,128)(2,1)}, bf16[2240,384]{1,0:T(8,128)(2,1)}, f32[256,128]{1,0:T(8,128)}) custom-call(s32[6]{0:T(128)} %stack.90.place_ref, bf16[1280,768]{1,0:T(8,128)(2,1)} %get-tuple-element.125.q_ref, bf16[2240,768]{1,0:T(8,128)(2,1)} %get-tuple-element.126.k_ref, ...), custom_call_target="tpu_custom_call" | custom-call | flops 26400000000 | bytes 72000000 | tf_op jit(solution)/shard_map/attend_back/pallas_call | solution.py:499
  224.1 10.3 %fold.5 = (bf16[4,2,96,960]{3,2,1,0:T(8,128)(2,1)}, bf16[4,2,96,960]{3,2,1,0:T(8,128)(2,1)}, bf16[2,4,96,768]{3,2,1,0:T(8,128)(2,1)}, bf16[2,4,96,768]{3,2,1,0:T(8,128)(2,1)}) custom-call(bf16[2,4,2,96,960]{4,3,2,1,0:T(8,128)(2,1)} %get-tuple-element.130.refs_0_.refs_2_, bf16[2,4,2,96,960]{4,3,2,1,0:T(8,128)(2,1)} %collective-permute-done.13.refs_1_.refs_3_, ...), custom_call_target="tpu_custom_call" | custom-call | flops 12778515456 | bytes 34850496 | tf_op jit(solution)/shard_map/fold/pallas_call | solution.py:755
  234.4 2.6 collective-permute-start.16
  236.9 10.4 %collective-permute-start.15 = (bf16[4,2,96,960]{3,2,1,0:T(8,128)(2,1)}, bf16[4,2,96,960]{3,2,1,0:T(8,128)(2,1)}, u32[]{:S(2)}, u32[]{:S(2)}) collective-permute-start(bf16[4,2,96,960]{3,2,1,0:T(8,128)(2,1)} %get-tuple-element.138), channel_id=1, source_target_pairs={{0,2},{2,0},{1,3},{3,1},{4,6},{6,4},{5,7},{7,5},{8,10},{10,8},{9,1... | collective-permute-start | bytes 4423688 | tf_op jit(solution)/shard_map/ppermute | solution.py:772
  247.3 10.9 %project_grad.2 = (bf16[4,2,96,576]{3,2,1,0:T(8,128)(2,1)}, bf16[4,2,96,576]{3,2,1,0:T(8,128)(2,1)}, f32[2,384]{1,0:T(2,128)}) custom-call(s32[6]{0:T(128)} %stack.90.place_ref, bf16[2240,768]{1,0:T(8,128)(2,1)} %windows.1.nw_ref, bf16[1280,384]{1,0:T(8,128)(2,1)} %get-tuple-element.143.dq_ref.refs_0_, bf16[2240,384]{1,0:T(8,128)(2,1)} %get-tuple-element.144.dk_ref.refs_2_, ...), custom_call_target="tpu_custom_call" | custom-call | flops 6600000000 | bytes 18000000 | tf_op jit(solution)/shard_map/project_grad/pallas_call | solution.py:271
  258.2 25.5 %attend_back.3 = (bf16[1280,384]{1,0:T(8,128)(2,1)}, bf16[2240,384]{1,0:T(8,128)(2,1)}, bf16[2240,384]{1,0:T(8,128)(2,1)}, f32[256,128]{1,0:T(8,128)}) custom-call(s32[6]{0:T(128)} %stack.90.place_ref, bf16[1280,768]{1,0:T(8,128)(2,1)} %get-tuple-element.125.q_ref, bf16[2240,768]{1,0:T(8,128)(2,1)} %get-tuple-element.126.k_ref, ...), custom_call_target="tpu_custom_call" | custom-call | flops 26400000000 | bytes 72000000 | tf_op jit(solution)/shard_map/attend_back/pallas_call | solution.py:499
  284.7 7.7 %fold.6 = (bf16[4,96,960]{2,1,0:T(8,128)(2,1)}, bf16[4,96,960]{2,1,0:T(8,128)(2,1)}, bf16[4,96,768]{2,1,0:T(8,128)(2,1)}, bf16[4,96,768]{2,1,0:T(8,128)(2,1)}, bf16[4,2,96,576]{3,2,1,0:T(8,128)(2,1)}) custom-call(bf16[4,2,96,960]{3,2,1,0:T(8,128)(2,1)} %get-tuple-element.137.refs_0_.refs_2_, bf16[4,2,96,960]{3,2,1,0:T(8,128)(2,1)} %collective-permute-done.15.refs_1_.refs_3_, ...), custom_call_target="tpu_custom_call" | custom-call | flops 7912467456 | bytes 21579456 | tf_op jit(solution)/shard_map/fold/pallas_call | solution.py:755
  292.4 16.3 %project_back.1 = (bf16[6,64,768]{2,1,0:T(8,128)(2,1)}, f32[16,64,768]{2,1,0:T(8,128)}, bf16[12,64,768]{2,1,0:T(8,128)(2,1)}) custom-call(s32[6]{0:T(128)} %stack.90.place_ref, bf16[1280,384]{1,0:T(8,128)(2,1)} %get-tuple-element.143.dq_ref.refs_0_, bf16[1280,384]{1,0:T(8,128)(2,1)} %get-tuple-element.152.refs_1_.dq_ref, ...), custom_call_target="tpu_custom_call" | custom-call | flops 15399999488 | bytes 42000000 | tf_op jit(solution)/shard_map/project_back/pallas_call | solution.py:331
  309.6 10.9 %project_grad.3 = (bf16[4,2,96,576]{3,2,1,0:T(8,128)(2,1)}, bf16[4,2,96,576]{3,2,1,0:T(8,128)(2,1)}, f32[2,384]{1,0:T(2,128)}) custom-call(s32[6]{0:T(128)} %stack.90.place_ref, bf16[2240,768]{1,0:T(8,128)(2,1)} %windows.1.nw_ref, bf16[1280,384]{1,0:T(8,128)(2,1)} %get-tuple-element.152.refs_1_.dq_ref, bf16[2240,384]{1,0:T(8,128)(2,1)} %get-tuple-element.153.refs_3_.dk_ref, ...), custom_call_target="tpu_custom_call" | custom-call | flops 6600000000 | bytes 18000000 | tf_op jit(solution)/shard_map/project_grad/pallas_call | solution.py:271
  320.4 1.5 collective-permute-start.26
  322.0 3.1 collective-permute-start.18
  326.0 1.3 collective-permute-start.19
  327.3 1.7 collective-permute-done.31.refs_1_
  329.0 3.9 fold.9
  332.9 1.8 slice_bitcast_fusion.5
  334.7 2.1 collective-permute-start.36
  336.8 1.8 collective-permute-start.38
  338.6 7.2 %collective-permute-done.26.refs_2_.refs_5_ = bf16[4,2,96,576]{3,2,1,0:T(8,128)(2,1)} collective-permute-done((bf16[4,2,96,576]{3,2,1,0:T(8,128)(2,1)}, bf16[4,2,96,576]{3,2,1,0:T(8,128)(2,1)}, u32[]{:S(2)}, u32[]{:S(2)}) %collective-permute-start.26) | collective-permute-done | bytes 884768 | tf_op jit(solution)/shard_map/ppermute | solution.py:772
  345.8 2.4 collective-permute-start.37
  348.2 4.7 %fold.7 = (bf16[4,96,576]{2,1,0:T(8,128)(2,1)}, bf16[4,96,576]{2,1,0:T(8,128)(2,1)}) custom-call(bf16[4,2,96,576]{3,2,1,0:T(8,128)(2,1)} %get-tuple-element.169.refs_0_.refs_3_, bf16[4,2,96,576]{3,2,1,0:T(8,128)(2,1)} %collective-permute-done.25.refs_1_.refs_4_, bf16[4,2,96,576]{3,2,1,0:T(8,128)(2,1)} %collective-permute-done.26.refs_2_.refs_5_, ...), custom_call_target="tpu_custom_call" | custom-call | flops 4019628800 | bytes 10962624 | tf_op jit(solution)/shard_map/fold/pallas_call | solution.py:755
  354.0 9.7 %finish.1 = (bf16[16,64,768]{2,1,0:T(8,128)(2,1)}, f32[8,768]{1,0:T(8,128)}) custom-call(f32[16,64,768]{2,1,0:T(8,128)} %get-tuple-element.156.own_ref, bf16[12,64,768]{2,1,0:T(8,128)(2,1)} %collective-permute-done.18.head_ref, bf16[6,64,768]{2,1,0:T(8,128)(2,1)} %copy-done.22, bf16[16,64,768]{2,1,0:T(8,128)(2,1)} %bitcast.77, f32[16,64,768]{2,1,0:T(8,128)} %bitcast.94, ...), custom_call_target="tpu_custom_call" | custom-call | flops 5500000256 | bytes 15000000 | tf_op jit(solution)/shard_map/finish/pallas_call | solution.py:709
  364.5 2.7 collective-permute-start.20
  368.1 2.1 collective-permute-start.33
  370.2 1.8 collective-permute-start.35
  372.6 2.7 collective-permute-start.21
  375.3 1.8 fusion.3
  377.6 2.0 collective-permute-start.22
  379.6 3.3 fold.8
  384.0 1.6 collective-permute-start.28
  385.5 2.3 collective-permute-start.30
  388.7 5.4 %collective-permute-done.34 = bf16[96,960]{1,0:T(8,128)(2,1)} collective-permute-done((bf16[96,960]{1,0:T(8,128)(2,1)}, bf16[96,960]{1,0:T(8,128)(2,1)}, u32[]{:S(2)}, u32[]{:S(2)}) %collective-permute-start.34) | collective-permute-done | bytes 184352 | tf_op jit(solution)/shard_map/ppermute | solution.py:776
  397.1 4.9 %collective-permute-done.29 = bf16[96,576]{1,0:T(8,128)(2,1)S(1)} collective-permute-done((bf16[96,576]{1,0:T(8,128)(2,1)S(1)}, bf16[96,576]{1,0:T(8,128)(2,1)S(1)}, u32[]{:S(2)}, u32[]{:S(2)}) %collective-permute-start.29) | collective-permute-done | bytes 110624 | tf_op jit(solution)/shard_map/ppermute | solution.py:776
  (186 shorter events, 31.9 us)
Async XLA Ops:
  7.2 130.2 %all-gather.3.cloned.1.call-start = ((), (), s32[]{:S(2)}) async-start(), calls=%async_computation | async-start | bytes 11354112 | tf_op jit(solution)/shard_map/all_gather | solution.py:839
  10.4 10.8 %copy-start.13 = (bf16[768]{0:T(1024)(128)(2,1)S(1)}, bf16[768]{0:T(1024)(128)(2,1)}, u32[]{:S(2)}) copy-start(bf16[768]{0:T(1024)(128)(2,1)} %param.27) | copy-start | bytes 4612
  10.5 10.8 %copy-start.4 = (bf16[96,3,192]{2,0,1:T(8,128)(2,1)S(1)}, bf16[96,3,192]{2,0,1:T(8,128)(2,1)}, u32[]{:S(2)}) copy-start(bf16[96,3,192]{2,0,1:T(8,128)(2,1)} %param.29) | copy-start | bytes 331780
  10.5 13.2 %collective-permute-start.4 = (bf16[96,576]{1,0:T(8,128)(2,1)S(1)}, bf16[96,576]{1,0:T(8,128)(2,1)S(1)}, u32[]{:S(2)}, u32[]{:S(2)}) collective-permute-start(bf16[96,576]{1,0:T(8,128)(2,1)S(1)} %copy.43), channel_id=1, source_target_pairs={{0,24},{8,0},{16,8},{24,16},{1,25},{9,1},{17,9},{25,17},{2,26},{10... | collective-permute-start | bytes 331784 | tf_op jit(solution)/shard_map/ppermute | solution.py:776
  15.6 10.7 %collective-permute-start.3 = (bf16[96,576]{1,0:T(8,128)(2,1)S(1)}, bf16[96,576]{1,0:T(8,128)(2,1)S(1)}, u32[]{:S(2)}, u32[]{:S(2)}) collective-permute-start(bf16[96,576]{1,0:T(8,128)(2,1)S(1)} %copy.43), channel_id=1, source_target_pairs={{0,16},{8,24},{16,0},{24,8},{1,17},{9,25},{17,1},{25,9},{2,18},{10... | collective-permute-start | bytes 331784 | tf_op jit(solution)/shard_map/ppermute | solution.py:776
  15.6 10.7 %collective-permute-start.2 = (bf16[96,576]{1,0:T(8,128)(2,1)S(1)}, bf16[96,576]{1,0:T(8,128)(2,1)S(1)}, u32[]{:S(2)}, u32[]{:S(2)}) collective-permute-start(bf16[96,576]{1,0:T(8,128)(2,1)S(1)} %copy.43), channel_id=1, source_target_pairs={{0,8},{8,16},{16,24},{24,0},{1,9},{9,17},{17,25},{25,1},{2,10},{10... | collective-permute-start | bytes 331784 | tf_op jit(solution)/shard_map/ppermute | solution.py:776
  16.6 32.1 %collective-permute-start = (bf16[6,64,768]{2,1,0:T(8,128)(2,1)S(1)}, bf16[6,64,768]{2,1,0:T(8,128)(2,1)}, u32[]{:S(2)}, u32[]{:S(2)}) collective-permute-start(bf16[6,64,768]{2,1,0:T(8,128)(2,1)S(1)} %bitcast.81), channel_id=1, source_target_pairs={{0,1},{1,2},{2,3},{4,5},{5,6},{6,7},{8,9},{9,10},{10,11},{12,13},{... | collective-permute-start | bytes 1769480 | tf_op jit(solution)/shard_map/ppermute | solution.py:835
  19.9 28.9 %collective-permute-start.1 = (bf16[12,64,768]{2,1,0:T(8,128)(2,1)}, bf16[12,64,768]{2,1,0:T(8,128)(2,1)}, u32[]{:S(2)}, u32[]{:S(2)}) collective-permute-start(bf16[12,64,768]{2,1,0:T(8,128)(2,1)} %bitcast.7), channel_id=1, source_target_pairs={{1,0},{2,1},{3,2},{5,4},{6,5},{7,6},{9,8},{10,9},{11,10},{13,12},{... | collective-permute-start | bytes 3538952 | tf_op jit(solution)/shard_map/ppermute | solution.py:836
  26.4 22.2 %collective-permute-start.6 = (bf16[4,48,576]{2,1,0:T(8,128)(2,1)S(1)}, bf16[4,48,576]{2,1,0:T(8,128)(2,1)S(1)}, u32[]{:S(2)}, u32[]{:S(2)}) collective-permute-start(bf16[4,48,576]{2,1,0:T(8,128)(2,1)S(1)} %get-tuple-element.228), channel_id=1, source_target_pairs={{0,2},{2,0},{1,3},{3,1},{4,6},{6,4},{5,7},{7,5},{8,10},{10,8},{9,1... | collective-permute-start | bytes 663560 | tf_op jit(solution)/shard_map/ppermute | solution.py:772
  28.0 20.6 %collective-permute-start.5 = (bf16[4,48,576]{2,1,0:T(8,128)(2,1)S(1)}, bf16[4,48,576]{2,1,0:T(8,128)(2,1)S(1)}, u32[]{:S(2)}, u32[]{:S(2)}) collective-permute-start(bf16[4,48,576]{2,1,0:T(8,128)(2,1)S(1)} %get-tuple-element.230), channel_id=1, source_target_pairs={{0,4},{4,0},{1,5},{5,1},{2,6},{6,2},{3,7},{7,3},{8,12},{12,8},{9,1... | collective-permute-start | bytes 663560 | tf_op jit(solution)/shard_map/ppermute | solution.py:772
  60.5 11.9 %collective-permute-start.7 = (bf16[2,4,48,576]{3,2,1,0:T(8,128)(2,1)S(1)}, bf16[2,4,48,576]{3,2,1,0:T(8,128)(2,1)S(1)}, u32[]{:S(2)}, u32[]{:S(2)}) collective-permute-start(bf16[2,4,48,576]{3,2,1,0:T(8,128)(2,1)S(1)} %pad_maximum_fusion.2), channel_id=1, source_target_pairs={{0,2},{2,0},{1,3},{3,1},{4,6},{6,4},{5,7},{7,5},{8,10},{10,8},{9,1... | collective-permute-start | bytes 1327112 | tf_op jit(solution)/shard_map/ppermute | solution.py:772
  60.5 11.6 %collective-permute-start.8 = (bf16[2,4,48,576]{3,2,1,0:T(8,128)(2,1)S(1)}, bf16[2,4,48,576]{3,2,1,0:T(8,128)(2,1)S(1)}, u32[]{:S(2)}, u32[]{:S(2)}) collective-permute-start(bf16[2,4,48,576]{3,2,1,0:T(8,128)(2,1)S(1)} %pad_maximum_fusion.3), channel_id=1, source_target_pairs={{0,4},{4,0},{1,5},{5,1},{2,6},{6,2},{3,7},{7,3},{8,12},{12,8},{9,1... | collective-permute-start | bytes 1327112 | tf_op jit(solution)/shard_map/ppermute | solution.py:772
  62.7 10.5 %collective-permute-start.11 = (bf16[4,1152]{1,0:T(4,128)(2,1)S(1)}, bf16[4,1152]{1,0:T(4,128)(2,1)S(1)}, u32[]{:S(2)}, u32[]{:S(2)}) collective-permute-start(bf16[4,1152]{1,0:T(4,128)(2,1)S(1)} %broadcast_select_fusion), channel_id=1, source_target_pairs={{0,1},{1,0},{2,3},{3,2},{4,5},{5,4},{6,7},{7,6},{8,9},{9,8},{10,11... | collective-permute-start | bytes 27656 | tf_op jit(solution)/shard_map/ppermute | solution.py:772
  72.4 7.4 %collective-permute-start.10 = (bf16[2,2,4,48,576]{4,3,2,1,0:T(8,128)(2,1)S(1)}, bf16[2,2,4,48,576]{4,3,2,1,0:T(8,128)(2,1)}, u32[]{:S(2)}, u32[]{:S(2)}) collective-permute-start(bf16[2,2,4,48,576]{4,3,2,1,0:T(8,128)(2,1)S(1)} %pad_maximum_fusion.1.refs_1_), channel_id=1, source_target_pairs={{0,1},{1,0},{2,3},{3,2},{4,5},{5,4},{6,7},{7,6},{8,9},{9,8},{10,11... | collective-permute-start | bytes 2654216 | tf_op jit(solution)/shard_map/ppermute | solution.py:772
  73.3 6.5 %collective-permute-start.9 = (bf16[2,2,4,48,576]{4,3,2,1,0:T(8,128)(2,1)S(1)}, bf16[2,2,4,48,576]{4,3,2,1,0:T(8,128)(2,1)S(1)}, u32[]{:S(2)}, u32[]{:S(2)}) collective-permute-start(bf16[2,2,4,48,576]{4,3,2,1,0:T(8,128)(2,1)S(1)} %pad_maximum_fusion.refs_0_), channel_id=1, source_target_pairs={{0,1},{1,0},{2,3},{3,2},{4,5},{5,4},{6,7},{7,6},{8,9},{9,8},{10,11... | collective-permute-start | bytes 2654216 | tf_op jit(solution)/shard_map/ppermute | solution.py:772
  73.4 4.9 %collective-permute-start.12 = (bf16[4,1152]{1,0:T(4,128)(2,1)S(1)}, bf16[4,1152]{1,0:T(4,128)(2,1)S(1)}, u32[]{:S(2)}, u32[]{:S(2)}) collective-permute-start(bf16[4,1152]{1,0:T(4,128)(2,1)S(1)} %fusion.15), channel_id=1, source_target_pairs={{0,2},{2,0},{1,3},{3,1},{4,6},{6,4},{5,7},{7,5},{8,10},{10,8},{9,1... | collective-permute-start | bytes 27656 | tf_op jit(solution)/shard_map/ppermute | solution.py:772
  195.7 28.4 %collective-permute-start.13 = (bf16[2,4,2,96,960]{4,3,2,1,0:T(8,128)(2,1)}, bf16[2,4,2,96,960]{4,3,2,1,0:T(8,128)(2,1)}, u32[]{:S(2)}, u32[]{:S(2)}) collective-permute-start(bf16[2,4,2,96,960]{4,3,2,1,0:T(8,128)(2,1)} %get-tuple-element.131), channel_id=1, source_target_pairs={{0,1},{1,0},{2,3},{3,2},{4,5},{5,4},{6,7},{7,6},{8,9},{9,8},{10,11... | collective-permute-start | bytes 8847368 | tf_op jit(solution)/shard_map/ppermute | solution.py:772
  198.2 25.8 %collective-permute-start.14 = (bf16[2,4,2,96,768]{4,3,2,1,0:T(8,128)(2,1)}, bf16[2,4,2,96,768]{4,3,2,1,0:T(8,128)(2,1)}, u32[]{:S(2)}, u32[]{:S(2)}) collective-permute-start(bf16[2,4,2,96,768]{4,3,2,1,0:T(8,128)(2,1)} %get-tuple-element.133), channel_id=1, source_target_pairs={{0,1},{1,0},{2,3},{3,2},{4,5},{5,4},{6,7},{7,6},{8,9},{9,8},{10,11... | collective-permute-start | bytes 7077896 | tf_op jit(solution)/shard_map/ppermute | solution.py:772
  234.4 49.4 %collective-permute-start.16 = (bf16[2,4,96,768]{3,2,1,0:T(8,128)(2,1)}, bf16[2,4,96,768]{3,2,1,0:T(8,128)(2,1)}, u32[]{:S(2)}, u32[]{:S(2)}) collective-permute-start(bf16[2,4,96,768]{3,2,1,0:T(8,128)(2,1)} %get-tuple-element.140), channel_id=1, source_target_pairs={{0,4},{4,0},{1,5},{5,1},{2,6},{6,2},{3,7},{7,3},{8,12},{12,8},{9,1... | collective-permute-start | bytes 3538952 | tf_op jit(solution)/shard_map/ppermute | solution.py:772
  236.9 46.9 %collective-permute-start.15 = (bf16[4,2,96,960]{3,2,1,0:T(8,128)(2,1)}, bf16[4,2,96,960]{3,2,1,0:T(8,128)(2,1)}, u32[]{:S(2)}, u32[]{:S(2)}) collective-permute-start(bf16[4,2,96,960]{3,2,1,0:T(8,128)(2,1)} %get-tuple-element.138), channel_id=1, source_target_pairs={{0,2},{2,0},{1,3},{3,1},{4,6},{6,4},{5,7},{7,5},{8,10},{10,8},{9,1... | collective-permute-start | bytes 4423688 | tf_op jit(solution)/shard_map/ppermute | solution.py:772
  258.2 25.5 %collective-permute-start.17 = (bf16[4,2,96,576]{3,2,1,0:T(8,128)(2,1)}, bf16[4,2,96,576]{3,2,1,0:T(8,128)(2,1)S(1)}, u32[]{:S(2)}, u32[]{:S(2)}) collective-permute-start(bf16[4,2,96,576]{3,2,1,0:T(8,128)(2,1)} %get-tuple-element.147), channel_id=1, source_target_pairs={{0,1},{1,0},{2,3},{3,2},{4,5},{5,4},{6,7},{7,6},{8,9},{9,8},{10,11... | collective-permute-start | bytes 2654216 | tf_op jit(solution)/shard_map/ppermute | solution.py:772
  308.8 13.1 %copy-start.9 = (f32[8,768]{1,0:T(8,128)S(1)}, f32[8,768]{1,0:T(8,128)}, u32[]{:S(2)}) copy-start(f32[8,768]{1,0:T(8,128)} %get-tuple-element.161) | copy-start | bytes 73732
  308.8 13.1 %copy-start.8 = (f32[4,1,768]{2,1,0:T(1,128)S(1)}, f32[4,1,768]{2,1,0:T(1,128)}, u32[]{:S(2)}) copy-start(f32[4,1,768]{2,1,0:T(1,128)} %get-tuple-element.162) | copy-start | bytes 36868
  308.8 13.1 %copy-start.5 = (f32[256,128]{1,0:T(8,128)S(1)}, f32[256,128]{1,0:T(8,128)}, u32[]{:S(2)}) copy-start(f32[256,128]{1,0:T(8,128)} %get-tuple-element.167) | copy-start | bytes 393220
  308.8 13.1 %copy-start.6 = (f32[256,128]{1,0:T(8,128)S(1)}, f32[256,128]{1,0:T(8,128)}, u32[]{:S(2)}) copy-start(f32[256,128]{1,0:T(8,128)} %get-tuple-element.168) | copy-start | bytes 393220
  308.8 16.4 %copy-start.11 = (f32[2,384]{1,0:T(2,128)S(1)}, f32[2,384]{1,0:T(2,128)}, u32[]{:S(2)}) copy-start(f32[2,384]{1,0:T(2,128)} %get-tuple-element.166) | copy-start | bytes 9220
  308.8 17.2 %collective-permute-start.32 = (bf16[4,96,768]{2,1,0:T(8,128)(2,1)}, bf16[4,96,768]{2,1,0:T(8,128)(2,1)}, u32[]{:S(2)}, u32[]{:S(2)}) collective-permute-start(bf16[4,96,768]{2,1,0:T(8,128)(2,1)} %get-tuple-element.177), channel_id=1, source_target_pairs={{0,2},{2,0},{1,3},{3,1},{4,6},{6,4},{5,7},{7,5},{8,10},{10,8},{9,1... | collective-permute-start | bytes 1769480 | tf_op jit(solution)/shard_map/ppermute | solution.py:772
  309.5 19.5 %collective-permute-start.31 = (bf16[4,96,960]{2,1,0:T(8,128)(2,1)}, bf16[4,96,960]{2,1,0:T(8,128)(2,1)}, u32[]{:S(2)}, u32[]{:S(2)}) collective-permute-start(bf16[4,96,960]{2,1,0:T(8,128)(2,1)} %get-tuple-element.175), channel_id=1, source_target_pairs={{0,4},{4,0},{1,5},{5,1},{2,6},{6,2},{3,7},{7,3},{8,12},{12,8},{9,1... | collective-permute-start | bytes 2211848 | tf_op jit(solution)/shard_map/ppermute | solution.py:772
  320.4 16.4 %collective-permute-start.25 = (bf16[4,2,96,576]{3,2,1,0:T(8,128)(2,1)}, bf16[4,2,96,576]{3,2,1,0:T(8,128)(2,1)}, u32[]{:S(2)}, u32[]{:S(2)}) collective-permute-start(bf16[4,2,96,576]{3,2,1,0:T(8,128)(2,1)} %get-tuple-element.170), channel_id=1, source_target_pairs={{0,1},{1,0},{2,3},{3,2},{4,5},{5,4},{6,7},{7,6},{8,9},{9,8},{10,11... | collective-permute-start | bytes 2654216 | tf_op jit(solution)/shard_map/ppermute | solution.py:772
  320.4 25.4 %collective-permute-start.26 = (bf16[4,2,96,576]{3,2,1,0:T(8,128)(2,1)}, bf16[4,2,96,576]{3,2,1,0:T(8,128)(2,1)}, u32[]{:S(2)}, u32[]{:S(2)}) collective-permute-start(bf16[4,2,96,576]{3,2,1,0:T(8,128)(2,1)} %get-tuple-element.171), channel_id=1, source_target_pairs={{0,2},{2,0},{1,3},{3,1},{4,6},{6,4},{5,7},{7,5},{8,10},{10,8},{9,1... | collective-permute-start | bytes 2654216 | tf_op jit(solution)/shard_map/ppermute | solution.py:772
  322.0 32.0 %collective-permute-start.18 = (bf16[12,64,768]{2,1,0:T(8,128)(2,1)}, bf16[12,64,768]{2,1,0:T(8,128)(2,1)}, u32[]{:S(2)}, u32[]{:S(2)}) collective-permute-start(bf16[12,64,768]{2,1,0:T(8,128)(2,1)} %get-tuple-element.157), channel_id=1, source_target_pairs={{0,1},{1,2},{2,3},{4,5},{5,6},{6,7},{8,9},{9,10},{10,11},{12,13},{... | collective-permute-start | bytes 3538952 | tf_op jit(solution)/shard_map/ppermute | solution.py:894
  326.0 26.9 %collective-permute-start.19 = (bf16[6,64,768]{2,1,0:T(8,128)(2,1)}, bf16[6,64,768]{2,1,0:T(8,128)(2,1)S(1)}, u32[]{:S(2)}, u32[]{:S(2)}) collective-permute-start(bf16[6,64,768]{2,1,0:T(8,128)(2,1)} %get-tuple-element.158), channel_id=1, source_target_pairs={{1,0},{2,1},{3,2},{5,4},{6,5},{7,6},{9,8},{10,9},{11,10},{13,12},{... | collective-permute-start | bytes 1769480 | tf_op jit(solution)/shard_map/ppermute | solution.py:893
  334.7 35.5 %collective-permute-start.36 = (bf16[96,768]{1,0:T(8,128)(2,1)}, bf16[96,768]{1,0:T(8,128)(2,1)S(1)}, u32[]{:S(2)}, u32[]{:S(2)}) collective-permute-start(bf16[96,768]{1,0:T(8,128)(2,1)} %get-tuple-element.221), channel_id=1, source_target_pairs={{0,8},{8,16},{16,24},{24,0},{1,9},{9,17},{17,25},{25,1},{2,10},{10... | collective-permute-start | bytes 442376 | tf_op jit(solution)/shard_map/ppermute | solution.py:776
  336.8 35.2 %collective-permute-start.38 = (bf16[96,768]{1,0:T(8,128)(2,1)}, bf16[96,768]{1,0:T(8,128)(2,1)}, u32[]{:S(2)}, u32[]{:S(2)}) collective-permute-start(bf16[96,768]{1,0:T(8,128)(2,1)} %get-tuple-element.222), channel_id=1, source_target_pairs={{0,24},{8,0},{16,8},{24,16},{1,25},{9,1},{17,9},{25,17},{2,26},{10... | collective-permute-start | bytes 442376 | tf_op jit(solution)/shard_map/ppermute | solution.py:776
  345.8 26.8 %collective-permute-start.37 = (bf16[96,768]{1,0:T(8,128)(2,1)}, bf16[96,768]{1,0:T(8,128)(2,1)}, u32[]{:S(2)}, u32[]{:S(2)}) collective-permute-start(bf16[96,768]{1,0:T(8,128)(2,1)} %get-tuple-element.223), channel_id=1, source_target_pairs={{0,16},{8,24},{16,0},{24,8},{1,17},{9,25},{17,1},{25,9},{2,18},{10... | collective-permute-start | bytes 442376 | tf_op jit(solution)/shard_map/ppermute | solution.py:776
  352.9 26.7 %collective-permute-start.27 = (bf16[4,96,576]{2,1,0:T(8,128)(2,1)}, bf16[4,96,576]{2,1,0:T(8,128)(2,1)}, u32[]{:S(2)}, u32[]{:S(2)}) collective-permute-start(bf16[4,96,576]{2,1,0:T(8,128)(2,1)} %get-tuple-element.173), channel_id=1, source_target_pairs={{0,4},{4,0},{1,5},{5,1},{2,6},{6,2},{3,7},{7,3},{8,12},{12,8},{9,1... | collective-permute-start | bytes 1327112 | tf_op jit(solution)/shard_map/ppermute | solution.py:772
  354.0 13.2 %copy-start.3 = (bf16[4,96,960]{2,1,0:T(8,128)(2,1)S(1)}, bf16[4,96,960]{2,1,0:T(8,128)(2,1)}, u32[]{:S(2)}) copy-start(bf16[4,96,960]{2,1,0:T(8,128)(2,1)} %get-tuple-element.178) | copy-start | bytes 2211844
  364.5 3.6 collective-permute-start.20
  368.1 19.7 %collective-permute-start.33 = (bf16[96,960]{1,0:T(8,128)(2,1)}, bf16[96,960]{1,0:T(8,128)(2,1)}, u32[]{:S(2)}, u32[]{:S(2)}) collective-permute-start(bf16[96,960]{1,0:T(8,128)(2,1)} %get-tuple-element.218), channel_id=1, source_target_pairs={{0,8},{8,16},{16,24},{24,0},{1,9},{9,17},{17,25},{25,1},{2,10},{10... | collective-permute-start | bytes 552968 | tf_op jit(solution)/shard_map/ppermute | solution.py:776
  370.2 18.3 %collective-permute-start.35 = (bf16[96,960]{1,0:T(8,128)(2,1)}, bf16[96,960]{1,0:T(8,128)(2,1)}, u32[]{:S(2)}, u32[]{:S(2)}) collective-permute-start(bf16[96,960]{1,0:T(8,128)(2,1)} %get-tuple-element.219), channel_id=1, source_target_pairs={{0,24},{8,0},{16,8},{24,16},{1,25},{9,1},{17,9},{25,17},{2,26},{10... | collective-permute-start | bytes 552968 | tf_op jit(solution)/shard_map/ppermute | solution.py:776
  372.0 22.1 %collective-permute-start.34 = (bf16[96,960]{1,0:T(8,128)(2,1)}, bf16[96,960]{1,0:T(8,128)(2,1)}, u32[]{:S(2)}, u32[]{:S(2)}) collective-permute-start(bf16[96,960]{1,0:T(8,128)(2,1)} %get-tuple-element.220), channel_id=1, source_target_pairs={{0,16},{8,24},{16,0},{24,8},{1,17},{9,25},{17,1},{25,9},{2,18},{10... | collective-permute-start | bytes 552968 | tf_op jit(solution)/shard_map/ppermute | solution.py:776
  372.6 5.0 %collective-permute-start.21 = (f32[26,512]{1,0:T(8,128)S(1)}, f32[26,512]{1,0:T(8,128)S(1)}, u32[]{:S(2)}, u32[]{:S(2)}) collective-permute-start(f32[26,512]{1,0:T(8,128)S(1)} %add.93), channel_id=1, source_target_pairs={{0,2},{2,0},{1,3},{3,1},{4,6},{6,4},{5,7},{7,5},{8,10},{10,8},{9,1... | collective-permute-start | bytes 159752 | tf_op jit(solution)/shard_map/ppermute | solution.py:772
  377.6 8.0 %collective-permute-start.22 = (f32[26,512]{1,0:T(8,128)S(1)}, f32[26,512]{1,0:T(8,128)S(1)}, u32[]{:S(2)}, u32[]{:S(2)}) collective-permute-start(f32[26,512]{1,0:T(8,128)S(1)} %add.94), channel_id=1, source_target_pairs={{0,4},{4,0},{1,5},{5,1},{2,6},{6,2},{3,7},{7,3},{8,12},{12,8},{9,1... | collective-permute-start | bytes 159752 | tf_op jit(solution)/shard_map/ppermute | solution.py:772
  384.0 13.1 %collective-permute-start.28 = (bf16[96,576]{1,0:T(8,128)(2,1)S(1)}, bf16[96,576]{1,0:T(8,128)(2,1)S(1)}, u32[]{:S(2)}, u32[]{:S(2)}) collective-permute-start(bf16[96,576]{1,0:T(8,128)(2,1)S(1)} %get-tuple-element.224), channel_id=1, source_target_pairs={{0,8},{8,16},{16,24},{24,0},{1,9},{9,17},{17,25},{25,1},{2,10},{10... | collective-permute-start | bytes 331784 | tf_op jit(solution)/shard_map/ppermute | solution.py:776
  385.5 11.5 %collective-permute-start.30 = (bf16[96,576]{1,0:T(8,128)(2,1)S(1)}, bf16[96,576]{1,0:T(8,128)(2,1)S(1)}, u32[]{:S(2)}, u32[]{:S(2)}) collective-permute-start(bf16[96,576]{1,0:T(8,128)(2,1)S(1)} %get-tuple-element.225), channel_id=1, source_target_pairs={{0,24},{8,0},{16,8},{24,16},{1,25},{9,1},{17,9},{25,17},{2,26},{10... | collective-permute-start | bytes 331784 | tf_op jit(solution)/shard_map/ppermute | solution.py:776
  387.9 14.1 %collective-permute-start.29 = (bf16[96,576]{1,0:T(8,128)(2,1)S(1)}, bf16[96,576]{1,0:T(8,128)(2,1)S(1)}, u32[]{:S(2)}, u32[]{:S(2)}) collective-permute-start(bf16[96,576]{1,0:T(8,128)(2,1)S(1)} %get-tuple-element.226), channel_id=1, source_target_pairs={{0,16},{8,24},{16,0},{24,8},{1,17},{9,25},{17,1},{25,9},{2,18},{10... | collective-permute-start | bytes 331784 | tf_op jit(solution)/shard_map/ppermute | solution.py:776
  388.5 8.2 %collective-permute-start.23 = (f32[26,512]{1,0:T(8,128)S(1)}, f32[26,512]{1,0:T(8,128)S(1)}, u32[]{:S(2)}, u32[]{:S(2)}) collective-permute-start(f32[26,512]{1,0:T(8,128)S(1)} %add.95), channel_id=1, source_target_pairs={{0,8},{8,0},{16,24},{24,16},{1,9},{9,1},{17,25},{25,17},{2,10},{10... | collective-permute-start | bytes 159752 | tf_op jit(solution)/shard_map/ppermute | solution.py:808
  396.7 7.3 %collective-permute-start.24 = (f32[26,512]{1,0:T(8,128)S(1)}, f32[26,512]{1,0:T(8,128)S(1)}, u32[]{:S(2)}, u32[]{:S(2)}) collective-permute-start(f32[26,512]{1,0:T(8,128)S(1)} %add.96), channel_id=1, source_target_pairs={{0,16},{8,24},{16,0},{24,8},{1,17},{9,25},{17,1},{25,9},{2,18},{10... | collective-permute-start | bytes 159752 | tf_op jit(solution)/shard_map/ppermute | solution.py:808
  (15 other events, 68.8 us)
Sparse Core Ops, SparseCore 0:
  10.9 94.1 all-gather.2

commit v3 on v2

--- a/solution.py
+++ b/solution.py
@@ -82,8 +82,13 @@
         high = jnp.concatenate([jnp.zeros_like(slab), slab], 1)
         return jnp.concatenate([jnp.zeros_like(low), low, high, jnp.zeros_like(high)], 0)
 
+    through = jnp.eye(HD, dtype=BF) * BF(HD ** (-0.5))
+    nothing = jnp.zeros_like(through)
+    through = jnp.concatenate(
+        [jnp.concatenate([through, nothing], 1), jnp.zeros((128, 128), BF), jnp.concatenate([nothing, through], 1)], 0
+    )
     return (
-        place(rel_height[::-1], rel_width[::-1], 2, 33),
+        place(rel_height[::-1], rel_width[::-1], 2, 33) + through,
         place(rel_height, rel_width, 0, 32),
     )
 
@@ -354,170 +359,207 @@
     return lane < HD if head == 0 else lane >= HD
 
 
-def window_split(slot, rows):
-    first = WIN - 2 * slot
-    return ((0, first * PITCH, 0), (first * PITCH, rows * PITCH, KEYS))
-
-
-def attend_body(place_ref, q_ref, k_ref, v_ref, rel_ref, tab_ref, o_ref, p_ref, *, rows, slots):
-    def variant(slot):
-        queries = q_ref[...]
-        count = rows * PITCH
-        lane = lax.broadcasted_iota(jnp.int32, (PITCH, 128), 1)
-        raw = mm(queries, rel_ref[...])
-        outs = [None, None]
-        for head in range(2):
-            base = 64 - 64 * head
-            parts = []
-            for r in range(rows):
-                here = raw[r * PITCH : (r + 1) * PITCH, 128 * head : 128 * head + 128]
-                along_row = pltpu.roll(here, (2 * slot + r) % WIN, 1)
-                along_col = pltpu.roll(here, 0, 1, stride=1, stride_axis=0)
-                both = jnp.where(lane < base + 32, along_row, along_col)
-                wanted = ((lane >= base + 15) & (lane < base + 29)) | ((lane >= base + 46) & (lane < base + 60))
-                parts.append(jnp.where(wanted, both, 0.0))
-            along = jnp.concatenate(parts, 0)
-            high = along.astype(BF).astype(F32)
-            extra = high + pltpu.roll(along - high, 114, 1)
-            wide = lax.broadcasted_iota(jnp.int32, (count, 128), 1)
-            extra = jnp.where(wide == base, 1.0, extra)
-            mine = head_lanes((count, 128), head)
-            left = jnp.where(mine, queries.astype(F32) * HD ** (-0.5), extra).astype(BF)
-            out_parts = []
-            for start, stop, key in window_split(slot, rows):
-                keys = k_ref[key : key + KEYS]
-                right = jnp.where(head_lanes((KEYS, 128), head), keys, tab_ref[head])
-                scores = mm_t(left[start:stop], right)
-                grown = jnp.exp(scores - jnp.max(scores, -1, keepdims=True))
-                probs = (grown * (1.0 / jnp.sum(grown, -1, keepdims=True))).astype(BF)
-                p_ref[0, head, start:stop, :] = probs
-                out_parts.append(mm(probs, v_ref[key : key + KEYS]))
-            outs[head] = jnp.concatenate(out_parts, 0)
-        o_ref[...] = jnp.where(head_lanes((count, 128), 0), outs[0], outs[1]).astype(BF)
-
-    for slot in range(slots):
-        pl.when(place_ref[0] == slot)(partial(variant, slot))
-
-
-def attend(slot, q, k, v, rel, table, rows, slots):
+def early_window(slot, rows):
+    return (WIN - 2 * slot) * PITCH - rows * PITCH // 2
+
+
+def lanes_of(pair):
+    return slice(128 * pair, 128 * pair + 128)
+
+
+def attend_body(place_ref, q_ref, k_ref, v_ref, rel_ref, tab_ref, o_ref, p_ref, *, rows):
+    slot = place_ref[0]
+    half = rows * PITCH // 2
+    lane = lax.broadcasted_iota(jnp.int32, (PITCH, 128), 1)
+    first = lax.broadcasted_iota(jnp.int32, (1, half), 1) < early_window(slot, rows)
+    turns = [lax.rem(2 * slot + r, WIN) for r in range(rows)]
+    heads = [(pair, head) for pair in range(q_ref.shape[1] // 128) for head in range(2)]
+    raws = [mm(q_ref[:, lanes_of(pair)], rel_ref[...]) for pair in range(len(heads) // 2)]
+
+    def extended(pair, head):
+        base = 64 - 64 * head
+        one = jnp.where(lane == base, 1.0, 0.0)
+        on_row = (lane >= base + 15) & (lane < base + 29)
+        on_col = (lane >= base + 46) & (lane < base + 60)
+        mine = head_lanes((PITCH, 128), head)
+        parts = []
+        for r in range(rows):
+            here = raws[pair][r * PITCH : (r + 1) * PITCH, lanes_of(head)]
+            along_row = pltpu.roll(here, turns[r], 1)
+            along_col = pltpu.roll(here, 0, 1, stride=1, stride_axis=0)
+            kept = jnp.where(mine, here, one)
+            both = jnp.where(on_row, along_row, jnp.where(on_col, along_col, kept))
+            high = both.astype(BF).astype(F32)
+            parts.append((high + pltpu.roll(both - high, 114, 1)).astype(BF))
+        return jnp.concatenate(parts, 0)
+
+    def scored(pair, head, left):
+        mine = head_lanes((KEYS, 128), head)
+        keys_a = jnp.where(mine, k_ref[0:KEYS, lanes_of(pair)], tab_ref[head])
+        keys_b = jnp.where(mine, k_ref[KEYS:, lanes_of(pair)], tab_ref[head])
+        scores = mm_t(keys_a, left)
+        return scores[:, :half], jnp.where(first, scores[:, half:], mm_t(keys_b, left[half:]))
+
+    def softmax(pair, head, pieces):
+        for i, piece in enumerate(pieces):
+            grown = jnp.exp(piece - jnp.max(piece, 0, keepdims=True))
+            probs = (grown * (1.0 / jnp.sum(grown, 0, keepdims=True))).astype(BF)
+            p_ref[pair, head, :, i * half : (i + 1) * half] = probs
+
+    def weighed(pair, head):
+        rows_of = slice(HD * head, HD * head + HD)
+        out = mm(v_ref[0:KEYS, lanes_of(pair)].T[rows_of], p_ref[pair, head])
+        late = mm(v_ref[KEYS:, lanes_of(pair)].T[rows_of], p_ref[pair, head, :, half:])
+        return jnp.concatenate([out[:, :half], jnp.where(first, out[:, half:], late)], 1)
+
+    lefts = [extended(*h) for h in heads]
+    scores = [scored(*h, left) for h, left in zip(heads, lefts)]
+    for h, pieces in zip(heads, scores):
+        softmax(*h, pieces)
+    outs = [weighed(*h) for h in heads]
+    for pair in range(len(heads) // 2):
+        o_ref[:, lanes_of(pair)] = jnp.concatenate(outs[2 * pair : 2 * pair + 2], 0).T.astype(BF)
+
+
+def attend(slot, q, k, v, rel, table, rows):
     queries = rows * PITCH
-    steps = SIDE * PAIRS
+    many = PAIRS // 2
+    of_k = pl.BlockSpec((EXT * PITCH, 128 * many), lambda b, p, s: (b, p))
+    of_q = pl.BlockSpec((queries, 128 * many), lambda b, p, s: (b, p))
     return pl.pallas_call(
-        partial(attend_body, rows=rows, slots=slots),
+        partial(attend_body, rows=rows),
         grid_spec=pltpu.PrefetchScalarGridSpec(
             num_scalar_prefetch=1,
-            grid=(SIDE, PAIRS),
-            in_specs=[
-                pl.BlockSpec((queries, 128), lambda b, p, s: (b, p)),
-                pl.BlockSpec((EXT * PITCH, 128), lambda b, p, s: (b, p)),
-                pl.BlockSpec((EXT * PITCH, 128), lambda b, p, s: (b, p)),
-                pl.BlockSpec((128, 256), lambda b, p, s: (0, 0)),
-                pl.BlockSpec((2, KEYS, 128), lambda b, p, s: (0, 0, 0)),
-            ],
+            grid=(SIDE, PAIRS // many),
+            in_specs=[of_q, of_k, of_k, whole((128, 256)), whole((2, KEYS, 128))],
             out_specs=[
-                pl.BlockSpec((queries, 128), lambda b, p, s: (b, p)),
-                pl.BlockSpec((1, 2, queries, KEYS), lambda b, p, s: (b * PAIRS + p, 0, 0, 0)),
+                of_q,
+                pl.BlockSpec((many, 2, KEYS, queries), lambda b, p, s: (b * (PAIRS // many) + p, 0, 0, 0)),
             ],
         ),
         out_shape=[
             jax.ShapeDtypeStruct((SIDE * queries, D), BF),
-            jax.ShapeDtypeStruct((steps, 2, queries, KEYS), BF),
+            jax.ShapeDtypeStruct((SIDE * PAIRS, 2, KEYS, queries), BF),
         ],
         compiler_params=pltpu.CompilerParams(vmem_limit_bytes=63 << 20),
-        cost_estimate=guess(43),
+        cost_estimate=guess(24),
         name="attend",
     )(slot, q, k, v, rel, table)
 
 
 def attend_back_body(
-    place_ref, q_ref, k_ref, v_ref, p_ref, do_ref, rel_ref, tab_ref,
-    dq_ref, dk_ref, dv_ref, drel_ref, *, rows, slots,
+    place_ref, q_ref, k_ref, v_ref, p_ref, do_ref, rel_ref, tab_ref, dq_ref, dk_ref, dv_ref, drel_ref, *, rows,
 ):
+    slot = place_ref[0]
     count = rows * PITCH
-
-    @pl.when((pl.program_id(0) == 0) & (pl.program_id(1) == 0))
+    half = count // 2
+    early = early_window(slot, rows)
+
+    @pl.when(pl.program_id(0) == 0)
     def _():
         drel_ref[...] = jnp.zeros_like(drel_ref)
 
-    def variant(slot):
-        queries = q_ref[...]
-        scaled = (queries.astype(F32) * HD ** (-0.5)).astype(BF)
-        lane = lax.broadcasted_iota(jnp.int32, (PITCH, 128), 1)
-        upstream = do_ref[...]
-        split = window_split(slot, rows)
-        grad_keys = [[None, None], [None, None]]
-        grad_values = [[None, None], [None, None]]
-        grad_left, grad_raw = [], []
-        for head in range(2):
-            base = 64 - 64 * head
-            grad_out = jnp.where(head_lanes((count, 128), head), upstream, jnp.zeros_like(upstream))
-            lefts = []
-            for w, (start, stop, key) in enumerate(split):
-                keys, values = k_ref[key : key + KEYS], v_ref[key : key + KEYS]
-                probs = p_ref[0, head, start:stop, :]
-                grad_probs = mm_t(grad_out[start:stop], values)
-                exact = probs.astype(F32)
-                inner = jnp.sum(exact * grad_probs, -1, keepdims=True)
-                grad_scores = (exact * (grad_probs - inner)).astype(BF)
-                grad_values[head][w] = t_mm(probs, grad_out[start:stop])
-                right = jnp.where(head_lanes((KEYS, 128), head), keys, tab_ref[head])
-                lefts.append(mm(grad_scores, right))
-                grad_keys[head][w] = t_mm(grad_scores, scaled[start:stop])
-            left = jnp.concatenate(lefts, 0)
-            grad_left.append(left)
-            parts = []
-            for r in range(rows):
-                here = left[r * PITCH : (r + 1) * PITCH]
-                on_row = jnp.where((lane >= base) & (lane < base + WIN), here, 0.0)
-                on_col = jnp.where((lane >= base + 32) & (lane < base + 32 + WIN), here, 0.0)
-                on_row = pltpu.roll(on_row, (2 * slot + r) % WIN, 1)
-                on_col = pltpu.roll(on_col, 0, 1, stride=1, stride_axis=0)
-                parts.append(on_row + on_col)
-            grad_raw.append(jnp.concatenate(parts, 0))
-        raw = jnp.concatenate(grad_raw, 1).astype(BF)
-        first = head_lanes((count, 128), 0)
-        direct = jnp.where(first, grad_left[0], grad_left[1]) * HD ** (-0.5)
-        dq_ref[...] = (direct + mm(raw, rel_ref[...])).astype(BF)
-        drel_ref[...] += t_mm(raw, queries)
-        first = head_lanes((KEYS, 128), 0)
-        for w, (_, _, key) in enumerate(split):
-            dk_ref[key : key + KEYS] = jnp.where(first, grad_keys[0][w], grad_keys[1][w]).astype(BF)
-            dv_ref[key : key + KEYS] = (grad_values[0][w] + grad_values[1][w]).astype(BF)
-
-    for slot in range(slots):
-        pl.when(place_ref[0] == slot)(partial(variant, slot))
-
-
-def attend_back(slot, q, k, v, probs, grad_out, rel, table, rows, slots, group):
+    lane = lax.broadcasted_iota(jnp.int32, (PITCH, 128), 1)
+    first = lax.broadcasted_iota(jnp.int32, (1, half), 1) < early
+    turns = [lax.rem(2 * slot + r, WIN) for r in range(rows)]
+    heads = [(pair, head) for pair in range(q_ref.shape[1] // 128) for head in range(2)]
+
+    def split(value, head):
+        spot = lax.broadcasted_iota(jnp.int32, (half, 128), 0)
+        mine = head_lanes((half, 128), head)
+        value = value.astype(F32)
+        top = jnp.where(mine, value[:half], 0.0)
+        mid = jnp.where(mine & (spot < early), value[half:], 0.0)
+        low = jnp.where(mine & (spot >= early), value[half:], 0.0)
+        return jnp.concatenate([top, mid], 0).astype(BF), low.astype(BF), (mid + low).astype(BF)
+
+    def upstream(pair, head):
+        return split(do_ref[:, lanes_of(pair)], head)
+
+    def probs_grad(pair, head, out_a, late):
+        whole_out = jnp.concatenate([out_a[:half], late], 0)
+        grad = mm_t(v_ref[0:KEYS, lanes_of(pair)], whole_out)
+        more = mm_t(v_ref[KEYS:, lanes_of(pair)], late)
+        return grad[:, :half], jnp.where(first, grad[:, half:], more)
+
+    def scores_grad(pair, head, pieces):
+        grads = []
+        for i, piece in enumerate(pieces):
+            exact = p_ref[pair, head, :, i * half : (i + 1) * half].astype(F32)
+            inner = jnp.sum(exact * piece, 0, keepdims=True)
+            grads.append((exact * (piece - inner)).astype(BF))
+        return jnp.concatenate(grads, 1)
+
+    def left_grad(pair, head, grad, turned):
+        spot = lax.broadcasted_iota(jnp.int32, (128, KEYS), 0)
+        mine = spot < HD if head == 0 else spot >= HD
+        left = mm(jnp.where(mine, turned[0], tab_ref[head]), grad)
+        late = mm(jnp.where(mine, turned[1], tab_ref[head]), grad[:, half:])
+        return jnp.concatenate([left[:, :half], jnp.where(first, left[:, half:], late)], 1).T
+
+    def raw_grad(head, left):
+        base = 64 - 64 * head
+        on_row = (lane >= base) & (lane < base + WIN)
+        on_col = (lane >= base + 32) & (lane < base + 32 + WIN)
+        parts = []
+        for r in range(rows):
+            here = left[r * PITCH : (r + 1) * PITCH]
+            along_row = pltpu.roll(jnp.where(on_row, here, 0.0), turns[r], 1)
+            along_col = pltpu.roll(jnp.where(on_col, here, 0.0), 0, 1, stride=1, stride_axis=0)
+            parts.append((along_row + along_col).astype(BF))
+        return jnp.concatenate(parts, 0)
+
+    outs = [upstream(*h) for h in heads]
+    pieces = [probs_grad(*h, out[0], out[2]) for h, out in zip(heads, outs)]
+    grads = [scores_grad(*h, piece) for h, piece in zip(heads, pieces)]
+    lefts = []
+    for pair in range(len(heads) // 2):
+        turned = [k_ref[w * KEYS : (w + 1) * KEYS, lanes_of(pair)].T for w in range(2)]
+        lefts += [left_grad(pair, head, grads[2 * pair + head], turned) for head in range(2)]
+    for pair in range(len(heads) // 2):
+        scaled = q_ref[:, lanes_of(pair)].astype(F32) * HD ** (-0.5)
+        owns = [split(scaled, head) for head in range(2)]
+        for w in range(2):
+            at = (slice(w * KEYS, (w + 1) * KEYS), lanes_of(pair))
+            part = slice(0, count) if w == 0 else slice(half, count)
+            dv_ref[at] = sum(mm(p_ref[pair, h, :, part], outs[2 * pair + h][w]) for h in range(2)).astype(BF)
+            dk_ref[at] = sum(mm(grads[2 * pair + h][:, part], owns[h][w]) for h in range(2)).astype(BF)
+    for pair in range(len(heads) // 2):
+        mine = lefts[2 * pair : 2 * pair + 2]
+        raw = jnp.concatenate([raw_grad(head, mine[head]) for head in range(2)], 1)
+        direct = jnp.where(head_lanes((count, 128), 0), *mine) * HD ** (-0.5)
+        dq_ref[:, lanes_of(pair)] = (direct + mm(raw, rel_ref[...])).astype(BF)
+        drel_ref[...] += t_mm(q_ref[:, lanes_of(pair)], raw)
+
+
+def attend_back(slot, q, k, v, probs, grad_out, rel, table, rows, group):
     queries = rows * PITCH
-    half = PAIRS // 2
-    pair = lambda p, s: p + half * (s[5] ^ (1 - group))
-    of_q = pl.BlockSpec((queries, 128), lambda b, p, s: (b, pair(p, s)))
-    of_k = pl.BlockSpec((EXT * PITCH, 128), lambda b, p, s: (b, pair(p, s)))
-    to_q = pl.BlockSpec((queries, 128), lambda b, p, s: (b, p))
-    to_k = pl.BlockSpec((EXT * PITCH, 128), lambda b, p, s: (b, p))
+    many = PAIRS // 2
+    half = lambda s: s[5] ^ (1 - group)
+    of_q = pl.BlockSpec((queries, 128 * many), lambda b, s: (b, half(s)))
+    of_k = pl.BlockSpec((EXT * PITCH, 128 * many), lambda b, s: (b, half(s)))
+    to_q = pl.BlockSpec((queries, 128 * many), lambda b, s: (b, 0))
+    to_k = pl.BlockSpec((EXT * PITCH, 128 * many), lambda b, s: (b, 0))
     return pl.pallas_call(
-        partial(attend_back_body, rows=rows, slots=slots),
+        partial(attend_back_body, rows=rows),
         grid_spec=pltpu.PrefetchScalarGridSpec(
             num_scalar_prefetch=1,
-            grid=(SIDE, half),
+            grid=(SIDE,),
             in_specs=[
                 of_q, of_k, of_k,
-                pl.BlockSpec((1, 2, queries, KEYS), lambda b, p, s: (b * PAIRS + pair(p, s), 0, 0, 0)),
-                of_q,
-                pl.BlockSpec((256, 128), lambda b, p, s: (0, 0)),
-                pl.BlockSpec((2, KEYS, 128), lambda b, p, s: (0, 0, 0)),
+                pl.BlockSpec((many, 2, KEYS, queries), lambda b, s: (b * 2 + half(s), 0, 0, 0)),
+                of_q, whole((256, 128)), whole((2, 128, KEYS)),
             ],
-            out_specs=[to_q, to_k, to_k, pl.BlockSpec((256, 128), lambda b, p, s: (0, 0))],
+            out_specs=[to_q, to_k, to_k, whole((128, 256))],
         ),
         out_shape=[
             jax.ShapeDtypeStruct((q.shape[0], D // 2), BF),
             jax.ShapeDtypeStruct((k.shape[0], D // 2), BF),
             jax.ShapeDtypeStruct((k.shape[0], D // 2), BF),
-            jax.ShapeDtypeStruct((256, 128), F32),
+            jax.ShapeDtypeStruct((128, 256), F32),
         ],
         compiler_params=pltpu.CompilerParams(vmem_limit_bytes=63 << 20),
-        cost_estimate=guess(24),
+        cost_estimate=guess(16),
         name="attend_back",
     )(slot, q, k, v, probs, grad_out, rel, table)
 
@@ -856,7 +898,7 @@
     q, k, v, weight = project(place, normed, pieces, qv_all, rows, depth)
     ahead, back = score_tables()
     rel_ahead, rel_back = offset_tables(rel_height, rel_width)
-    attended, probs = attend(place, q, k, v, rel_ahead.T, jnp.asarray(ahead, BF), rows, slots)
+    attended, probs = attend(place, q, k, v, rel_ahead.T, jnp.asarray(ahead, BF), rows)
 
     vec_two = jnp.concatenate(
         [output_bias[None], second_gain[None], second_shift[None], down_bias[None], jnp.zeros((4, D), BF)], 0
@@ -868,10 +910,10 @@
         rows, shards,
     )
     grad_windows = grad_out.reshape(-1, D)
-    table = jnp.asarray(back, BF)
+    table = jnp.asarray(back.transpose(0, 2, 1), BF)
     if fast:
         a_got, b_got = swap(a_send, "c"), swap(b_send, "c")
-    *half0, drel0 = attend_back(place, q, k, v, probs, grad_windows, rel_back, table, rows, slots, 0)
+    *half0, drel0 = attend_back(place, q, k, v, probs, grad_windows, rel_back, table, rows, 0)
     if fast:
         a, b = [a_keep, a_got], [b_keep, b_got]
         a_away, a_here, b_away, b_here = fold((a, 1, 0, 1), (a, 1, 0, 0), (b, 1, 2, 1), (b, 1, 2, 0))
@@ -880,7 +922,7 @@
     first_send, first_keep, first_bias = project_grad(place, normed, *half0, rows, shards)
     if fast:
         first_got = swap(first_send, "c")
-    *half1, drel1 = attend_back(place, q, k, v, probs, grad_windows, rel_back, table, rows, slots, 1)
+    *half1, drel1 = attend_back(place, q, k, v, probs, grad_windows, rel_back, table, rows, 1)
     if fast:
         a, b = [a_here, a_got], [b_here, b_got]
         a_away, a_here, b_away, b_here, crossing = fold(
@@ -923,7 +965,7 @@
             for send, keep in pairs
         ]
         grad_up, grad_wo = a[:, :hidden], a[:, hidden:]
-    drel = (drel0 + drel1).reshape(4, 64, 128)
+    drel = (drel0 + drel1).T.reshape(4, 64, 128)
     drel = drel[1, :, :HD] + drel[2, :, HD:]
     grad_qv = jnp.where(y == 0, jnp.concatenate([last_bias, first_bias], 1), jnp.concatenate([first_bias, last_bias], 1))
     small = jnp.concatenate(

time: 421 us -> 364 us (0.86); the launches traced: 413 us -> 363 us
  Pallas kernels: 256 us -> 203 us
  waiting for transfers between devices: 47.1 us -> 59.4 us
  starting transfers between devices: 63.5 us -> 52.6 us
    pallas_call x3, Pallas kernels: 94.3 us -> 41.8 us  [the longest x2 22.8 us: attend_back(): pl.pallas_call(partial(attend_back_body, rows=rows), grid_spec=pltpu.Pref...]
    ppermute x21, waiting for transfers between devices: 34.1 us -> 46.1 us  [swap(): return lax.ppermute(value, axis, SWAP)]
    ppermute x21, starting transfers between devices: 33.8 us -> 23.1 us  [swap(): return lax.ppermute(value, axis, SWAP)]
  transfers between devices with their start and end apart: 40 -> 40, of which waited for: 9 -> 11; matrix products, arithmetic and copies ran while one was open for 6% -> 7% of each run, Pallas kernels for 39% -> 31%
where the time goes in v3:
time: 364 us; the launch traced here: 363 us
  Pallas kernels  203 us (56%)
  waiting for transfers between devices  59.4 us (16%)
  starting transfers between devices  52.6 us (14%)
  local copies, waits for them, and re-layouts  23.2 us (6%)
  between operations  14.7 us (4%)
  other arithmetic  9.65 us (3%)
    pallas_call x1, Pallas kernels, feed(): pl.pallas_call(partial(feed_body, rows=rows), grid_spec=pltpu.PrefetchSca...  58.3 us
    ppermute x21, waiting for transfers between devices, swap(): return lax.ppermute(value, axis, SWAP)  46.1 us
    pallas_call x5, Pallas kernels, fold(): pl.pallas_call(partial(fold_body, plan=plan), grid=(count,), in_specs=in_...  29.9 us
    ppermute x21, starting transfers between devices, swap(): return lax.ppermute(value, axis, SWAP)  23.1 us
    pallas_call x2, Pallas kernels, attend_back(): pl.pallas_call(partial(attend_back_body, rows=rows), grid_spec=pltpu.Pref...  22.8 us
    pallas_call x2, Pallas kernels, project_grad(): pl.pallas_call(partial(project_grad_body, rows=rows, parts=parts), grid_s...  21.9 us
    ppermute x12, starting transfers between devices, shift(): lax.ppermute(value, 'z', [(i, (i + by) % count) for i in range(count)])  21.1 us
    pallas_call x1, Pallas kernels, attend(): pl.pallas_call(partial(attend_body, rows=rows), grid_spec=pltpu.PrefetchS...  18.9 us
  transfers between devices with their start and end apart: 40, of which 11 were waited for; matrix products, arithmetic and copies ran while one was open for 7% of the time, Pallas kernels for 31%

profile of v3, /device:TPU:0, one launch (start us, length us, event | category | flops | bytes accessed | tf_op | source)
XLA Modules:
  0.0 362.9 jit_solution(10102331410068704330)
XLA Ops:
  7.2 1.9 concatenate.67
  10.5 5.1 %collective-permute-start.4 = (bf16[96,576]{1,0:T(8,128)(2,1)S(1)}, bf16[96,576]{1,0:T(8,128)(2,1)S(1)}, u32[]{:S(2)}, u32[]{:S(2)}) collective-permute-start(bf16[96,576]{1,0:T(8,128)(2,1)S(1)} %copy.43), channel_id=1, source_target_pairs={{0,24},{8,0},{16,8},{24,16},{1,25},{9,1},{17,9},{25,17},{2,26},{10... | collective-permute-start | bytes 331784 | tf_op jit(solution)/shard_map/ppermute | solution.py:818
  16.7 2.1 collective-permute-start
  23.7 2.6 collective-permute-done.3
  26.4 1.6 collective-permute-start.6
  28.1 1.6 collective-permute-start.5
  30.2 18.4 %collective-permute-done.6 = bf16[4,48,576]{2,1,0:T(8,128)(2,1)S(1)} collective-permute-done((bf16[4,48,576]{2,1,0:T(8,128)(2,1)S(1)}, bf16[4,48,576]{2,1,0:T(8,128)(2,1)S(1)}, u32[]{:S(2)}, u32[]{:S(2)}) %collective-permute-start.6) | collective-permute-done | bytes 221216 | tf_op jit(solution)/shard_map/ppermute | solution.py:814
  48.7 11.7 %windows.1.nw_ref = bf16[2240,768]{1,0:T(8,128)(2,1)} custom-call(s32[6]{0:T(128)} %stack.90.place_ref, bf16[6,64,768]{2,1,0:T(8,128)(2,1)} %collective-permute-done.above_ref, bf16[16,64,768]{2,1,0:T(8,128)(2,1)} %bitcast.78, bf16[12,64,768]{2,1,0:T(8,128)(2,1)} %collective-permute-done.1.below_ref, f32[8,768]{1,0:T(8,128)} %maximum_convert_fusion.vec_ref), custom_call_target="tpu_custom_call" | custom-call | flops 8800000000 | bytes 24000000 | tf_op jit(solution)/shard_map/windows/pallas_call | solution.py:149
  60.5 1.4 collective-permute-start.8
  66.0 6.0 %collective-permute-done.8 = bf16[2,4,48,576]{3,2,1,0:T(8,128)(2,1)S(1)} collective-permute-done((bf16[2,4,48,576]{3,2,1,0:T(8,128)(2,1)S(1)}, bf16[2,4,48,576]{3,2,1,0:T(8,128)(2,1)S(1)}, u32[]{:S(2)}, u32[]{:S(2)}) %collective-permute-start.8) | collective-permute-done | bytes 442400 | tf_op jit(solution)/shard_map/ppermute | solution.py:814
  73.2 2.7 collective-permute-start.12
  80.6 13.8 %project.1 = (bf16[1280,768]{1,0:T(8,128)(2,1)}, bf16[2240,768]{1,0:T(8,128)(2,1)}, bf16[2240,768]{1,0:T(8,128)(2,1)}, bf16[768,2304]{1,0:T(8,128)(2,1)}) custom-call(s32[6]{0:T(128)} %stack.90.place_ref, bf16[2240,768]{1,0:T(8,128)(2,1)} %windows.1.nw_ref, bf16[2,2,4,48,576]{4,3,2,1,0:T(8,128)(2,1)} %copy-done.2, bf16[2,2,4,48,576]{4,3,2,1,0:T(8,128)(2,1)} %copy-done.1, ...), custom_call_target="tpu_custom_call" | custom-call | flops 19800000512 | bytes 54000000 | tf_op jit(solution)/shard_map/project/pallas_call | solution.py:214
  94.4 18.9 %attend.1 = (bf16[1280,768]{1,0:T(8,128)(2,1)}, bf16[30,2,224,256]{3,2,1,0:T(8,128)(2,1)}) custom-call(s32[6]{0:T(128)} %stack.90.place_ref, bf16[1280,768]{1,0:T(8,128)(2,1)} %get-tuple-element.125.q_ref, bf16[2240,768]{1,0:T(8,128)(2,1)} %get-tuple-element.126.k_ref, bf16[2240,768]{1,0:T(8,128)(2,1)} %get-tuple-element.127.v_ref, ...), custom_call_target="tpu_custom_call" | custom-call | flops 26400000000 | bytes 72000000 | tf_op jit(solution)/shard_map/attend/pallas_call | solution.py:429
  113.3 58.3 %feed.1 = (bf16[1024,768]{1,0:T(8,128)(2,1)}, f32[1024,768]{1,0:T(8,128)}, bf16[5,16,16,768]{3,2,1,0:T(8,128)(2,1)}, bf16[2,4,2,96,960]{4,3,2,1,0:T(8,128)(2,1)}...) custom-call(s32[6]{0:T(128)} %stack.90.place_ref, ...), custom_call_target="tpu_custom_call" | custom-call | flops 60500000768 | bytes 165000000 | tf_op jit(solution)/shard_map/feed/pallas_call | solution.py:696
  173.6 11.4 %attend_back.2 = (bf16[1280,384]{1,0:T(8,128)(2,1)}, bf16[2240,384]{1,0:T(8,128)(2,1)}, bf16[2240,384]{1,0:T(8,128)(2,1)}, f32[128,256]{1,0:T(8,128)}) custom-call(s32[6]{0:T(128)} %stack.90.place_ref, bf16[1280,768]{1,0:T(8,128)(2,1)} %get-tuple-element.125.q_ref, bf16[2240,768]{1,0:T(8,128)(2,1)} %get-tuple-element.126.k_ref, ...), custom_call_target="tpu_custom_call" | custom-call | flops 17600000000 | bytes 48000000 | tf_op jit(solution)/shard_map/attend_back/pallas_call | solution.py:543
  185.1 10.3 %fold.5 = (bf16[4,2,96,960]{3,2,1,0:T(8,128)(2,1)}, bf16[4,2,96,960]{3,2,1,0:T(8,128)(2,1)}, bf16[2,4,96,768]{3,2,1,0:T(8,128)(2,1)}, bf16[2,4,96,768]{3,2,1,0:T(8,128)(2,1)}) custom-call(bf16[2,4,2,96,960]{4,3,2,1,0:T(8,128)(2,1)} %get-tuple-element.130.refs_0_.refs_2_, bf16[2,4,2,96,960]{4,3,2,1,0:T(8,128)(2,1)} %collective-permute-done.13.refs_1_.refs_3_, ...), custom_call_target="tpu_custom_call" | custom-call | flops 12778515456 | bytes 34850496 | tf_op jit(solution)/shard_map/fold/pallas_call | solution.py:797
  195.4 2.7 collective-permute-start.16
  198.1 1.4 collective-permute-start.15
  199.5 11.1 %project_grad.2 = (bf16[4,2,96,576]{3,2,1,0:T(8,128)(2,1)}, bf16[4,2,96,576]{3,2,1,0:T(8,128)(2,1)}, f32[2,384]{1,0:T(2,128)}) custom-call(s32[6]{0:T(128)} %stack.90.place_ref, bf16[2240,768]{1,0:T(8,128)(2,1)} %windows.1.nw_ref, bf16[1280,384]{1,0:T(8,128)(2,1)} %get-tuple-element.143.dq_ref.refs_0_, bf16[2240,384]{1,0:T(8,128)(2,1)} %get-tuple-element.144.dk_ref.refs_2_, ...), custom_call_target="tpu_custom_call" | custom-call | flops 6600000000 | bytes 18000000 | tf_op jit(solution)/shard_map/project_grad/pallas_call | solution.py:276
  210.6 11.4 %attend_back.3 = (bf16[1280,384]{1,0:T(8,128)(2,1)}, bf16[2240,384]{1,0:T(8,128)(2,1)}, bf16[2240,384]{1,0:T(8,128)(2,1)}, f32[128,256]{1,0:T(8,128)}) custom-call(s32[6]{0:T(128)} %stack.90.place_ref, bf16[1280,768]{1,0:T(8,128)(2,1)} %get-tuple-element.125.q_ref, bf16[2240,768]{1,0:T(8,128)(2,1)} %get-tuple-element.126.k_ref, ...), custom_call_target="tpu_custom_call" | custom-call | flops 17600000000 | bytes 48000000 | tf_op jit(solution)/shard_map/attend_back/pallas_call | solution.py:543
  222.1 2.6 collective-permute-done.16.refs_5_.refs_7_
  224.7 9.9 %collective-permute-done.15.refs_1_.refs_3_ = bf16[4,2,96,960]{3,2,1,0:T(8,128)(2,1)} collective-permute-done((bf16[4,2,96,960]{3,2,1,0:T(8,128)(2,1)}, bf16[4,2,96,960]{3,2,1,0:T(8,128)(2,1)}, u32[]{:S(2)}, u32[]{:S(2)}) %collective-permute-start.15) | collective-permute-done | bytes 1474592 | tf_op jit(solution)/shard_map/ppermute | solution.py:814
  234.5 7.7 %fold.6 = (bf16[4,96,960]{2,1,0:T(8,128)(2,1)}, bf16[4,96,960]{2,1,0:T(8,128)(2,1)}, bf16[4,96,768]{2,1,0:T(8,128)(2,1)}, bf16[4,96,768]{2,1,0:T(8,128)(2,1)}, bf16[4,2,96,576]{3,2,1,0:T(8,128)(2,1)}) custom-call(bf16[4,2,96,960]{3,2,1,0:T(8,128)(2,1)} %get-tuple-element.137.refs_0_.refs_2_, bf16[4,2,96,960]{3,2,1,0:T(8,128)(2,1)} %collective-permute-done.15.refs_1_.refs_3_, ...), custom_call_target="tpu_custom_call" | custom-call | flops 7912467456 | bytes 21579456 | tf_op jit(solution)/shard_map/fold/pallas_call | solution.py:797
  242.2 16.2 %project_back.1 = (bf16[6,64,768]{2,1,0:T(8,128)(2,1)}, f32[16,64,768]{2,1,0:T(8,128)}, bf16[12,64,768]{2,1,0:T(8,128)(2,1)}) custom-call(s32[6]{0:T(128)} %stack.90.place_ref, bf16[1280,384]{1,0:T(8,128)(2,1)} %get-tuple-element.143.dq_ref.refs_0_, bf16[1280,384]{1,0:T(8,128)(2,1)} %get-tuple-element.152.refs_1_.dq_ref, ...), custom_call_target="tpu_custom_call" | custom-call | flops 15399999488 | bytes 42000000 | tf_op jit(solution)/shard_map/project_back/pallas_call | solution.py:336
  258.5 1.5 collective-permute-start.32
  260.3 10.8 %project_grad.3 = (bf16[4,2,96,576]{3,2,1,0:T(8,128)(2,1)}, bf16[4,2,96,576]{3,2,1,0:T(8,128)(2,1)}, f32[2,384]{1,0:T(2,128)}) custom-call(s32[6]{0:T(128)} %stack.90.place_ref, bf16[2240,768]{1,0:T(8,128)(2,1)} %windows.1.nw_ref, bf16[1280,384]{1,0:T(8,128)(2,1)} %get-tuple-element.152.refs_1_.dq_ref, bf16[2240,384]{1,0:T(8,128)(2,1)} %get-tuple-element.153.refs_3_.dk_ref, ...), custom_call_target="tpu_custom_call" | custom-call | flops 6600000000 | bytes 18000000 | tf_op jit(solution)/shard_map/project_grad/pallas_call | solution.py:276
  272.0 3.2 collective-permute-start.18
  276.1 1.3 collective-permute-start.19
  278.4 3.9 %fold.9 = (bf16[4,96,960]{2,1,0:T(8,128)(2,1)}, bf16[4,96,768]{2,1,0:T(8,128)(2,1)}) custom-call(bf16[4,96,960]{2,1,0:T(8,128)(2,1)} %get-tuple-element.174.refs_0_, bf16[4,96,960]{2,1,0:T(8,128)(2,1)} %collective-permute-done.31.refs_1_, bf16[4,96,768]{2,1,0:T(8,128)(2,1)} %get-tuple-element.176.refs_2_, bf16[4,96,768]{2,1,0:T(8,128)(2,1)} %collective-permute-done.32.refs_3_), custom_call_target="tpu_custom_call" | custom-call | flops 2559814400 | bytes 6981312 | tf_op jit(solution)/shard_map/fold/pallas_call | solution.py:797
  282.3 1.8 slice_bitcast_fusion.5
  284.1 2.3 collective-permute-start.36
  286.3 1.6 collective-permute-start.38
  287.9 7.7 %collective-permute-done.26.refs_2_.refs_5_ = bf16[4,2,96,576]{3,2,1,0:T(8,128)(2,1)} collective-permute-done((bf16[4,2,96,576]{3,2,1,0:T(8,128)(2,1)}, bf16[4,2,96,576]{3,2,1,0:T(8,128)(2,1)}, u32[]{:S(2)}, u32[]{:S(2)}) %collective-permute-start.26) | collective-permute-done | bytes 884768 | tf_op jit(solution)/shard_map/ppermute | solution.py:814
  295.7 2.3 collective-permute-start.37
  297.9 4.7 %fold.7 = (bf16[4,96,576]{2,1,0:T(8,128)(2,1)}, bf16[4,96,576]{2,1,0:T(8,128)(2,1)}) custom-call(bf16[4,2,96,576]{3,2,1,0:T(8,128)(2,1)} %get-tuple-element.169.refs_0_.refs_3_, bf16[4,2,96,576]{3,2,1,0:T(8,128)(2,1)} %collective-permute-done.25.refs_1_.refs_4_, bf16[4,2,96,576]{3,2,1,0:T(8,128)(2,1)} %collective-permute-done.26.refs_2_.refs_5_, ...), custom_call_target="tpu_custom_call" | custom-call | flops 4019628800 | bytes 10962624 | tf_op jit(solution)/shard_map/fold/pallas_call | solution.py:797
  302.6 1.7 collective-permute-start.27
  304.3 9.7 %finish.1 = (bf16[16,64,768]{2,1,0:T(8,128)(2,1)}, f32[8,768]{1,0:T(8,128)}) custom-call(f32[16,64,768]{2,1,0:T(8,128)} %get-tuple-element.156.own_ref, bf16[12,64,768]{2,1,0:T(8,128)(2,1)} %collective-permute-done.18.head_ref, bf16[6,64,768]{2,1,0:T(8,128)(2,1)} %copy-done.20, bf16[16,64,768]{2,1,0:T(8,128)(2,1)} %bitcast.79, f32[16,64,768]{2,1,0:T(8,128)} %bitcast.96, ...), custom_call_target="tpu_custom_call" | custom-call | flops 5500000256 | bytes 15000000 | tf_op jit(solution)/shard_map/finish/pallas_call | solution.py:751
  314.9 2.3 collective-permute-start.20
  318.0 2.2 collective-permute-start.33
  320.3 1.6 collective-permute-start.35
  322.4 2.7 collective-permute-start.21
  325.1 1.8 fusion.3
  327.3 1.7 collective-permute-start.22
  329.1 3.3 fold.8
  333.4 1.9 collective-permute-start.28
  335.3 2.0 collective-permute-start.30
  338.6 5.5 %collective-permute-done.34 = bf16[96,960]{1,0:T(8,128)(2,1)} collective-permute-done((bf16[96,960]{1,0:T(8,128)(2,1)}, bf16[96,960]{1,0:T(8,128)(2,1)}, u32[]{:S(2)}, u32[]{:S(2)}) %collective-permute-start.34) | collective-permute-done | bytes 184352 | tf_op jit(solution)/shard_map/ppermute | solution.py:818
  346.7 5.2 %collective-permute-done.29 = bf16[96,576]{1,0:T(8,128)(2,1)S(1)} collective-permute-done((bf16[96,576]{1,0:T(8,128)(2,1)S(1)}, bf16[96,576]{1,0:T(8,128)(2,1)S(1)}, u32[]{:S(2)}, u32[]{:S(2)}) %collective-permute-start.29) | collective-permute-done | bytes 110624 | tf_op jit(solution)/shard_map/ppermute | solution.py:818
  (186 shorter events, 34.6 us)
Async XLA Ops:
  7.2 106.1 %all-gather.3.cloned.1.call-start = ((), (), s32[]{:S(2)}) async-start(), calls=%async_computation | async-start | bytes 11354112 | tf_op jit(solution)/shard_map/all_gather | solution.py:881
  10.5 10.8 %copy-start.11 = (bf16[768]{0:T(1024)(128)(2,1)S(1)}, bf16[768]{0:T(1024)(128)(2,1)}, u32[]{:S(2)}) copy-start(bf16[768]{0:T(1024)(128)(2,1)} %param.27) | copy-start | bytes 4612
  10.5 10.8 %copy-start.12 = (bf16[768]{0:T(1024)(128)(2,1)S(1)}, bf16[768]{0:T(1024)(128)(2,1)}, u32[]{:S(2)}) copy-start(bf16[768]{0:T(1024)(128)(2,1)} %param.28) | copy-start | bytes 4612
  10.5 10.8 %copy-start.4 = (bf16[96,3,192]{2,0,1:T(8,128)(2,1)S(1)}, bf16[96,3,192]{2,0,1:T(8,128)(2,1)}, u32[]{:S(2)}) copy-start(bf16[96,3,192]{2,0,1:T(8,128)(2,1)} %param.29) | copy-start | bytes 331780
  10.5 13.2 %collective-permute-start.4 = (bf16[96,576]{1,0:T(8,128)(2,1)S(1)}, bf16[96,576]{1,0:T(8,128)(2,1)S(1)}, u32[]{:S(2)}, u32[]{:S(2)}) collective-permute-start(bf16[96,576]{1,0:T(8,128)(2,1)S(1)} %copy.43), channel_id=1, source_target_pairs={{0,24},{8,0},{16,8},{24,16},{1,25},{9,1},{17,9},{25,17},{2,26},{10... | collective-permute-start | bytes 331784 | tf_op jit(solution)/shard_map/ppermute | solution.py:818
  15.6 10.7 %collective-permute-start.3 = (bf16[96,576]{1,0:T(8,128)(2,1)S(1)}, bf16[96,576]{1,0:T(8,128)(2,1)S(1)}, u32[]{:S(2)}, u32[]{:S(2)}) collective-permute-start(bf16[96,576]{1,0:T(8,128)(2,1)S(1)} %copy.43), channel_id=1, source_target_pairs={{0,16},{8,24},{16,0},{24,8},{1,17},{9,25},{17,1},{25,9},{2,18},{10... | collective-permute-start | bytes 331784 | tf_op jit(solution)/shard_map/ppermute | solution.py:818
  15.6 10.7 %collective-permute-start.2 = (bf16[96,576]{1,0:T(8,128)(2,1)S(1)}, bf16[96,576]{1,0:T(8,128)(2,1)S(1)}, u32[]{:S(2)}, u32[]{:S(2)}) collective-permute-start(bf16[96,576]{1,0:T(8,128)(2,1)S(1)} %copy.43), channel_id=1, source_target_pairs={{0,8},{8,16},{16,24},{24,0},{1,9},{9,17},{17,25},{25,1},{2,10},{10... | collective-permute-start | bytes 331784 | tf_op jit(solution)/shard_map/ppermute | solution.py:818
  16.7 32.1 %collective-permute-start = (bf16[6,64,768]{2,1,0:T(8,128)(2,1)S(1)}, bf16[6,64,768]{2,1,0:T(8,128)(2,1)}, u32[]{:S(2)}, u32[]{:S(2)}) collective-permute-start(bf16[6,64,768]{2,1,0:T(8,128)(2,1)S(1)} %bitcast.83), channel_id=1, source_target_pairs={{0,1},{1,2},{2,3},{4,5},{5,6},{6,7},{8,9},{9,10},{10,11},{12,13},{... | collective-permute-start | bytes 1769480 | tf_op jit(solution)/shard_map/ppermute | solution.py:877
  19.9 28.9 %collective-permute-start.1 = (bf16[12,64,768]{2,1,0:T(8,128)(2,1)}, bf16[12,64,768]{2,1,0:T(8,128)(2,1)}, u32[]{:S(2)}, u32[]{:S(2)}) collective-permute-start(bf16[12,64,768]{2,1,0:T(8,128)(2,1)} %bitcast.7), channel_id=1, source_target_pairs={{1,0},{2,1},{3,2},{5,4},{6,5},{7,6},{9,8},{10,9},{11,10},{13,12},{... | collective-permute-start | bytes 3538952 | tf_op jit(solution)/shard_map/ppermute | solution.py:878
  26.4 22.2 %collective-permute-start.6 = (bf16[4,48,576]{2,1,0:T(8,128)(2,1)S(1)}, bf16[4,48,576]{2,1,0:T(8,128)(2,1)S(1)}, u32[]{:S(2)}, u32[]{:S(2)}) collective-permute-start(bf16[4,48,576]{2,1,0:T(8,128)(2,1)S(1)} %get-tuple-element.228), channel_id=1, source_target_pairs={{0,2},{2,0},{1,3},{3,1},{4,6},{6,4},{5,7},{7,5},{8,10},{10,8},{9,1... | collective-permute-start | bytes 663560 | tf_op jit(solution)/shard_map/ppermute | solution.py:814
  28.1 20.6 %collective-permute-start.5 = (bf16[4,48,576]{2,1,0:T(8,128)(2,1)S(1)}, bf16[4,48,576]{2,1,0:T(8,128)(2,1)S(1)}, u32[]{:S(2)}, u32[]{:S(2)}) collective-permute-start(bf16[4,48,576]{2,1,0:T(8,128)(2,1)S(1)} %get-tuple-element.230), channel_id=1, source_target_pairs={{0,4},{4,0},{1,5},{5,1},{2,6},{6,2},{3,7},{7,3},{8,12},{12,8},{9,1... | collective-permute-start | bytes 663560 | tf_op jit(solution)/shard_map/ppermute | solution.py:814
  60.5 11.7 %collective-permute-start.7 = (bf16[2,4,48,576]{3,2,1,0:T(8,128)(2,1)S(1)}, bf16[2,4,48,576]{3,2,1,0:T(8,128)(2,1)S(1)}, u32[]{:S(2)}, u32[]{:S(2)}) collective-permute-start(bf16[2,4,48,576]{3,2,1,0:T(8,128)(2,1)S(1)} %pad_maximum_fusion.2), channel_id=1, source_target_pairs={{0,2},{2,0},{1,3},{3,1},{4,6},{6,4},{5,7},{7,5},{8,10},{10,8},{9,1... | collective-permute-start | bytes 1327112 | tf_op jit(solution)/shard_map/ppermute | solution.py:814
  60.5 11.4 %collective-permute-start.8 = (bf16[2,4,48,576]{3,2,1,0:T(8,128)(2,1)S(1)}, bf16[2,4,48,576]{3,2,1,0:T(8,128)(2,1)S(1)}, u32[]{:S(2)}, u32[]{:S(2)}) collective-permute-start(bf16[2,4,48,576]{3,2,1,0:T(8,128)(2,1)S(1)} %pad_maximum_fusion.3), channel_id=1, source_target_pairs={{0,4},{4,0},{1,5},{5,1},{2,6},{6,2},{3,7},{7,3},{8,12},{12,8},{9,1... | collective-permute-start | bytes 1327112 | tf_op jit(solution)/shard_map/ppermute | solution.py:814
  62.7 10.4 %collective-permute-start.11 = (bf16[4,1152]{1,0:T(4,128)(2,1)S(1)}, bf16[4,1152]{1,0:T(4,128)(2,1)S(1)}, u32[]{:S(2)}, u32[]{:S(2)}) collective-permute-start(bf16[4,1152]{1,0:T(4,128)(2,1)S(1)} %broadcast_select_fusion), channel_id=1, source_target_pairs={{0,1},{1,0},{2,3},{3,2},{4,5},{5,4},{6,7},{7,6},{8,9},{9,8},{10,11... | collective-permute-start | bytes 27656 | tf_op jit(solution)/shard_map/ppermute | solution.py:814
  72.1 7.5 %collective-permute-start.10 = (bf16[2,2,4,48,576]{4,3,2,1,0:T(8,128)(2,1)S(1)}, bf16[2,2,4,48,576]{4,3,2,1,0:T(8,128)(2,1)}, u32[]{:S(2)}, u32[]{:S(2)}) collective-permute-start(bf16[2,2,4,48,576]{4,3,2,1,0:T(8,128)(2,1)S(1)} %pad_maximum_fusion.1.refs_1_), channel_id=1, source_target_pairs={{0,1},{1,0},{2,3},{3,2},{4,5},{5,4},{6,7},{7,6},{8,9},{9,8},{10,11... | collective-permute-start | bytes 2654216 | tf_op jit(solution)/shard_map/ppermute | solution.py:814
  73.1 6.5 %collective-permute-start.9 = (bf16[2,2,4,48,576]{4,3,2,1,0:T(8,128)(2,1)S(1)}, bf16[2,2,4,48,576]{4,3,2,1,0:T(8,128)(2,1)S(1)}, u32[]{:S(2)}, u32[]{:S(2)}) collective-permute-start(bf16[2,2,4,48,576]{4,3,2,1,0:T(8,128)(2,1)S(1)} %pad_maximum_fusion.refs_0_), channel_id=1, source_target_pairs={{0,1},{1,0},{2,3},{3,2},{4,5},{5,4},{6,7},{7,6},{8,9},{9,8},{10,11... | collective-permute-start | bytes 2654216 | tf_op jit(solution)/shard_map/ppermute | solution.py:814
  73.2 4.9 %collective-permute-start.12 = (bf16[4,1152]{1,0:T(4,128)(2,1)S(1)}, bf16[4,1152]{1,0:T(4,128)(2,1)S(1)}, u32[]{:S(2)}, u32[]{:S(2)}) collective-permute-start(bf16[4,1152]{1,0:T(4,128)(2,1)S(1)} %fusion.21), channel_id=1, source_target_pairs={{0,2},{2,0},{1,3},{3,1},{4,6},{6,4},{5,7},{7,5},{8,10},{10,8},{9,1... | collective-permute-start | bytes 27656 | tf_op jit(solution)/shard_map/ppermute | solution.py:814
  171.6 13.5 %collective-permute-start.13 = (bf16[2,4,2,96,960]{4,3,2,1,0:T(8,128)(2,1)}, bf16[2,4,2,96,960]{4,3,2,1,0:T(8,128)(2,1)}, u32[]{:S(2)}, u32[]{:S(2)}) collective-permute-start(bf16[2,4,2,96,960]{4,3,2,1,0:T(8,128)(2,1)} %get-tuple-element.131), channel_id=1, source_target_pairs={{0,1},{1,0},{2,3},{3,2},{4,5},{5,4},{6,7},{7,6},{8,9},{9,8},{10,11... | collective-permute-start | bytes 8847368 | tf_op jit(solution)/shard_map/ppermute | solution.py:814
  171.9 13.2 %collective-permute-start.14 = (bf16[2,4,2,96,768]{4,3,2,1,0:T(8,128)(2,1)}, bf16[2,4,2,96,768]{4,3,2,1,0:T(8,128)(2,1)}, u32[]{:S(2)}, u32[]{:S(2)}) collective-permute-start(bf16[2,4,2,96,768]{4,3,2,1,0:T(8,128)(2,1)} %get-tuple-element.133), channel_id=1, source_target_pairs={{0,1},{1,0},{2,3},{3,2},{4,5},{5,4},{6,7},{7,6},{8,9},{9,8},{10,11... | collective-permute-start | bytes 7077896 | tf_op jit(solution)/shard_map/ppermute | solution.py:814
  195.4 29.2 %collective-permute-start.16 = (bf16[2,4,96,768]{3,2,1,0:T(8,128)(2,1)}, bf16[2,4,96,768]{3,2,1,0:T(8,128)(2,1)}, u32[]{:S(2)}, u32[]{:S(2)}) collective-permute-start(bf16[2,4,96,768]{3,2,1,0:T(8,128)(2,1)} %get-tuple-element.140), channel_id=1, source_target_pairs={{0,4},{4,0},{1,5},{5,1},{2,6},{6,2},{3,7},{7,3},{8,12},{12,8},{9,1... | collective-permute-start | bytes 3538952 | tf_op jit(solution)/shard_map/ppermute | solution.py:814
  198.1 36.4 %collective-permute-start.15 = (bf16[4,2,96,960]{3,2,1,0:T(8,128)(2,1)}, bf16[4,2,96,960]{3,2,1,0:T(8,128)(2,1)}, u32[]{:S(2)}, u32[]{:S(2)}) collective-permute-start(bf16[4,2,96,960]{3,2,1,0:T(8,128)(2,1)} %get-tuple-element.138), channel_id=1, source_target_pairs={{0,2},{2,0},{1,3},{3,1},{4,6},{6,4},{5,7},{7,5},{8,10},{10,8},{9,1... | collective-permute-start | bytes 4423688 | tf_op jit(solution)/shard_map/ppermute | solution.py:814
  210.6 11.4 %collective-permute-start.17 = (bf16[4,2,96,576]{3,2,1,0:T(8,128)(2,1)}, bf16[4,2,96,576]{3,2,1,0:T(8,128)(2,1)}, u32[]{:S(2)}, u32[]{:S(2)}) collective-permute-start(bf16[4,2,96,576]{3,2,1,0:T(8,128)(2,1)} %get-tuple-element.147), channel_id=1, source_target_pairs={{0,1},{1,0},{2,3},{3,2},{4,5},{5,4},{6,7},{7,6},{8,9},{9,8},{10,11... | collective-permute-start | bytes 2654216 | tf_op jit(solution)/shard_map/ppermute | solution.py:814
  242.2 16.2 %copy-start.19 = (bf16[4,96,768]{2,1,0:T(8,128)(2,1)S(1)}, bf16[4,96,768]{2,1,0:T(8,128)(2,1)}, u32[]{:S(2)}) copy-start(bf16[4,96,768]{2,1,0:T(8,128)(2,1)} %get-tuple-element.177) | copy-start | bytes 1769476
  258.5 13.4 %copy-start.5 = (f32[128,256]{1,0:T(8,128)S(1)}, f32[128,256]{1,0:T(8,128)}, u32[]{:S(2)}) copy-start(f32[128,256]{1,0:T(8,128)} %get-tuple-element.167) | copy-start | bytes 393220
  258.5 13.4 %copy-start.6 = (f32[128,256]{1,0:T(8,128)S(1)}, f32[128,256]{1,0:T(8,128)}, u32[]{:S(2)}) copy-start(f32[128,256]{1,0:T(8,128)} %get-tuple-element.168) | copy-start | bytes 393220
  258.5 16.8 %copy-start.9 = (f32[2,384]{1,0:T(2,128)S(1)}, f32[2,384]{1,0:T(2,128)}, u32[]{:S(2)}) copy-start(f32[2,384]{1,0:T(2,128)} %get-tuple-element.166) | copy-start | bytes 9220
  258.5 17.6 %collective-permute-start.32 = (bf16[4,96,768]{2,1,0:T(8,128)(2,1)S(1)}, bf16[4,96,768]{2,1,0:T(8,128)(2,1)}, u32[]{:S(2)}, u32[]{:S(2)}) collective-permute-start(bf16[4,96,768]{2,1,0:T(8,128)(2,1)S(1)} %copy-done.19), channel_id=1, source_target_pairs={{0,2},{2,0},{1,3},{3,1},{4,6},{6,4},{5,7},{7,5},{8,10},{10,8},{9,1... | collective-permute-start | bytes 1769480 | tf_op jit(solution)/shard_map/ppermute | solution.py:814
  260.0 18.4 %collective-permute-start.31 = (bf16[4,96,960]{2,1,0:T(8,128)(2,1)}, bf16[4,96,960]{2,1,0:T(8,128)(2,1)}, u32[]{:S(2)}, u32[]{:S(2)}) collective-permute-start(bf16[4,96,960]{2,1,0:T(8,128)(2,1)} %get-tuple-element.175), channel_id=1, source_target_pairs={{0,4},{4,0},{1,5},{5,1},{2,6},{6,2},{3,7},{7,3},{8,12},{12,8},{9,1... | collective-permute-start | bytes 2211848 | tf_op jit(solution)/shard_map/ppermute | solution.py:814
  271.2 15.2 %collective-permute-start.25 = (bf16[4,2,96,576]{3,2,1,0:T(8,128)(2,1)}, bf16[4,2,96,576]{3,2,1,0:T(8,128)(2,1)}, u32[]{:S(2)}, u32[]{:S(2)}) collective-permute-start(bf16[4,2,96,576]{3,2,1,0:T(8,128)(2,1)} %get-tuple-element.170), channel_id=1, source_target_pairs={{0,1},{1,0},{2,3},{3,2},{4,5},{5,4},{6,7},{7,6},{8,9},{9,8},{10,11... | collective-permute-start | bytes 2654216 | tf_op jit(solution)/shard_map/ppermute | solution.py:814
  271.2 24.5 %collective-permute-start.26 = (bf16[4,2,96,576]{3,2,1,0:T(8,128)(2,1)}, bf16[4,2,96,576]{3,2,1,0:T(8,128)(2,1)}, u32[]{:S(2)}, u32[]{:S(2)}) collective-permute-start(bf16[4,2,96,576]{3,2,1,0:T(8,128)(2,1)} %get-tuple-element.171), channel_id=1, source_target_pairs={{0,2},{2,0},{1,3},{3,1},{4,6},{6,4},{5,7},{7,5},{8,10},{10,8},{9,1... | collective-permute-start | bytes 2654216 | tf_op jit(solution)/shard_map/ppermute | solution.py:814
  272.0 32.4 %collective-permute-start.18 = (bf16[12,64,768]{2,1,0:T(8,128)(2,1)}, bf16[12,64,768]{2,1,0:T(8,128)(2,1)}, u32[]{:S(2)}, u32[]{:S(2)}) collective-permute-start(bf16[12,64,768]{2,1,0:T(8,128)(2,1)} %get-tuple-element.157), channel_id=1, source_target_pairs={{0,1},{1,2},{2,3},{4,5},{5,6},{6,7},{8,9},{9,10},{10,11},{12,13},{... | collective-permute-start | bytes 3538952 | tf_op jit(solution)/shard_map/ppermute | solution.py:936
  276.1 26.5 %collective-permute-start.19 = (bf16[6,64,768]{2,1,0:T(8,128)(2,1)}, bf16[6,64,768]{2,1,0:T(8,128)(2,1)S(1)}, u32[]{:S(2)}, u32[]{:S(2)}) collective-permute-start(bf16[6,64,768]{2,1,0:T(8,128)(2,1)} %get-tuple-element.158), channel_id=1, source_target_pairs={{1,0},{2,1},{3,2},{5,4},{6,5},{7,6},{9,8},{10,9},{11,10},{13,12},{... | collective-permute-start | bytes 1769480 | tf_op jit(solution)/shard_map/ppermute | solution.py:935
  284.1 36.2 %collective-permute-start.36 = (bf16[96,768]{1,0:T(8,128)(2,1)}, bf16[96,768]{1,0:T(8,128)(2,1)S(1)}, u32[]{:S(2)}, u32[]{:S(2)}) collective-permute-start(bf16[96,768]{1,0:T(8,128)(2,1)} %get-tuple-element.221), channel_id=1, source_target_pairs={{0,8},{8,16},{16,24},{24,0},{1,9},{9,17},{17,25},{25,1},{2,10},{10... | collective-permute-start | bytes 442376 | tf_op jit(solution)/shard_map/ppermute | solution.py:818
  286.3 35.6 %collective-permute-start.38 = (bf16[96,768]{1,0:T(8,128)(2,1)}, bf16[96,768]{1,0:T(8,128)(2,1)}, u32[]{:S(2)}, u32[]{:S(2)}) collective-permute-start(bf16[96,768]{1,0:T(8,128)(2,1)} %get-tuple-element.222), channel_id=1, source_target_pairs={{0,24},{8,0},{16,8},{24,16},{1,25},{9,1},{17,9},{25,17},{2,26},{10... | collective-permute-start | bytes 442376 | tf_op jit(solution)/shard_map/ppermute | solution.py:818
  295.7 26.7 %collective-permute-start.37 = (bf16[96,768]{1,0:T(8,128)(2,1)}, bf16[96,768]{1,0:T(8,128)(2,1)}, u32[]{:S(2)}, u32[]{:S(2)}) collective-permute-start(bf16[96,768]{1,0:T(8,128)(2,1)} %get-tuple-element.223), channel_id=1, source_target_pairs={{0,16},{8,24},{16,0},{24,8},{1,17},{9,25},{17,1},{25,9},{2,18},{10... | collective-permute-start | bytes 442376 | tf_op jit(solution)/shard_map/ppermute | solution.py:818
  302.6 26.5 %collective-permute-start.27 = (bf16[4,96,576]{2,1,0:T(8,128)(2,1)}, bf16[4,96,576]{2,1,0:T(8,128)(2,1)}, u32[]{:S(2)}, u32[]{:S(2)}) collective-permute-start(bf16[4,96,576]{2,1,0:T(8,128)(2,1)} %get-tuple-element.173), channel_id=1, source_target_pairs={{0,4},{4,0},{1,5},{5,1},{2,6},{6,2},{3,7},{7,3},{8,12},{12,8},{9,1... | collective-permute-start | bytes 1327112 | tf_op jit(solution)/shard_map/ppermute | solution.py:814
  304.3 12.8 %copy-start.3 = (bf16[4,96,960]{2,1,0:T(8,128)(2,1)S(1)}, bf16[4,96,960]{2,1,0:T(8,128)(2,1)}, u32[]{:S(2)}) copy-start(bf16[4,96,960]{2,1,0:T(8,128)(2,1)} %get-tuple-element.178) | copy-start | bytes 2211844
  314.9 3.2 collective-permute-start.20
  318.0 19.3 %collective-permute-start.33 = (bf16[96,960]{1,0:T(8,128)(2,1)}, bf16[96,960]{1,0:T(8,128)(2,1)}, u32[]{:S(2)}, u32[]{:S(2)}) collective-permute-start(bf16[96,960]{1,0:T(8,128)(2,1)} %get-tuple-element.218), channel_id=1, source_target_pairs={{0,8},{8,16},{16,24},{24,0},{1,9},{9,17},{17,25},{25,1},{2,10},{10... | collective-permute-start | bytes 552968 | tf_op jit(solution)/shard_map/ppermute | solution.py:818
  320.3 17.8 %collective-permute-start.35 = (bf16[96,960]{1,0:T(8,128)(2,1)}, bf16[96,960]{1,0:T(8,128)(2,1)}, u32[]{:S(2)}, u32[]{:S(2)}) collective-permute-start(bf16[96,960]{1,0:T(8,128)(2,1)} %get-tuple-element.219), channel_id=1, source_target_pairs={{0,24},{8,0},{16,8},{24,16},{1,25},{9,1},{17,9},{25,17},{2,26},{10... | collective-permute-start | bytes 552968 | tf_op jit(solution)/shard_map/ppermute | solution.py:818
  321.9 22.1 %collective-permute-start.34 = (bf16[96,960]{1,0:T(8,128)(2,1)}, bf16[96,960]{1,0:T(8,128)(2,1)}, u32[]{:S(2)}, u32[]{:S(2)}) collective-permute-start(bf16[96,960]{1,0:T(8,128)(2,1)} %get-tuple-element.220), channel_id=1, source_target_pairs={{0,16},{8,24},{16,0},{24,8},{1,17},{9,25},{17,1},{25,9},{2,18},{10... | collective-permute-start | bytes 552968 | tf_op jit(solution)/shard_map/ppermute | solution.py:818
  322.4 5.0 %collective-permute-start.21 = (f32[26,512]{1,0:T(8,128)S(1)}, f32[26,512]{1,0:T(8,128)S(1)}, u32[]{:S(2)}, u32[]{:S(2)}) collective-permute-start(f32[26,512]{1,0:T(8,128)S(1)} %add.101), channel_id=1, source_target_pairs={{0,2},{2,0},{1,3},{3,1},{4,6},{6,4},{5,7},{7,5},{8,10},{10,8},{9,1... | collective-permute-start | bytes 159752 | tf_op jit(solution)/shard_map/ppermute | solution.py:814
  327.3 8.0 %collective-permute-start.22 = (f32[26,512]{1,0:T(8,128)S(1)}, f32[26,512]{1,0:T(8,128)S(1)}, u32[]{:S(2)}, u32[]{:S(2)}) collective-permute-start(f32[26,512]{1,0:T(8,128)S(1)} %add.102), channel_id=1, source_target_pairs={{0,4},{4,0},{1,5},{5,1},{2,6},{6,2},{3,7},{7,3},{8,12},{12,8},{9,1... | collective-permute-start | bytes 159752 | tf_op jit(solution)/shard_map/ppermute | solution.py:814
  333.4 13.3 %collective-permute-start.28 = (bf16[96,576]{1,0:T(8,128)(2,1)S(1)}, bf16[96,576]{1,0:T(8,128)(2,1)S(1)}, u32[]{:S(2)}, u32[]{:S(2)}) collective-permute-start(bf16[96,576]{1,0:T(8,128)(2,1)S(1)} %get-tuple-element.224), channel_id=1, source_target_pairs={{0,8},{8,16},{16,24},{24,0},{1,9},{9,17},{17,25},{25,1},{2,10},{10... | collective-permute-start | bytes 331784 | tf_op jit(solution)/shard_map/ppermute | solution.py:818
  335.3 11.4 %collective-permute-start.30 = (bf16[96,576]{1,0:T(8,128)(2,1)S(1)}, bf16[96,576]{1,0:T(8,128)(2,1)S(1)}, u32[]{:S(2)}, u32[]{:S(2)}) collective-permute-start(bf16[96,576]{1,0:T(8,128)(2,1)S(1)} %get-tuple-element.225), channel_id=1, source_target_pairs={{0,24},{8,0},{16,8},{24,16},{1,25},{9,1},{17,9},{25,17},{2,26},{10... | collective-permute-start | bytes 331784 | tf_op jit(solution)/shard_map/ppermute | solution.py:818
  337.3 14.6 %collective-permute-start.29 = (bf16[96,576]{1,0:T(8,128)(2,1)S(1)}, bf16[96,576]{1,0:T(8,128)(2,1)S(1)}, u32[]{:S(2)}, u32[]{:S(2)}) collective-permute-start(bf16[96,576]{1,0:T(8,128)(2,1)S(1)} %get-tuple-element.226), channel_id=1, source_target_pairs={{0,16},{8,24},{16,0},{24,8},{1,17},{9,25},{17,1},{25,9},{2,18},{10... | collective-permute-start | bytes 331784 | tf_op jit(solution)/shard_map/ppermute | solution.py:818
  338.1 8.5 %collective-permute-start.23 = (f32[26,512]{1,0:T(8,128)S(1)}, f32[26,512]{1,0:T(8,128)S(1)}, u32[]{:S(2)}, u32[]{:S(2)}) collective-permute-start(f32[26,512]{1,0:T(8,128)S(1)} %add.103), channel_id=1, source_target_pairs={{0,8},{8,0},{16,24},{24,16},{1,9},{9,1},{17,25},{25,17},{2,10},{10... | collective-permute-start | bytes 159752 | tf_op jit(solution)/shard_map/ppermute | solution.py:850
  346.6 7.3 %collective-permute-start.24 = (f32[26,512]{1,0:T(8,128)S(1)}, f32[26,512]{1,0:T(8,128)S(1)}, u32[]{:S(2)}, u32[]{:S(2)}) collective-permute-start(f32[26,512]{1,0:T(8,128)S(1)} %add.104), channel_id=1, source_target_pairs={{0,16},{8,24},{16,0},{24,8},{1,17},{9,25},{17,1},{25,9},{2,18},{10... | collective-permute-start | bytes 159752 | tf_op jit(solution)/shard_map/ppermute | solution.py:850
  (13 other events, 57.9 us)
Sparse Core Ops, SparseCore 0:
  10.9 93.9 all-gather.2

commit v4 on v3

--- a/solution.py
+++ b/solution.py
@@ -230,17 +230,16 @@
     )(place, normed, *pieces, bias)
 
 
-def store_shards(place_ref, refs, value, first=0, lane=0):
+def store_shards(place_ref, refs, value, first=0):
     z, x = place_ref[1], place_ref[2]
     count, _, depth = refs.shape[:3]
-    lanes = slice(lane, lane + value.shape[1])
     if depth % 32:
-        refs[:, :, :, lanes] = value.reshape(count, 2, depth, value.shape[1])
+        refs[...] = value.reshape(refs.shape)
         return
     for zd in range(value.shape[0] // (2 * depth)):
         for xd in range(2):
             start = (zd * 2 + xd) * depth
-            refs[lax.rem(first + zd - z + count, count), x ^ xd, :, lanes] = value[start : start + depth]
+            refs[lax.rem(first + zd - z + count, count), x ^ xd] = value[start : start + depth]
 
 
 def project_grad_body(place_ref, nw_ref, dq_ref, dk_ref, dv_ref, send_ref, keep_ref, bias_ref, *, rows, parts):
@@ -564,24 +563,39 @@
     )(slot, q, k, v, probs, grad_out, rel, table)
 
 
-def chunk_of(step, place):
-    return (place[3] ^ (1 - step % 2)) * 2 + (place[4] ^ (1 - step // 2))
-
-
-def feed_body(
-    place_ref, o_ref, x_ref, g_ref, wo_ref, up_ref, down_ref, vec_ref, bias_ref,
-    out_ref, dh_ref, do_ref, gas_ref, gak_ref, gbs_ref, gbk_ref, gvec_ref, gbias_ref,
-    nat_ref, onat_ref, n2_ref, h_ref, y_ref, dn_ref, a_ref, du_ref, w_ref, *, rows,
-):
+def feed_body(place_ref, o_ref, x_ref, g_ref, vec_ref, bias_ref, rest_ref, *refs, rows):
+    (
+        out_ref, dh_ref, do_ref, grad_ref, gas_ref, gak_ref, gvec_ref, gbias_ref,
+        nat_ref, onat_ref, n2_ref, n2t_ref, gt_ref, h_ref, y_ref, dn_ref, a_ref, du_ref, w_ref,
+        up_ref, down_ref, slots_ref, sems,
+    ) = refs
     step = pl.program_id(0)
     steps = rows * GRID // 256
     lines = 256 // GRID
     width = D // 4
+    y, c = place_ref[3], place_ref[4]
+    buffer = lax.rem(step, 2)
+
+    def fetch(chunk, where):
+        for i, ref in enumerate((up_ref, down_ref)):
+            source = rest_ref.at[:, chunk, :, pl.ds(i * D, D)]
+            pltpu.make_async_copy(source, ref.at[where], sems.at[where, i]).start()
 
     @pl.when(step == 0)
     def _():
+        pltpu.make_async_copy(rest_ref.at[:, :, :, pl.ds(2 * D, 256)], slots_ref, sems.at[2, 0]).start()
+        fetch(step, buffer)
+
+    @pl.when(step < pl.num_programs(0) - 1)
+    def _():
+        fetch(step + 1, 1 - buffer)
+
+    @pl.when(step == 0)
+    def _():
+        pltpu.make_async_copy(slots_ref, slots_ref, sems.at[2, 0]).wait()
+
         for t in range(4):
-            w_ref[:, t * width : (t + 1) * width] = wo_ref[:, t, :, 0:width].reshape(D, width)
+            w_ref[:, t * width : (t + 1) * width] = slots_ref[:, t, :, 0:width].reshape(D, width)
 
         def one(i, carry):
             at = pl.ds(pl.multiple_of(i * 256, 256), 256)
@@ -593,45 +607,47 @@
             hidden = x_ref[at, :].astype(F32) + mm_t(natural, w_ref[...]) + vec_ref[0:1]
             h_ref[at, :] = hidden
             hat, _ = norm_parts(hidden)
-            n2_ref[at, :] = (hat * vec_ref[1:2] + vec_ref[2:3]).astype(BF)
+            normed = (hat * vec_ref[1:2] + vec_ref[2:3]).astype(BF)
+            n2_ref[at, :] = normed
+            n2t_ref[:, at] = normed.T
+            gt_ref[:, at] = g_ref[at, :].T
             y_ref[at, :] = jnp.zeros((256, D), F32)
             dn_ref[at, :] = jnp.zeros((256, D), F32)
             return carry
 
         lax.fori_loop(0, steps, one, 0)
 
-    up = up_ref[...].reshape(D, D)
-    down = down_ref[...].reshape(D, D)
-
-    def two(i, total):
-        at = pl.ds(pl.multiple_of(i * 256, 256), 256)
+    pltpu.make_async_copy(up_ref.at[buffer], up_ref.at[buffer], sems.at[buffer, 0]).wait()
+    pltpu.make_async_copy(down_ref.at[buffer], down_ref.at[buffer], sems.at[buffer, 1]).wait()
+    up, down = up_ref[buffer].reshape(D, D), down_ref[buffer].reshape(D, D)
+    total = jnp.zeros((1, D), F32)
+
+    def inward(i):
+        at = slice(i * 512, i * 512 + 512)
         upper = mm(n2_ref[at, :], up) + bias_ref[...].reshape(1, D)
         cdf = 0.5 * (1.0 + lax.erf(upper * (1.0 / math.sqrt(2.0))))
-        active = (upper * cdf).astype(BF)
-        a_ref[at, :] = active
-        y_ref[at, :] += mm_t(active, down)
+        a_ref[at, :] = (upper * cdf).astype(BF)
         slope = cdf + upper * jnp.exp(-0.5 * upper * upper) * (1.0 / math.sqrt(2.0 * math.pi))
         delta = (mm(g_ref[at, :], down) * slope).astype(BF)
         du_ref[at, :] = delta
-        dn_ref[at, :] += mm_t(delta, up)
-        return total + jnp.sum(delta.astype(F32), 0, keepdims=True)
-
-    total = lax.fori_loop(0, steps, two, jnp.zeros((1, D), F32))
+        return jnp.sum(delta.astype(F32), 0, keepdims=True)
+
+    def outward(i):
+        at = slice(i * 512, i * 512 + 512)
+        y_ref[at, :] += mm_t(a_ref[at, :], down)
+        dn_ref[at, :] += mm_t(du_ref[at, :], up)
+
+    for i in range(rows * GRID // 512):
+        total = total + inward(i)
+        if i:
+            outward(i - 1)
+    outward(rows * GRID // 512 - 1)
     gbias_ref[...] = total.reshape(gbias_ref.shape)
-    grad_up = t_mm(n2_ref[...], du_ref[...]).astype(BF)
-    grad_down = t_mm(g_ref[...], a_ref[...]).astype(BF)
-
-    other_chip = 1 - step % 2
-
-    @pl.when(step < 2)
-    def _():
-        store_shards(place_ref, gas_ref.at[other_chip], grad_up)
-        store_shards(place_ref, gbs_ref.at[other_chip], grad_down)
-
-    @pl.when(step >= 2)
-    def _():
-        store_shards(place_ref, gak_ref.at[other_chip], grad_up)
-        store_shards(place_ref, gbk_ref.at[other_chip], grad_down)
+    grad_up = mm(n2t_ref[...], du_ref[...]).astype(BF)
+    grad_down = mm(gt_ref[...], a_ref[...]).astype(BF)
+    shape = (grad_ref.shape[0], grad_ref.shape[1], D)
+    grad_ref[:, :, 0:D] = grad_up.reshape(shape)
+    grad_ref[:, :, D:] = grad_down.reshape(shape)
 
     @pl.when(step == pl.num_programs(0) - 1)
     def _():
@@ -665,62 +681,64 @@
         grad_wo = t_mm(n2_ref[...], onat_ref[...]).astype(BF)
         for sibling, ref in ((1, gas_ref), (0, gak_ref)):
             for t in range(4):
-                @pl.when(place_ref[4] ^ (t % 2) == sibling)
+                @pl.when(c ^ (t % 2) == sibling)
                 def _(t=t, ref=ref):
                     store_shards(
-                        place_ref, ref.at[place_ref[3] ^ (t // 2)], grad_wo[:, t * width : (t + 1) * width], lane=D
+                        place_ref, ref.at[y ^ (t // 2)], grad_wo[:, t * width : (t + 1) * width]
                     )
 
 
 def feed(place, o, x, g, rest, vectors, up_bias, rows, shards):
     tokens = rows * GRID
     blocks, chunks, depth = rest.shape[:3]
-    width = D // chunks
-    slab = lambda column: pl.BlockSpec(
-        (blocks, None, depth, D), lambda s, p: (0, chunk_of(s, p), 0, column)
-    )
-    line = pl.BlockSpec((None, 1, D), lambda s, p: (chunk_of(s, p), 0, 0))
+    line = pl.BlockSpec((None, 1, D), lambda s, p: (s, 0, 0))
     grid = (SIDE, rows, PITCH, D)
-    first = jax.ShapeDtypeStruct((*shards, D + width), BF)
-    second = jax.ShapeDtypeStruct((*shards, D), BF)
+    out = jax.ShapeDtypeStruct((*shards, D // chunks), BF)
     shapes = [
         jax.ShapeDtypeStruct((tokens, D), BF),
         jax.ShapeDtypeStruct((tokens, D), F32),
         jax.ShapeDtypeStruct(grid, BF),
-        first, first, second, second,
+        jax.ShapeDtypeStruct((blocks, chunks, depth, 2 * D), BF),
+        out, out,
         jax.ShapeDtypeStruct((8, D), F32),
         jax.ShapeDtypeStruct((chunks, 1, D), F32),
     ]
     specs = [whole(s.shape) for s in shapes]
-    specs[8] = line
+    specs[3] = pl.BlockSpec((blocks, None, depth, 2 * D), lambda s, p: (0, s, 0, 0))
+    specs[7] = line
     return pl.pallas_call(
         partial(feed_body, rows=rows),
         grid_spec=pltpu.PrefetchScalarGridSpec(
             num_scalar_prefetch=1,
             grid=(chunks,),
             in_specs=[
-                whole(grid), whole((tokens, D)), whole((tokens, D)),
-                pl.BlockSpec((blocks, chunks, depth, 256), lambda s, p: (0, 0, 0, 2 * D // 256), pipeline_mode=pl.Buffered(1)),
-                slab(0), slab(1), whole((8, D)), line,
+                whole(grid), whole((tokens, D)), whole((tokens, D)), whole((8, D)), line,
+                pl.BlockSpec(memory_space=pl.ANY),
             ],
             out_specs=specs,
             scratch_shapes=[
                 pltpu.VMEM((256 // GRID, GRID + PITCH, D), F32),
                 pltpu.VMEM((tokens, D), BF),
                 pltpu.VMEM((tokens, D), BF),
+                pltpu.VMEM((D, tokens), BF),
+                pltpu.VMEM((D, tokens), BF),
                 pltpu.VMEM((tokens, D), F32),
                 pltpu.VMEM((tokens, D), F32),
                 pltpu.VMEM((tokens, D), F32),
                 pltpu.VMEM((tokens, D), BF),
                 pltpu.VMEM((tokens, D), BF),
                 pltpu.VMEM((D, D), BF),
+                pltpu.VMEM((2, blocks, depth, D), BF),
+                pltpu.VMEM((2, blocks, depth, D), BF),
+                pltpu.VMEM((blocks, chunks, depth, 256), BF),
+                pltpu.SemaphoreType.DMA((3, 2)),
             ],
         ),
         out_shape=shapes,
         compiler_params=pltpu.CompilerParams(vmem_limit_bytes=63 << 20),
-        cost_estimate=guess(55),
+        cost_estimate=guess(50),
         name="feed",
-    )(place, o, x, g, rest, rest, rest, vectors, up_bias)
+    )(place, o, x, g, vectors, up_bias, rest)
 
 
 def finish_body(own_ref, head_ref, tail_ref, x_ref, dh_ref, vec_ref, out_ref, sum_ref):
@@ -832,6 +850,10 @@
     return first, second, swap(first, "c"), swap(second, "c")
 
 
+def after(value, *others):
+    return lax.optimization_barrier((value, *others))
+
+
 def along_z(pieces):
     count = pieces.shape[0]
     total = pieces[0].astype(F32)
@@ -904,67 +926,67 @@
         [output_bias[None], second_gain[None], second_shift[None], down_bias[None], jnp.zeros((4, D), BF)], 0
     ).astype(F32)
     (
-        output, grad_hidden, grad_out, a_send, a_keep, b_send, b_keep, grad_vec, grad_up_bias,
+        output, grad_hidden, grad_out, grad_feed, out_send, out_keep, grad_vec, grad_up_bias,
     ) = feed(
         place, attended.reshape(SIDE, rows, PITCH, D), features, cotangent, rest_all, vec_two, up_bias_all,
         rows, shards,
     )
     grad_windows = grad_out.reshape(-1, D)
     table = jnp.asarray(back.transpose(0, 2, 1), BF)
+    grad_feed = lax.psum_scatter(
+        grad_feed.reshape(8 * count, depth, 2 * hidden), AXES, scatter_dimension=0
+    ).astype(F32)
+    grad_up, grad_down = grad_feed[:, :hidden], grad_feed[:, hidden:]
     if fast:
-        a_got, b_got = swap(a_send, "c"), swap(b_send, "c")
+        out_got = swap(out_send, "c")
     *half0, drel0 = attend_back(place, q, k, v, probs, grad_windows, rel_back, table, rows, 0)
-    if fast:
-        a, b = [a_keep, a_got], [b_keep, b_got]
-        a_away, a_here, b_away, b_here = fold((a, 1, 0, 1), (a, 1, 0, 0), (b, 1, 2, 1), (b, 1, 2, 0))
-        place, a_away, b_away = lax.optimization_barrier((place, a_away, b_away))
-        a_got, b_got = swap(a_away, "y"), swap(b_away, "x")
     first_send, first_keep, first_bias = project_grad(place, normed, *half0, rows, shards)
     if fast:
         first_got = swap(first_send, "c")
     *half1, drel1 = attend_back(place, q, k, v, probs, grad_windows, rel_back, table, rows, 1)
     if fast:
-        a, b = [a_here, a_got], [b_here, b_got]
-        a_away, a_here, b_away, b_here, crossing = fold(
-            (a, 0, 1, 1), (a, 0, 1, 0), (b, 1, 0, 1), (b, 1, 0, 0), ([first_keep, first_got], 0, None, None)
+        first, out = [first_keep, first_got], [out_keep, out_got]
+        first_away, first_here, out_away, out_here = fold(
+            (first, 0, 1, 1), (first, 0, 1, 0), (out, 1, 2, 1), (out, 1, 2, 0)
         )
-        place, a_away, b_away, crossing = lax.optimization_barrier((place, a_away, b_away, crossing))
-        a_got, b_got, crossing = swap(a_away, "x"), swap(b_away, "y"), swap(crossing, "y")
+        place, first_away, out_away = after(place, first_away, out_away)
+        first_got, out_got = swap(first_away, "x"), swap(out_away, "x")
     dqs, dks, dvs = zip(half0, half1)
     to_above, total, to_below = project_back(place, dqs, dks, dvs, weight, rows, slots)
+    place, to_above, to_below = after(place, to_above, to_below)
     from_below = lax.ppermute(to_above, pair, down_pairs)
     from_above = lax.ppermute(to_below, pair, up_pairs)
-    place, to_above = lax.optimization_barrier((place, to_above))
     last_send, last_keep, last_bias = project_grad(place, normed, *half1, rows, shards)
     if fast:
         last_got = swap(last_send, "c")
-        a, b = fold(([a_here, a_got], 0, None, None), ([b_here, b_got], 0, None, None))
-        a, b = along_z(a), along_z(b)
-        grad_up, grad_wo, grad_down = a[:, :hidden], a[:, hidden:], b
+        first_got, out_got, last_keep = after(first_got, out_got, last_keep)
+        crossing, out_away, out_here = fold(
+            ([first_here, first_got], 0, None, None), ([out_here, out_got], 1, 0, 1), ([out_here, out_got], 1, 0, 0)
+        )
+        crossing, out_got = swap(crossing, "y"), swap(out_away, "y")
     grad_features, sums_one = finish(
         total, from_above, from_below, grid_x, grad_hidden.reshape(rows, GRID, D), vec_one
     )
     if fast:
-        last = [last_keep, last_got, crossing]
+        last = [last_keep, last_got]
         away, here = fold((last, 0, 1, 1), (last, 0, 1, 0))
-        (last,) = fold(([here, swap(away, "x")], 0, None, None))
-        grad_qkv = along_z(last)
+        last, out = fold(([here, swap(away, "x"), crossing], 0, None, None), ([out_here, out_got], 0, None, None))
+        grad_qkv, grad_wo = along_z(last), along_z(out)
     else:
         pairs = [
-            (a_send, a_keep), (b_send, b_keep),
+            (out_send, out_keep),
             [
                 jnp.where(y == 0, jnp.stack([last, first]), jnp.stack([first, last]))
                 for first, last in ((first_send, last_send), (first_keep, last_keep))
             ],
         ]
-        a, grad_down, grad_qkv = [
+        grad_wo, grad_qkv = [
             lax.psum_scatter(
                 jnp.stack([keep, send], 3).transpose(1, 2, 0, 3, 4, 5).reshape(8 * count, depth, -1),
                 AXES, scatter_dimension=0,
             ).astype(F32)
             for send, keep in pairs
         ]
-        grad_up, grad_wo = a[:, :hidden], a[:, hidden:]
     drel = (drel0 + drel1).T.reshape(4, 64, 128)
     drel = drel[1, :, :HD] + drel[2, :, HD:]
     grad_qv = jnp.where(y == 0, jnp.concatenate([last_bias, first_bias], 1), jnp.concatenate([first_bias, last_bias], 1))

time: 364 us -> 344 us (0.945)
  Pallas kernels: 203 us -> 183 us
  waiting for transfers between devices: 59.4 us -> 69.5 us
  starting transfers between devices: 52.6 us -> 45.6 us
    pallas_call x5 -> x4, Pallas kernels: 29.9 us -> 16.9 us  [fold(): pl.pallas_call(partial(fold_body, plan=plan), grid=(count,), in_specs=in_...]
    ppermute x21 -> x19, waiting for transfers between devices: 46.1 us -> 57.8 us  [swap(): return lax.ppermute(value, axis, SWAP)]
    pallas_call x1, Pallas kernels: 58.3 us -> 50.4 us  [feed(): pl.pallas_call(partial(feed_body, rows=rows), grid_spec=pltpu.PrefetchSca...]
    ppermute x21 -> x19, starting transfers between devices: 23.1 us -> 16.8 us  [swap(): return lax.ppermute(value, axis, SWAP)]
    ppermute x12 -> x9, starting transfers between devices: 21.1 us -> 15.4 us  [shift(): lax.ppermute(value, 'z', [(i, (i + by) % count) for i in range(count)])]
    ppermute x2, starting transfers between devices: 0.52 us -> 5.26 us  [sum_all(): lax.ppermute(value, 'z', [(i, i ^ step) for i in range(count)])]
    ppermute x12 -> x9, waiting for transfers between devices: 13.2 us -> 10 us  [shift(): lax.ppermute(value, 'z', [(i, (i + by) % count) for i in range(count)])]
  transfers between devices with their start and end apart: 40 -> 36, of which waited for: 11 -> 9; matrix products, arithmetic and copies ran while one was open for 7% -> 7% of each run, Pallas kernels for 31% -> 39%
where the time goes in v4:
time: 344 us; the launch traced here: 343 us
  Pallas kernels  183 us (53%)
  waiting for transfers between devices  69.5 us (20%)
  starting transfers between devices  45.6 us (13%)
  local copies, waits for them, and re-layouts  20.3 us (6%)
  between operations  14.7 us (4%)
  other arithmetic  9.05 us (3%)
    ppermute x19, waiting for transfers between devices, swap(): return lax.ppermute(value, axis, SWAP)  57.8 us
    pallas_call x1, Pallas kernels, feed(): pl.pallas_call(partial(feed_body, rows=rows), grid_spec=pltpu.PrefetchSca...  50.4 us
    pallas_call x2, Pallas kernels, attend_back(): pl.pallas_call(partial(attend_back_body, rows=rows), grid_spec=pltpu.Pref...  23.2 us
    pallas_call x2, Pallas kernels, project_grad(): pl.pallas_call(partial(project_grad_body, rows=rows, parts=parts), grid_s...  22.3 us
    pallas_call x1, Pallas kernels, attend(): pl.pallas_call(partial(attend_body, rows=rows), grid_spec=pltpu.PrefetchS...  18.9 us
    pallas_call x4, Pallas kernels, fold(): pl.pallas_call(partial(fold_body, plan=plan), grid=(count,), in_specs=in_...  16.9 us
    ppermute x19, starting transfers between devices, swap(): return lax.ppermute(value, axis, SWAP)  16.8 us
    pallas_call x1, Pallas kernels, project_back(): pl.pallas_call(partial(project_back_body, rows=rows), grid_spec=pltpu.Pre...  16.4 us
  transfers between devices with their start and end apart: 36, of which 9 were waited for; matrix products, arithmetic and copies ran while one was open for 7% of the time, Pallas kernels for 39%

profile of v4, /device:TPU:0, one launch (start us, length us, event | category | flops | bytes accessed | tf_op | source)
XLA Modules:
  0.0 342.6 jit_solution(4646844463621973945)
XLA Ops:
  7.3 1.9 concatenate.68
  9.2 1.1 copy.42
  10.5 5.1 %collective-permute-start.4 = (bf16[96,576]{1,0:T(8,128)(2,1)S(1)}, bf16[96,576]{1,0:T(8,128)(2,1)S(1)}, u32[]{:S(2)}, u32[]{:S(2)}) collective-permute-start(bf16[96,576]{1,0:T(8,128)(2,1)S(1)} %copy.43), channel_id=1, source_target_pairs={{0,24},{8,0},{16,8},{24,16},{1,25},{9,1},{17,9},{25,17},{2,26},{10... | collective-permute-start | bytes 331784 | tf_op jit(solution)/shard_map/ppermute | solution.py:836
  15.6 1.0 collective-permute-start.2
  16.7 2.1 collective-permute-start
  18.8 1.1 slice.198
  19.9 1.3 collective-permute-start.1
  23.7 2.6 collective-permute-done.3
  26.4 1.6 collective-permute-start.6
  28.1 1.6 collective-permute-start.5
  30.2 18.1 %collective-permute-done.6 = bf16[4,48,576]{2,1,0:T(8,128)(2,1)S(1)} collective-permute-done((bf16[4,48,576]{2,1,0:T(8,128)(2,1)S(1)}, bf16[4,48,576]{2,1,0:T(8,128)(2,1)S(1)}, u32[]{:S(2)}, u32[]{:S(2)}) %collective-permute-start.6) | collective-permute-done | bytes 221216 | tf_op jit(solution)/shard_map/ppermute | solution.py:832
  48.5 11.8 %windows.1.nw_ref = bf16[2240,768]{1,0:T(8,128)(2,1)} custom-call(s32[6]{0:T(128)} %stack.90.place_ref, bf16[6,64,768]{2,1,0:T(8,128)(2,1)} %collective-permute-done.above_ref, bf16[16,64,768]{2,1,0:T(8,128)(2,1)} %bitcast.72, bf16[12,64,768]{2,1,0:T(8,128)(2,1)} %collective-permute-done.1.below_ref, f32[8,768]{1,0:T(8,128)} %maximum_convert_fusion.vec_ref), custom_call_target="tpu_custom_call" | custom-call | flops 8800000000 | bytes 24000000 | tf_op jit(solution)/shard_map/windows/pallas_call | solution.py:149
  60.3 1.4 collective-permute-start.8
  65.8 5.7 %collective-permute-done.8 = bf16[2,4,48,576]{3,2,1,0:T(8,128)(2,1)S(1)} collective-permute-done((bf16[2,4,48,576]{3,2,1,0:T(8,128)(2,1)S(1)}, bf16[2,4,48,576]{3,2,1,0:T(8,128)(2,1)S(1)}, u32[]{:S(2)}, u32[]{:S(2)}) %collective-permute-start.8) | collective-permute-done | bytes 442400 | tf_op jit(solution)/shard_map/ppermute | solution.py:832
  72.7 2.7 collective-permute-start.12
  80.1 13.8 %project.1 = (bf16[1280,768]{1,0:T(8,128)(2,1)}, bf16[2240,768]{1,0:T(8,128)(2,1)}, bf16[2240,768]{1,0:T(8,128)(2,1)}, bf16[768,2304]{1,0:T(8,128)(2,1)}) custom-call(s32[6]{0:T(128)} %stack.90.place_ref, bf16[2240,768]{1,0:T(8,128)(2,1)} %windows.1.nw_ref, bf16[2,2,4,48,576]{4,3,2,1,0:T(8,128)(2,1)} %copy-done.2, bf16[2,2,4,48,576]{4,3,2,1,0:T(8,128)(2,1)} %copy-done.1, ...), custom_call_target="tpu_custom_call" | custom-call | flops 19800000512 | bytes 54000000 | tf_op jit(solution)/shard_map/project/pallas_call | solution.py:214
  93.9 18.9 %attend.1 = (bf16[1280,768]{1,0:T(8,128)(2,1)}, bf16[30,2,224,256]{3,2,1,0:T(8,128)(2,1)}) custom-call(s32[6]{0:T(128)} %stack.90.place_ref, bf16[1280,768]{1,0:T(8,128)(2,1)} %get-tuple-element.123.q_ref, bf16[2240,768]{1,0:T(8,128)(2,1)} %get-tuple-element.124.k_ref, bf16[2240,768]{1,0:T(8,128)(2,1)} %get-tuple-element.125.v_ref, ...), custom_call_target="tpu_custom_call" | custom-call | flops 26400000000 | bytes 72000000 | tf_op jit(solution)/shard_map/attend/pallas_call | solution.py:428
  112.8 50.4 %feed.1 = (bf16[1024,768]{1,0:T(8,128)(2,1)}, f32[1024,768]{1,0:T(8,128)}, bf16[5,16,16,768]{3,2,1,0:T(8,128)(2,1)}, bf16[8,4,96,1536]{3,2,1,0:T(8,128)(2,1)}, b...) custom-call(s32[6]{0:T(128)} %stack.90.place_ref, ...), custom_call_target="tpu_custom_call" | custom-call | flops 54999998464 | bytes 150000000 | tf_op jit(solution)/shard_map/feed/pallas_call | solution.py:709
  163.6 11.6 %attend_back.2 = (bf16[1280,384]{1,0:T(8,128)(2,1)}, bf16[2240,384]{1,0:T(8,128)(2,1)}, bf16[2240,384]{1,0:T(8,128)(2,1)}, f32[128,256]{1,0:T(8,128)}) custom-call(s32[6]{0:T(128)} %stack.90.place_ref, bf16[1280,768]{1,0:T(8,128)(2,1)} %get-tuple-element.123.q_ref, bf16[2240,768]{1,0:T(8,128)(2,1)} %get-tuple-element.124.k_ref, ...), custom_call_target="tpu_custom_call" | custom-call | flops 17600000000 | bytes 48000000 | tf_op jit(solution)/shard_map/attend_back/pallas_call | solution.py:542
  175.3 11.1 %project_grad.2 = (bf16[4,2,96,576]{3,2,1,0:T(8,128)(2,1)}, bf16[4,2,96,576]{3,2,1,0:T(8,128)(2,1)}, f32[2,384]{1,0:T(2,128)}) custom-call(s32[6]{0:T(128)} %stack.90.place_ref, bf16[2240,768]{1,0:T(8,128)(2,1)} %windows.1.nw_ref, bf16[1280,384]{1,0:T(8,128)(2,1)} %get-tuple-element.130.dq_ref.refs_0_, bf16[2240,384]{1,0:T(8,128)(2,1)} %get-tuple-element.131.dk_ref.refs_2_, ...), custom_call_target="tpu_custom_call" | custom-call | flops 6600000000 | bytes 18000000 | tf_op jit(solution)/shard_map/project_grad/pallas_call | solution.py:275
  186.6 11.6 %attend_back.3 = (bf16[1280,384]{1,0:T(8,128)(2,1)}, bf16[2240,384]{1,0:T(8,128)(2,1)}, bf16[2240,384]{1,0:T(8,128)(2,1)}, f32[128,256]{1,0:T(8,128)}) custom-call(s32[6]{0:T(128)} %stack.90.place_ref, bf16[1280,768]{1,0:T(8,128)(2,1)} %get-tuple-element.123.q_ref, bf16[2240,768]{1,0:T(8,128)(2,1)} %get-tuple-element.124.k_ref, ...), custom_call_target="tpu_custom_call" | custom-call | flops 17600000000 | bytes 48000000 | tf_op jit(solution)/shard_map/attend_back/pallas_call | solution.py:542
  199.1 5.4 %fold.4 = (bf16[4,96,576]{2,1,0:T(8,128)(2,1)}, bf16[4,96,576]{2,1,0:T(8,128)(2,1)}, bf16[2,4,96,192]{3,2,1,0:T(8,128)(2,1)}, bf16[2,4,96,192]{3,2,1,0:T(8,128)(2,1)}) custom-call(bf16[4,2,96,576]{3,2,1,0:T(8,128)(2,1)} %get-tuple-element.133.refs_0_.refs_2_, bf16[4,2,96,576]{3,2,1,0:T(8,128)(2,1)} %copy-done.20, ...), custom_call_target="tpu_custom_call" | custom-call | flops 4344032256 | bytes 11847360 | tf_op jit(solution)/shard_map/fold/pallas_call | solution.py:815
  204.5 16.4 %project_back.1 = (bf16[6,64,768]{2,1,0:T(8,128)(2,1)}, f32[16,64,768]{2,1,0:T(8,128)}, bf16[12,64,768]{2,1,0:T(8,128)(2,1)}) custom-call(s32[6]{0:T(128)} %stack.90.place_ref, bf16[1280,384]{1,0:T(8,128)(2,1)} %get-tuple-element.130.dq_ref.refs_0_, bf16[1280,384]{1,0:T(8,128)(2,1)} %get-tuple-element.140.refs_1_.dq_ref, ...), custom_call_target="tpu_custom_call" | custom-call | flops 15399999488 | bytes 42000000 | tf_op jit(solution)/shard_map/project_back/pallas_call | solution.py:335
  220.9 3.3 collective-permute-start.15
  224.2 11.2 %project_grad.3 = (bf16[4,2,96,576]{3,2,1,0:T(8,128)(2,1)}, bf16[4,2,96,576]{3,2,1,0:T(8,128)(2,1)}, f32[2,384]{1,0:T(2,128)}) custom-call(s32[6]{0:T(128)} %stack.90.place_ref, bf16[2240,768]{1,0:T(8,128)(2,1)} %windows.1.nw_ref, bf16[1280,384]{1,0:T(8,128)(2,1)} %get-tuple-element.140.refs_1_.dq_ref, bf16[2240,384]{1,0:T(8,128)(2,1)} %get-tuple-element.141.refs_3_.dk_ref, ...), custom_call_target="tpu_custom_call" | custom-call | flops 6600000000 | bytes 18000000 | tf_op jit(solution)/shard_map/project_grad/pallas_call | solution.py:275
  235.9 2.4 collective-permute-start.22
  238.8 1.3 collective-permute-start.16
  240.8 26.1 %collective-permute-done.23.refs_3_.refs_5_ = bf16[2,4,96,192]{3,2,1,0:T(8,128)(2,1)} collective-permute-done((bf16[2,4,96,192]{3,2,1,0:T(8,128)(2,1)}, bf16[2,4,96,192]{3,2,1,0:T(8,128)(2,1)}, u32[]{:S(2)}, u32[]{:S(2)}) %collective-permute-start.23) | collective-permute-done | bytes 294944 | tf_op jit(solution)/shard_map/ppermute | solution.py:832
  267.0 3.7 %fold.6 = (bf16[4,96,576]{2,1,0:T(8,128)(2,1)}, bf16[4,96,192]{2,1,0:T(8,128)(2,1)}, bf16[4,96,192]{2,1,0:T(8,128)(2,1)}) custom-call(bf16[4,96,576]{2,1,0:T(8,128)(2,1)} %get-tuple-element.166.refs_0_, bf16[4,96,576]{2,1,0:T(8,128)(2,1)} %collective-permute-done.22.refs_1_, bf16[2,4,96,192]{3,2,1,0:T(8,128)(2,1)} %get-tuple-element.168.refs_2_.refs_4_, ...), custom_call_target="tpu_custom_call" | custom-call | flops 2235411200 | bytes 6096576 | tf_op jit(solution)/shard_map/fold/pallas_call | solution.py:815
  271.1 1.6 collective-permute-start.26
  272.8 4.3 %fold.5 = (bf16[4,96,576]{2,1,0:T(8,128)(2,1)}, bf16[4,96,576]{2,1,0:T(8,128)(2,1)}) custom-call(bf16[4,2,96,576]{3,2,1,0:T(8,128)(2,1)} %get-tuple-element.162.refs_0_.refs_2_, bf16[4,2,96,576]{3,2,1,0:T(8,128)(2,1)} %collective-permute-done.24.refs_1_.refs_3_, bf16[4,2,96,576]{3,2,1,0:T(8,128)(2,1)} %get-tuple-element.162.refs_0_.refs_2_, ...), custom_call_target="tpu_custom_call" | custom-call | flops 3046419200 | bytes 8308416 | tf_op jit(solution)/shard_map/fold/pallas_call | solution.py:815
  277.0 1.7 collective-permute-start.25
  278.8 9.7 %finish.1 = (bf16[16,64,768]{2,1,0:T(8,128)(2,1)}, f32[8,768]{1,0:T(8,128)}) custom-call(f32[16,64,768]{2,1,0:T(8,128)} %get-tuple-element.144.own_ref, bf16[12,64,768]{2,1,0:T(8,128)(2,1)} %collective-permute-done.15.head_ref, bf16[6,64,768]{2,1,0:T(8,128)(2,1)} %collective-permute-done.16.tail_ref, bf16[16,64,768]{2,1,0:T(8,128)(2,1)} %bitcast.73, ...), custom_call_target="tpu_custom_call" | custom-call | flops 5500000256 | bytes 15000000 | tf_op jit(solution)/shard_map/finish/pallas_call | solution.py:769
  289.3 1.2 collective-permute-done.17
  291.0 6.6 %collective-permute-done.18 = f32[26,512]{1,0:T(8,128)S(1)} collective-permute-done((f32[26,512]{1,0:T(8,128)S(1)}, f32[26,512]{1,0:T(8,128)S(1)}, u32[]{:S(2)}, u32[]{:S(2)}) %collective-permute-start.18) | collective-permute-done | bytes 53280 | tf_op jit(solution)/shard_map/ppermute | solution.py:832
  297.7 1.5 collective-permute-start.19
  299.2 3.5 %fold.7 = (bf16[4,96,576]{2,1,0:T(8,128)(2,1)}, bf16[4,96,192]{2,1,0:T(8,128)(2,1)}) custom-call(bf16[4,96,576]{2,1,0:T(8,128)(2,1)} %get-tuple-element.164.refs_0_, bf16[4,96,576]{2,1,0:T(8,128)(2,1)} %collective-permute-done.25.refs_1_, bf16[4,96,576]{2,1,0:T(8,128)(2,1)} %collective-permute-done.26.refs_2_, ...), custom_call_target="tpu_custom_call" | custom-call | flops 1992108800 | bytes 5433024 | tf_op jit(solution)/shard_map/fold/pallas_call | solution.py:815
  303.6 2.3 collective-permute-start.31
  305.8 1.7 collective-permute-start.33
  308.2 1.1 slice_bitcast_fusion.2
  309.3 1.9 collective-permute-start.28
  311.2 2.0 collective-permute-start.30
  313.9 1.2 collective-permute-start.20
  315.1 5.2 %collective-permute-done.32 = bf16[96,192]{1,0:T(8,128)(2,1)S(1)} collective-permute-done((bf16[96,192]{1,0:T(8,128)(2,1)S(1)}, bf16[96,192]{1,0:T(8,128)(2,1)S(1)}, u32[]{:S(2)}, u32[]{:S(2)}) %collective-permute-start.32) | collective-permute-done | bytes 36896 | tf_op jit(solution)/shard_map/ppermute | solution.py:836
  320.3 1.5 fusion.11
  321.8 1.6 collective-permute-done.20
  323.4 4.1 %collective-permute-start.21 = (f32[26,512]{1,0:T(8,128)S(1)}, f32[26,512]{1,0:T(8,128)S(1)}, u32[]{:S(2)}, u32[]{:S(2)}) collective-permute-start(f32[26,512]{1,0:T(8,128)S(1)} %add.97), channel_id=1, source_target_pairs={{0,16},{8,24},{16,0},{24,8},{1,17},{9,25},{17,1},{25,9},{2,18},{10... | collective-permute-start | bytes 159752 | tf_op jit(solution)/shard_map/ppermute | solution.py:872
  327.6 2.2 collective-permute-done.29
  (178 shorter events, 26.6 us)
Async XLA Ops:
  7.2 9.5 %copy-start = (bf16[1024,768]{1,0:T(8,128)(2,1)S(1)}, bf16[1024,768]{1,0:T(8,128)(2,1)}, u32[]{:S(2)}) copy-start(bf16[1024,768]{1,0:T(8,128)(2,1)} %x_ref.1) | copy-start | bytes 4718596
  7.2 105.6 %all-gather.3.cloned.1.call-start = ((), (), s32[]{:S(2)}) async-start(), calls=%async_computation.2 | async-start | bytes 11354112 | tf_op jit(solution)/shard_map/all_gather | solution.py:903
  9.2 324.7 %reduce-scatter.2.cloned.1.call-start = ((), (), s32[]{:S(2)}) async-start(), calls=%async_computation.1 | async-start | bytes 9732096 | tf_op jit(solution)/shard_map/reduce_scatter | solution.py:936
  10.3 10.9 %copy-start.18 = (bf16[2,192]{1,0:T(2,128)(2,1)S(1)}, bf16[2,192]{1,0:T(2,128)(2,1)}, u32[]{:S(2)}) copy-start(bf16[2,192]{1,0:T(2,128)(2,1)} %param.30) | copy-start | bytes 2308
  10.3 11.0 %copy-start.12 = (bf16[768]{0:T(1024)(128)(2,1)S(1)}, bf16[768]{0:T(1024)(128)(2,1)}, u32[]{:S(2)}) copy-start(bf16[768]{0:T(1024)(128)(2,1)} %param.27) | copy-start | bytes 4612
  10.3 11.0 %copy-start.13 = (bf16[768]{0:T(1024)(128)(2,1)S(1)}, bf16[768]{0:T(1024)(128)(2,1)}, u32[]{:S(2)}) copy-start(bf16[768]{0:T(1024)(128)(2,1)} %param.28) | copy-start | bytes 4612
  10.4 11.0 %copy-start.3 = (bf16[96,3,192]{2,0,1:T(8,128)(2,1)S(1)}, bf16[96,3,192]{2,0,1:T(8,128)(2,1)}, u32[]{:S(2)}) copy-start(bf16[96,3,192]{2,0,1:T(8,128)(2,1)} %param.29) | copy-start | bytes 331780
  10.5 13.2 %collective-permute-start.4 = (bf16[96,576]{1,0:T(8,128)(2,1)S(1)}, bf16[96,576]{1,0:T(8,128)(2,1)S(1)}, u32[]{:S(2)}, u32[]{:S(2)}) collective-permute-start(bf16[96,576]{1,0:T(8,128)(2,1)S(1)} %copy.43), channel_id=1, source_target_pairs={{0,24},{8,0},{16,8},{24,16},{1,25},{9,1},{17,9},{25,17},{2,26},{10... | collective-permute-start | bytes 331784 | tf_op jit(solution)/shard_map/ppermute | solution.py:836
  15.6 10.7 %collective-permute-start.3 = (bf16[96,576]{1,0:T(8,128)(2,1)S(1)}, bf16[96,576]{1,0:T(8,128)(2,1)S(1)}, u32[]{:S(2)}, u32[]{:S(2)}) collective-permute-start(bf16[96,576]{1,0:T(8,128)(2,1)S(1)} %copy.43), channel_id=1, source_target_pairs={{0,16},{8,24},{16,0},{24,8},{1,17},{9,25},{17,1},{25,9},{2,18},{10... | collective-permute-start | bytes 331784 | tf_op jit(solution)/shard_map/ppermute | solution.py:836
  15.6 10.7 %collective-permute-start.2 = (bf16[96,576]{1,0:T(8,128)(2,1)S(1)}, bf16[96,576]{1,0:T(8,128)(2,1)S(1)}, u32[]{:S(2)}, u32[]{:S(2)}) collective-permute-start(bf16[96,576]{1,0:T(8,128)(2,1)S(1)} %copy.43), channel_id=1, source_target_pairs={{0,8},{8,16},{16,24},{24,0},{1,9},{9,17},{17,25},{25,1},{2,10},{10... | collective-permute-start | bytes 331784 | tf_op jit(solution)/shard_map/ppermute | solution.py:836
  16.7 31.8 %collective-permute-start = (bf16[6,64,768]{2,1,0:T(8,128)(2,1)S(1)}, bf16[6,64,768]{2,1,0:T(8,128)(2,1)}, u32[]{:S(2)}, u32[]{:S(2)}) collective-permute-start(bf16[6,64,768]{2,1,0:T(8,128)(2,1)S(1)} %bitcast.77), channel_id=1, source_target_pairs={{0,1},{1,2},{2,3},{4,5},{5,6},{6,7},{8,9},{9,10},{10,11},{12,13},{... | collective-permute-start | bytes 1769480 | tf_op jit(solution)/shard_map/ppermute | solution.py:899
  19.9 28.6 %collective-permute-start.1 = (bf16[12,64,768]{2,1,0:T(8,128)(2,1)}, bf16[12,64,768]{2,1,0:T(8,128)(2,1)}, u32[]{:S(2)}, u32[]{:S(2)}) collective-permute-start(bf16[12,64,768]{2,1,0:T(8,128)(2,1)} %bitcast.7), channel_id=1, source_target_pairs={{1,0},{2,1},{3,2},{5,4},{6,5},{7,6},{9,8},{10,9},{11,10},{13,12},{... | collective-permute-start | bytes 3538952 | tf_op jit(solution)/shard_map/ppermute | solution.py:900
  26.4 21.9 %collective-permute-start.6 = (bf16[4,48,576]{2,1,0:T(8,128)(2,1)S(1)}, bf16[4,48,576]{2,1,0:T(8,128)(2,1)S(1)}, u32[]{:S(2)}, u32[]{:S(2)}) collective-permute-start(bf16[4,48,576]{2,1,0:T(8,128)(2,1)S(1)} %get-tuple-element.220), channel_id=1, source_target_pairs={{0,2},{2,0},{1,3},{3,1},{4,6},{6,4},{5,7},{7,5},{8,10},{10,8},{9,1... | collective-permute-start | bytes 663560 | tf_op jit(solution)/shard_map/ppermute | solution.py:832
  28.1 20.3 %collective-permute-start.5 = (bf16[4,48,576]{2,1,0:T(8,128)(2,1)S(1)}, bf16[4,48,576]{2,1,0:T(8,128)(2,1)S(1)}, u32[]{:S(2)}, u32[]{:S(2)}) collective-permute-start(bf16[4,48,576]{2,1,0:T(8,128)(2,1)S(1)} %get-tuple-element.222), channel_id=1, source_target_pairs={{0,4},{4,0},{1,5},{5,1},{2,6},{6,2},{3,7},{7,3},{8,12},{12,8},{9,1... | collective-permute-start | bytes 663560 | tf_op jit(solution)/shard_map/ppermute | solution.py:832
  60.3 11.5 %collective-permute-start.7 = (bf16[2,4,48,576]{3,2,1,0:T(8,128)(2,1)S(1)}, bf16[2,4,48,576]{3,2,1,0:T(8,128)(2,1)S(1)}, u32[]{:S(2)}, u32[]{:S(2)}) collective-permute-start(bf16[2,4,48,576]{3,2,1,0:T(8,128)(2,1)S(1)} %pad_maximum_fusion.2), channel_id=1, source_target_pairs={{0,2},{2,0},{1,3},{3,1},{4,6},{6,4},{5,7},{7,5},{8,10},{10,8},{9,1... | collective-permute-start | bytes 1327112 | tf_op jit(solution)/shard_map/ppermute | solution.py:832
  60.3 11.2 %collective-permute-start.8 = (bf16[2,4,48,576]{3,2,1,0:T(8,128)(2,1)S(1)}, bf16[2,4,48,576]{3,2,1,0:T(8,128)(2,1)S(1)}, u32[]{:S(2)}, u32[]{:S(2)}) collective-permute-start(bf16[2,4,48,576]{3,2,1,0:T(8,128)(2,1)S(1)} %pad_maximum_fusion.3), channel_id=1, source_target_pairs={{0,4},{4,0},{1,5},{5,1},{2,6},{6,2},{3,7},{7,3},{8,12},{12,8},{9,1... | collective-permute-start | bytes 1327112 | tf_op jit(solution)/shard_map/ppermute | solution.py:832
  62.5 10.1 %collective-permute-start.11 = (bf16[4,1152]{1,0:T(4,128)(2,1)S(1)}, bf16[4,1152]{1,0:T(4,128)(2,1)S(1)}, u32[]{:S(2)}, u32[]{:S(2)}) collective-permute-start(bf16[4,1152]{1,0:T(4,128)(2,1)S(1)} %broadcast_select_fusion), channel_id=1, source_target_pairs={{0,1},{1,0},{2,3},{3,2},{4,5},{5,4},{6,7},{7,6},{8,9},{9,8},{10,11... | collective-permute-start | bytes 27656 | tf_op jit(solution)/shard_map/ppermute | solution.py:832
  71.7 7.5 %collective-permute-start.10 = (bf16[2,2,4,48,576]{4,3,2,1,0:T(8,128)(2,1)S(1)}, bf16[2,2,4,48,576]{4,3,2,1,0:T(8,128)(2,1)}, u32[]{:S(2)}, u32[]{:S(2)}) collective-permute-start(bf16[2,2,4,48,576]{4,3,2,1,0:T(8,128)(2,1)S(1)} %pad_maximum_fusion.1.refs_1_), channel_id=1, source_target_pairs={{0,1},{1,0},{2,3},{3,2},{4,5},{5,4},{6,7},{7,6},{8,9},{9,8},{10,11... | collective-permute-start | bytes 2654216 | tf_op jit(solution)/shard_map/ppermute | solution.py:832
  72.6 6.5 %copy-start.2 = (bf16[2,2,4,48,576]{4,3,2,1,0:T(8,128)(2,1)}, bf16[2,2,4,48,576]{4,3,2,1,0:T(8,128)(2,1)S(1)}, u32[]{:S(2)}) copy-start(bf16[2,2,4,48,576]{4,3,2,1,0:T(8,128)(2,1)S(1)} %pad_maximum_fusion.refs_0_) | copy-start | bytes 2654212
  72.6 6.5 %collective-permute-start.9 = (bf16[2,2,4,48,576]{4,3,2,1,0:T(8,128)(2,1)S(1)}, bf16[2,2,4,48,576]{4,3,2,1,0:T(8,128)(2,1)S(1)}, u32[]{:S(2)}, u32[]{:S(2)}) collective-permute-start(bf16[2,2,4,48,576]{4,3,2,1,0:T(8,128)(2,1)S(1)} %pad_maximum_fusion.refs_0_), channel_id=1, source_target_pairs={{0,1},{1,0},{2,3},{3,2},{4,5},{5,4},{6,7},{7,6},{8,9},{9,8},{10,11... | collective-permute-start | bytes 2654216 | tf_op jit(solution)/shard_map/ppermute | solution.py:832
  72.7 4.9 %collective-permute-start.12 = (bf16[4,1152]{1,0:T(4,128)(2,1)S(1)}, bf16[4,1152]{1,0:T(4,128)(2,1)S(1)}, u32[]{:S(2)}, u32[]{:S(2)}) collective-permute-start(bf16[4,1152]{1,0:T(4,128)(2,1)S(1)} %fusion.19), channel_id=1, source_target_pairs={{0,2},{2,0},{1,3},{3,1},{4,6},{6,4},{5,7},{7,5},{8,10},{10,8},{9,1... | collective-permute-start | bytes 27656 | tf_op jit(solution)/shard_map/ppermute | solution.py:832
  163.3 34.9 %collective-permute-start.14 = (bf16[2,4,2,96,192]{4,3,2,1,0:T(8,128)(2,1)}, bf16[2,4,2,96,192]{4,3,2,1,0:T(8,128)(2,1)}, u32[]{:S(2)}, u32[]{:S(2)}) collective-permute-start(bf16[2,4,2,96,192]{4,3,2,1,0:T(8,128)(2,1)} %get-tuple-element.136), channel_id=1, source_target_pairs={{0,1},{1,0},{2,3},{3,2},{4,5},{5,4},{6,7},{7,6},{8,9},{9,8},{10,11... | collective-permute-start | bytes 1769480 | tf_op jit(solution)/shard_map/ppermute | solution.py:832
  186.4 11.8 %collective-permute-start.13 = (bf16[4,2,96,576]{3,2,1,0:T(8,128)(2,1)}, bf16[4,2,96,576]{3,2,1,0:T(8,128)(2,1)S(1)}, u32[]{:S(2)}, u32[]{:S(2)}) collective-permute-start(bf16[4,2,96,576]{3,2,1,0:T(8,128)(2,1)} %get-tuple-element.134), channel_id=1, source_target_pairs={{0,1},{1,0},{2,3},{3,2},{4,5},{5,4},{6,7},{7,6},{8,9},{9,8},{10,11... | collective-permute-start | bytes 2654216 | tf_op jit(solution)/shard_map/ppermute | solution.py:832
  220.9 17.5 %copy-start.4 = (f32[128,256]{1,0:T(8,128)S(1)}, f32[128,256]{1,0:T(8,128)}, u32[]{:S(2)}) copy-start(f32[128,256]{1,0:T(8,128)} %get-tuple-element.157) | copy-start | bytes 393220
  220.9 17.5 %copy-start.5 = (f32[128,256]{1,0:T(8,128)S(1)}, f32[128,256]{1,0:T(8,128)}, u32[]{:S(2)}) copy-start(f32[128,256]{1,0:T(8,128)} %get-tuple-element.158) | copy-start | bytes 393220
  220.9 17.5 %copy-start.8 = (f32[8,768]{1,0:T(8,128)S(1)}, f32[8,768]{1,0:T(8,128)}, u32[]{:S(2)}) copy-start(f32[8,768]{1,0:T(8,128)} %get-tuple-element.151) | copy-start | bytes 73732
  220.9 17.5 %copy-start.7 = (f32[4,1,768]{2,1,0:T(1,128)S(1)}, f32[4,1,768]{2,1,0:T(1,128)}, u32[]{:S(2)}) copy-start(f32[4,1,768]{2,1,0:T(1,128)} %get-tuple-element.152) | copy-start | bytes 36868
  220.9 17.8 %copy-start.21 = (bf16[6,64,768]{2,1,0:T(8,128)(2,1)S(1)}, bf16[6,64,768]{2,1,0:T(8,128)(2,1)}, u32[]{:S(2)}) copy-start(bf16[6,64,768]{2,1,0:T(8,128)(2,1)} %get-tuple-element.148) | copy-start | bytes 1769476
  220.9 19.1 %copy-start.10 = (f32[2,384]{1,0:T(2,128)S(1)}, f32[2,384]{1,0:T(2,128)}, u32[]{:S(2)}) copy-start(f32[2,384]{1,0:T(2,128)} %get-tuple-element.156) | copy-start | bytes 9220
  220.9 57.8 %collective-permute-start.15 = (bf16[12,64,768]{2,1,0:T(8,128)(2,1)}, bf16[12,64,768]{2,1,0:T(8,128)(2,1)}, u32[]{:S(2)}, u32[]{:S(2)}) collective-permute-start(bf16[12,64,768]{2,1,0:T(8,128)(2,1)} %get-tuple-element.147), channel_id=1, source_target_pairs={{0,1},{1,2},{2,3},{4,5},{5,6},{6,7},{8,9},{9,10},{10,11},{12,13},{... | collective-permute-start | bytes 3538952 | tf_op jit(solution)/shard_map/ppermute | solution.py:958
  235.4 37.3 %collective-permute-start.24 = (bf16[4,2,96,576]{3,2,1,0:T(8,128)(2,1)}, bf16[4,2,96,576]{3,2,1,0:T(8,128)(2,1)}, u32[]{:S(2)}, u32[]{:S(2)}) collective-permute-start(bf16[4,2,96,576]{3,2,1,0:T(8,128)(2,1)} %get-tuple-element.163), channel_id=1, source_target_pairs={{0,1},{1,0},{2,3},{3,2},{4,5},{5,4},{6,7},{7,6},{8,9},{9,8},{10,11... | collective-permute-start | bytes 2654216 | tf_op jit(solution)/shard_map/ppermute | solution.py:832
  235.9 31.1 %collective-permute-start.22 = (bf16[4,96,576]{2,1,0:T(8,128)(2,1)}, bf16[4,96,576]{2,1,0:T(8,128)(2,1)}, u32[]{:S(2)}, u32[]{:S(2)}) collective-permute-start(bf16[4,96,576]{2,1,0:T(8,128)(2,1)} %get-tuple-element.159), channel_id=1, source_target_pairs={{0,4},{4,0},{1,5},{5,1},{2,6},{6,2},{3,7},{7,3},{8,12},{12,8},{9,1... | collective-permute-start | bytes 1327112 | tf_op jit(solution)/shard_map/ppermute | solution.py:832
  238.5 28.5 %collective-permute-start.23 = (bf16[2,4,96,192]{3,2,1,0:T(8,128)(2,1)}, bf16[2,4,96,192]{3,2,1,0:T(8,128)(2,1)}, u32[]{:S(2)}, u32[]{:S(2)}) collective-permute-start(bf16[2,4,96,192]{3,2,1,0:T(8,128)(2,1)} %get-tuple-element.160), channel_id=1, source_target_pairs={{0,4},{4,0},{1,5},{5,1},{2,6},{6,2},{3,7},{7,3},{8,12},{12,8},{9,1... | collective-permute-start | bytes 884744 | tf_op jit(solution)/shard_map/ppermute | solution.py:832
  238.8 40.0 %collective-permute-start.16 = (bf16[6,64,768]{2,1,0:T(8,128)(2,1)S(1)}, bf16[6,64,768]{2,1,0:T(8,128)(2,1)}, u32[]{:S(2)}, u32[]{:S(2)}) collective-permute-start(bf16[6,64,768]{2,1,0:T(8,128)(2,1)S(1)} %copy-done.21), channel_id=1, source_target_pairs={{1,0},{2,1},{3,2},{5,4},{6,5},{7,6},{9,8},{10,9},{11,10},{13,12},{... | collective-permute-start | bytes 1769480 | tf_op jit(solution)/shard_map/ppermute | solution.py:957
  270.7 28.5 %collective-permute-start.27 = (bf16[4,96,192]{2,1,0:T(8,128)(2,1)}, bf16[4,96,192]{2,1,0:T(8,128)(2,1)}, u32[]{:S(2)}, u32[]{:S(2)}) collective-permute-start(bf16[4,96,192]{2,1,0:T(8,128)(2,1)} %get-tuple-element.172), channel_id=1, source_target_pairs={{0,2},{2,0},{1,3},{3,1},{4,6},{6,4},{5,7},{7,5},{8,10},{10,8},{9,1... | collective-permute-start | bytes 442376 | tf_op jit(solution)/shard_map/ppermute | solution.py:832
  271.1 28.0 %collective-permute-start.26 = (bf16[4,96,576]{2,1,0:T(8,128)(2,1)}, bf16[4,96,576]{2,1,0:T(8,128)(2,1)}, u32[]{:S(2)}, u32[]{:S(2)}) collective-permute-start(bf16[4,96,576]{2,1,0:T(8,128)(2,1)} %get-tuple-element.170), channel_id=1, source_target_pairs={{0,2},{2,0},{1,3},{3,1},{4,6},{6,4},{5,7},{7,5},{8,10},{10,8},{9,1... | collective-permute-start | bytes 1327112 | tf_op jit(solution)/shard_map/ppermute | solution.py:832
  277.0 22.1 %collective-permute-start.25 = (bf16[4,96,576]{2,1,0:T(8,128)(2,1)}, bf16[4,96,576]{2,1,0:T(8,128)(2,1)}, u32[]{:S(2)}, u32[]{:S(2)}) collective-permute-start(bf16[4,96,576]{2,1,0:T(8,128)(2,1)} %get-tuple-element.165), channel_id=1, source_target_pairs={{0,4},{4,0},{1,5},{5,1},{2,6},{6,2},{3,7},{7,3},{8,12},{12,8},{9,1... | collective-permute-start | bytes 1327112 | tf_op jit(solution)/shard_map/ppermute | solution.py:832
  289.3 1.3 collective-permute-start.17
  290.6 7.1 %collective-permute-start.18 = (f32[26,512]{1,0:T(8,128)S(1)}, f32[26,512]{1,0:T(8,128)S(1)}, u32[]{:S(2)}, u32[]{:S(2)}) collective-permute-start(f32[26,512]{1,0:T(8,128)S(1)} %add.94), channel_id=1, source_target_pairs={{0,2},{2,0},{1,3},{3,1},{4,6},{6,4},{5,7},{7,5},{8,10},{10,8},{9,1... | collective-permute-start | bytes 159752 | tf_op jit(solution)/shard_map/ppermute | solution.py:832
  297.7 13.5 %collective-permute-start.19 = (f32[26,512]{1,0:T(8,128)S(1)}, f32[26,512]{1,0:T(8,128)S(1)}, u32[]{:S(2)}, u32[]{:S(2)}) collective-permute-start(f32[26,512]{1,0:T(8,128)S(1)} %add.95), channel_id=1, source_target_pairs={{0,4},{4,0},{1,5},{5,1},{2,6},{6,2},{3,7},{7,3},{8,12},{12,8},{9,1... | collective-permute-start | bytes 159752 | tf_op jit(solution)/shard_map/ppermute | solution.py:832
  303.6 9.6 %collective-permute-start.31 = (bf16[96,192]{1,0:T(8,128)(2,1)S(1)}, bf16[96,192]{1,0:T(8,128)(2,1)S(1)}, u32[]{:S(2)}, u32[]{:S(2)}) collective-permute-start(bf16[96,192]{1,0:T(8,128)(2,1)S(1)} %get-tuple-element.223), channel_id=1, source_target_pairs={{0,8},{8,16},{16,24},{24,0},{1,9},{9,17},{17,25},{25,1},{2,10},{10... | collective-permute-start | bytes 110600 | tf_op jit(solution)/shard_map/ppermute | solution.py:836
  305.8 8.1 %collective-permute-start.33 = (bf16[96,192]{1,0:T(8,128)(2,1)S(1)}, bf16[96,192]{1,0:T(8,128)(2,1)S(1)}, u32[]{:S(2)}, u32[]{:S(2)}) collective-permute-start(bf16[96,192]{1,0:T(8,128)(2,1)S(1)} %get-tuple-element.224), channel_id=1, source_target_pairs={{0,24},{8,0},{16,8},{24,16},{1,25},{9,1},{17,9},{25,17},{2,26},{10... | collective-permute-start | bytes 110600 | tf_op jit(solution)/shard_map/ppermute | solution.py:836
  307.5 12.8 %collective-permute-start.32 = (bf16[96,192]{1,0:T(8,128)(2,1)S(1)}, bf16[96,192]{1,0:T(8,128)(2,1)S(1)}, u32[]{:S(2)}, u32[]{:S(2)}) collective-permute-start(bf16[96,192]{1,0:T(8,128)(2,1)S(1)} %get-tuple-element.225), channel_id=1, source_target_pairs={{0,16},{8,24},{16,0},{24,8},{1,17},{9,25},{17,1},{25,9},{2,18},{10... | collective-permute-start | bytes 110600 | tf_op jit(solution)/shard_map/ppermute | solution.py:836
  309.3 18.3 %collective-permute-start.28 = (bf16[96,576]{1,0:T(8,128)(2,1)S(1)}, bf16[96,576]{1,0:T(8,128)(2,1)S(1)}, u32[]{:S(2)}, u32[]{:S(2)}) collective-permute-start(bf16[96,576]{1,0:T(8,128)(2,1)S(1)} %get-tuple-element.216), channel_id=1, source_target_pairs={{0,8},{8,16},{16,24},{24,0},{1,9},{9,17},{17,25},{25,1},{2,10},{10... | collective-permute-start | bytes 331784 | tf_op jit(solution)/shard_map/ppermute | solution.py:836
  311.2 16.4 %collective-permute-start.30 = (bf16[96,576]{1,0:T(8,128)(2,1)S(1)}, bf16[96,576]{1,0:T(8,128)(2,1)S(1)}, u32[]{:S(2)}, u32[]{:S(2)}) collective-permute-start(bf16[96,576]{1,0:T(8,128)(2,1)S(1)} %get-tuple-element.217), channel_id=1, source_target_pairs={{0,24},{8,0},{16,8},{24,16},{1,25},{9,1},{17,9},{25,17},{2,26},{10... | collective-permute-start | bytes 331784 | tf_op jit(solution)/shard_map/ppermute | solution.py:836
  313.2 16.5 %collective-permute-start.29 = (bf16[96,576]{1,0:T(8,128)(2,1)S(1)}, bf16[96,576]{1,0:T(8,128)(2,1)S(1)}, u32[]{:S(2)}, u32[]{:S(2)}) collective-permute-start(bf16[96,576]{1,0:T(8,128)(2,1)S(1)} %get-tuple-element.218), channel_id=1, source_target_pairs={{0,16},{8,24},{16,0},{24,8},{1,17},{9,25},{17,1},{25,9},{2,18},{10... | collective-permute-start | bytes 331784 | tf_op jit(solution)/shard_map/ppermute | solution.py:836
  313.9 9.5 %collective-permute-start.20 = (f32[26,512]{1,0:T(8,128)S(1)}, f32[26,512]{1,0:T(8,128)S(1)}, u32[]{:S(2)}, u32[]{:S(2)}) collective-permute-start(f32[26,512]{1,0:T(8,128)S(1)} %add.96), channel_id=1, source_target_pairs={{0,8},{8,0},{16,24},{24,16},{1,9},{9,1},{17,25},{25,17},{2,10},{10... | collective-permute-start | bytes 159752 | tf_op jit(solution)/shard_map/ppermute | solution.py:872
  323.4 8.3 %collective-permute-start.21 = (f32[26,512]{1,0:T(8,128)S(1)}, f32[26,512]{1,0:T(8,128)S(1)}, u32[]{:S(2)}, u32[]{:S(2)}) collective-permute-start(f32[26,512]{1,0:T(8,128)S(1)} %add.97), channel_id=1, source_target_pairs={{0,16},{8,24},{16,0},{24,8},{1,17},{9,25},{17,1},{25,9},{2,18},{10... | collective-permute-start | bytes 159752 | tf_op jit(solution)/shard_map/ppermute | solution.py:872
  (10 other events, 30.4 us)
Sparse Core Ops, SparseCore 0:
  10.9 93.9 all-gather.2
  163.4 160.0 reduce-scatter.1

commit v5 on v4

--- a/solution.py
+++ b/solution.py
@@ -97,7 +97,7 @@
     return pl.BlockSpec(shape, lambda *_: (0,) * len(shape), pipeline_mode=pl.Buffered(1))
 
 
-def windows_body(place_ref, above_ref, x_ref, below_ref, vec_ref, nw_ref, nat_ref, *, rows):
+def windows_body(place_ref, above_ref, x_ref, below_ref, vec_ref, nw_ref, turned_ref, own_ref, nat_ref, *, rows):
     band = pl.program_id(0)
     slot = place_ref[0]
     above, below = above_ref.shape[0], below_ref.shape[0]
@@ -143,6 +143,9 @@
 
             lax.fori_loop(0, EXT, one, 0)
 
+    turned_ref[...] = nw_ref[...].T
+    own_ref[...] = nw_ref[pl.ds(pl.multiple_of(slot * 2 * PITCH, 2 * PITCH), rows * PITCH), :].T
+
 
 def windows(place, above, x, below, vectors):
     rows = x.shape[0]
@@ -152,10 +155,18 @@
             num_scalar_prefetch=1,
             grid=(SIDE,),
             in_specs=[whole(above.shape), whole(x.shape), whole(below.shape), whole((8, D))],
-            out_specs=pl.BlockSpec((EXT * PITCH, D), lambda b, s: (b, 0)),
+            out_specs=[
+                pl.BlockSpec((EXT * PITCH, D), lambda b, s: (b, 0)),
+                pl.BlockSpec((None, D, EXT * PITCH), lambda b, s: (b, 0, 0)),
+                pl.BlockSpec((None, D, rows * PITCH), lambda b, s: (b, 0, 0)),
+            ],
             scratch_shapes=[pltpu.VMEM((EXT, GRID + PITCH, D), F32)],
         ),
-        out_shape=jax.ShapeDtypeStruct((SIDE * EXT * PITCH, D), BF),
+        out_shape=[
+            jax.ShapeDtypeStruct((SIDE * EXT * PITCH, D), BF),
+            jax.ShapeDtypeStruct((SIDE, D, EXT * PITCH), BF),
+            jax.ShapeDtypeStruct((SIDE, D, rows * PITCH), BF),
+        ],
         compiler_params=pltpu.CompilerParams(vmem_limit_bytes=63 << 20),
         cost_estimate=guess(8),
         name="windows",
@@ -173,18 +184,14 @@
             w_ref[...] = pieces[0][...]
             return
         half = depth // 2
-        for sibling in range(2):
-            for part in range(2):
-                ref = pieces[2 * sibling + part]
-                count = ref.shape[2]
-                for first in range(2):
-                    for second in range(2):
-                        dy, dx = (first, second) if part == 0 else (second, first)
-                        from_slot = (y ^ dy) * 2 + (c ^ sibling)
-                        for dz in range(count):
-                            group = lax.rem(z - dz + count, count) * 2 + (x ^ dx)
-                            at = pl.multiple_of(group * depth + part * half, half)
-                            stage_ref[from_slot, pl.ds(at, half), :] = ref[first, second, dz]
+        for index, ref in enumerate(pieces):
+            sibling, part, dx, dy = index // 8, index // 4 % 2, index // 2 % 2, index % 2
+            count = ref.shape[0]
+            from_slot = (y ^ dy) * 2 + (c ^ sibling)
+            for dz in range(count):
+                group = lax.rem(z - dz + count, count) * 2 + (x ^ dx)
+                at = pl.multiple_of(group * depth + part * half, half)
+                stage_ref[from_slot, pl.ds(at, half), :] = ref[dz]
 
         def join(i, carry):
             at = pl.ds(pl.multiple_of(i * 64, 64), 64)
@@ -242,23 +249,22 @@
             refs[lax.rem(first + zd - z + count, count), x ^ xd] = value[start : start + depth]
 
 
-def project_grad_body(place_ref, nw_ref, dq_ref, dk_ref, dv_ref, send_ref, keep_ref, bias_ref, *, rows, parts):
+def project_grad_body(place_ref, turned_ref, own_ref, dq_ref, dk_ref, dv_ref, send_ref, keep_ref, bias_ref, *, parts):
     step = pl.program_id(0)
-    slot, c = place_ref[0], place_ref[4]
+    c = place_ref[4]
     width = D // 4
-    lines = rows * PITCH
 
     @pl.when(step == 0)
     def _():
         bias_ref[0:1] = jnp.sum(dq_ref[...].astype(F32), 0, keepdims=True)
         bias_ref[1:2] = jnp.sum(dv_ref[...].astype(F32), 0, keepdims=True)
 
-    grad_q = None
-    for b in range(SIDE):
-        start = pl.multiple_of(b * EXT * PITCH + slot * 2 * PITCH, 2 * PITCH)
-        term = t_mm(nw_ref[pl.ds(start, lines), :], dq_ref[b * lines : (b + 1) * lines])
-        grad_q = term if grad_q is None else grad_q + term
-    grads = [grad_q.astype(BF)] + [t_mm(nw_ref[...], ref[...]).astype(BF) for ref in (dk_ref, dv_ref)]
+    def over_bands(left, right):
+        lines = left.shape[2]
+        return sum(mm(left[b], right(slice(b * lines, (b + 1) * lines))) for b in range(SIDE)).astype(BF)
+
+    both = over_bands(turned_ref, lambda at: jnp.concatenate([dk_ref[at], dv_ref[at]], 1))
+    grads = [over_bands(own_ref, lambda at: dq_ref[at]), both[:, : D // 2], both[:, D // 2 :]]
     first = step * (keep_ref.shape[0] // parts)
     for core in range(2):
         value = jnp.concatenate([g[:, core * width : (core + 1) * width] for g in grads], 1)
@@ -268,17 +274,18 @@
                 store_shards(place_ref, ref, value, first)
 
 
-def project_grad(place, normed, dq, dk, dv, rows, shards):
+def project_grad(place, turned, own, dq, dk, dv, shards):
     count, depth = shards[1], shards[3]
     parts = 2 if depth % 32 == 0 else 1
     out = jax.ShapeDtypeStruct((count, 2, depth, 3 * D // 4), BF)
     return pl.pallas_call(
-        partial(project_grad_body, rows=rows, parts=parts),
+        partial(project_grad_body, parts=parts),
         grid_spec=pltpu.PrefetchScalarGridSpec(
             num_scalar_prefetch=1,
             grid=(parts,),
             in_specs=[
-                pl.BlockSpec((normed.shape[0], D // parts), lambda i, s: (0, i)),
+                pl.BlockSpec((SIDE, D // parts, turned.shape[2]), lambda i, s: (0, i, 0)),
+                pl.BlockSpec((SIDE, D // parts, own.shape[2]), lambda i, s: (0, i, 0)),
                 whole(dq.shape), whole(dk.shape), whole(dv.shape),
             ],
             out_specs=[whole(out.shape), whole(out.shape), whole((2, D // 2))],
@@ -287,68 +294,54 @@
         compiler_params=pltpu.CompilerParams(vmem_limit_bytes=63 << 20),
         cost_estimate=guess(6),
         name="project_grad",
-    )(place, normed, dq, dk, dv)
+    )(place, turned, own, dq, dk, dv)
 
 
 def project_back_body(place_ref, *refs, rows):
     dqs, dks, dvs = refs[0:2], refs[2:4], refs[4:6]
-    w_ref, above_ref, own_ref, below_ref, nat_ref, dq_ref, dk_ref, dv_ref = refs[6:]
-    band = pl.program_id(0)
+    w_ref, above_ref, own_ref, below_ref, all_ref, dq_ref, dk_ref, dv_ref = refs[6:]
     slot, y = place_ref[0], place_ref[5]
     above, below = above_ref.shape[0], below_ref.shape[0]
-
-    @pl.when(band == 0)
-    def _():
-        nat_ref[...] = jnp.zeros_like(nat_ref)
-
     for halves, ref in ((dqs, dq_ref), (dks, dk_ref), (dvs, dv_ref)):
         for i in range(2):
             at = pl.multiple_of((y ^ (1 - i)) * (D // 2), D // 2)
             ref[:, pl.ds(at, D // 2)] = halves[i][...]
     grad = mm_t(dk_ref[...], w_ref[:, D : 2 * D]) + mm_t(dv_ref[...], w_ref[:, 2 * D :])
-    grad = grad.reshape(EXT, PITCH, D)
     direct = mm_t(dq_ref[...], w_ref[:, 0:D]).reshape(rows, PITCH, D)
-    base = above - 2 * slot
-    for b in range(SIDE):
-        @pl.when(band == b)
-        def _(b=b):
-            at = slice(WIN * b, WIN * b + PITCH)
-            nat_ref[pl.ds(base, EXT), at, :] = grad
-            nat_ref[above : above + rows, at, :] += direct
-
-    @pl.when(band == SIDE - 1)
-    def _():
-        above_ref[...] = nat_ref[0:above, 0:GRID, :].astype(BF)
-        own_ref[...] = nat_ref[above : above + rows, 0:GRID, :]
-        below_ref[...] = nat_ref[above + rows :, 0:GRID, :].astype(BF)
-
-
-def project_back(place, dqs, dks, dvs, weight, rows, slots):
-    above, below = 2 * (slots - 1), WIN - 2
+    all_ref[0:above] = jnp.zeros((above, PITCH, D), F32)
+    all_ref[above + rows :] = jnp.zeros((below, PITCH, D), F32)
+    all_ref[pl.ds(above - 2 * slot, EXT)] = grad.reshape(EXT, PITCH, D)
+    above_ref[...] = all_ref[0:above].astype(BF)
+    own_ref[...] = all_ref[above : above + rows] + direct
+    below_ref[...] = all_ref[above + rows :].astype(BF)
+
+
+def project_back(place, dqs, dks, dvs, weight, rows):
+    above, below = 8, WIN - 2
     of_k = pl.BlockSpec((EXT * PITCH, D // 2), lambda b, s: (b, 0))
     of_q = pl.BlockSpec((rows * PITCH, D // 2), lambda b, s: (b, 0))
-    shapes = [
-        jax.ShapeDtypeStruct((above, GRID, D), BF),
-        jax.ShapeDtypeStruct((rows, GRID, D), F32),
-        jax.ShapeDtypeStruct((below, GRID, D), BF),
-    ]
+    part = lambda n: pl.BlockSpec((None, n, PITCH, D), lambda b, s: (b, 0, 0, 0))
     return pl.pallas_call(
         partial(project_back_body, rows=rows),
         grid_spec=pltpu.PrefetchScalarGridSpec(
             num_scalar_prefetch=1,
             grid=(SIDE,),
             in_specs=[of_q, of_q, of_k, of_k, of_k, of_k, whole((D, 3 * D))],
-            out_specs=[whole(s.shape) for s in shapes],
+            out_specs=[part(above), part(rows), part(below)],
             scratch_shapes=[
-                pltpu.VMEM((above + rows + below, GRID + PITCH, D), F32),
+                pltpu.VMEM((above + rows + below, PITCH, D), F32),
                 pltpu.VMEM((rows * PITCH, D), BF),
                 pltpu.VMEM((EXT * PITCH, D), BF),
                 pltpu.VMEM((EXT * PITCH, D), BF),
             ],
         ),
-        out_shape=shapes,
+        out_shape=[
+            jax.ShapeDtypeStruct((SIDE, above, PITCH, D), BF),
+            jax.ShapeDtypeStruct((SIDE, rows, PITCH, D), F32),
+            jax.ShapeDtypeStruct((SIDE, below, PITCH, D), BF),
+        ],
         compiler_params=pltpu.CompilerParams(vmem_limit_bytes=63 << 20),
-        cost_estimate=guess(14),
+        cost_estimate=guess(10),
         name="project_back",
     )(place, *dqs, *dks, *dvs, weight)
 
@@ -615,7 +608,7 @@
             dn_ref[at, :] = jnp.zeros((256, D), F32)
             return carry
 
-        lax.fori_loop(0, steps, one, 0)
+        lax.fori_loop(0, steps, one, 0, unroll=2)
 
     pltpu.make_async_copy(up_ref.at[buffer], up_ref.at[buffer], sems.at[buffer, 0]).wait()
     pltpu.make_async_copy(down_ref.at[buffer], down_ref.at[buffer], sems.at[buffer, 1]).wait()
@@ -677,7 +670,7 @@
                 do_ref[b, pl.ds(i * lines, lines)] = jnp.where(keep, piece, 0.0).astype(BF)
             return carry
 
-        lax.fori_loop(0, steps, three, 0)
+        lax.fori_loop(0, steps, three, 0, unroll=2)
         grad_wo = t_mm(n2_ref[...], onat_ref[...]).astype(BF)
         for sibling, ref in ((1, gas_ref), (0, gak_ref)):
             for t in range(4):
@@ -741,39 +734,47 @@
     )(place, o, x, g, vectors, up_bias, rest)
 
 
-def finish_body(own_ref, head_ref, tail_ref, x_ref, dh_ref, vec_ref, out_ref, sum_ref):
-    rows, below, above = own_ref.shape[0], head_ref.shape[0], tail_ref.shape[0]
-    sum_ref[...] = jnp.zeros_like(sum_ref)
-
-    def line(i, low, high):
-        grad = own_ref[i]
-        if low:
-            grad = grad + head_ref[i].astype(F32)
-        if high:
-            grad = grad + tail_ref[i - (rows - above)].astype(F32)
+def finish_body(own_ref, head_ref, tail_ref, x_ref, dh_ref, vec_ref, out_ref, sum_ref, nat_ref, *, heads, tails):
+    step = pl.program_id(0)
+
+    @pl.when(step == 0)
+    def _():
+        sum_ref[...] = jnp.zeros_like(sum_ref)
+
+    has_head = step < heads
+    has_tail = step >= pl.num_programs(0) - tails
+    for i in range(own_ref.shape[1]):
+        for b in range(SIDE):
+            grad = own_ref[b, i] + jnp.where(has_head, head_ref[b, i].astype(F32), 0.0)
+            grad = grad + jnp.where(has_tail, tail_ref[b, i].astype(F32), 0.0)
+            nat_ref[i, WIN * b : WIN * b + PITCH, :] = grad
+        grad = nat_ref[i, 0:GRID, :]
         hat, inverse = norm_parts(x_ref[i].astype(F32))
         out_ref[i] = (dh_ref[i] + norm_back(grad, hat, inverse, vec_ref[0:1])).astype(BF)
         sum_ref[0:1] += jnp.sum(grad * hat, 0, keepdims=True)
         sum_ref[1:2] += jnp.sum(grad, 0, keepdims=True)
 
-    def over(start, stop, low, high):
-        lax.fori_loop(start, stop, lambda i, carry: (line(i, low, high), carry)[1], 0)
-
-    over(0, rows - above, True, False)
-    over(rows - above, below, True, True)
-    over(below, rows, False, True)
-
 
 def finish(own, head, tail, x, dh, vectors):
-    shapes = [jax.ShapeDtypeStruct(own.shape, BF), jax.ShapeDtypeStruct((8, D), F32)]
+    rows, lines = own.shape[1], 4
+    heads, tails = head.shape[1] // lines, tail.shape[1] // lines
+    steps = rows // lines
+    banded = lambda index: pl.BlockSpec((SIDE, lines, PITCH, D), lambda i: (0, index(i), 0, 0))
+    plain = pl.BlockSpec((lines, GRID, D), lambda i: (i, 0, 0))
     return pl.pallas_call(
-        finish_body,
-        grid=(1,),
-        in_specs=[whole(v.shape) for v in (own, head, tail, x, dh, vectors)],
-        out_specs=[whole(v.shape) for v in shapes],
-        out_shape=shapes,
+        partial(finish_body, heads=heads, tails=tails),
+        grid=(steps,),
+        in_specs=[
+            banded(lambda i: i),
+            banded(lambda i: jnp.minimum(i, heads - 1)),
+            banded(lambda i: jnp.maximum(i - (steps - tails), 0)),
+            plain, plain, whole(vectors.shape),
+        ],
+        out_specs=[plain, whole((8, D))],
+        out_shape=[jax.ShapeDtypeStruct((rows, GRID, D), BF), jax.ShapeDtypeStruct((8, D), F32)],
+        scratch_shapes=[pltpu.VMEM((lines, GRID + PITCH, D), F32)],
         compiler_params=pltpu.CompilerParams(vmem_limit_bytes=63 << 20),
-        cost_estimate=guess(5),
+        cost_estimate=guess(6),
         name="finish",
     )(own, head, tail, x, dh, vectors)
 
@@ -836,18 +837,16 @@
     return lax.ppermute(value, "z", [(i, (i + by) % count) for i in range(count)])
 
 
-def gather_lines(shard, count):
+def spread_plane(shard, count):
     half = shard.shape[0] // 2
     lines = [shard] + [shift(shard, count, k) for k in range(1, count)]
     first = jnp.stack([line[:half] for line in lines])
     second = jnp.stack([line[half:] for line in lines])
-    return jnp.stack([first, swap(first, "x")]), jnp.stack([second, swap(second, "y")])
-
-
-def gather_planes(first, second):
-    first = jnp.stack([first, swap(first, "y")])
-    second = jnp.stack([second, swap(second, "x")])
-    return first, second, swap(first, "c"), swap(second, "c")
+    first_x, second_y = swap(first, "x"), swap(second, "y")
+    return [
+        first, swap(first, "y"), first_x, swap(first_x, "y"),
+        second, second_y, swap(second, "x"), swap(second_y, "x"),
+    ]
 
 
 def after(value, *others):
@@ -909,11 +908,11 @@
     up_bias_all = biases[:, 2 * width :].reshape(slots, 1, hidden)
 
     vec_one = jnp.concatenate([first_gain[None], first_shift[None], jnp.zeros((6, D), BF)], 0).astype(F32)
-    normed = windows(place, from_above, grid_x, from_below, vec_one)
+    normed, turned, turned_own = windows(place, from_above, grid_x, from_below, vec_one)
     if fast:
-        lines = gather_lines(qkv_weight.reshape(depth, 3 * width), count)
-        normed, *lines = lax.optimization_barrier((normed, *lines))
-        pieces = gather_planes(*lines)
+        pieces = spread_plane(qkv_weight.reshape(depth, 3 * width), count)
+        normed, pieces[3], pieces[7] = after(normed, pieces[3], pieces[7])
+        pieces += [swap(piece, "c") for piece in pieces]
     else:
         full = lax.all_gather(qkv_weight, AXES, axis=0).reshape(2 * count, slots, depth, 3, width)
         pieces = [full.transpose(0, 2, 3, 1, 4).reshape(D, 3 * D)]
@@ -940,7 +939,7 @@
     if fast:
         out_got = swap(out_send, "c")
     *half0, drel0 = attend_back(place, q, k, v, probs, grad_windows, rel_back, table, rows, 0)
-    first_send, first_keep, first_bias = project_grad(place, normed, *half0, rows, shards)
+    first_send, first_keep, first_bias = project_grad(place, turned, turned_own, *half0, shards)
     if fast:
         first_got = swap(first_send, "c")
     *half1, drel1 = attend_back(place, q, k, v, probs, grad_windows, rel_back, table, rows, 1)
@@ -952,25 +951,27 @@
         place, first_away, out_away = after(place, first_away, out_away)
         first_got, out_got = swap(first_away, "x"), swap(out_away, "x")
     dqs, dks, dvs = zip(half0, half1)
-    to_above, total, to_below = project_back(place, dqs, dks, dvs, weight, rows, slots)
+    to_above, total, to_below = project_back(place, dqs, dks, dvs, weight, rows)
     place, to_above, to_below = after(place, to_above, to_below)
     from_below = lax.ppermute(to_above, pair, down_pairs)
     from_above = lax.ppermute(to_below, pair, up_pairs)
-    last_send, last_keep, last_bias = project_grad(place, normed, *half1, rows, shards)
+    last_send, last_keep, last_bias = project_grad(place, turned, turned_own, *half1, shards)
     if fast:
         last_got = swap(last_send, "c")
-        first_got, out_got, last_keep = after(first_got, out_got, last_keep)
-        crossing, out_away, out_here = fold(
-            ([first_here, first_got], 0, None, None), ([out_here, out_got], 1, 0, 1), ([out_here, out_got], 1, 0, 0)
-        )
-        crossing, out_got = swap(crossing, "y"), swap(out_away, "y")
     grad_features, sums_one = finish(
         total, from_above, from_below, grid_x, grad_hidden.reshape(rows, GRID, D), vec_one
     )
     if fast:
+        sums_one, last_got = after(sums_one, last_got)
         last = [last_keep, last_got]
         away, here = fold((last, 0, 1, 1), (last, 0, 1, 0))
-        last, out = fold(([here, swap(away, "x"), crossing], 0, None, None), ([out_here, out_got], 0, None, None))
+        got = swap(away, "x")
+        crossing, out_away, out_here = fold(
+            ([first_here, first_got], 0, None, None), ([out_here, out_got], 1, 0, 1), ([out_here, out_got], 1, 0, 0)
+        )
+        crossing, out_away, sums_one = after(crossing, out_away, sums_one)
+        crossing, out_got = swap(crossing, "y"), swap(out_away, "y")
+        last, out = fold(([here, got, crossing], 0, None, None), ([out_here, out_got], 0, None, None))
         grad_qkv, grad_wo = along_z(last), along_z(out)
     else:
         pairs = [

time: 344 us -> 336 us (0.977)
  waiting for transfers between devices: 69.5 us -> 64.3 us
  Pallas kernels: 183 us -> 178 us
  starting transfers between devices: 45.6 us -> 49.6 us
    ppermute x9, waiting for transfers between devices: 10 us -> 5.28 us  [shift(): lax.ppermute(value, 'z', [(i, (i + by) % count) for i in range(count)])]
    ppermute x19 -> x27, waiting for transfers between devices: 57.8 us -> 53.5 us  [swap(): return lax.ppermute(value, axis, SWAP)]
    ppermute x2, waiting for transfers between devices: 1.63 us -> 5.49 us  [sum_all(): lax.ppermute(value, 'z', [(i, i ^ step) for i in range(count)])]
    ppermute x19 -> x27, starting transfers between devices: 16.8 us -> 18.2 us  [swap(): return lax.ppermute(value, axis, SWAP)]
  transfers between devices with their start and end apart: 36 -> 44, of which waited for: 9 -> 17; matrix products, arithmetic and copies ran while one was open for 7% -> 7% of each run, Pallas kernels for 39% -> 39%
where the time goes in v5:
time: 336 us; the launch traced here: 334 us
  Pallas kernels  178 us (53%)
  waiting for transfers between devices  64.3 us (19%)
  starting transfers between devices  49.6 us (15%)
  local copies, waits for them, and re-layouts  19.3 us (6%)
  between operations  14.7 us (4%)
  other arithmetic  8.15 us (2%)
    ppermute x27, waiting for transfers between devices, swap(): return lax.ppermute(value, axis, SWAP)  53.5 us
    pallas_call x1, Pallas kernels, feed(): pl.pallas_call(partial(feed_body, rows=rows), grid_spec=pltpu.PrefetchSca...  49 us
    pallas_call x2, Pallas kernels, attend_back(): pl.pallas_call(partial(attend_back_body, rows=rows), grid_spec=pltpu.Pref...  23 us
    pallas_call x2, Pallas kernels, project_grad(): pl.pallas_call(partial(project_grad_body, parts=parts), grid_spec=pltpu.P...  21.7 us
    pallas_call x1, Pallas kernels, attend(): pl.pallas_call(partial(attend_body, rows=rows), grid_spec=pltpu.PrefetchS...  18.9 us
    ppermute x27, starting transfers between devices, swap(): return lax.ppermute(value, axis, SWAP)  18.2 us
    pallas_call x4, Pallas kernels, fold(): pl.pallas_call(partial(fold_body, plan=plan), grid=(count,), in_specs=in_...  16.6 us
    ppermute x9, starting transfers between devices, shift(): lax.ppermute(value, 'z', [(i, (i + by) % count) for i in range(count)])  16.2 us
  transfers between devices with their start and end apart: 44, of which 17 were waited for; matrix products, arithmetic and copies ran while one was open for 7% of the time, Pallas kernels for 39%

profile of v5, /device:TPU:0, one launch (start us, length us, event | category | flops | bytes accessed | tf_op | source)
XLA Modules:
  0.0 334.1 jit_solution(14087023326431579284)
XLA Ops:
  7.3 1.9 concatenate.68
  11.1 5.0 %collective-permute-start.4 = (bf16[96,576]{1,0:T(8,128)(2,1)}, bf16[96,576]{1,0:T(8,128)(2,1)}, u32[]{:S(2)}, u32[]{:S(2)}) collective-permute-start(bf16[96,576]{1,0:T(8,128)(2,1)} %copy.43), channel_id=1, source_target_pairs={{0,24},{8,0},{16,8},{24,16},{1,25},{9,1},{17,9},{25,17},{2,26},{10... | collective-permute-start | bytes 331784 | tf_op jit(solution)/shard_map/ppermute | solution.py:837
  18.9 3.2 collective-permute-start
  24.0 1.3 collective-permute-start.1
  26.1 1.2 collective-permute-done.3
  29.2 1.9 collective-permute-start.5
  31.8 2.1 collective-permute-start.7
  37.0 1.7 collective-permute-start.6
  38.7 18.8 %collective-permute-done.7.refs_5_ = bf16[4,48,576]{2,1,0:T(8,128)(2,1)S(1)} collective-permute-done((bf16[4,48,576]{2,1,0:T(8,128)(2,1)}, bf16[4,48,576]{2,1,0:T(8,128)(2,1)S(1)}, u32[]{:S(2)}, u32[]{:S(2)}) %collective-permute-start.7) | collective-permute-done | bytes 221216 | tf_op jit(solution)/shard_map/ppermute | solution.py:833
  57.5 1.5 collective-permute-start.8
  59.1 1.2 collective-permute-done.9.refs_1_
  60.3 2.5 collective-permute-done.6.refs_3_
  63.7 1.6 collective-permute-start.10
  65.5 13.9 %windows.1 = (bf16[2240,768]{1,0:T(8,128)(2,1)}, bf16[5,768,448]{2,1,0:T(8,128)(2,1)}, bf16[5,768,256]{2,1,0:T(8,128)(2,1)}) custom-call(s32[6]{0:T(128)} %stack.54.place_ref, bf16[6,64,768]{2,1,0:T(8,128)(2,1)} %collective-permute-done.above_ref, bf16[16,64,768]{2,1,0:T(8,128)(2,1)} %bitcast.62, bf16[12,64,768]{2,1,0:T(8,128)(2,1)} %collective-permute-done.1.below_ref, ...), custom_call_target="tpu_custom_call" | custom-call | flops 8800000000 | bytes 24000000 | tf_op jit(solution)/shard_map/windows/pallas_call | solution.py:152
  83.8 13.8 %project.1 = (bf16[1280,768]{1,0:T(8,128)(2,1)}, bf16[2240,768]{1,0:T(8,128)(2,1)}, bf16[2240,768]{1,0:T(8,128)(2,1)}, bf16[768,2304]{1,0:T(8,128)(2,1)}) custom-call(s32[6]{0:T(128)} %stack.54.place_ref, bf16[2240,768]{1,0:T(8,128)(2,1)} %get-tuple-element.126.nw_ref, bf16[4,48,576]{2,1,0:T(8,128)(2,1)} %copy-done.2, ...), custom_call_target="tpu_custom_call" | custom-call | flops 19800000512 | bytes 54000000 | tf_op jit(solution)/shard_map/project/pallas_call | solution.py:221
  97.6 18.9 %attend.1 = (bf16[1280,768]{1,0:T(8,128)(2,1)}, bf16[30,2,224,256]{3,2,1,0:T(8,128)(2,1)}) custom-call(s32[6]{0:T(128)} %stack.54.place_ref, bf16[1280,768]{1,0:T(8,128)(2,1)} %get-tuple-element.129.q_ref, bf16[2240,768]{1,0:T(8,128)(2,1)} %get-tuple-element.130.k_ref, bf16[2240,768]{1,0:T(8,128)(2,1)} %get-tuple-element.131.v_ref, ...), custom_call_target="tpu_custom_call" | custom-call | flops 26400000000 | bytes 72000000 | tf_op jit(solution)/shard_map/attend/pallas_call | solution.py:421
  116.5 49.0 %feed.1 = (bf16[1024,768]{1,0:T(8,128)(2,1)}, f32[1024,768]{1,0:T(8,128)}, bf16[5,16,16,768]{3,2,1,0:T(8,128)(2,1)}, bf16[8,4,96,1536]{3,2,1,0:T(8,128)(2,1)}, b...) custom-call(s32[6]{0:T(128)} %stack.54.place_ref, ...), custom_call_target="tpu_custom_call" | custom-call | flops 54999998464 | bytes 150000000 | tf_op jit(solution)/shard_map/feed/pallas_call | solution.py:702
  165.9 11.4 %attend_back.2 = (bf16[1280,384]{1,0:T(8,128)(2,1)}, bf16[2240,384]{1,0:T(8,128)(2,1)}, bf16[2240,384]{1,0:T(8,128)(2,1)}, f32[128,256]{1,0:T(8,128)}) custom-call(s32[6]{0:T(128)} %stack.54.place_ref, bf16[1280,768]{1,0:T(8,128)(2,1)} %get-tuple-element.129.q_ref, bf16[2240,768]{1,0:T(8,128)(2,1)} %get-tuple-element.130.k_ref, ...), custom_call_target="tpu_custom_call" | custom-call | flops 17600000000 | bytes 48000000 | tf_op jit(solution)/shard_map/attend_back/pallas_call | solution.py:535
  177.3 10.9 %project_grad.2 = (bf16[4,2,96,576]{3,2,1,0:T(8,128)(2,1)}, bf16[4,2,96,576]{3,2,1,0:T(8,128)(2,1)}, f32[2,384]{1,0:T(2,128)}) custom-call(s32[6]{0:T(128)} %stack.54.place_ref, bf16[5,768,448]{2,1,0:T(8,128)(2,1)} %get-tuple-element.134.turned_ref, bf16[5,768,256]{2,1,0:T(8,128)(2,1)} %get-tuple-element.135.own_ref, ...), custom_call_target="tpu_custom_call" | custom-call | flops 6600000000 | bytes 18000000 | tf_op jit(solution)/shard_map/project_grad/pallas_call | solution.py:281
  188.4 11.5 %attend_back.3 = (bf16[1280,384]{1,0:T(8,128)(2,1)}, bf16[2240,384]{1,0:T(8,128)(2,1)}, bf16[2240,384]{1,0:T(8,128)(2,1)}, f32[128,256]{1,0:T(8,128)}) custom-call(s32[6]{0:T(128)} %stack.54.place_ref, bf16[1280,768]{1,0:T(8,128)(2,1)} %get-tuple-element.129.q_ref, bf16[2240,768]{1,0:T(8,128)(2,1)} %get-tuple-element.130.k_ref, ...), custom_call_target="tpu_custom_call" | custom-call | flops 17600000000 | bytes 48000000 | tf_op jit(solution)/shard_map/attend_back/pallas_call | solution.py:535
  200.0 5.3 %fold.4 = (bf16[4,96,576]{2,1,0:T(8,128)(2,1)}, bf16[4,96,576]{2,1,0:T(8,128)(2,1)}, bf16[2,4,96,192]{3,2,1,0:T(8,128)(2,1)}, bf16[2,4,96,192]{3,2,1,0:T(8,128)(2,1)}) custom-call(bf16[4,2,96,576]{3,2,1,0:T(8,128)(2,1)} %get-tuple-element.141.refs_0_.refs_2_, bf16[4,2,96,576]{3,2,1,0:T(8,128)(2,1)} %collective-permute-done.21.refs_1_.refs_3_, ...), custom_call_target="tpu_custom_call" | custom-call | flops 4344032256 | bytes 11847360 | tf_op jit(solution)/shard_map/fold/pallas_call | solution.py:816
  205.3 13.9 %project_back.1 = (bf16[5,8,16,768]{3,2,1,0:T(8,128)(2,1)}, f32[5,16,16,768]{3,2,1,0:T(8,128)}, bf16[5,12,16,768]{3,2,1,0:T(8,128)(2,1)}) custom-call(s32[6]{0:T(128)} %stack.54.place_ref, bf16[1280,384]{1,0:T(8,128)(2,1)} %get-tuple-element.138.dq_ref.refs_0_, bf16[1280,384]{1,0:T(8,128)(2,1)} %get-tuple-element.148.refs_1_.dq_ref, ...), custom_call_target="tpu_custom_call" | custom-call | flops 11000000512 | bytes 30000000 | tf_op jit(solution)/shard_map/project_back/pallas_call | solution.py:324
  219.2 3.3 collective-permute-start.23
  222.6 1.3 collective-permute-start.24
  224.7 1.5 collective-permute-start.25
  226.2 10.8 %project_grad.3 = (bf16[4,2,96,576]{3,2,1,0:T(8,128)(2,1)}, bf16[4,2,96,576]{3,2,1,0:T(8,128)(2,1)}, f32[2,384]{1,0:T(2,128)}) custom-call(s32[6]{0:T(128)} %stack.54.place_ref, bf16[5,768,448]{2,1,0:T(8,128)(2,1)} %get-tuple-element.134.turned_ref, bf16[5,768,256]{2,1,0:T(8,128)(2,1)} %get-tuple-element.135.own_ref, ...), custom_call_target="tpu_custom_call" | custom-call | flops 6600000000 | bytes 18000000 | tf_op jit(solution)/shard_map/project_grad/pallas_call | solution.py:281
  238.4 12.8 %collective-permute-done.25.refs_1_ = bf16[4,96,576]{2,1,0:T(8,128)(2,1)} collective-permute-done((bf16[4,96,576]{2,1,0:T(8,128)(2,1)}, bf16[4,96,576]{2,1,0:T(8,128)(2,1)}, u32[]{:S(2)}, u32[]{:S(2)}) %collective-permute-start.25) | collective-permute-done | bytes 442400 | tf_op jit(solution)/shard_map/ppermute | solution.py:833
  251.1 3.7 %fold.5 = (bf16[4,96,576]{2,1,0:T(8,128)(2,1)}, bf16[4,96,192]{2,1,0:T(8,128)(2,1)}, bf16[4,96,192]{2,1,0:T(8,128)(2,1)}) custom-call(bf16[4,96,576]{2,1,0:T(8,128)(2,1)} %get-tuple-element.161.refs_0_, bf16[4,96,576]{2,1,0:T(8,128)(2,1)} %collective-permute-done.25.refs_1_, bf16[2,4,96,192]{3,2,1,0:T(8,128)(2,1)} %get-tuple-element.163.refs_2_.refs_4_, ...), custom_call_target="tpu_custom_call" | custom-call | flops 2235411200 | bytes 6096576 | tf_op jit(solution)/shard_map/fold/pallas_call | solution.py:816
  254.9 7.4 %finish.1 = (bf16[16,64,768]{2,1,0:T(8,128)(2,1)}, f32[8,768]{1,0:T(8,128)}) custom-call(f32[5,16,16,768]{3,2,1,0:T(8,128)} %get-tuple-element.152.own_ref, bf16[5,12,16,768]{3,2,1,0:T(8,128)(2,1)} %collective-permute-done.23.head_ref, bf16[5,8,16,768]{3,2,1,0:T(8,128)(2,1)} %collective-permute-done.24.tail_ref, bf16[16,64,768]{2,1,0:T(8,128)(2,1)} %bitcast.63, ...), custom_call_target="tpu_custom_call" | custom-call | flops 6600000000 | bytes 18000000 | tf_op jit(solution)/shard_map/finish/pallas_call | solution.py:764
  264.6 1.7 collective-permute-start.29
  266.3 3.1 collective-permute-done.29
  269.7 5.5 %collective-permute-done.30 = f32[26,512]{1,0:T(8,128)S(1)} collective-permute-done((f32[26,512]{1,0:T(8,128)S(1)}, f32[26,512]{1,0:T(8,128)S(1)}, u32[]{:S(2)}, u32[]{:S(2)}) %collective-permute-start.30) | collective-permute-done | bytes 53280 | tf_op jit(solution)/shard_map/ppermute | solution.py:833
  275.1 5.9 %collective-permute-start.31 = (f32[26,512]{1,0:T(8,128)S(1)}, f32[26,512]{1,0:T(8,128)S(1)}, u32[]{:S(2)}, u32[]{:S(2)}) collective-permute-start(f32[26,512]{1,0:T(8,128)S(1)} %add.96), channel_id=1, source_target_pairs={{0,8},{8,0},{16,24},{24,16},{1,9},{9,1},{17,25},{25,17},{2,10},{10... | collective-permute-start | bytes 159752 | tf_op jit(solution)/shard_map/ppermute | solution.py:871
  281.2 1.9 collective-permute-start.34
  283.1 3.7 %collective-permute-done.31 = f32[26,512]{1,0:T(8,128)S(1)} collective-permute-done((f32[26,512]{1,0:T(8,128)S(1)}, f32[26,512]{1,0:T(8,128)S(1)}, u32[]{:S(2)}, u32[]{:S(2)}) %collective-permute-start.31) | collective-permute-done | bytes 53280 | tf_op jit(solution)/shard_map/ppermute | solution.py:871
  286.9 4.1 %fold.6 = (bf16[4,96,576]{2,1,0:T(8,128)(2,1)}, bf16[4,96,576]{2,1,0:T(8,128)(2,1)}) custom-call(bf16[4,2,96,576]{3,2,1,0:T(8,128)(2,1)} %get-tuple-element.176.refs_0_.refs_2_, bf16[4,2,96,576]{3,2,1,0:T(8,128)(2,1)} %collective-permute-done.27.refs_1_.refs_3_, bf16[4,2,96,576]{3,2,1,0:T(8,128)(2,1)} %get-tuple-element.176.refs_0_.refs_2_, ...), custom_call_target="tpu_custom_call" | custom-call | flops 3046419200 | bytes 8308416 | tf_op jit(solution)/shard_map/fold/pallas_call | solution.py:816
  291.0 1.7 collective-permute-done.32
  294.9 2.2 collective-permute-done.34.refs_2_
  297.1 5.2 %collective-permute-done.33.refs_1_ = bf16[4,96,576]{2,1,0:T(8,128)(2,1)} collective-permute-done((bf16[4,96,576]{2,1,0:T(8,128)(2,1)}, bf16[4,96,576]{2,1,0:T(8,128)(2,1)}, u32[]{:S(2)}, u32[]{:S(2)}) %collective-permute-start.33) | collective-permute-done | bytes 442400 | tf_op jit(solution)/shard_map/ppermute | solution.py:833
  302.3 3.6 %fold.7 = (bf16[4,96,576]{2,1,0:T(8,128)(2,1)}, bf16[4,96,192]{2,1,0:T(8,128)(2,1)}) custom-call(bf16[4,96,576]{2,1,0:T(8,128)(2,1)} %get-tuple-element.178.refs_0_, bf16[4,96,576]{2,1,0:T(8,128)(2,1)} %collective-permute-done.33.refs_1_, bf16[4,96,576]{2,1,0:T(8,128)(2,1)} %collective-permute-done.34.refs_2_, ...), custom_call_target="tpu_custom_call" | custom-call | flops 1992108800 | bytes 5433024 | tf_op jit(solution)/shard_map/fold/pallas_call | solution.py:816
  306.7 2.1 collective-permute-start.39
  308.8 2.1 collective-permute-start.41
  312.7 1.9 collective-permute-start.36
  314.6 2.0 collective-permute-start.38
  316.6 1.3 collective-permute-start.37
  317.9 1.5 fusion.11
  319.6 1.2 collective-permute-done.38
  320.8 2.6 collective-permute-done.37
  (206 shorter events, 32.8 us)
Async XLA Ops:
  7.2 109.3 %all-gather.3.cloned.1.call-start = ((), (), s32[]{:S(2)}) async-start(), calls=%async_computation.2 | async-start | bytes 11354112 | tf_op jit(solution)/shard_map/all_gather | solution.py:902
  9.2 316.2 %reduce-scatter.2.cloned.1.call-start = ((), (), s32[]{:S(2)}) async-start(), calls=%async_computation.1 | async-start | bytes 9732096 | tf_op jit(solution)/shard_map/reduce_scatter | solution.py:935
  11.1 12.8 %collective-permute-start.4 = (bf16[96,576]{1,0:T(8,128)(2,1)}, bf16[96,576]{1,0:T(8,128)(2,1)}, u32[]{:S(2)}, u32[]{:S(2)}) collective-permute-start(bf16[96,576]{1,0:T(8,128)(2,1)} %copy.43), channel_id=1, source_target_pairs={{0,24},{8,0},{16,8},{24,16},{1,25},{9,1},{17,9},{25,17},{2,26},{10... | collective-permute-start | bytes 331784 | tf_op jit(solution)/shard_map/ppermute | solution.py:837
  16.2 11.2 %collective-permute-start.3 = (bf16[96,576]{1,0:T(8,128)(2,1)}, bf16[96,576]{1,0:T(8,128)(2,1)}, u32[]{:S(2)}, u32[]{:S(2)}) collective-permute-start(bf16[96,576]{1,0:T(8,128)(2,1)} %copy.43), channel_id=1, source_target_pairs={{0,16},{8,24},{16,0},{24,8},{1,17},{9,25},{17,1},{25,9},{2,18},{10... | collective-permute-start | bytes 331784 | tf_op jit(solution)/shard_map/ppermute | solution.py:837
  16.2 12.0 %collective-permute-start.2 = (bf16[96,576]{1,0:T(8,128)(2,1)}, bf16[96,576]{1,0:T(8,128)(2,1)}, u32[]{:S(2)}, u32[]{:S(2)}) collective-permute-start(bf16[96,576]{1,0:T(8,128)(2,1)} %copy.43), channel_id=1, source_target_pairs={{0,8},{8,16},{16,24},{24,0},{1,9},{9,17},{17,25},{25,1},{2,10},{10... | collective-permute-start | bytes 331784 | tf_op jit(solution)/shard_map/ppermute | solution.py:837
  18.7 17.9 %collective-permute-start.19 = (bf16[4,1152]{1,0:T(4,128)(2,1)S(1)}, bf16[4,1152]{1,0:T(4,128)(2,1)S(1)}, u32[]{:S(2)}, u32[]{:S(2)}) collective-permute-start(bf16[4,1152]{1,0:T(4,128)(2,1)S(1)} %broadcast_select_fusion), channel_id=1, source_target_pairs={{0,1},{1,0},{2,3},{3,2},{4,5},{5,4},{6,7},{7,6},{8,9},{9,8},{10,11... | collective-permute-start | bytes 27656 | tf_op jit(solution)/shard_map/ppermute | solution.py:833
  18.9 44.9 %collective-permute-start = (bf16[6,64,768]{2,1,0:T(8,128)(2,1)S(1)}, bf16[6,64,768]{2,1,0:T(8,128)(2,1)}, u32[]{:S(2)}, u32[]{:S(2)}) collective-permute-start(bf16[6,64,768]{2,1,0:T(8,128)(2,1)S(1)} %bitcast.66), channel_id=1, source_target_pairs={{0,1},{1,2},{2,3},{4,5},{5,6},{6,7},{8,9},{9,10},{10,11},{12,13},{... | collective-permute-start | bytes 1769480 | tf_op jit(solution)/shard_map/ppermute | solution.py:898
  24.0 41.4 %collective-permute-start.1 = (bf16[12,64,768]{2,1,0:T(8,128)(2,1)S(1)}, bf16[12,64,768]{2,1,0:T(8,128)(2,1)}, u32[]{:S(2)}, u32[]{:S(2)}) collective-permute-start(bf16[12,64,768]{2,1,0:T(8,128)(2,1)S(1)} %bitcast.64), channel_id=1, source_target_pairs={{1,0},{2,1},{3,2},{5,4},{6,5},{7,6},{9,8},{10,9},{11,10},{13,12},{... | collective-permute-start | bytes 3538952 | tf_op jit(solution)/shard_map/ppermute | solution.py:899
  29.2 50.2 %copy-start.2 = (bf16[4,48,576]{2,1,0:T(8,128)(2,1)}, bf16[4,48,576]{2,1,0:T(8,128)(2,1)S(1)}, u32[]{:S(2)}) copy-start(bf16[4,48,576]{2,1,0:T(8,128)(2,1)S(1)} %pad_maximum_fusion.refs_0_) | copy-start | bytes 663556
  29.2 7.8 %collective-permute-start.5 = (bf16[4,48,576]{2,1,0:T(8,128)(2,1)S(1)}, bf16[4,48,576]{2,1,0:T(8,128)(2,1)S(1)}, u32[]{:S(2)}, u32[]{:S(2)}) collective-permute-start(bf16[4,48,576]{2,1,0:T(8,128)(2,1)S(1)} %pad_maximum_fusion.refs_0_), channel_id=1, source_target_pairs={{0,4},{4,0},{1,5},{5,1},{2,6},{6,2},{3,7},{7,3},{8,12},{12,8},{9,1... | collective-permute-start | bytes 663560 | tf_op jit(solution)/shard_map/ppermute | solution.py:833
  31.8 25.7 %collective-permute-start.7 = (bf16[4,48,576]{2,1,0:T(8,128)(2,1)}, bf16[4,48,576]{2,1,0:T(8,128)(2,1)S(1)}, u32[]{:S(2)}, u32[]{:S(2)}) collective-permute-start(bf16[4,48,576]{2,1,0:T(8,128)(2,1)} %pad_maximum_fusion.1.refs_4_), channel_id=1, source_target_pairs={{0,2},{2,0},{1,3},{3,1},{4,6},{6,4},{5,7},{7,5},{8,10},{10,8},{9,1... | collective-permute-start | bytes 663560 | tf_op jit(solution)/shard_map/ppermute | solution.py:833
  36.7 23.6 %collective-permute-start.9 = (bf16[4,48,576]{2,1,0:T(8,128)(2,1)S(1)}, bf16[4,48,576]{2,1,0:T(8,128)(2,1)}, u32[]{:S(2)}, u32[]{:S(2)}) collective-permute-start(bf16[4,48,576]{2,1,0:T(8,128)(2,1)S(1)} %pad_maximum_fusion.refs_0_), channel_id=1, source_target_pairs={{0,2},{2,0},{1,3},{3,1},{4,6},{6,4},{5,7},{7,5},{8,10},{10,8},{9,1... | collective-permute-start | bytes 663560 | tf_op jit(solution)/shard_map/ppermute | solution.py:833
  37.0 28.3 %copy-start.18 = (bf16[4,48,576]{2,1,0:T(8,128)(2,1)}, bf16[4,48,576]{2,1,0:T(8,128)(2,1)S(1)}, u32[]{:S(2)}) copy-start(bf16[4,48,576]{2,1,0:T(8,128)(2,1)S(1)} %collective-permute-done.5.refs_2_) | copy-start | bytes 663556
  37.0 25.8 %collective-permute-start.6 = (bf16[4,48,576]{2,1,0:T(8,128)(2,1)S(1)}, bf16[4,48,576]{2,1,0:T(8,128)(2,1)S(1)}, u32[]{:S(2)}, u32[]{:S(2)}) collective-permute-start(bf16[4,48,576]{2,1,0:T(8,128)(2,1)S(1)} %collective-permute-done.5.refs_2_), channel_id=1, source_target_pairs={{0,2},{2,0},{1,3},{3,1},{4,6},{6,4},{5,7},{7,5},{8,10},{10,8},{9,1... | collective-permute-start | bytes 663560 | tf_op jit(solution)/shard_map/ppermute | solution.py:833
  57.5 6.2 %collective-permute-start.8 = (bf16[4,48,576]{2,1,0:T(8,128)(2,1)S(1)}, bf16[4,48,576]{2,1,0:T(8,128)(2,1)S(1)}, u32[]{:S(2)}, u32[]{:S(2)}) collective-permute-start(bf16[4,48,576]{2,1,0:T(8,128)(2,1)S(1)} %collective-permute-done.7.refs_5_), channel_id=1, source_target_pairs={{0,4},{4,0},{1,5},{5,1},{2,6},{6,2},{3,7},{7,3},{8,12},{12,8},{9,1... | collective-permute-start | bytes 663560 | tf_op jit(solution)/shard_map/ppermute | solution.py:833
  60.3 19.1 %collective-permute-start.20 = (bf16[4,1152]{1,0:T(4,128)(2,1)S(1)}, bf16[4,1152]{1,0:T(4,128)(2,1)S(1)}, u32[]{:S(2)}, u32[]{:S(2)}) collective-permute-start(bf16[4,1152]{1,0:T(4,128)(2,1)S(1)} %fusion.19), channel_id=1, source_target_pairs={{0,2},{2,0},{1,3},{3,1},{4,6},{6,4},{5,7},{7,5},{8,10},{10,8},{9,1... | collective-permute-start | bytes 27656 | tf_op jit(solution)/shard_map/ppermute | solution.py:833
  62.8 17.0 %collective-permute-start.11 = (bf16[4,48,576]{2,1,0:T(8,128)(2,1)S(1)}, bf16[4,48,576]{2,1,0:T(8,128)(2,1)}, u32[]{:S(2)}, u32[]{:S(2)}) collective-permute-start(bf16[4,48,576]{2,1,0:T(8,128)(2,1)S(1)} %pad_maximum_fusion.refs_0_), channel_id=1, source_target_pairs={{0,1},{1,0},{2,3},{3,2},{4,5},{5,4},{6,7},{7,6},{8,9},{9,8},{10,11... | collective-permute-start | bytes 663560 | tf_op jit(solution)/shard_map/ppermute | solution.py:833
  63.7 16.6 %collective-permute-start.15 = (bf16[4,48,576]{2,1,0:T(8,128)(2,1)}, bf16[4,48,576]{2,1,0:T(8,128)(2,1)}, u32[]{:S(2)}, u32[]{:S(2)}) collective-permute-start(bf16[4,48,576]{2,1,0:T(8,128)(2,1)} %pad_maximum_fusion.1.refs_4_), channel_id=1, source_target_pairs={{0,1},{1,0},{2,3},{3,2},{4,5},{5,4},{6,7},{7,6},{8,9},{9,8},{10,11... | collective-permute-start | bytes 663560 | tf_op jit(solution)/shard_map/ppermute | solution.py:833
  63.7 16.3 %collective-permute-start.10 = (bf16[4,48,576]{2,1,0:T(8,128)(2,1)}, bf16[4,48,576]{2,1,0:T(8,128)(2,1)}, u32[]{:S(2)}, u32[]{:S(2)}) collective-permute-start(bf16[4,48,576]{2,1,0:T(8,128)(2,1)} %pad_maximum_fusion.1.refs_4_), channel_id=1, source_target_pairs={{0,4},{4,0},{1,5},{5,1},{2,6},{6,2},{3,7},{7,3},{8,12},{12,8},{9,1... | collective-permute-start | bytes 663560 | tf_op jit(solution)/shard_map/ppermute | solution.py:833
  65.3 15.2 %collective-permute-start.12 = (bf16[4,48,576]{2,1,0:T(8,128)(2,1)}, bf16[4,48,576]{2,1,0:T(8,128)(2,1)}, u32[]{:S(2)}, u32[]{:S(2)}) collective-permute-start(bf16[4,48,576]{2,1,0:T(8,128)(2,1)} %collective-permute-done.9.refs_1_), channel_id=1, source_target_pairs={{0,1},{1,0},{2,3},{3,2},{4,5},{5,4},{6,7},{7,6},{8,9},{9,8},{10,11... | collective-permute-start | bytes 663560 | tf_op jit(solution)/shard_map/ppermute | solution.py:833
  79.4 2.9 collective-permute-start.13
  79.8 2.5 collective-permute-start.16
  80.0 2.3 collective-permute-start.17
  80.3 2.7 collective-permute-start.14
  80.5 3.3 collective-permute-start.18
  165.5 34.4 %collective-permute-start.22 = (bf16[2,4,2,96,192]{4,3,2,1,0:T(8,128)(2,1)}, bf16[2,4,2,96,192]{4,3,2,1,0:T(8,128)(2,1)}, u32[]{:S(2)}, u32[]{:S(2)}) collective-permute-start(bf16[2,4,2,96,192]{4,3,2,1,0:T(8,128)(2,1)} %get-tuple-element.144), channel_id=1, source_target_pairs={{0,1},{1,0},{2,3},{3,2},{4,5},{5,4},{6,7},{7,6},{8,9},{9,8},{10,11... | collective-permute-start | bytes 1769480 | tf_op jit(solution)/shard_map/ppermute | solution.py:833
  188.2 11.8 %collective-permute-start.21 = (bf16[4,2,96,576]{3,2,1,0:T(8,128)(2,1)}, bf16[4,2,96,576]{3,2,1,0:T(8,128)(2,1)}, u32[]{:S(2)}, u32[]{:S(2)}) collective-permute-start(bf16[4,2,96,576]{3,2,1,0:T(8,128)(2,1)} %get-tuple-element.142), channel_id=1, source_target_pairs={{0,1},{1,0},{2,3},{3,2},{4,5},{5,4},{6,7},{7,6},{8,9},{9,8},{10,11... | collective-permute-start | bytes 2654216 | tf_op jit(solution)/shard_map/ppermute | solution.py:833
  205.3 18.9 %copy-start.16 = (bf16[2,4,96,192]{3,2,1,0:T(8,128)(2,1)S(1)}, bf16[2,4,96,192]{3,2,1,0:T(8,128)(2,1)}, u32[]{:S(2)}) copy-start(bf16[2,4,96,192]{3,2,1,0:T(8,128)(2,1)} %get-tuple-element.164) | copy-start | bytes 884740
  219.2 35.7 %collective-permute-start.23 = (bf16[5,12,16,768]{3,2,1,0:T(8,128)(2,1)}, bf16[5,12,16,768]{3,2,1,0:T(8,128)(2,1)}, u32[]{:S(2)}, u32[]{:S(2)}) collective-permute-start(bf16[5,12,16,768]{3,2,1,0:T(8,128)(2,1)} %get-tuple-element.155), channel_id=1, source_target_pairs={{0,1},{1,2},{2,3},{4,5},{5,6},{6,7},{8,9},{9,10},{10,11},{12,13},{... | collective-permute-start | bytes 4423688 | tf_op jit(solution)/shard_map/ppermute | solution.py:957
  222.6 32.2 %collective-permute-start.24 = (bf16[5,8,16,768]{3,2,1,0:T(8,128)(2,1)}, bf16[5,8,16,768]{3,2,1,0:T(8,128)(2,1)}, u32[]{:S(2)}, u32[]{:S(2)}) collective-permute-start(bf16[5,8,16,768]{3,2,1,0:T(8,128)(2,1)} %get-tuple-element.156), channel_id=1, source_target_pairs={{1,0},{2,1},{3,2},{5,4},{6,5},{7,6},{9,8},{10,9},{11,10},{13,12},{... | collective-permute-start | bytes 2949128 | tf_op jit(solution)/shard_map/ppermute | solution.py:956
  224.1 14.2 %collective-permute-start.26 = (bf16[2,4,96,192]{3,2,1,0:T(8,128)(2,1)S(1)}, bf16[2,4,96,192]{3,2,1,0:T(8,128)(2,1)S(1)}, u32[]{:S(2)}, u32[]{:S(2)}) collective-permute-start(bf16[2,4,96,192]{3,2,1,0:T(8,128)(2,1)S(1)} %copy-done.16), channel_id=1, source_target_pairs={{0,4},{4,0},{1,5},{5,1},{2,6},{6,2},{3,7},{7,3},{8,12},{12,8},{9,1... | collective-permute-start | bytes 884744 | tf_op jit(solution)/shard_map/ppermute | solution.py:833
  224.7 26.4 %collective-permute-start.25 = (bf16[4,96,576]{2,1,0:T(8,128)(2,1)}, bf16[4,96,576]{2,1,0:T(8,128)(2,1)}, u32[]{:S(2)}, u32[]{:S(2)}) collective-permute-start(bf16[4,96,576]{2,1,0:T(8,128)(2,1)} %get-tuple-element.162), channel_id=1, source_target_pairs={{0,4},{4,0},{1,5},{5,1},{2,6},{6,2},{3,7},{7,3},{8,12},{12,8},{9,1... | collective-permute-start | bytes 1327112 | tf_op jit(solution)/shard_map/ppermute | solution.py:833
  237.0 25.2 %collective-permute-start.27 = (bf16[4,2,96,576]{3,2,1,0:T(8,128)(2,1)}, bf16[4,2,96,576]{3,2,1,0:T(8,128)(2,1)}, u32[]{:S(2)}, u32[]{:S(2)}) collective-permute-start(bf16[4,2,96,576]{3,2,1,0:T(8,128)(2,1)} %get-tuple-element.169), channel_id=1, source_target_pairs={{0,1},{1,0},{2,3},{3,2},{4,5},{5,4},{6,7},{7,6},{8,9},{9,8},{10,11... | collective-permute-start | bytes 2654216 | tf_op jit(solution)/shard_map/ppermute | solution.py:833
  254.8 26.2 %copy-start.28 = (bf16[4,96,192]{2,1,0:T(8,128)(2,1)S(1)}, bf16[4,96,192]{2,1,0:T(8,128)(2,1)}, u32[]{:S(2)}) copy-start(bf16[4,96,192]{2,1,0:T(8,128)(2,1)} %get-tuple-element.182) | copy-start | bytes 442372
  263.0 1.6 collective-permute-start.28
  264.6 4.8 %collective-permute-start.29 = (f32[26,512]{1,0:T(8,128)S(1)}, f32[26,512]{1,0:T(8,128)S(1)}, u32[]{:S(2)}, u32[]{:S(2)}) collective-permute-start(f32[26,512]{1,0:T(8,128)S(1)} %add.94), channel_id=1, source_target_pairs={{0,2},{2,0},{1,3},{3,1},{4,6},{6,4},{5,7},{7,5},{8,10},{10,8},{9,1... | collective-permute-start | bytes 159752 | tf_op jit(solution)/shard_map/ppermute | solution.py:833
  269.5 5.7 %collective-permute-start.30 = (f32[26,512]{1,0:T(8,128)S(1)}, f32[26,512]{1,0:T(8,128)S(1)}, u32[]{:S(2)}, u32[]{:S(2)}) collective-permute-start(f32[26,512]{1,0:T(8,128)S(1)} %add.95), channel_id=1, source_target_pairs={{0,4},{4,0},{1,5},{5,1},{2,6},{6,2},{3,7},{7,3},{8,12},{12,8},{9,1... | collective-permute-start | bytes 159752 | tf_op jit(solution)/shard_map/ppermute | solution.py:833
  275.1 11.7 %collective-permute-start.31 = (f32[26,512]{1,0:T(8,128)S(1)}, f32[26,512]{1,0:T(8,128)S(1)}, u32[]{:S(2)}, u32[]{:S(2)}) collective-permute-start(f32[26,512]{1,0:T(8,128)S(1)} %add.96), channel_id=1, source_target_pairs={{0,8},{8,0},{16,24},{24,16},{1,9},{9,1},{17,25},{25,17},{2,10},{10... | collective-permute-start | bytes 159752 | tf_op jit(solution)/shard_map/ppermute | solution.py:871
  281.1 13.8 %collective-permute-start.35 = (bf16[4,96,192]{2,1,0:T(8,128)(2,1)S(1)}, bf16[4,96,192]{2,1,0:T(8,128)(2,1)S(1)}, u32[]{:S(2)}, u32[]{:S(2)}) collective-permute-start(bf16[4,96,192]{2,1,0:T(8,128)(2,1)S(1)} %copy-done.28), channel_id=1, source_target_pairs={{0,2},{2,0},{1,3},{3,1},{4,6},{6,4},{5,7},{7,5},{8,10},{10,8},{9,1... | collective-permute-start | bytes 442376 | tf_op jit(solution)/shard_map/ppermute | solution.py:833
  281.2 15.9 %collective-permute-start.34 = (bf16[4,96,576]{2,1,0:T(8,128)(2,1)}, bf16[4,96,576]{2,1,0:T(8,128)(2,1)}, u32[]{:S(2)}, u32[]{:S(2)}) collective-permute-start(bf16[4,96,576]{2,1,0:T(8,128)(2,1)} %get-tuple-element.180), channel_id=1, source_target_pairs={{0,2},{2,0},{1,3},{3,1},{4,6},{6,4},{5,7},{7,5},{8,10},{10,8},{9,1... | collective-permute-start | bytes 1327112 | tf_op jit(solution)/shard_map/ppermute | solution.py:833
  286.9 5.9 %collective-permute-start.32 = (f32[26,512]{1,0:T(8,128)S(1)}, f32[26,512]{1,0:T(8,128)S(1)}, u32[]{:S(2)}, u32[]{:S(2)}) collective-permute-start(f32[26,512]{1,0:T(8,128)S(1)} %add.97), channel_id=1, source_target_pairs={{0,16},{8,24},{16,0},{24,8},{1,17},{9,25},{17,1},{25,9},{2,18},{10... | collective-permute-start | bytes 159752 | tf_op jit(solution)/shard_map/ppermute | solution.py:871
  291.0 11.3 %collective-permute-start.33 = (bf16[4,96,576]{2,1,0:T(8,128)(2,1)}, bf16[4,96,576]{2,1,0:T(8,128)(2,1)}, u32[]{:S(2)}, u32[]{:S(2)}) collective-permute-start(bf16[4,96,576]{2,1,0:T(8,128)(2,1)} %get-tuple-element.179), channel_id=1, source_target_pairs={{0,4},{4,0},{1,5},{5,1},{2,6},{6,2},{3,7},{7,3},{8,12},{12,8},{9,1... | collective-permute-start | bytes 1327112 | tf_op jit(solution)/shard_map/ppermute | solution.py:833
  306.7 9.9 %collective-permute-start.39 = (bf16[96,192]{1,0:T(8,128)(2,1)S(1)}, bf16[96,192]{1,0:T(8,128)(2,1)S(1)}, u32[]{:S(2)}, u32[]{:S(2)}) collective-permute-start(bf16[96,192]{1,0:T(8,128)(2,1)S(1)} %get-tuple-element.229), channel_id=1, source_target_pairs={{0,8},{8,16},{16,24},{24,0},{1,9},{9,17},{17,25},{25,1},{2,10},{10... | collective-permute-start | bytes 110600 | tf_op jit(solution)/shard_map/ppermute | solution.py:837
  308.8 9.0 %collective-permute-start.41 = (bf16[96,192]{1,0:T(8,128)(2,1)S(1)}, bf16[96,192]{1,0:T(8,128)(2,1)S(1)}, u32[]{:S(2)}, u32[]{:S(2)}) collective-permute-start(bf16[96,192]{1,0:T(8,128)(2,1)S(1)} %get-tuple-element.230), channel_id=1, source_target_pairs={{0,24},{8,0},{16,8},{24,16},{1,25},{9,1},{17,9},{25,17},{2,26},{10... | collective-permute-start | bytes 110600 | tf_op jit(solution)/shard_map/ppermute | solution.py:837
  311.0 6.9 %collective-permute-start.40 = (bf16[96,192]{1,0:T(8,128)(2,1)S(1)}, bf16[96,192]{1,0:T(8,128)(2,1)S(1)}, u32[]{:S(2)}, u32[]{:S(2)}) collective-permute-start(bf16[96,192]{1,0:T(8,128)(2,1)S(1)} %get-tuple-element.231), channel_id=1, source_target_pairs={{0,16},{8,24},{16,0},{24,8},{1,17},{9,25},{17,1},{25,9},{2,18},{10... | collective-permute-start | bytes 110600 | tf_op jit(solution)/shard_map/ppermute | solution.py:837
  312.7 6.9 %collective-permute-start.36 = (bf16[96,576]{1,0:T(8,128)(2,1)S(1)}, bf16[96,576]{1,0:T(8,128)(2,1)S(1)}, u32[]{:S(2)}, u32[]{:S(2)}) collective-permute-start(bf16[96,576]{1,0:T(8,128)(2,1)S(1)} %get-tuple-element.226), channel_id=1, source_target_pairs={{0,8},{8,16},{16,24},{24,0},{1,9},{9,17},{17,25},{25,1},{2,10},{10... | collective-permute-start | bytes 331784 | tf_op jit(solution)/shard_map/ppermute | solution.py:837
  314.6 6.2 %collective-permute-start.38 = (bf16[96,576]{1,0:T(8,128)(2,1)S(1)}, bf16[96,576]{1,0:T(8,128)(2,1)S(1)}, u32[]{:S(2)}, u32[]{:S(2)}) collective-permute-start(bf16[96,576]{1,0:T(8,128)(2,1)S(1)} %get-tuple-element.227), channel_id=1, source_target_pairs={{0,24},{8,0},{16,8},{24,16},{1,25},{9,1},{17,9},{25,17},{2,26},{10... | collective-permute-start | bytes 331784 | tf_op jit(solution)/shard_map/ppermute | solution.py:837
  316.6 6.8 %collective-permute-start.37 = (bf16[96,576]{1,0:T(8,128)(2,1)S(1)}, bf16[96,576]{1,0:T(8,128)(2,1)S(1)}, u32[]{:S(2)}, u32[]{:S(2)}) collective-permute-start(bf16[96,576]{1,0:T(8,128)(2,1)S(1)} %get-tuple-element.228), channel_id=1, source_target_pairs={{0,16},{8,24},{16,0},{24,8},{1,17},{9,25},{17,1},{25,9},{2,18},{10... | collective-permute-start | bytes 331784 | tf_op jit(solution)/shard_map/ppermute | solution.py:837
  (26 other events, 260.9 us)
Sparse Core Ops, SparseCore 0:
  11.5 95.9 all-gather.2
  165.7 146.0 reduce-scatter.1

commit v6 on v5

--- a/solution.py
+++ b/solution.py
@@ -97,7 +97,7 @@
     return pl.BlockSpec(shape, lambda *_: (0,) * len(shape), pipeline_mode=pl.Buffered(1))
 
 
-def windows_body(place_ref, above_ref, x_ref, below_ref, vec_ref, nw_ref, turned_ref, own_ref, nat_ref, *, rows):
+def windows_body(place_ref, above_ref, x_ref, below_ref, vec_ref, nw_ref, nat_ref, *, rows):
     band = pl.program_id(0)
     slot = place_ref[0]
     above, below = above_ref.shape[0], below_ref.shape[0]
@@ -126,8 +126,8 @@
             nat_ref[at, 0:GRID, :] = jnp.where(inside, normed(below_ref[i]), 0.0)
             return carry
 
-        lax.fori_loop(0, EXT, clear, 0)
-        lax.fori_loop(0, rows, own, 0)
+        lax.fori_loop(0, EXT, clear, 0, unroll=4)
+        lax.fori_loop(0, rows, own, 0, unroll=2)
         lax.fori_loop(0, 2 * slot, before, 0)
         lax.fori_loop(0, EXT - rows - 2 * slot, after, 0)
 
@@ -141,10 +141,7 @@
                 nw_ref[pl.ds(start, PITCH), :] = jnp.where(keep, piece, 0.0).astype(BF)
                 return carry
 
-            lax.fori_loop(0, EXT, one, 0)
-
-    turned_ref[...] = nw_ref[...].T
-    own_ref[...] = nw_ref[pl.ds(pl.multiple_of(slot * 2 * PITCH, 2 * PITCH), rows * PITCH), :].T
+            lax.fori_loop(0, EXT, one, 0, unroll=4)
 
 
 def windows(place, above, x, below, vectors):
@@ -155,18 +152,10 @@
             num_scalar_prefetch=1,
             grid=(SIDE,),
             in_specs=[whole(above.shape), whole(x.shape), whole(below.shape), whole((8, D))],
-            out_specs=[
-                pl.BlockSpec((EXT * PITCH, D), lambda b, s: (b, 0)),
-                pl.BlockSpec((None, D, EXT * PITCH), lambda b, s: (b, 0, 0)),
-                pl.BlockSpec((None, D, rows * PITCH), lambda b, s: (b, 0, 0)),
-            ],
+            out_specs=pl.BlockSpec((EXT * PITCH, D), lambda b, s: (b, 0)),
             scratch_shapes=[pltpu.VMEM((EXT, GRID + PITCH, D), F32)],
         ),
-        out_shape=[
-            jax.ShapeDtypeStruct((SIDE * EXT * PITCH, D), BF),
-            jax.ShapeDtypeStruct((SIDE, D, EXT * PITCH), BF),
-            jax.ShapeDtypeStruct((SIDE, D, rows * PITCH), BF),
-        ],
+        out_shape=jax.ShapeDtypeStruct((SIDE * EXT * PITCH, D), BF),
         compiler_params=pltpu.CompilerParams(vmem_limit_bytes=63 << 20),
         cost_estimate=guess(8),
         name="windows",
@@ -174,7 +163,7 @@
 
 
 def project_body(place_ref, nw_ref, *refs, rows, depth):
-    *pieces, bias_ref, q_ref, k_ref, v_ref, w_ref, stage_ref = refs
+    *pieces, bias_ref, q_ref, k_ref, v_ref, w_ref, turned_ref, turned_own_ref, stage_ref = refs
     slot, z, x, y, c = (place_ref[i] for i in range(5))
     width = D // 4
 
@@ -208,6 +197,8 @@
     q_ref[...] = (mm(own, w_ref[:, 0:D]) + bias_ref[0:1]).astype(BF)
     k_ref[...] = mm(normed, w_ref[:, D : 2 * D]).astype(BF)
     v_ref[...] = (mm(normed, w_ref[:, 2 * D :]) + bias_ref[1:2]).astype(BF)
+    turned_ref[...] = normed.T
+    turned_own_ref[...] = own.T
 
 
 def guess(us):
@@ -224,12 +215,18 @@
             num_scalar_prefetch=1,
             grid=(SIDE,),
             in_specs=[of_k] + [whole(p.shape) for p in pieces] + [whole((2, D))],
-            out_specs=[of_q, of_k, of_k, whole((D, 3 * D))],
+            out_specs=[
+                of_q, of_k, of_k, whole((D, 3 * D)),
+                pl.BlockSpec((None, D, EXT * PITCH), lambda b, s: (b, 0, 0)),
+                pl.BlockSpec((None, D, rows * PITCH), lambda b, s: (b, 0, 0)),
+            ],
             scratch_shapes=[pltpu.VMEM((4, D, 3 * D // 4), BF)],
         ),
         out_shape=[
             jax.ShapeDtypeStruct((SIDE * rows * PITCH, D), BF), keys, keys,
             jax.ShapeDtypeStruct((D, 3 * D), BF),
+            jax.ShapeDtypeStruct((SIDE, D, EXT * PITCH), BF),
+            jax.ShapeDtypeStruct((SIDE, D, rows * PITCH), BF),
         ],
         compiler_params=pltpu.CompilerParams(vmem_limit_bytes=63 << 20),
         cost_estimate=guess(18),
@@ -908,7 +905,7 @@
     up_bias_all = biases[:, 2 * width :].reshape(slots, 1, hidden)
 
     vec_one = jnp.concatenate([first_gain[None], first_shift[None], jnp.zeros((6, D), BF)], 0).astype(F32)
-    normed, turned, turned_own = windows(place, from_above, grid_x, from_below, vec_one)
+    normed = windows(place, from_above, grid_x, from_below, vec_one)
     if fast:
         pieces = spread_plane(qkv_weight.reshape(depth, 3 * width), count)
         normed, pieces[3], pieces[7] = after(normed, pieces[3], pieces[7])
@@ -916,7 +913,7 @@
     else:
         full = lax.all_gather(qkv_weight, AXES, axis=0).reshape(2 * count, slots, depth, 3, width)
         pieces = [full.transpose(0, 2, 3, 1, 4).reshape(D, 3 * D)]
-    q, k, v, weight = project(place, normed, pieces, qv_all, rows, depth)
+    q, k, v, weight, turned, turned_own = project(place, normed, pieces, qv_all, rows, depth)
     ahead, back = score_tables()
     rel_ahead, rel_back = offset_tables(rel_height, rel_width)
     attended, probs = attend(place, q, k, v, rel_ahead.T, jnp.asarray(ahead, BF), rows)

time: 336 us -> 333 us (level)
    ppermute x9, waiting for transfers between devices: 5.28 us -> 9.52 us  [shift(): lax.ppermute(value, 'z', [(i, (i + by) % count) for i in range(count)])]
    pallas_call x1, Pallas kernels: 13.9 us -> 10.1 us  [windows(): pl.pallas_call(partial(windows_body, rows=rows), grid_spec=pltpu.Prefetch...]
  transfers between devices with their start and end apart: 44 -> 44, of which waited for: 17 -> 16; matrix products, arithmetic and copies ran while one was open for 7% -> 7% of each run, Pallas kernels for 39% -> 38%
where the time goes in v6:
time: 333 us; the launch traced here: 332 us
  Pallas kernels  176 us (53%)
  waiting for transfers between devices  66.3 us (20%)
  starting transfers between devices  47.6 us (14%)
  local copies, waits for them, and re-layouts  19.3 us (6%)
  between operations  14.7 us (4%)
  other arithmetic  8.13 us (2%)
    ppermute x27, waiting for transfers between devices, swap(): return lax.ppermute(value, axis, SWAP)  53.5 us
    pallas_call x1, Pallas kernels, feed(): pl.pallas_call(partial(feed_body, rows=rows), grid_spec=pltpu.PrefetchSca...  49 us
    pallas_call x2, Pallas kernels, attend_back(): pl.pallas_call(partial(attend_back_body, rows=rows), grid_spec=pltpu.Pref...  23 us
    pallas_call x2, Pallas kernels, project_grad(): pl.pallas_call(partial(project_grad_body, parts=parts), grid_spec=pltpu.P...  21.7 us
    ppermute x27, starting transfers between devices, swap(): return lax.ppermute(value, axis, SWAP)  19.6 us
    pallas_call x1, Pallas kernels, attend(): pl.pallas_call(partial(attend_body, rows=rows), grid_spec=pltpu.PrefetchS...  18.9 us
    pallas_call x4, Pallas kernels, fold(): pl.pallas_call(partial(fold_body, plan=plan), grid=(count,), in_specs=in_...  16.5 us
    pallas_call x1, Pallas kernels, project(): pl.pallas_call(partial(project_body, rows=rows, depth=depth), grid_spec=p...  15.1 us
  transfers between devices with their start and end apart: 44, of which 16 were waited for; matrix products, arithmetic and copies ran while one was open for 7% of the time, Pallas kernels for 38%

profile of v6, /device:TPU:0, one launch (start us, length us, event | category | flops | bytes accessed | tf_op | source)
XLA Modules:
  0.0 331.8 jit_solution(16025081403833858946)
XLA Ops:
  7.3 1.9 concatenate.68
  11.1 5.0 %collective-permute-start.4 = (bf16[96,576]{1,0:T(8,128)(2,1)}, bf16[96,576]{1,0:T(8,128)(2,1)}, u32[]{:S(2)}, u32[]{:S(2)}) collective-permute-start(bf16[96,576]{1,0:T(8,128)(2,1)} %copy.43), channel_id=1, source_target_pairs={{0,24},{8,0},{16,8},{24,16},{1,25},{9,1},{17,9},{25,17},{2,26},{10... | collective-permute-start | bytes 331784 | tf_op jit(solution)/shard_map/ppermute | solution.py:834
  18.9 3.2 collective-permute-start
  23.9 1.3 collective-permute-start.1
  26.1 1.2 collective-permute-done.3
  29.2 1.9 collective-permute-start.5
  31.8 2.1 collective-permute-start.7
  37.0 1.7 collective-permute-start.6
  38.7 18.8 %collective-permute-done.7.refs_5_ = bf16[4,48,576]{2,1,0:T(8,128)(2,1)S(1)} collective-permute-done((bf16[4,48,576]{2,1,0:T(8,128)(2,1)}, bf16[4,48,576]{2,1,0:T(8,128)(2,1)S(1)}, u32[]{:S(2)}, u32[]{:S(2)}) %collective-permute-start.7) | collective-permute-done | bytes 221216 | tf_op jit(solution)/shard_map/ppermute | solution.py:830
  57.5 1.5 collective-permute-start.8
  59.1 1.2 collective-permute-done.9.refs_1_
  60.3 2.5 collective-permute-done.6.refs_3_
  63.7 1.6 collective-permute-start.10
  65.5 10.1 %windows.1.nw_ref = bf16[2240,768]{1,0:T(8,128)(2,1)} custom-call(s32[6]{0:T(128)} %stack.54.place_ref, bf16[6,64,768]{2,1,0:T(8,128)(2,1)} %collective-permute-done.above_ref, bf16[16,64,768]{2,1,0:T(8,128)(2,1)} %bitcast.62, bf16[12,64,768]{2,1,0:T(8,128)(2,1)} %collective-permute-done.1.below_ref, f32[8,768]{1,0:T(8,128)} %maximum_convert_fusion.vec_ref), custom_call_target="tpu_custom_call" | custom-call | flops 8800000000 | bytes 24000000 | tf_op jit(solution)/shard_map/windows/pallas_call | solution.py:149
  80.1 15.1 %project.1 = (bf16[1280,768]{1,0:T(8,128)(2,1)}, bf16[2240,768]{1,0:T(8,128)(2,1)}, bf16[2240,768]{1,0:T(8,128)(2,1)}, bf16[768,2304]{1,0:T(8,128)(2,1)}, bf16[5...) custom-call(s32[6]{0:T(128)} %stack.54.place_ref, bf16[2240,768]{1,0:T(8,128)(2,1)} %windows.1.nw_ref, ...), custom_call_target="tpu_custom_call" | custom-call | flops 19800000512 | bytes 54000000 | tf_op jit(solution)/shard_map/project/pallas_call | solution.py:212
  95.2 18.9 %attend.1 = (bf16[1280,768]{1,0:T(8,128)(2,1)}, bf16[30,2,224,256]{3,2,1,0:T(8,128)(2,1)}) custom-call(s32[6]{0:T(128)} %stack.54.place_ref, bf16[1280,768]{1,0:T(8,128)(2,1)} %get-tuple-element.127.q_ref, bf16[2240,768]{1,0:T(8,128)(2,1)} %get-tuple-element.128.k_ref, bf16[2240,768]{1,0:T(8,128)(2,1)} %get-tuple-element.129.v_ref, ...), custom_call_target="tpu_custom_call" | custom-call | flops 26400000000 | bytes 72000000 | tf_op jit(solution)/shard_map/attend/pallas_call | solution.py:418
  114.1 49.0 %feed.1 = (bf16[1024,768]{1,0:T(8,128)(2,1)}, f32[1024,768]{1,0:T(8,128)}, bf16[5,16,16,768]{3,2,1,0:T(8,128)(2,1)}, bf16[8,4,96,1536]{3,2,1,0:T(8,128)(2,1)}, b...) custom-call(s32[6]{0:T(128)} %stack.54.place_ref, ...), custom_call_target="tpu_custom_call" | custom-call | flops 54999998464 | bytes 150000000 | tf_op jit(solution)/shard_map/feed/pallas_call | solution.py:699
  163.4 11.4 %attend_back.2 = (bf16[1280,384]{1,0:T(8,128)(2,1)}, bf16[2240,384]{1,0:T(8,128)(2,1)}, bf16[2240,384]{1,0:T(8,128)(2,1)}, f32[128,256]{1,0:T(8,128)}) custom-call(s32[6]{0:T(128)} %stack.54.place_ref, bf16[1280,768]{1,0:T(8,128)(2,1)} %get-tuple-element.127.q_ref, bf16[2240,768]{1,0:T(8,128)(2,1)} %get-tuple-element.128.k_ref, ...), custom_call_target="tpu_custom_call" | custom-call | flops 17600000000 | bytes 48000000 | tf_op jit(solution)/shard_map/attend_back/pallas_call | solution.py:532
  174.8 10.9 %project_grad.2 = (bf16[4,2,96,576]{3,2,1,0:T(8,128)(2,1)}, bf16[4,2,96,576]{3,2,1,0:T(8,128)(2,1)}, f32[2,384]{1,0:T(2,128)}) custom-call(s32[6]{0:T(128)} %stack.54.place_ref, bf16[5,768,448]{2,1,0:T(8,128)(2,1)} %get-tuple-element.132.turned_ref, bf16[5,768,256]{2,1,0:T(8,128)(2,1)} %get-tuple-element.133.own_ref, ...), custom_call_target="tpu_custom_call" | custom-call | flops 6600000000 | bytes 18000000 | tf_op jit(solution)/shard_map/project_grad/pallas_call | solution.py:278
  186.0 11.6 %attend_back.3 = (bf16[1280,384]{1,0:T(8,128)(2,1)}, bf16[2240,384]{1,0:T(8,128)(2,1)}, bf16[2240,384]{1,0:T(8,128)(2,1)}, f32[128,256]{1,0:T(8,128)}) custom-call(s32[6]{0:T(128)} %stack.54.place_ref, bf16[1280,768]{1,0:T(8,128)(2,1)} %get-tuple-element.127.q_ref, bf16[2240,768]{1,0:T(8,128)(2,1)} %get-tuple-element.128.k_ref, ...), custom_call_target="tpu_custom_call" | custom-call | flops 17600000000 | bytes 48000000 | tf_op jit(solution)/shard_map/attend_back/pallas_call | solution.py:532
  197.6 5.1 %fold.4 = (bf16[4,96,576]{2,1,0:T(8,128)(2,1)}, bf16[4,96,576]{2,1,0:T(8,128)(2,1)}, bf16[2,4,96,192]{3,2,1,0:T(8,128)(2,1)}, bf16[2,4,96,192]{3,2,1,0:T(8,128)(2,1)}) custom-call(bf16[4,2,96,576]{3,2,1,0:T(8,128)(2,1)} %get-tuple-element.139.refs_0_.refs_2_, bf16[4,2,96,576]{3,2,1,0:T(8,128)(2,1)} %collective-permute-done.21.refs_1_.refs_3_, ...), custom_call_target="tpu_custom_call" | custom-call | flops 4344032256 | bytes 11847360 | tf_op jit(solution)/shard_map/fold/pallas_call | solution.py:813
  202.7 14.0 %project_back.1 = (bf16[5,8,16,768]{3,2,1,0:T(8,128)(2,1)}, f32[5,16,16,768]{3,2,1,0:T(8,128)}, bf16[5,12,16,768]{3,2,1,0:T(8,128)(2,1)}) custom-call(s32[6]{0:T(128)} %stack.54.place_ref, bf16[1280,384]{1,0:T(8,128)(2,1)} %get-tuple-element.136.dq_ref.refs_0_, bf16[1280,384]{1,0:T(8,128)(2,1)} %get-tuple-element.146.refs_1_.dq_ref, ...), custom_call_target="tpu_custom_call" | custom-call | flops 11000000512 | bytes 30000000 | tf_op jit(solution)/shard_map/project_back/pallas_call | solution.py:321
  216.7 3.3 collective-permute-start.23
  220.1 1.3 collective-permute-start.24
  221.6 1.3 collective-permute-start.26
  223.7 10.8 %project_grad.3 = (bf16[4,2,96,576]{3,2,1,0:T(8,128)(2,1)}, bf16[4,2,96,576]{3,2,1,0:T(8,128)(2,1)}, f32[2,384]{1,0:T(2,128)}) custom-call(s32[6]{0:T(128)} %stack.54.place_ref, bf16[5,768,448]{2,1,0:T(8,128)(2,1)} %get-tuple-element.132.turned_ref, bf16[5,768,256]{2,1,0:T(8,128)(2,1)} %get-tuple-element.133.own_ref, ...), custom_call_target="tpu_custom_call" | custom-call | flops 6600000000 | bytes 18000000 | tf_op jit(solution)/shard_map/project_grad/pallas_call | solution.py:278
  235.8 13.9 %collective-permute-done.25.refs_1_ = bf16[4,96,576]{2,1,0:T(8,128)(2,1)} collective-permute-done((bf16[4,96,576]{2,1,0:T(8,128)(2,1)}, bf16[4,96,576]{2,1,0:T(8,128)(2,1)}, u32[]{:S(2)}, u32[]{:S(2)}) %collective-permute-start.25) | collective-permute-done | bytes 442400 | tf_op jit(solution)/shard_map/ppermute | solution.py:830
  249.7 3.7 %fold.5 = (bf16[4,96,576]{2,1,0:T(8,128)(2,1)}, bf16[4,96,192]{2,1,0:T(8,128)(2,1)}, bf16[4,96,192]{2,1,0:T(8,128)(2,1)}) custom-call(bf16[4,96,576]{2,1,0:T(8,128)(2,1)} %get-tuple-element.159.refs_0_, bf16[4,96,576]{2,1,0:T(8,128)(2,1)} %collective-permute-done.25.refs_1_, bf16[2,4,96,192]{3,2,1,0:T(8,128)(2,1)} %get-tuple-element.161.refs_2_.refs_4_, ...), custom_call_target="tpu_custom_call" | custom-call | flops 2235411200 | bytes 6096576 | tf_op jit(solution)/shard_map/fold/pallas_call | solution.py:813
  253.4 7.4 %finish.1 = (bf16[16,64,768]{2,1,0:T(8,128)(2,1)}, f32[8,768]{1,0:T(8,128)}) custom-call(f32[5,16,16,768]{3,2,1,0:T(8,128)} %get-tuple-element.150.own_ref, bf16[5,12,16,768]{3,2,1,0:T(8,128)(2,1)} %collective-permute-done.23.head_ref, bf16[5,8,16,768]{3,2,1,0:T(8,128)(2,1)} %collective-permute-done.24.tail_ref, bf16[16,64,768]{2,1,0:T(8,128)(2,1)} %bitcast.63, ...), custom_call_target="tpu_custom_call" | custom-call | flops 6600000000 | bytes 18000000 | tf_op jit(solution)/shard_map/finish/pallas_call | solution.py:761
  262.9 2.1 collective-permute-start.29
  265.1 3.1 collective-permute-done.29
  268.3 5.5 %collective-permute-done.30 = f32[26,512]{1,0:T(8,128)S(1)} collective-permute-done((f32[26,512]{1,0:T(8,128)S(1)}, f32[26,512]{1,0:T(8,128)S(1)}, u32[]{:S(2)}, u32[]{:S(2)}) %collective-permute-start.30) | collective-permute-done | bytes 53280 | tf_op jit(solution)/shard_map/ppermute | solution.py:830
  273.8 3.0 collective-permute-start.31
  277.2 1.6 collective-permute-start.34
  278.8 1.3 collective-permute-done.31
  281.1 4.2 %fold.6 = (bf16[4,96,576]{2,1,0:T(8,128)(2,1)}, bf16[4,96,576]{2,1,0:T(8,128)(2,1)}) custom-call(bf16[4,2,96,576]{3,2,1,0:T(8,128)(2,1)} %get-tuple-element.174.refs_0_.refs_2_, bf16[4,2,96,576]{3,2,1,0:T(8,128)(2,1)} %collective-permute-done.27.refs_1_.refs_3_, bf16[4,2,96,576]{3,2,1,0:T(8,128)(2,1)} %get-tuple-element.174.refs_0_.refs_2_, ...), custom_call_target="tpu_custom_call" | custom-call | flops 3046419200 | bytes 8308416 | tf_op jit(solution)/shard_map/fold/pallas_call | solution.py:813
  285.3 1.4 collective-permute-start.33
  286.7 1.9 collective-permute-done.32
  290.7 2.6 collective-permute-done.34.refs_2_
  293.4 3.6 %collective-permute-done.33.refs_1_ = bf16[4,96,576]{2,1,0:T(8,128)(2,1)} collective-permute-done((bf16[4,96,576]{2,1,0:T(8,128)(2,1)}, bf16[4,96,576]{2,1,0:T(8,128)(2,1)}, u32[]{:S(2)}, u32[]{:S(2)}) %collective-permute-start.33) | collective-permute-done | bytes 442400 | tf_op jit(solution)/shard_map/ppermute | solution.py:830
  297.0 3.5 %fold.7 = (bf16[4,96,576]{2,1,0:T(8,128)(2,1)}, bf16[4,96,192]{2,1,0:T(8,128)(2,1)}) custom-call(bf16[4,96,576]{2,1,0:T(8,128)(2,1)} %get-tuple-element.176.refs_0_, bf16[4,96,576]{2,1,0:T(8,128)(2,1)} %collective-permute-done.33.refs_1_, bf16[4,96,576]{2,1,0:T(8,128)(2,1)} %collective-permute-done.34.refs_2_, ...), custom_call_target="tpu_custom_call" | custom-call | flops 1992108800 | bytes 5433024 | tf_op jit(solution)/shard_map/fold/pallas_call | solution.py:813
  301.4 2.3 collective-permute-start.39
  303.6 1.6 collective-permute-start.41
  306.3 1.9 collective-permute-start.36
  308.2 2.0 collective-permute-start.38
  311.3 2.2 collective-permute-done.40
  313.6 1.5 fusion.11
  315.0 6.0 %collective-permute-done.37 = bf16[96,576]{1,0:T(8,128)(2,1)S(1)} collective-permute-done((bf16[96,576]{1,0:T(8,128)(2,1)S(1)}, bf16[96,576]{1,0:T(8,128)(2,1)S(1)}, u32[]{:S(2)}, u32[]{:S(2)}) %collective-permute-start.37) | collective-permute-done | bytes 110624 | tf_op jit(solution)/shard_map/ppermute | solution.py:834
  (206 shorter events, 34.1 us)
Async XLA Ops:
  7.2 106.9 %all-gather.3.cloned.1.call-start = ((), (), s32[]{:S(2)}) async-start(), calls=%async_computation.2 | async-start | bytes 11354112 | tf_op jit(solution)/shard_map/all_gather | solution.py:899
  9.2 313.9 %reduce-scatter.2.cloned.1.call-start = ((), (), s32[]{:S(2)}) async-start(), calls=%async_computation.1 | async-start | bytes 9732096 | tf_op jit(solution)/shard_map/reduce_scatter | solution.py:932
  11.1 12.8 %collective-permute-start.4 = (bf16[96,576]{1,0:T(8,128)(2,1)}, bf16[96,576]{1,0:T(8,128)(2,1)}, u32[]{:S(2)}, u32[]{:S(2)}) collective-permute-start(bf16[96,576]{1,0:T(8,128)(2,1)} %copy.43), channel_id=1, source_target_pairs={{0,24},{8,0},{16,8},{24,16},{1,25},{9,1},{17,9},{25,17},{2,26},{10... | collective-permute-start | bytes 331784 | tf_op jit(solution)/shard_map/ppermute | solution.py:834
  16.2 11.2 %collective-permute-start.3 = (bf16[96,576]{1,0:T(8,128)(2,1)}, bf16[96,576]{1,0:T(8,128)(2,1)}, u32[]{:S(2)}, u32[]{:S(2)}) collective-permute-start(bf16[96,576]{1,0:T(8,128)(2,1)} %copy.43), channel_id=1, source_target_pairs={{0,16},{8,24},{16,0},{24,8},{1,17},{9,25},{17,1},{25,9},{2,18},{10... | collective-permute-start | bytes 331784 | tf_op jit(solution)/shard_map/ppermute | solution.py:834
  16.2 12.0 %collective-permute-start.2 = (bf16[96,576]{1,0:T(8,128)(2,1)}, bf16[96,576]{1,0:T(8,128)(2,1)}, u32[]{:S(2)}, u32[]{:S(2)}) collective-permute-start(bf16[96,576]{1,0:T(8,128)(2,1)} %copy.43), channel_id=1, source_target_pairs={{0,8},{8,16},{16,24},{24,0},{1,9},{9,17},{17,25},{25,1},{2,10},{10... | collective-permute-start | bytes 331784 | tf_op jit(solution)/shard_map/ppermute | solution.py:834
  18.7 17.9 %collective-permute-start.19 = (bf16[4,1152]{1,0:T(4,128)(2,1)S(1)}, bf16[4,1152]{1,0:T(4,128)(2,1)S(1)}, u32[]{:S(2)}, u32[]{:S(2)}) collective-permute-start(bf16[4,1152]{1,0:T(4,128)(2,1)S(1)} %broadcast_select_fusion), channel_id=1, source_target_pairs={{0,1},{1,0},{2,3},{3,2},{4,5},{5,4},{6,7},{7,6},{8,9},{9,8},{10,11... | collective-permute-start | bytes 27656 | tf_op jit(solution)/shard_map/ppermute | solution.py:830
  18.9 44.9 %collective-permute-start = (bf16[6,64,768]{2,1,0:T(8,128)(2,1)S(1)}, bf16[6,64,768]{2,1,0:T(8,128)(2,1)}, u32[]{:S(2)}, u32[]{:S(2)}) collective-permute-start(bf16[6,64,768]{2,1,0:T(8,128)(2,1)S(1)} %bitcast.66), channel_id=1, source_target_pairs={{0,1},{1,2},{2,3},{4,5},{5,6},{6,7},{8,9},{9,10},{10,11},{12,13},{... | collective-permute-start | bytes 1769480 | tf_op jit(solution)/shard_map/ppermute | solution.py:895
  23.9 41.4 %collective-permute-start.1 = (bf16[12,64,768]{2,1,0:T(8,128)(2,1)S(1)}, bf16[12,64,768]{2,1,0:T(8,128)(2,1)}, u32[]{:S(2)}, u32[]{:S(2)}) collective-permute-start(bf16[12,64,768]{2,1,0:T(8,128)(2,1)S(1)} %bitcast.64), channel_id=1, source_target_pairs={{1,0},{2,1},{3,2},{5,4},{6,5},{7,6},{9,8},{10,9},{11,10},{13,12},{... | collective-permute-start | bytes 3538952 | tf_op jit(solution)/shard_map/ppermute | solution.py:896
  29.2 46.5 %copy-start.2 = (bf16[4,48,576]{2,1,0:T(8,128)(2,1)}, bf16[4,48,576]{2,1,0:T(8,128)(2,1)S(1)}, u32[]{:S(2)}) copy-start(bf16[4,48,576]{2,1,0:T(8,128)(2,1)S(1)} %pad_maximum_fusion.refs_0_) | copy-start | bytes 663556
  29.2 7.8 %collective-permute-start.5 = (bf16[4,48,576]{2,1,0:T(8,128)(2,1)S(1)}, bf16[4,48,576]{2,1,0:T(8,128)(2,1)S(1)}, u32[]{:S(2)}, u32[]{:S(2)}) collective-permute-start(bf16[4,48,576]{2,1,0:T(8,128)(2,1)S(1)} %pad_maximum_fusion.refs_0_), channel_id=1, source_target_pairs={{0,4},{4,0},{1,5},{5,1},{2,6},{6,2},{3,7},{7,3},{8,12},{12,8},{9,1... | collective-permute-start | bytes 663560 | tf_op jit(solution)/shard_map/ppermute | solution.py:830
  31.8 25.7 %collective-permute-start.7 = (bf16[4,48,576]{2,1,0:T(8,128)(2,1)}, bf16[4,48,576]{2,1,0:T(8,128)(2,1)S(1)}, u32[]{:S(2)}, u32[]{:S(2)}) collective-permute-start(bf16[4,48,576]{2,1,0:T(8,128)(2,1)} %pad_maximum_fusion.1.refs_4_), channel_id=1, source_target_pairs={{0,2},{2,0},{1,3},{3,1},{4,6},{6,4},{5,7},{7,5},{8,10},{10,8},{9,1... | collective-permute-start | bytes 663560 | tf_op jit(solution)/shard_map/ppermute | solution.py:830
  36.6 23.6 %collective-permute-start.9 = (bf16[4,48,576]{2,1,0:T(8,128)(2,1)S(1)}, bf16[4,48,576]{2,1,0:T(8,128)(2,1)}, u32[]{:S(2)}, u32[]{:S(2)}) collective-permute-start(bf16[4,48,576]{2,1,0:T(8,128)(2,1)S(1)} %pad_maximum_fusion.refs_0_), channel_id=1, source_target_pairs={{0,2},{2,0},{1,3},{3,1},{4,6},{6,4},{5,7},{7,5},{8,10},{10,8},{9,1... | collective-permute-start | bytes 663560 | tf_op jit(solution)/shard_map/ppermute | solution.py:830
  37.0 28.3 %copy-start.18 = (bf16[4,48,576]{2,1,0:T(8,128)(2,1)}, bf16[4,48,576]{2,1,0:T(8,128)(2,1)S(1)}, u32[]{:S(2)}) copy-start(bf16[4,48,576]{2,1,0:T(8,128)(2,1)S(1)} %collective-permute-done.5.refs_2_) | copy-start | bytes 663556
  37.0 25.8 %collective-permute-start.6 = (bf16[4,48,576]{2,1,0:T(8,128)(2,1)S(1)}, bf16[4,48,576]{2,1,0:T(8,128)(2,1)S(1)}, u32[]{:S(2)}, u32[]{:S(2)}) collective-permute-start(bf16[4,48,576]{2,1,0:T(8,128)(2,1)S(1)} %collective-permute-done.5.refs_2_), channel_id=1, source_target_pairs={{0,2},{2,0},{1,3},{3,1},{4,6},{6,4},{5,7},{7,5},{8,10},{10,8},{9,1... | collective-permute-start | bytes 663560 | tf_op jit(solution)/shard_map/ppermute | solution.py:830
  57.5 6.2 %collective-permute-start.8 = (bf16[4,48,576]{2,1,0:T(8,128)(2,1)S(1)}, bf16[4,48,576]{2,1,0:T(8,128)(2,1)S(1)}, u32[]{:S(2)}, u32[]{:S(2)}) collective-permute-start(bf16[4,48,576]{2,1,0:T(8,128)(2,1)S(1)} %collective-permute-done.7.refs_5_), channel_id=1, source_target_pairs={{0,4},{4,0},{1,5},{5,1},{2,6},{6,2},{3,7},{7,3},{8,12},{12,8},{9,1... | collective-permute-start | bytes 663560 | tf_op jit(solution)/shard_map/ppermute | solution.py:830
  60.3 15.4 %collective-permute-start.20 = (bf16[4,1152]{1,0:T(4,128)(2,1)S(1)}, bf16[4,1152]{1,0:T(4,128)(2,1)S(1)}, u32[]{:S(2)}, u32[]{:S(2)}) collective-permute-start(bf16[4,1152]{1,0:T(4,128)(2,1)S(1)} %fusion.19), channel_id=1, source_target_pairs={{0,2},{2,0},{1,3},{3,1},{4,6},{6,4},{5,7},{7,5},{8,10},{10,8},{9,1... | collective-permute-start | bytes 27656 | tf_op jit(solution)/shard_map/ppermute | solution.py:830
  62.8 13.2 %collective-permute-start.11 = (bf16[4,48,576]{2,1,0:T(8,128)(2,1)S(1)}, bf16[4,48,576]{2,1,0:T(8,128)(2,1)}, u32[]{:S(2)}, u32[]{:S(2)}) collective-permute-start(bf16[4,48,576]{2,1,0:T(8,128)(2,1)S(1)} %pad_maximum_fusion.refs_0_), channel_id=1, source_target_pairs={{0,1},{1,0},{2,3},{3,2},{4,5},{5,4},{6,7},{7,6},{8,9},{9,8},{10,11... | collective-permute-start | bytes 663560 | tf_op jit(solution)/shard_map/ppermute | solution.py:830
  63.7 12.8 %collective-permute-start.15 = (bf16[4,48,576]{2,1,0:T(8,128)(2,1)}, bf16[4,48,576]{2,1,0:T(8,128)(2,1)}, u32[]{:S(2)}, u32[]{:S(2)}) collective-permute-start(bf16[4,48,576]{2,1,0:T(8,128)(2,1)} %pad_maximum_fusion.1.refs_4_), channel_id=1, source_target_pairs={{0,1},{1,0},{2,3},{3,2},{4,5},{5,4},{6,7},{7,6},{8,9},{9,8},{10,11... | collective-permute-start | bytes 663560 | tf_op jit(solution)/shard_map/ppermute | solution.py:830
  63.7 12.5 %collective-permute-start.10 = (bf16[4,48,576]{2,1,0:T(8,128)(2,1)}, bf16[4,48,576]{2,1,0:T(8,128)(2,1)}, u32[]{:S(2)}, u32[]{:S(2)}) collective-permute-start(bf16[4,48,576]{2,1,0:T(8,128)(2,1)} %pad_maximum_fusion.1.refs_4_), channel_id=1, source_target_pairs={{0,4},{4,0},{1,5},{5,1},{2,6},{6,2},{3,7},{7,3},{8,12},{12,8},{9,1... | collective-permute-start | bytes 663560 | tf_op jit(solution)/shard_map/ppermute | solution.py:830
  65.3 11.4 %collective-permute-start.12 = (bf16[4,48,576]{2,1,0:T(8,128)(2,1)}, bf16[4,48,576]{2,1,0:T(8,128)(2,1)}, u32[]{:S(2)}, u32[]{:S(2)}) collective-permute-start(bf16[4,48,576]{2,1,0:T(8,128)(2,1)} %collective-permute-done.9.refs_1_), channel_id=1, source_target_pairs={{0,1},{1,0},{2,3},{3,2},{4,5},{5,4},{6,7},{7,6},{8,9},{9,8},{10,11... | collective-permute-start | bytes 663560 | tf_op jit(solution)/shard_map/ppermute | solution.py:830
  75.7 2.9 collective-permute-start.13
  76.1 2.5 collective-permute-start.16
  76.2 2.3 collective-permute-start.17
  76.6 2.7 collective-permute-start.14
  76.8 3.3 %collective-permute-start.18 = (bf16[4,48,576]{2,1,0:T(8,128)(2,1)}, bf16[4,48,576]{2,1,0:T(8,128)(2,1)}, u32[]{:S(2)}, u32[]{:S(2)}) collective-permute-start(bf16[4,48,576]{2,1,0:T(8,128)(2,1)} %copy-done.23), channel_id=1, source_target_pairs={{0,1},{1,0},{2,3},{3,2},{4,5},{5,4},{6,7},{7,6},{8,9},{9,8},{10,11... | collective-permute-start | bytes 663560 | tf_op jit(solution)/shard_map/ppermute | solution.py:830
  163.1 34.4 %collective-permute-start.22 = (bf16[2,4,2,96,192]{4,3,2,1,0:T(8,128)(2,1)}, bf16[2,4,2,96,192]{4,3,2,1,0:T(8,128)(2,1)}, u32[]{:S(2)}, u32[]{:S(2)}) collective-permute-start(bf16[2,4,2,96,192]{4,3,2,1,0:T(8,128)(2,1)} %get-tuple-element.142), channel_id=1, source_target_pairs={{0,1},{1,0},{2,3},{3,2},{4,5},{5,4},{6,7},{7,6},{8,9},{9,8},{10,11... | collective-permute-start | bytes 1769480 | tf_op jit(solution)/shard_map/ppermute | solution.py:830
  185.7 11.9 %collective-permute-start.21 = (bf16[4,2,96,576]{3,2,1,0:T(8,128)(2,1)}, bf16[4,2,96,576]{3,2,1,0:T(8,128)(2,1)}, u32[]{:S(2)}, u32[]{:S(2)}) collective-permute-start(bf16[4,2,96,576]{3,2,1,0:T(8,128)(2,1)} %get-tuple-element.140), channel_id=1, source_target_pairs={{0,1},{1,0},{2,3},{3,2},{4,5},{5,4},{6,7},{7,6},{8,9},{9,8},{10,11... | collective-permute-start | bytes 2654216 | tf_op jit(solution)/shard_map/ppermute | solution.py:830
  202.7 18.9 %copy-start.16 = (bf16[2,4,96,192]{3,2,1,0:T(8,128)(2,1)S(1)}, bf16[2,4,96,192]{3,2,1,0:T(8,128)(2,1)}, u32[]{:S(2)}) copy-start(bf16[2,4,96,192]{3,2,1,0:T(8,128)(2,1)} %get-tuple-element.162) | copy-start | bytes 884740
  216.7 36.7 %collective-permute-start.23 = (bf16[5,12,16,768]{3,2,1,0:T(8,128)(2,1)}, bf16[5,12,16,768]{3,2,1,0:T(8,128)(2,1)}, u32[]{:S(2)}, u32[]{:S(2)}) collective-permute-start(bf16[5,12,16,768]{3,2,1,0:T(8,128)(2,1)} %get-tuple-element.153), channel_id=1, source_target_pairs={{0,1},{1,2},{2,3},{4,5},{5,6},{6,7},{8,9},{9,10},{10,11},{12,13},{... | collective-permute-start | bytes 4423688 | tf_op jit(solution)/shard_map/ppermute | solution.py:954
  220.1 33.3 %collective-permute-start.24 = (bf16[5,8,16,768]{3,2,1,0:T(8,128)(2,1)}, bf16[5,8,16,768]{3,2,1,0:T(8,128)(2,1)}, u32[]{:S(2)}, u32[]{:S(2)}) collective-permute-start(bf16[5,8,16,768]{3,2,1,0:T(8,128)(2,1)} %get-tuple-element.154), channel_id=1, source_target_pairs={{1,0},{2,1},{3,2},{5,4},{6,5},{7,6},{9,8},{10,9},{11,10},{13,12},{... | collective-permute-start | bytes 2949128 | tf_op jit(solution)/shard_map/ppermute | solution.py:953
  221.6 14.2 %collective-permute-start.26 = (bf16[2,4,96,192]{3,2,1,0:T(8,128)(2,1)S(1)}, bf16[2,4,96,192]{3,2,1,0:T(8,128)(2,1)S(1)}, u32[]{:S(2)}, u32[]{:S(2)}) collective-permute-start(bf16[2,4,96,192]{3,2,1,0:T(8,128)(2,1)S(1)} %copy-done.16), channel_id=1, source_target_pairs={{0,4},{4,0},{1,5},{5,1},{2,6},{6,2},{3,7},{7,3},{8,12},{12,8},{9,1... | collective-permute-start | bytes 884744 | tf_op jit(solution)/shard_map/ppermute | solution.py:830
  222.9 26.8 %collective-permute-start.25 = (bf16[4,96,576]{2,1,0:T(8,128)(2,1)}, bf16[4,96,576]{2,1,0:T(8,128)(2,1)}, u32[]{:S(2)}, u32[]{:S(2)}) collective-permute-start(bf16[4,96,576]{2,1,0:T(8,128)(2,1)} %get-tuple-element.160), channel_id=1, source_target_pairs={{0,4},{4,0},{1,5},{5,1},{2,6},{6,2},{3,7},{7,3},{8,12},{12,8},{9,1... | collective-permute-start | bytes 1327112 | tf_op jit(solution)/shard_map/ppermute | solution.py:830
  234.5 26.3 %collective-permute-start.27 = (bf16[4,2,96,576]{3,2,1,0:T(8,128)(2,1)}, bf16[4,2,96,576]{3,2,1,0:T(8,128)(2,1)}, u32[]{:S(2)}, u32[]{:S(2)}) collective-permute-start(bf16[4,2,96,576]{3,2,1,0:T(8,128)(2,1)} %get-tuple-element.167), channel_id=1, source_target_pairs={{0,1},{1,0},{2,3},{3,2},{4,5},{5,4},{6,7},{7,6},{8,9},{9,8},{10,11... | collective-permute-start | bytes 2654216 | tf_op jit(solution)/shard_map/ppermute | solution.py:830
  253.4 23.4 %copy-start.28 = (bf16[4,96,192]{2,1,0:T(8,128)(2,1)S(1)}, bf16[4,96,192]{2,1,0:T(8,128)(2,1)}, u32[]{:S(2)}) copy-start(bf16[4,96,192]{2,1,0:T(8,128)(2,1)} %get-tuple-element.180) | copy-start | bytes 442372
  261.6 1.3 collective-permute-start.28
  262.9 5.3 %collective-permute-start.29 = (f32[26,512]{1,0:T(8,128)S(1)}, f32[26,512]{1,0:T(8,128)S(1)}, u32[]{:S(2)}, u32[]{:S(2)}) collective-permute-start(f32[26,512]{1,0:T(8,128)S(1)} %add.94), channel_id=1, source_target_pairs={{0,2},{2,0},{1,3},{3,1},{4,6},{6,4},{5,7},{7,5},{8,10},{10,8},{9,1... | collective-permute-start | bytes 159752 | tf_op jit(solution)/shard_map/ppermute | solution.py:830
  268.2 5.6 %collective-permute-start.30 = (f32[26,512]{1,0:T(8,128)S(1)}, f32[26,512]{1,0:T(8,128)S(1)}, u32[]{:S(2)}, u32[]{:S(2)}) collective-permute-start(f32[26,512]{1,0:T(8,128)S(1)} %add.95), channel_id=1, source_target_pairs={{0,4},{4,0},{1,5},{5,1},{2,6},{6,2},{3,7},{7,3},{8,12},{12,8},{9,1... | collective-permute-start | bytes 159752 | tf_op jit(solution)/shard_map/ppermute | solution.py:830
  273.8 6.3 %collective-permute-start.31 = (f32[26,512]{1,0:T(8,128)S(1)}, f32[26,512]{1,0:T(8,128)S(1)}, u32[]{:S(2)}, u32[]{:S(2)}) collective-permute-start(f32[26,512]{1,0:T(8,128)S(1)} %add.96), channel_id=1, source_target_pairs={{0,8},{8,0},{16,24},{24,16},{1,9},{9,1},{17,25},{25,17},{2,10},{10... | collective-permute-start | bytes 159752 | tf_op jit(solution)/shard_map/ppermute | solution.py:868
  276.8 13.9 %collective-permute-start.35 = (bf16[4,96,192]{2,1,0:T(8,128)(2,1)S(1)}, bf16[4,96,192]{2,1,0:T(8,128)(2,1)S(1)}, u32[]{:S(2)}, u32[]{:S(2)}) collective-permute-start(bf16[4,96,192]{2,1,0:T(8,128)(2,1)S(1)} %copy-done.28), channel_id=1, source_target_pairs={{0,2},{2,0},{1,3},{3,1},{4,6},{6,4},{5,7},{7,5},{8,10},{10,8},{9,1... | collective-permute-start | bytes 442376 | tf_op jit(solution)/shard_map/ppermute | solution.py:830
  277.2 16.1 %collective-permute-start.34 = (bf16[4,96,576]{2,1,0:T(8,128)(2,1)}, bf16[4,96,576]{2,1,0:T(8,128)(2,1)}, u32[]{:S(2)}, u32[]{:S(2)}) collective-permute-start(bf16[4,96,576]{2,1,0:T(8,128)(2,1)} %get-tuple-element.178), channel_id=1, source_target_pairs={{0,2},{2,0},{1,3},{3,1},{4,6},{6,4},{5,7},{7,5},{8,10},{10,8},{9,1... | collective-permute-start | bytes 1327112 | tf_op jit(solution)/shard_map/ppermute | solution.py:830
  280.1 8.5 %collective-permute-start.32 = (f32[26,512]{1,0:T(8,128)S(1)}, f32[26,512]{1,0:T(8,128)S(1)}, u32[]{:S(2)}, u32[]{:S(2)}) collective-permute-start(f32[26,512]{1,0:T(8,128)S(1)} %add.97), channel_id=1, source_target_pairs={{0,16},{8,24},{16,0},{24,8},{1,17},{9,25},{17,1},{25,9},{2,18},{10... | collective-permute-start | bytes 159752 | tf_op jit(solution)/shard_map/ppermute | solution.py:868
  285.3 11.7 %collective-permute-start.33 = (bf16[4,96,576]{2,1,0:T(8,128)(2,1)}, bf16[4,96,576]{2,1,0:T(8,128)(2,1)}, u32[]{:S(2)}, u32[]{:S(2)}) collective-permute-start(bf16[4,96,576]{2,1,0:T(8,128)(2,1)} %get-tuple-element.177), channel_id=1, source_target_pairs={{0,4},{4,0},{1,5},{5,1},{2,6},{6,2},{3,7},{7,3},{8,12},{12,8},{9,1... | collective-permute-start | bytes 1327112 | tf_op jit(solution)/shard_map/ppermute | solution.py:830
  301.4 8.8 %collective-permute-start.39 = (bf16[96,192]{1,0:T(8,128)(2,1)S(1)}, bf16[96,192]{1,0:T(8,128)(2,1)S(1)}, u32[]{:S(2)}, u32[]{:S(2)}) collective-permute-start(bf16[96,192]{1,0:T(8,128)(2,1)S(1)} %get-tuple-element.227), channel_id=1, source_target_pairs={{0,8},{8,16},{16,24},{24,0},{1,9},{9,17},{17,25},{25,1},{2,10},{10... | collective-permute-start | bytes 110600 | tf_op jit(solution)/shard_map/ppermute | solution.py:834
  303.6 7.7 %collective-permute-start.41 = (bf16[96,192]{1,0:T(8,128)(2,1)S(1)}, bf16[96,192]{1,0:T(8,128)(2,1)S(1)}, u32[]{:S(2)}, u32[]{:S(2)}) collective-permute-start(bf16[96,192]{1,0:T(8,128)(2,1)S(1)} %get-tuple-element.228), channel_id=1, source_target_pairs={{0,24},{8,0},{16,8},{24,16},{1,25},{9,1},{17,9},{25,17},{2,26},{10... | collective-permute-start | bytes 110600 | tf_op jit(solution)/shard_map/ppermute | solution.py:834
  305.3 8.3 %collective-permute-start.40 = (bf16[96,192]{1,0:T(8,128)(2,1)S(1)}, bf16[96,192]{1,0:T(8,128)(2,1)S(1)}, u32[]{:S(2)}, u32[]{:S(2)}) collective-permute-start(bf16[96,192]{1,0:T(8,128)(2,1)S(1)} %get-tuple-element.229), channel_id=1, source_target_pairs={{0,16},{8,24},{16,0},{24,8},{1,17},{9,25},{17,1},{25,9},{2,18},{10... | collective-permute-start | bytes 110600 | tf_op jit(solution)/shard_map/ppermute | solution.py:834
  306.3 8.7 %collective-permute-start.36 = (bf16[96,576]{1,0:T(8,128)(2,1)S(1)}, bf16[96,576]{1,0:T(8,128)(2,1)S(1)}, u32[]{:S(2)}, u32[]{:S(2)}) collective-permute-start(bf16[96,576]{1,0:T(8,128)(2,1)S(1)} %get-tuple-element.224), channel_id=1, source_target_pairs={{0,8},{8,16},{16,24},{24,0},{1,9},{9,17},{17,25},{25,1},{2,10},{10... | collective-permute-start | bytes 331784 | tf_op jit(solution)/shard_map/ppermute | solution.py:834
  308.2 6.8 %collective-permute-start.38 = (bf16[96,576]{1,0:T(8,128)(2,1)S(1)}, bf16[96,576]{1,0:T(8,128)(2,1)S(1)}, u32[]{:S(2)}, u32[]{:S(2)}) collective-permute-start(bf16[96,576]{1,0:T(8,128)(2,1)S(1)} %get-tuple-element.225), channel_id=1, source_target_pairs={{0,24},{8,0},{16,8},{24,16},{1,25},{9,1},{17,9},{25,17},{2,26},{10... | collective-permute-start | bytes 331784 | tf_op jit(solution)/shard_map/ppermute | solution.py:834
  310.2 10.9 %collective-permute-start.37 = (bf16[96,576]{1,0:T(8,128)(2,1)S(1)}, bf16[96,576]{1,0:T(8,128)(2,1)S(1)}, u32[]{:S(2)}, u32[]{:S(2)}) collective-permute-start(bf16[96,576]{1,0:T(8,128)(2,1)S(1)} %get-tuple-element.226), channel_id=1, source_target_pairs={{0,16},{8,24},{16,0},{24,8},{1,17},{9,25},{17,1},{25,9},{2,18},{10... | collective-permute-start | bytes 331784 | tf_op jit(solution)/shard_map/ppermute | solution.py:834
  (26 other events, 253.3 us)
Sparse Core Ops, SparseCore 0:
  11.5 95.9 all-gather.2
  163.3 149.3 reduce-scatter.1

commit v7 on v6

--- a/solution.py
+++ b/solution.py
@@ -895,6 +895,7 @@
     from_above = lax.ppermute(grid_x[rows - above :], pair, up_pairs)
     from_below = lax.ppermute(grid_x[:below], pair, down_pairs)
 
+    qkv_rows, up_weight = after(qkv_weight.reshape(depth, 3 * width), up_weight)
     rest = jnp.concatenate([up_weight, down_weight, output_weight, jnp.zeros((depth, 256 - width), BF)], 1)
     rest_all = lax.all_gather(rest, AXES, axis=0).reshape(2 * count, slots, depth, 2 * hidden + 256)
     biases = jnp.concatenate([qv_bias.reshape(-1), up_bias])
@@ -907,7 +908,7 @@
     vec_one = jnp.concatenate([first_gain[None], first_shift[None], jnp.zeros((6, D), BF)], 0).astype(F32)
     normed = windows(place, from_above, grid_x, from_below, vec_one)
     if fast:
-        pieces = spread_plane(qkv_weight.reshape(depth, 3 * width), count)
+        pieces = spread_plane(qkv_rows, count)
         normed, pieces[3], pieces[7] = after(normed, pieces[3], pieces[7])
         pieces += [swap(piece, "c") for piece in pieces]
     else:

time: 333 us -> 340 us (1.021)
  local copies, waits for them, and re-layouts: 19.3 us -> 23.3 us
  transfers between devices with their start and end apart: 44 -> 44, of which waited for: 16 -> 13; matrix products, arithmetic and copies ran while one was open for 7% -> 7% of each run, Pallas kernels for 38% -> 37%
where the time goes in v7:
time: 340 us; the launch traced here: 339 us
  Pallas kernels  176 us (52%)
  waiting for transfers between devices  66.2 us (19%)
  starting transfers between devices  50.7 us (15%)
  local copies, waits for them, and re-layouts  23.3 us (7%)
  between operations  14.6 us (4%)
  other arithmetic  8.04 us (2%)
    ppermute x27, waiting for transfers between devices, swap(): return lax.ppermute(value, axis, SWAP)  56 us
    pallas_call x1, Pallas kernels, feed(): pl.pallas_call(partial(feed_body, rows=rows), grid_spec=pltpu.PrefetchSca...  49 us
    pallas_call x2, Pallas kernels, attend_back(): pl.pallas_call(partial(attend_back_body, rows=rows), grid_spec=pltpu.Pref...  23 us
    pallas_call x2, Pallas kernels, project_grad(): pl.pallas_call(partial(project_grad_body, parts=parts), grid_spec=pltpu.P...  21.7 us
    ppermute x27, starting transfers between devices, swap(): return lax.ppermute(value, axis, SWAP)  19.7 us
    pallas_call x1, Pallas kernels, attend(): pl.pallas_call(partial(attend_body, rows=rows), grid_spec=pltpu.PrefetchS...  18.9 us
    pallas_call x4, Pallas kernels, fold(): pl.pallas_call(partial(fold_body, plan=plan), grid=(count,), in_specs=in_...  16.4 us
    pallas_call x1, Pallas kernels, project(): pl.pallas_call(partial(project_body, rows=rows, depth=depth), grid_spec=p...  15.2 us
  transfers between devices with their start and end apart: 44, of which 13 were waited for; matrix products, arithmetic and copies ran while one was open for 7% of the time, Pallas kernels for 37%

profile of v7, /device:TPU:0, one launch (start us, length us, event | category | flops | bytes accessed | tf_op | source)
XLA Modules:
  0.0 338.5 jit_solution(9565456224926646552)
XLA Ops:
  7.3 1.2 copy.39
  8.4 1.8 concatenate.68
  10.5 5.1 %collective-permute-start.4 = (bf16[96,576]{1,0:T(8,128)(2,1)S(1)}, bf16[96,576]{1,0:T(8,128)(2,1)}, u32[]{:S(2)}, u32[]{:S(2)}) collective-permute-start(bf16[96,576]{1,0:T(8,128)(2,1)S(1)} %copy.40), channel_id=1, source_target_pairs={{0,24},{8,0},{16,8},{24,16},{1,25},{9,1},{17,9},{25,17},{2,26},{10... | collective-permute-start | bytes 331784 | tf_op jit(solution)/shard_map/ppermute | solution.py:834
  15.6 1.0 collective-permute-start.2
  18.8 3.2 collective-permute-start
  24.2 1.3 collective-permute-start.1
  28.2 1.6 collective-permute-start.5
  29.8 2.6 collective-permute-start.7
  37.8 2.0 collective-permute-start.6
  39.9 17.9 %collective-permute-done.7.refs_5_ = bf16[4,48,576]{2,1,0:T(8,128)(2,1)S(1)} collective-permute-done((bf16[4,48,576]{2,1,0:T(8,128)(2,1)S(1)}, bf16[4,48,576]{2,1,0:T(8,128)(2,1)S(1)}, u32[]{:S(2)}, u32[]{:S(2)}) %collective-permute-start.7) | collective-permute-done | bytes 221216 | tf_op jit(solution)/shard_map/ppermute | solution.py:830
  57.7 1.5 collective-permute-start.8
  59.3 1.2 collective-permute-done.9.refs_1_
  60.5 2.5 collective-permute-done.6.refs_3_
  63.9 1.6 collective-permute-start.10
  65.7 10.1 %windows.1.nw_ref = bf16[2240,768]{1,0:T(8,128)(2,1)} custom-call(s32[6]{0:T(128)} %stack.54.place_ref, bf16[6,64,768]{2,1,0:T(8,128)(2,1)} %collective-permute-done.above_ref, bf16[16,64,768]{2,1,0:T(8,128)(2,1)} %bitcast.66, bf16[12,64,768]{2,1,0:T(8,128)(2,1)} %collective-permute-done.1.below_ref, f32[8,768]{1,0:T(8,128)} %maximum_convert_fusion.vec_ref), custom_call_target="tpu_custom_call" | custom-call | flops 8800000000 | bytes 24000000 | tf_op jit(solution)/shard_map/windows/pallas_call | solution.py:149
  80.9 15.2 %project.1 = (bf16[1280,768]{1,0:T(8,128)(2,1)}, bf16[2240,768]{1,0:T(8,128)(2,1)}, bf16[2240,768]{1,0:T(8,128)(2,1)}, bf16[768,2304]{1,0:T(8,128)(2,1)}, bf16[5...) custom-call(s32[6]{0:T(128)} %stack.54.place_ref, bf16[2240,768]{1,0:T(8,128)(2,1)} %windows.1.nw_ref, ...), custom_call_target="tpu_custom_call" | custom-call | flops 19800000512 | bytes 54000000 | tf_op jit(solution)/shard_map/project/pallas_call | solution.py:212
  96.1 18.9 %attend.1 = (bf16[1280,768]{1,0:T(8,128)(2,1)}, bf16[30,2,224,256]{3,2,1,0:T(8,128)(2,1)}) custom-call(s32[6]{0:T(128)} %stack.54.place_ref, bf16[1280,768]{1,0:T(8,128)(2,1)} %get-tuple-element.130.q_ref, bf16[2240,768]{1,0:T(8,128)(2,1)} %get-tuple-element.131.k_ref, bf16[2240,768]{1,0:T(8,128)(2,1)} %get-tuple-element.132.v_ref, ...), custom_call_target="tpu_custom_call" | custom-call | flops 26400000000 | bytes 72000000 | tf_op jit(solution)/shard_map/attend/pallas_call | solution.py:418
  115.0 49.0 %feed.1 = (bf16[1024,768]{1,0:T(8,128)(2,1)}, f32[1024,768]{1,0:T(8,128)}, bf16[5,16,16,768]{3,2,1,0:T(8,128)(2,1)}, bf16[8,4,96,1536]{3,2,1,0:T(8,128)(2,1)}, b...) custom-call(s32[6]{0:T(128)} %stack.54.place_ref, ...), custom_call_target="tpu_custom_call" | custom-call | flops 54999998464 | bytes 150000000 | tf_op jit(solution)/shard_map/feed/pallas_call | solution.py:699
  164.3 11.4 %attend_back.2 = (bf16[1280,384]{1,0:T(8,128)(2,1)}, bf16[2240,384]{1,0:T(8,128)(2,1)}, bf16[2240,384]{1,0:T(8,128)(2,1)}, f32[128,256]{1,0:T(8,128)}) custom-call(s32[6]{0:T(128)} %stack.54.place_ref, bf16[1280,768]{1,0:T(8,128)(2,1)} %get-tuple-element.130.q_ref, bf16[2240,768]{1,0:T(8,128)(2,1)} %get-tuple-element.131.k_ref, ...), custom_call_target="tpu_custom_call" | custom-call | flops 17600000000 | bytes 48000000 | tf_op jit(solution)/shard_map/attend_back/pallas_call | solution.py:532
  175.7 10.9 %project_grad.2 = (bf16[4,2,96,576]{3,2,1,0:T(8,128)(2,1)}, bf16[4,2,96,576]{3,2,1,0:T(8,128)(2,1)}, f32[2,384]{1,0:T(2,128)}) custom-call(s32[6]{0:T(128)} %stack.54.place_ref, bf16[5,768,448]{2,1,0:T(8,128)(2,1)} %get-tuple-element.136.turned_ref, bf16[5,768,256]{2,1,0:T(8,128)(2,1)} %get-tuple-element.137.own_ref, ...), custom_call_target="tpu_custom_call" | custom-call | flops 6600000000 | bytes 18000000 | tf_op jit(solution)/shard_map/project_grad/pallas_call | solution.py:278
  186.9 11.6 %attend_back.3 = (bf16[1280,384]{1,0:T(8,128)(2,1)}, bf16[2240,384]{1,0:T(8,128)(2,1)}, bf16[2240,384]{1,0:T(8,128)(2,1)}, f32[128,256]{1,0:T(8,128)}) custom-call(s32[6]{0:T(128)} %stack.54.place_ref, bf16[1280,768]{1,0:T(8,128)(2,1)} %get-tuple-element.130.q_ref, bf16[2240,768]{1,0:T(8,128)(2,1)} %get-tuple-element.131.k_ref, ...), custom_call_target="tpu_custom_call" | custom-call | flops 17600000000 | bytes 48000000 | tf_op jit(solution)/shard_map/attend_back/pallas_call | solution.py:532
  199.5 5.1 %fold.4 = (bf16[4,96,576]{2,1,0:T(8,128)(2,1)}, bf16[4,96,576]{2,1,0:T(8,128)(2,1)}, bf16[2,4,96,192]{3,2,1,0:T(8,128)(2,1)}, bf16[2,4,96,192]{3,2,1,0:T(8,128)(2,1)}) custom-call(bf16[4,2,96,576]{3,2,1,0:T(8,128)(2,1)} %get-tuple-element.143.refs_0_.refs_2_, bf16[4,2,96,576]{3,2,1,0:T(8,128)(2,1)} %copy-done.11, ...), custom_call_target="tpu_custom_call" | custom-call | flops 4344032256 | bytes 11847360 | tf_op jit(solution)/shard_map/fold/pallas_call | solution.py:813
  204.6 13.9 %project_back.1 = (bf16[5,8,16,768]{3,2,1,0:T(8,128)(2,1)}, f32[5,16,16,768]{3,2,1,0:T(8,128)}, bf16[5,12,16,768]{3,2,1,0:T(8,128)(2,1)}) custom-call(s32[6]{0:T(128)} %stack.54.place_ref, bf16[1280,384]{1,0:T(8,128)(2,1)} %get-tuple-element.140.dq_ref.refs_0_, bf16[1280,384]{1,0:T(8,128)(2,1)} %get-tuple-element.150.refs_1_.dq_ref, ...), custom_call_target="tpu_custom_call" | custom-call | flops 11000000512 | bytes 30000000 | tf_op jit(solution)/shard_map/project_back/pallas_call | solution.py:321
  218.5 3.3 collective-permute-start.23
  221.8 1.3 collective-permute-start.24
  224.2 1.1 collective-permute-start.25
  225.4 10.9 %project_grad.3 = (bf16[4,2,96,576]{3,2,1,0:T(8,128)(2,1)}, bf16[4,2,96,576]{3,2,1,0:T(8,128)(2,1)}, f32[2,384]{1,0:T(2,128)}) custom-call(s32[6]{0:T(128)} %stack.54.place_ref, bf16[5,768,448]{2,1,0:T(8,128)(2,1)} %get-tuple-element.136.turned_ref, bf16[5,768,256]{2,1,0:T(8,128)(2,1)} %get-tuple-element.137.own_ref, ...), custom_call_target="tpu_custom_call" | custom-call | flops 6600000000 | bytes 18000000 | tf_op jit(solution)/shard_map/project_grad/pallas_call | solution.py:278
  237.7 13.5 %collective-permute-done.25.refs_1_ = bf16[4,96,576]{2,1,0:T(8,128)(2,1)} collective-permute-done((bf16[4,96,576]{2,1,0:T(8,128)(2,1)S(1)}, bf16[4,96,576]{2,1,0:T(8,128)(2,1)}, u32[]{:S(2)}, u32[]{:S(2)}) %collective-permute-start.25) | collective-permute-done | bytes 442400 | tf_op jit(solution)/shard_map/ppermute | solution.py:830
  251.2 3.7 %fold.5 = (bf16[4,96,576]{2,1,0:T(8,128)(2,1)}, bf16[4,96,192]{2,1,0:T(8,128)(2,1)}, bf16[4,96,192]{2,1,0:T(8,128)(2,1)}) custom-call(bf16[4,96,576]{2,1,0:T(8,128)(2,1)} %get-tuple-element.163.refs_0_, bf16[4,96,576]{2,1,0:T(8,128)(2,1)} %collective-permute-done.25.refs_1_, bf16[2,4,96,192]{3,2,1,0:T(8,128)(2,1)} %get-tuple-element.165.refs_2_.refs_4_, ...), custom_call_target="tpu_custom_call" | custom-call | flops 2235411200 | bytes 6096576 | tf_op jit(solution)/shard_map/fold/pallas_call | solution.py:813
  254.9 7.5 %finish.1 = (bf16[16,64,768]{2,1,0:T(8,128)(2,1)}, f32[8,768]{1,0:T(8,128)}) custom-call(f32[5,16,16,768]{3,2,1,0:T(8,128)} %get-tuple-element.154.own_ref, bf16[5,12,16,768]{3,2,1,0:T(8,128)(2,1)} %collective-permute-done.23.head_ref, bf16[5,8,16,768]{3,2,1,0:T(8,128)(2,1)} %collective-permute-done.24.tail_ref, bf16[16,64,768]{2,1,0:T(8,128)(2,1)} %bitcast.67, ...), custom_call_target="tpu_custom_call" | custom-call | flops 6600000000 | bytes 18000000 | tf_op jit(solution)/shard_map/finish/pallas_call | solution.py:761
  265.3 4.7 %collective-permute-done.29 = f32[26,512]{1,0:T(8,128)S(1)} collective-permute-done((f32[26,512]{1,0:T(8,128)S(1)}, f32[26,512]{1,0:T(8,128)S(1)}, u32[]{:S(2)}, u32[]{:S(2)}) %collective-permute-start.29) | collective-permute-done | bytes 53280 | tf_op jit(solution)/shard_map/ppermute | solution.py:830
  270.8 3.7 %collective-permute-done.30 = f32[26,512]{1,0:T(8,128)S(1)} collective-permute-done((f32[26,512]{1,0:T(8,128)S(1)}, f32[26,512]{1,0:T(8,128)S(1)}, u32[]{:S(2)}, u32[]{:S(2)}) %collective-permute-start.30) | collective-permute-done | bytes 53280 | tf_op jit(solution)/shard_map/ppermute | solution.py:830
  274.6 6.7 %collective-permute-start.31 = (f32[26,512]{1,0:T(8,128)S(1)}, f32[26,512]{1,0:T(8,128)S(1)}, u32[]{:S(2)}, u32[]{:S(2)}) collective-permute-start(f32[26,512]{1,0:T(8,128)S(1)} %add.96), channel_id=1, source_target_pairs={{0,8},{8,0},{16,24},{24,16},{1,9},{9,1},{17,25},{25,17},{2,10},{10... | collective-permute-start | bytes 159752 | tf_op jit(solution)/shard_map/ppermute | solution.py:868
  281.4 1.9 collective-permute-start.34
  283.3 3.0 collective-permute-done.31
  286.5 4.1 %fold.6 = (bf16[4,96,576]{2,1,0:T(8,128)(2,1)}, bf16[4,96,576]{2,1,0:T(8,128)(2,1)}) custom-call(bf16[4,2,96,576]{3,2,1,0:T(8,128)(2,1)} %get-tuple-element.178.refs_0_.refs_2_, bf16[4,2,96,576]{3,2,1,0:T(8,128)(2,1)} %collective-permute-done.27.refs_1_.refs_3_, bf16[4,2,96,576]{3,2,1,0:T(8,128)(2,1)} %get-tuple-element.178.refs_0_.refs_2_, ...), custom_call_target="tpu_custom_call" | custom-call | flops 3046419200 | bytes 8308416 | tf_op jit(solution)/shard_map/fold/pallas_call | solution.py:813
  290.6 1.6 collective-permute-start.33
  294.3 5.1 %collective-permute-done.34.refs_2_ = bf16[4,96,576]{2,1,0:T(8,128)(2,1)} collective-permute-done((bf16[4,96,576]{2,1,0:T(8,128)(2,1)S(1)}, bf16[4,96,576]{2,1,0:T(8,128)(2,1)}, u32[]{:S(2)}, u32[]{:S(2)}) %collective-permute-start.34) | collective-permute-done | bytes 442400 | tf_op jit(solution)/shard_map/ppermute | solution.py:830
  299.5 5.4 %collective-permute-done.33.refs_1_ = bf16[4,96,576]{2,1,0:T(8,128)(2,1)} collective-permute-done((bf16[4,96,576]{2,1,0:T(8,128)(2,1)}, bf16[4,96,576]{2,1,0:T(8,128)(2,1)}, u32[]{:S(2)}, u32[]{:S(2)}) %collective-permute-start.33) | collective-permute-done | bytes 442400 | tf_op jit(solution)/shard_map/ppermute | solution.py:830
  304.9 3.5 %fold.7 = (bf16[4,96,576]{2,1,0:T(8,128)(2,1)}, bf16[4,96,192]{2,1,0:T(8,128)(2,1)}) custom-call(bf16[4,96,576]{2,1,0:T(8,128)(2,1)} %get-tuple-element.180.refs_0_, bf16[4,96,576]{2,1,0:T(8,128)(2,1)} %collective-permute-done.33.refs_1_, bf16[4,96,576]{2,1,0:T(8,128)(2,1)} %collective-permute-done.34.refs_2_, ...), custom_call_target="tpu_custom_call" | custom-call | flops 1992108800 | bytes 5433024 | tf_op jit(solution)/shard_map/fold/pallas_call | solution.py:813
  309.4 3.8 %collective-permute-start.41 = (bf16[96,192]{1,0:T(8,128)(2,1)S(1)}, bf16[96,192]{1,0:T(8,128)(2,1)S(1)}, u32[]{:S(2)}, u32[]{:S(2)}) collective-permute-start(bf16[96,192]{1,0:T(8,128)(2,1)S(1)} %get-tuple-element.232), channel_id=1, source_target_pairs={{0,24},{8,0},{16,8},{24,16},{1,25},{9,1},{17,9},{25,17},{2,26},{10... | collective-permute-start | bytes 110600 | tf_op jit(solution)/shard_map/ppermute | solution.py:834
  314.0 1.1 slice_bitcast_fusion.2
  315.2 3.8 %collective-permute-start.38 = (bf16[96,576]{1,0:T(8,128)(2,1)S(1)}, bf16[96,576]{1,0:T(8,128)(2,1)S(1)}, u32[]{:S(2)}, u32[]{:S(2)}) collective-permute-start(bf16[96,576]{1,0:T(8,128)(2,1)S(1)} %get-tuple-element.229), channel_id=1, source_target_pairs={{0,24},{8,0},{16,8},{24,16},{1,25},{9,1},{17,9},{25,17},{2,26},{10... | collective-permute-start | bytes 331784 | tf_op jit(solution)/shard_map/ppermute | solution.py:834
  319.2 1.5 fusion.11
  320.7 1.4 collective-permute-done.36
  322.1 5.7 %collective-permute-done.37 = bf16[96,576]{1,0:T(8,128)(2,1)S(1)} collective-permute-done((bf16[96,576]{1,0:T(8,128)(2,1)S(1)}, bf16[96,576]{1,0:T(8,128)(2,1)S(1)}, u32[]{:S(2)}, u32[]{:S(2)}) %collective-permute-start.37) | collective-permute-done | bytes 110624 | tf_op jit(solution)/shard_map/ppermute | solution.py:834
  327.8 1.0 fusion.1
  329.8 1.0 bitcast_convert_fusion
  (190 shorter events, 33.1 us)
Async XLA Ops:
  7.2 107.8 %all-gather.3.cloned.1.call-start = ((), (), s32[]{:S(2)}) async-start(), calls=%async_computation.2 | async-start | bytes 11354112 | tf_op jit(solution)/shard_map/all_gather | solution.py:900
  10.3 319.5 %reduce-scatter.2.cloned.1.call-start = ((), (), s32[]{:S(2)}) async-start(), calls=%async_computation.1 | async-start | bytes 9732096 | tf_op jit(solution)/shard_map/reduce_scatter | solution.py:933
  10.5 13.7 %collective-permute-start.4 = (bf16[96,576]{1,0:T(8,128)(2,1)S(1)}, bf16[96,576]{1,0:T(8,128)(2,1)}, u32[]{:S(2)}, u32[]{:S(2)}) collective-permute-start(bf16[96,576]{1,0:T(8,128)(2,1)S(1)} %copy.40), channel_id=1, source_target_pairs={{0,24},{8,0},{16,8},{24,16},{1,25},{9,1},{17,9},{25,17},{2,26},{10... | collective-permute-start | bytes 331784 | tf_op jit(solution)/shard_map/ppermute | solution.py:834
  15.6 10.7 %collective-permute-start.3 = (bf16[96,576]{1,0:T(8,128)(2,1)S(1)}, bf16[96,576]{1,0:T(8,128)(2,1)}, u32[]{:S(2)}, u32[]{:S(2)}) collective-permute-start(bf16[96,576]{1,0:T(8,128)(2,1)S(1)} %copy.40), channel_id=1, source_target_pairs={{0,16},{8,24},{16,0},{24,8},{1,17},{9,25},{17,1},{25,9},{2,18},{10... | collective-permute-start | bytes 331784 | tf_op jit(solution)/shard_map/ppermute | solution.py:834
  15.6 11.6 %collective-permute-start.2 = (bf16[96,576]{1,0:T(8,128)(2,1)S(1)}, bf16[96,576]{1,0:T(8,128)(2,1)}, u32[]{:S(2)}, u32[]{:S(2)}) collective-permute-start(bf16[96,576]{1,0:T(8,128)(2,1)S(1)} %copy.40), channel_id=1, source_target_pairs={{0,8},{8,16},{16,24},{24,0},{1,9},{9,17},{17,25},{25,1},{2,10},{10... | collective-permute-start | bytes 331784 | tf_op jit(solution)/shard_map/ppermute | solution.py:834
  18.7 19.1 %collective-permute-start.19 = (bf16[4,1152]{1,0:T(4,128)(2,1)}, bf16[4,1152]{1,0:T(4,128)(2,1)S(1)}, u32[]{:S(2)}, u32[]{:S(2)}) collective-permute-start(bf16[4,1152]{1,0:T(4,128)(2,1)} %broadcast_select_fusion), channel_id=1, source_target_pairs={{0,1},{1,0},{2,3},{3,2},{4,5},{5,4},{6,7},{7,6},{8,9},{9,8},{10,11... | collective-permute-start | bytes 27656 | tf_op jit(solution)/shard_map/ppermute | solution.py:830
  18.8 45.1 %collective-permute-start = (bf16[6,64,768]{2,1,0:T(8,128)(2,1)S(1)}, bf16[6,64,768]{2,1,0:T(8,128)(2,1)}, u32[]{:S(2)}, u32[]{:S(2)}) collective-permute-start(bf16[6,64,768]{2,1,0:T(8,128)(2,1)S(1)} %bitcast.70), channel_id=1, source_target_pairs={{0,1},{1,2},{2,3},{4,5},{5,6},{6,7},{8,9},{9,10},{10,11},{12,13},{... | collective-permute-start | bytes 1769480 | tf_op jit(solution)/shard_map/ppermute | solution.py:895
  24.2 41.3 %collective-permute-start.1 = (bf16[12,64,768]{2,1,0:T(8,128)(2,1)S(1)}, bf16[12,64,768]{2,1,0:T(8,128)(2,1)}, u32[]{:S(2)}, u32[]{:S(2)}) collective-permute-start(bf16[12,64,768]{2,1,0:T(8,128)(2,1)S(1)} %bitcast.68), channel_id=1, source_target_pairs={{1,0},{2,1},{3,2},{5,4},{6,5},{7,6},{9,8},{10,9},{11,10},{13,12},{... | collective-permute-start | bytes 3538952 | tf_op jit(solution)/shard_map/ppermute | solution.py:896
  28.1 47.6 %copy-start.1 = (bf16[4,48,576]{2,1,0:T(8,128)(2,1)}, bf16[4,48,576]{2,1,0:T(8,128)(2,1)S(1)}, u32[]{:S(2)}) copy-start(bf16[4,48,576]{2,1,0:T(8,128)(2,1)S(1)} %pad_maximum_fusion.refs_0_) | copy-start | bytes 663556
  28.2 9.7 %collective-permute-start.5 = (bf16[4,48,576]{2,1,0:T(8,128)(2,1)S(1)}, bf16[4,48,576]{2,1,0:T(8,128)(2,1)S(1)}, u32[]{:S(2)}, u32[]{:S(2)}) collective-permute-start(bf16[4,48,576]{2,1,0:T(8,128)(2,1)S(1)} %pad_maximum_fusion.refs_0_), channel_id=1, source_target_pairs={{0,4},{4,0},{1,5},{5,1},{2,6},{6,2},{3,7},{7,3},{8,12},{12,8},{9,1... | collective-permute-start | bytes 663560 | tf_op jit(solution)/shard_map/ppermute | solution.py:830
  29.8 46.0 %copy-start.2 = (bf16[4,48,576]{2,1,0:T(8,128)(2,1)}, bf16[4,48,576]{2,1,0:T(8,128)(2,1)S(1)}, u32[]{:S(2)}) copy-start(bf16[4,48,576]{2,1,0:T(8,128)(2,1)S(1)} %pad_maximum_fusion.1.refs_4_) | copy-start | bytes 663556
  29.8 27.9 %collective-permute-start.7 = (bf16[4,48,576]{2,1,0:T(8,128)(2,1)S(1)}, bf16[4,48,576]{2,1,0:T(8,128)(2,1)S(1)}, u32[]{:S(2)}, u32[]{:S(2)}) collective-permute-start(bf16[4,48,576]{2,1,0:T(8,128)(2,1)S(1)} %pad_maximum_fusion.1.refs_4_), channel_id=1, source_target_pairs={{0,2},{2,0},{1,3},{3,1},{4,6},{6,4},{5,7},{7,5},{8,10},{10,8},{9,1... | collective-permute-start | bytes 663560 | tf_op jit(solution)/shard_map/ppermute | solution.py:830
  37.8 22.6 %collective-permute-start.9 = (bf16[4,48,576]{2,1,0:T(8,128)(2,1)S(1)}, bf16[4,48,576]{2,1,0:T(8,128)(2,1)}, u32[]{:S(2)}, u32[]{:S(2)}) collective-permute-start(bf16[4,48,576]{2,1,0:T(8,128)(2,1)S(1)} %pad_maximum_fusion.refs_0_), channel_id=1, source_target_pairs={{0,2},{2,0},{1,3},{3,1},{4,6},{6,4},{5,7},{7,5},{8,10},{10,8},{9,1... | collective-permute-start | bytes 663560 | tf_op jit(solution)/shard_map/ppermute | solution.py:830
  37.8 27.7 %copy-start.14 = (bf16[4,48,576]{2,1,0:T(8,128)(2,1)}, bf16[4,48,576]{2,1,0:T(8,128)(2,1)S(1)}, u32[]{:S(2)}) copy-start(bf16[4,48,576]{2,1,0:T(8,128)(2,1)S(1)} %collective-permute-done.5.refs_2_) | copy-start | bytes 663556
  37.8 25.1 %collective-permute-start.6 = (bf16[4,48,576]{2,1,0:T(8,128)(2,1)S(1)}, bf16[4,48,576]{2,1,0:T(8,128)(2,1)S(1)}, u32[]{:S(2)}, u32[]{:S(2)}) collective-permute-start(bf16[4,48,576]{2,1,0:T(8,128)(2,1)S(1)} %collective-permute-done.5.refs_2_), channel_id=1, source_target_pairs={{0,2},{2,0},{1,3},{3,1},{4,6},{6,4},{5,7},{7,5},{8,10},{10,8},{9,1... | collective-permute-start | bytes 663560 | tf_op jit(solution)/shard_map/ppermute | solution.py:830
  57.7 6.2 %collective-permute-start.8 = (bf16[4,48,576]{2,1,0:T(8,128)(2,1)S(1)}, bf16[4,48,576]{2,1,0:T(8,128)(2,1)S(1)}, u32[]{:S(2)}, u32[]{:S(2)}) collective-permute-start(bf16[4,48,576]{2,1,0:T(8,128)(2,1)S(1)} %collective-permute-done.7.refs_5_), channel_id=1, source_target_pairs={{0,4},{4,0},{1,5},{5,1},{2,6},{6,2},{3,7},{7,3},{8,12},{12,8},{9,1... | collective-permute-start | bytes 663560 | tf_op jit(solution)/shard_map/ppermute | solution.py:830
  60.5 15.3 %collective-permute-start.20 = (bf16[4,1152]{1,0:T(4,128)(2,1)S(1)}, bf16[4,1152]{1,0:T(4,128)(2,1)S(1)}, u32[]{:S(2)}, u32[]{:S(2)}) collective-permute-start(bf16[4,1152]{1,0:T(4,128)(2,1)S(1)} %fusion.19), channel_id=1, source_target_pairs={{0,2},{2,0},{1,3},{3,1},{4,6},{6,4},{5,7},{7,5},{8,10},{10,8},{9,1... | collective-permute-start | bytes 27656 | tf_op jit(solution)/shard_map/ppermute | solution.py:830
  63.0 13.2 %collective-permute-start.11 = (bf16[4,48,576]{2,1,0:T(8,128)(2,1)S(1)}, bf16[4,48,576]{2,1,0:T(8,128)(2,1)}, u32[]{:S(2)}, u32[]{:S(2)}) collective-permute-start(bf16[4,48,576]{2,1,0:T(8,128)(2,1)S(1)} %pad_maximum_fusion.refs_0_), channel_id=1, source_target_pairs={{0,1},{1,0},{2,3},{3,2},{4,5},{5,4},{6,7},{7,6},{8,9},{9,8},{10,11... | collective-permute-start | bytes 663560 | tf_op jit(solution)/shard_map/ppermute | solution.py:830
  63.9 12.8 %collective-permute-start.15 = (bf16[4,48,576]{2,1,0:T(8,128)(2,1)S(1)}, bf16[4,48,576]{2,1,0:T(8,128)(2,1)}, u32[]{:S(2)}, u32[]{:S(2)}) collective-permute-start(bf16[4,48,576]{2,1,0:T(8,128)(2,1)S(1)} %pad_maximum_fusion.1.refs_4_), channel_id=1, source_target_pairs={{0,1},{1,0},{2,3},{3,2},{4,5},{5,4},{6,7},{7,6},{8,9},{9,8},{10,11... | collective-permute-start | bytes 663560 | tf_op jit(solution)/shard_map/ppermute | solution.py:830
  63.9 12.4 %collective-permute-start.10 = (bf16[4,48,576]{2,1,0:T(8,128)(2,1)S(1)}, bf16[4,48,576]{2,1,0:T(8,128)(2,1)}, u32[]{:S(2)}, u32[]{:S(2)}) collective-permute-start(bf16[4,48,576]{2,1,0:T(8,128)(2,1)S(1)} %pad_maximum_fusion.1.refs_4_), channel_id=1, source_target_pairs={{0,4},{4,0},{1,5},{5,1},{2,6},{6,2},{3,7},{7,3},{8,12},{12,8},{9,1... | collective-permute-start | bytes 663560 | tf_op jit(solution)/shard_map/ppermute | solution.py:830
  65.5 11.4 %collective-permute-start.12 = (bf16[4,48,576]{2,1,0:T(8,128)(2,1)}, bf16[4,48,576]{2,1,0:T(8,128)(2,1)}, u32[]{:S(2)}, u32[]{:S(2)}) collective-permute-start(bf16[4,48,576]{2,1,0:T(8,128)(2,1)} %collective-permute-done.9.refs_1_), channel_id=1, source_target_pairs={{0,1},{1,0},{2,3},{3,2},{4,5},{5,4},{6,7},{7,6},{8,9},{9,8},{10,11... | collective-permute-start | bytes 663560 | tf_op jit(solution)/shard_map/ppermute | solution.py:830
  75.8 2.9 collective-permute-start.13
  76.2 3.2 collective-permute-start.16
  76.3 3.0 collective-permute-start.17
  76.7 3.4 %collective-permute-start.14 = (bf16[4,48,576]{2,1,0:T(8,128)(2,1)}, bf16[4,48,576]{2,1,0:T(8,128)(2,1)S(1)}, u32[]{:S(2)}, u32[]{:S(2)}) collective-permute-start(bf16[4,48,576]{2,1,0:T(8,128)(2,1)} %copy-done.17), channel_id=1, source_target_pairs={{0,1},{1,0},{2,3},{3,2},{4,5},{5,4},{6,7},{7,6},{8,9},{9,8},{10,11... | collective-permute-start | bytes 663560 | tf_op jit(solution)/shard_map/ppermute | solution.py:830
  76.9 3.2 collective-permute-start.18
  164.0 34.5 %collective-permute-start.22 = (bf16[2,4,2,96,192]{4,3,2,1,0:T(8,128)(2,1)}, bf16[2,4,2,96,192]{4,3,2,1,0:T(8,128)(2,1)}, u32[]{:S(2)}, u32[]{:S(2)}) collective-permute-start(bf16[2,4,2,96,192]{4,3,2,1,0:T(8,128)(2,1)} %get-tuple-element.146), channel_id=1, source_target_pairs={{0,1},{1,0},{2,3},{3,2},{4,5},{5,4},{6,7},{7,6},{8,9},{9,8},{10,11... | collective-permute-start | bytes 1769480 | tf_op jit(solution)/shard_map/ppermute | solution.py:830
  186.6 11.9 %collective-permute-start.21 = (bf16[4,2,96,576]{3,2,1,0:T(8,128)(2,1)}, bf16[4,2,96,576]{3,2,1,0:T(8,128)(2,1)S(1)}, u32[]{:S(2)}, u32[]{:S(2)}) collective-permute-start(bf16[4,2,96,576]{3,2,1,0:T(8,128)(2,1)} %get-tuple-element.144), channel_id=1, source_target_pairs={{0,1},{1,0},{2,3},{3,2},{4,5},{5,4},{6,7},{7,6},{8,9},{9,8},{10,11... | collective-permute-start | bytes 2654216 | tf_op jit(solution)/shard_map/ppermute | solution.py:830
  218.5 36.4 %collective-permute-start.23 = (bf16[5,12,16,768]{3,2,1,0:T(8,128)(2,1)}, bf16[5,12,16,768]{3,2,1,0:T(8,128)(2,1)}, u32[]{:S(2)}, u32[]{:S(2)}) collective-permute-start(bf16[5,12,16,768]{3,2,1,0:T(8,128)(2,1)} %get-tuple-element.157), channel_id=1, source_target_pairs={{0,1},{1,2},{2,3},{4,5},{5,6},{6,7},{8,9},{9,10},{10,11},{12,13},{... | collective-permute-start | bytes 4423688 | tf_op jit(solution)/shard_map/ppermute | solution.py:955
  221.8 33.0 %collective-permute-start.24 = (bf16[5,8,16,768]{3,2,1,0:T(8,128)(2,1)}, bf16[5,8,16,768]{3,2,1,0:T(8,128)(2,1)}, u32[]{:S(2)}, u32[]{:S(2)}) collective-permute-start(bf16[5,8,16,768]{3,2,1,0:T(8,128)(2,1)} %get-tuple-element.158), channel_id=1, source_target_pairs={{1,0},{2,1},{3,2},{5,4},{6,5},{7,6},{9,8},{10,9},{11,10},{13,12},{... | collective-permute-start | bytes 2949128 | tf_op jit(solution)/shard_map/ppermute | solution.py:954
  223.3 14.3 %collective-permute-start.26 = (bf16[2,4,96,192]{3,2,1,0:T(8,128)(2,1)}, bf16[2,4,96,192]{3,2,1,0:T(8,128)(2,1)}, u32[]{:S(2)}, u32[]{:S(2)}) collective-permute-start(bf16[2,4,96,192]{3,2,1,0:T(8,128)(2,1)} %get-tuple-element.166), channel_id=1, source_target_pairs={{0,4},{4,0},{1,5},{5,1},{2,6},{6,2},{3,7},{7,3},{8,12},{12,8},{9,1... | collective-permute-start | bytes 884744 | tf_op jit(solution)/shard_map/ppermute | solution.py:830
  224.2 27.0 %collective-permute-start.25 = (bf16[4,96,576]{2,1,0:T(8,128)(2,1)S(1)}, bf16[4,96,576]{2,1,0:T(8,128)(2,1)}, u32[]{:S(2)}, u32[]{:S(2)}) collective-permute-start(bf16[4,96,576]{2,1,0:T(8,128)(2,1)S(1)} %copy-done.13), channel_id=1, source_target_pairs={{0,4},{4,0},{1,5},{5,1},{2,6},{6,2},{3,7},{7,3},{8,12},{12,8},{9,1... | collective-permute-start | bytes 1327112 | tf_op jit(solution)/shard_map/ppermute | solution.py:830
  236.3 26.1 %collective-permute-start.27 = (bf16[4,2,96,576]{3,2,1,0:T(8,128)(2,1)}, bf16[4,2,96,576]{3,2,1,0:T(8,128)(2,1)}, u32[]{:S(2)}, u32[]{:S(2)}) collective-permute-start(bf16[4,2,96,576]{3,2,1,0:T(8,128)(2,1)} %get-tuple-element.171), channel_id=1, source_target_pairs={{0,1},{1,0},{2,3},{3,2},{4,5},{5,4},{6,7},{7,6},{8,9},{9,8},{10,11... | collective-permute-start | bytes 2654216 | tf_op jit(solution)/shard_map/ppermute | solution.py:830
  254.9 26.5 %copy-start.12 = (bf16[4,96,576]{2,1,0:T(8,128)(2,1)S(1)}, bf16[4,96,576]{2,1,0:T(8,128)(2,1)}, u32[]{:S(2)}) copy-start(bf16[4,96,576]{2,1,0:T(8,128)(2,1)} %get-tuple-element.182) | copy-start | bytes 1327108
  263.2 1.6 collective-permute-start.28
  264.9 5.1 %collective-permute-start.29 = (f32[26,512]{1,0:T(8,128)S(1)}, f32[26,512]{1,0:T(8,128)S(1)}, u32[]{:S(2)}, u32[]{:S(2)}) collective-permute-start(f32[26,512]{1,0:T(8,128)S(1)} %add.94), channel_id=1, source_target_pairs={{0,2},{2,0},{1,3},{3,1},{4,6},{6,4},{5,7},{7,5},{8,10},{10,8},{9,1... | collective-permute-start | bytes 159752 | tf_op jit(solution)/shard_map/ppermute | solution.py:830
  270.0 4.5 %collective-permute-start.30 = (f32[26,512]{1,0:T(8,128)S(1)}, f32[26,512]{1,0:T(8,128)S(1)}, u32[]{:S(2)}, u32[]{:S(2)}) collective-permute-start(f32[26,512]{1,0:T(8,128)S(1)} %add.95), channel_id=1, source_target_pairs={{0,4},{4,0},{1,5},{5,1},{2,6},{6,2},{3,7},{7,3},{8,12},{12,8},{9,1... | collective-permute-start | bytes 159752 | tf_op jit(solution)/shard_map/ppermute | solution.py:830
  274.6 11.8 %collective-permute-start.31 = (f32[26,512]{1,0:T(8,128)S(1)}, f32[26,512]{1,0:T(8,128)S(1)}, u32[]{:S(2)}, u32[]{:S(2)}) collective-permute-start(f32[26,512]{1,0:T(8,128)S(1)} %add.96), channel_id=1, source_target_pairs={{0,8},{8,0},{16,24},{24,16},{1,9},{9,1},{17,25},{25,17},{2,10},{10... | collective-permute-start | bytes 159752 | tf_op jit(solution)/shard_map/ppermute | solution.py:868
  281.3 13.0 %collective-permute-start.35 = (bf16[4,96,192]{2,1,0:T(8,128)(2,1)S(1)}, bf16[4,96,192]{2,1,0:T(8,128)(2,1)}, u32[]{:S(2)}, u32[]{:S(2)}) collective-permute-start(bf16[4,96,192]{2,1,0:T(8,128)(2,1)S(1)} %copy-done.23), channel_id=1, source_target_pairs={{0,2},{2,0},{1,3},{3,1},{4,6},{6,4},{5,7},{7,5},{8,10},{10,8},{9,1... | collective-permute-start | bytes 442376 | tf_op jit(solution)/shard_map/ppermute | solution.py:830
  281.4 18.0 %collective-permute-start.34 = (bf16[4,96,576]{2,1,0:T(8,128)(2,1)S(1)}, bf16[4,96,576]{2,1,0:T(8,128)(2,1)}, u32[]{:S(2)}, u32[]{:S(2)}) collective-permute-start(bf16[4,96,576]{2,1,0:T(8,128)(2,1)S(1)} %copy-done.12), channel_id=1, source_target_pairs={{0,2},{2,0},{1,3},{3,1},{4,6},{6,4},{5,7},{7,5},{8,10},{10,8},{9,1... | collective-permute-start | bytes 1327112 | tf_op jit(solution)/shard_map/ppermute | solution.py:830
  286.4 5.8 %collective-permute-start.32 = (f32[26,512]{1,0:T(8,128)S(1)}, f32[26,512]{1,0:T(8,128)S(1)}, u32[]{:S(2)}, u32[]{:S(2)}) collective-permute-start(f32[26,512]{1,0:T(8,128)S(1)} %add.97), channel_id=1, source_target_pairs={{0,16},{8,24},{16,0},{24,8},{1,17},{9,25},{17,1},{25,9},{2,18},{10... | collective-permute-start | bytes 159752 | tf_op jit(solution)/shard_map/ppermute | solution.py:868
  290.6 14.3 %collective-permute-start.33 = (bf16[4,96,576]{2,1,0:T(8,128)(2,1)}, bf16[4,96,576]{2,1,0:T(8,128)(2,1)}, u32[]{:S(2)}, u32[]{:S(2)}) collective-permute-start(bf16[4,96,576]{2,1,0:T(8,128)(2,1)} %get-tuple-element.181), channel_id=1, source_target_pairs={{0,4},{4,0},{1,5},{5,1},{2,6},{6,2},{3,7},{7,3},{8,12},{12,8},{9,1... | collective-permute-start | bytes 1327112 | tf_op jit(solution)/shard_map/ppermute | solution.py:830
  309.3 9.6 %collective-permute-start.39 = (bf16[96,192]{1,0:T(8,128)(2,1)S(1)}, bf16[96,192]{1,0:T(8,128)(2,1)S(1)}, u32[]{:S(2)}, u32[]{:S(2)}) collective-permute-start(bf16[96,192]{1,0:T(8,128)(2,1)S(1)} %get-tuple-element.231), channel_id=1, source_target_pairs={{0,8},{8,16},{16,24},{24,0},{1,9},{9,17},{17,25},{25,1},{2,10},{10... | collective-permute-start | bytes 110600 | tf_op jit(solution)/shard_map/ppermute | solution.py:834
  309.4 9.9 %collective-permute-start.41 = (bf16[96,192]{1,0:T(8,128)(2,1)S(1)}, bf16[96,192]{1,0:T(8,128)(2,1)S(1)}, u32[]{:S(2)}, u32[]{:S(2)}) collective-permute-start(bf16[96,192]{1,0:T(8,128)(2,1)S(1)} %get-tuple-element.232), channel_id=1, source_target_pairs={{0,24},{8,0},{16,8},{24,16},{1,25},{9,1},{17,9},{25,17},{2,26},{10... | collective-permute-start | bytes 110600 | tf_op jit(solution)/shard_map/ppermute | solution.py:834
  313.2 6.1 %collective-permute-start.40 = (bf16[96,192]{1,0:T(8,128)(2,1)S(1)}, bf16[96,192]{1,0:T(8,128)(2,1)S(1)}, u32[]{:S(2)}, u32[]{:S(2)}) collective-permute-start(bf16[96,192]{1,0:T(8,128)(2,1)S(1)} %get-tuple-element.233), channel_id=1, source_target_pairs={{0,16},{8,24},{16,0},{24,8},{1,17},{9,25},{17,1},{25,9},{2,18},{10... | collective-permute-start | bytes 110600 | tf_op jit(solution)/shard_map/ppermute | solution.py:834
  315.0 7.1 %collective-permute-start.36 = (bf16[96,576]{1,0:T(8,128)(2,1)S(1)}, bf16[96,576]{1,0:T(8,128)(2,1)S(1)}, u32[]{:S(2)}, u32[]{:S(2)}) collective-permute-start(bf16[96,576]{1,0:T(8,128)(2,1)S(1)} %get-tuple-element.228), channel_id=1, source_target_pairs={{0,8},{8,16},{16,24},{24,0},{1,9},{9,17},{17,25},{25,1},{2,10},{10... | collective-permute-start | bytes 331784 | tf_op jit(solution)/shard_map/ppermute | solution.py:834
  315.2 7.0 %collective-permute-start.38 = (bf16[96,576]{1,0:T(8,128)(2,1)S(1)}, bf16[96,576]{1,0:T(8,128)(2,1)S(1)}, u32[]{:S(2)}, u32[]{:S(2)}) collective-permute-start(bf16[96,576]{1,0:T(8,128)(2,1)S(1)} %get-tuple-element.229), channel_id=1, source_target_pairs={{0,24},{8,0},{16,8},{24,16},{1,25},{9,1},{17,9},{25,17},{2,26},{10... | collective-permute-start | bytes 331784 | tf_op jit(solution)/shard_map/ppermute | solution.py:834
  318.9 8.9 %collective-permute-start.37 = (bf16[96,576]{1,0:T(8,128)(2,1)S(1)}, bf16[96,576]{1,0:T(8,128)(2,1)S(1)}, u32[]{:S(2)}, u32[]{:S(2)}) collective-permute-start(bf16[96,576]{1,0:T(8,128)(2,1)S(1)} %get-tuple-element.230), channel_id=1, source_target_pairs={{0,16},{8,24},{16,0},{24,8},{1,17},{9,25},{17,1},{25,9},{2,18},{10... | collective-permute-start | bytes 331784 | tf_op jit(solution)/shard_map/ppermute | solution.py:834
  (20 other events, 203.6 us)
Sparse Core Ops, SparseCore 0:
  11.5 95.9 all-gather.2
  164.2 145.4 reduce-scatter.1
